TPU v7x, 32 devices: a whole 2x2x4 slice. The times are simulated.
32 devices in a mesh: grp: 16 (over z, x, core), uly: 2 (over y).
Axes of the slice: x: 2, y: 2, z: 4, core: 2. Of those that a mesh axis runs over, the one named last changes fastest.
Arguments:
- queries: bfloat16 [4096, 32, 128], P(('grp', 'uly')), may hold values from -16 to 16
- keys: bfloat16 [4096, 4, 128], P(('grp', 'uly')), may hold values from -8 to 8
- values: bfloat16 [4096, 4, 128], P(('grp', 'uly')), may hold values from -6 to 6
- output_cotangent: bfloat16 [4096, 32, 128], P(('grp', 'uly')), may hold values from -6 to 6
- block_lists: int32 [128, 1], replicated, may hold values from 0 to 127, as said below
- list_counts: int32 [128], replicated, may hold values from 0 to 1, as said below
Outputs:
- attended: bfloat16 [4096, 32, 128], P(('grp', 'uly'))
- query_grad: bfloat16 [4096, 32, 128], P(('grp', 'uly'))
- key_gradient: bfloat16 [4096, 4, 128], P(('grp', 'uly'))
- value_gradient: bfloat16 [4096, 4, 128], P(('grp', 'uly'))
Inputs may be any that keep to these rules, and one draw needn't show every extreme that they name: `block_lists`: calling an aligned run of 8 blocks a group: every entry of block b's list is a block of another group than b's, and the entries of all lists of one group, counted or not, lie in pairwise different groups. `list_counts`: some block counts all 1 entries in every draw.
All inputs are finite; a program needn't handle non-finite values.
Results may differ from a plain program's by a relative error of at most 0.039.
Values may be sent and summed in bfloat16 or wider, within the bound.
No kernel may reach another device: no remote copies, remote signals or barrier semaphores. Data moves between devices by JAX's collectives and lax.ppermute only.
A program may use at most 128 MiB of HBM per device.

v0:
```python
import jax
import jax.numpy as jnp
from jax import lax
from jax.sharding import PartitionSpec as P


def on_device(queries, keys, values, output_cotangent, block_lists, list_counts):
    uly_count = lax.axis_size("uly")
    grp_count = lax.axis_size("grp")
    my_group = lax.axis_index("grp")
    tokens, head_count, head_width = queries.shape
    kv_heads = keys.shape[1]
    copies = max(1, uly_count // kv_heads)
    blocks_all, remote = block_lists.shape
    per_group = blocks_all // grp_count
    block_tok = tokens * uly_count // per_group
    group_tok = tokens * uly_count
    score_scale = head_width ** (-0.5)
    lists = block_lists.reshape(grp_count, per_group, remote)
    counted = (jnp.arange(remote)[None, :] < list_counts[:, None]).reshape(
        grp_count, per_group, remote
    )
    wanted = (lists // per_group == my_group) & counted
    send_place = jnp.sum(jnp.where(wanted, lists % per_group, 0), axis=(1, 2))
    sending = jnp.any(wanted, axis=(1, 2))
    mine_source = lax.dynamic_index_in_dim(lists, my_group, 0, keepdims=False) // per_group
    mine_counted = lax.dynamic_index_in_dim(counted, my_group, 0, keepdims=False)
    trip_count = jnp.max(jnp.sum(mine_counted.astype(jnp.int32), axis=1))

    def to_blocks(array_in):
        return array_in.reshape((per_group, block_tok) + array_in.shape[1:])

    keys_wide = jnp.repeat(keys, copies, axis=1)
    values_wide = jnp.repeat(values, copies, axis=1)
    query_heads, grad_heads, key_heads, value_heads = (
        lax.all_to_all(queries, "uly", split_axis=1, concat_axis=0, tiled=True),
        lax.all_to_all(output_cotangent, "uly", split_axis=1, concat_axis=0, tiled=True),
        lax.all_to_all(keys_wide, "uly", split_axis=1, concat_axis=0, tiled=True),
        lax.all_to_all(values_wide, "uly", split_axis=1, concat_axis=0, tiled=True),
    )
    stacked = jnp.stack([to_blocks(key_heads), to_blocks(value_heads)])
    outgoing = jnp.take(stacked, send_place, axis=1)
    arrived = lax.all_to_all(outgoing, "grp", split_axis=1, concat_axis=1, tiled=True)
    kv_local = key_heads.shape[1]
    heads_local = query_heads.shape[1]
    heads_per_group = heads_local // kv_local
    query_blk = query_heads.reshape(per_group, block_tok, kv_local, heads_per_group, head_width)
    grad_blk = grad_heads.reshape(per_group, block_tok, kv_local, heads_per_group, head_width)
    key_blk = to_blocks(key_heads)
    value_blk = to_blocks(value_heads)
    far_keys = arrived[0]
    far_values = arrived[1]
    causal = jnp.arange(block_tok)[:, None] >= jnp.arange(block_tok)[None, :]

    def logits(key_rows):
        return (
            jnp.einsum("pqkgd,pjkd->pkgqj", query_blk, key_rows, preferred_element_type=jnp.float32)
            * score_scale
        )

    def slot_rows(slot_index):
        source = lax.dynamic_index_in_dim(mine_source, slot_index, 1, keepdims=False)
        counted_slot = lax.dynamic_index_in_dim(mine_counted, slot_index, 1, keepdims=False)
        return (
            jnp.take(far_keys, source, axis=0),
            jnp.take(far_values, source, axis=0),
            counted_slot,
            source,
        )

    def masked(scores, counted_slot):
        return jnp.where(counted_slot[:, None, None, None, None], scores, -jnp.inf)

    near_scores = jnp.where(causal, logits(key_blk), -jnp.inf)
    highest = jnp.max(near_scores, axis=-1)
    denominator = jnp.sum(jnp.exp(near_scores - highest[..., None]), axis=-1)

    def max_sweep(slot_index, state_pair):
        highest, denominator = state_pair
        key_rows, value_rows, counted_slot, source = slot_rows(slot_index)
        scores = masked(logits(key_rows), counted_slot)
        new_highest = jnp.maximum(highest, jnp.max(scores, axis=-1))
        denominator = denominator * jnp.exp(highest - new_highest) + jnp.sum(
            jnp.exp(scores - new_highest[..., None]), axis=-1
        )
        return (new_highest, denominator)

    highest, denominator = lax.fori_loop(0, trip_count, max_sweep, (highest, denominator))
    log_total = highest + jnp.log(denominator)

    def softmax_weights(scores):
        return jnp.exp(scores - log_total[..., None])

    summed = jnp.einsum(
        "pkgqj,pjkd->pqkgd",
        softmax_weights(near_scores).astype(jnp.bfloat16),
        value_blk,
        preferred_element_type=jnp.float32,
    )

    def value_sweep(slot_index, summed):
        key_rows, value_rows, counted_slot, source = slot_rows(slot_index)
        weights = softmax_weights(masked(logits(key_rows), counted_slot)).astype(jnp.bfloat16)
        return summed + jnp.einsum(
            "pkgqj,pjkd->pqkgd", weights, value_rows, preferred_element_type=jnp.float32
        )

    summed = lax.fori_loop(0, trip_count, value_sweep, summed)
    attended_blk = summed.astype(jnp.bfloat16)
    row_delta = jnp.transpose(
        jnp.sum(grad_blk.astype(jnp.float32) * attended_blk.astype(jnp.float32), axis=-1),
        (0, 2, 3, 1),
    )

    def backward(scores, key_rows, value_rows):
        probs = softmax_weights(scores)
        weights = probs.astype(jnp.bfloat16)
        dprobs = jnp.einsum(
            "pqkgd,pjkd->pkgqj", grad_blk, value_rows, preferred_element_type=jnp.float32
        )
        dscores = (probs * (dprobs - row_delta[..., None])).astype(jnp.bfloat16)
        query_term = jnp.einsum(
            "pkgqj,pjkd->pqkgd", dscores, key_rows, preferred_element_type=jnp.float32
        )
        key_term = (
            jnp.einsum("pkgqj,pqkgd->pjkd", dscores, query_blk, preferred_element_type=jnp.float32)
            * score_scale
        )
        value_term = jnp.einsum(
            "pkgqj,pqkgd->pjkd", weights, grad_blk, preferred_element_type=jnp.float32
        )
        return (query_term, key_term, value_term)

    query_sum, key_near, value_near = backward(near_scores, key_blk, value_blk)
    far_grads = jnp.zeros((2, grp_count, block_tok, kv_local, head_width), jnp.float32)

    def grad_sweep(slot_index, state_pair):
        query_sum, far_grads = state_pair
        key_rows, value_rows, counted_slot, source = slot_rows(slot_index)
        query_term, key_term, value_term = backward(
            masked(logits(key_rows), counted_slot), key_rows, value_rows
        )
        routing = (
            (source[:, None] == jnp.arange(grp_count)[None, :]) & counted_slot[:, None]
        ).astype(jnp.float32)
        routed = jnp.einsum(
            "ps,xpjkd->xsjkd",
            routing,
            jnp.stack([key_term, value_term]),
            precision=lax.Precision.HIGHEST,
        )
        return (query_sum + query_term, far_grads + routed)

    query_sum, far_grads = lax.fori_loop(0, trip_count, grad_sweep, (query_sum, far_grads))
    owners = ((send_place[:, None] == jnp.arange(per_group)[None, :]) & sending[:, None]).astype(
        jnp.float32
    )
    returned = lax.all_to_all(far_grads, "grp", split_axis=1, concat_axis=1, tiled=True)
    landed = jnp.einsum("sp,xsjkd->xpjkd", owners, returned, precision=lax.Precision.HIGHEST)
    key_local = (key_near + landed[0]).reshape(group_tok, kv_local, head_width)
    value_local = (value_near + landed[1]).reshape(group_tok, kv_local, head_width)
    attended_rows = attended_blk.reshape(group_tok, heads_local, head_width)
    query_rows = (
        (query_sum * score_scale).astype(jnp.bfloat16).reshape(group_tok, heads_local, head_width)
    )
    attended, query_grad = (
        lax.all_to_all(attended_rows, "uly", split_axis=0, concat_axis=1, tiled=True),
        lax.all_to_all(query_rows, "uly", split_axis=0, concat_axis=1, tiled=True),
    )
    key_parts, value_parts = (
        lax.all_to_all(key_local, "uly", split_axis=0, concat_axis=1, tiled=True),
        lax.all_to_all(value_local, "uly", split_axis=0, concat_axis=1, tiled=True),
    )
    key_gradient = jnp.sum(key_parts.reshape(tokens, kv_heads, copies, head_width), axis=2).astype(
        jnp.bfloat16
    )
    value_gradient = jnp.sum(
        value_parts.reshape(tokens, kv_heads, copies, head_width), axis=2
    ).astype(jnp.bfloat16)
    return (attended, query_grad, key_gradient, value_gradient)


def solution(mesh):
    placed = (
        P(("grp", "uly"), None, None),
        P(("grp", "uly"), None, None),
        P(("grp", "uly"), None, None),
        P(("grp", "uly"), None, None),
        P(),
        P(),
    )
    return jax.shard_map(
        on_device,
        mesh=mesh,
        in_specs=placed,
        out_specs=(
            P(("grp", "uly"), None, None),
            P(("grp", "uly"), None, None),
            P(("grp", "uly"), None, None),
            P(("grp", "uly"), None, None),
        ),
        check_vma=False,
    )
```

profile of v0, /device:TPU:0, one launch (start us, length us, event | category | flops | bytes accessed | tf_op | source)
XLA Modules:
  0.0 215.2 jit_solution(12773727700696270377)
XLA Ops:
  2.3 4.2 %all-to-all-start = ((bf16[128,4,128]{2,0,1:T(8,128)(2,1)}), bf16[128,4,128]{2,0,1:T(8,128)(2,1)S(1)}, u32[]{:S(2)}, u32[]{:S(2)}) async-start(bf16[128,4,128]{2,0,1:T(8,128)(2,1)} %copy.88), calls=%async_computation | async-start | bytes 262144 | tf_op jit(solution)/shard_map/all_to_all | solution.py:38
  11.4 2.6 %copy.90 = bf16[128,32,128]{2,0,1:T(8,128)(2,1)} copy(bf16[128,32,128]{2,1,0:T(8,128)(2,1)} %param.14) | data formatting | bytes 2097152 | tf_op args[0]
  15.4 3.4 %all-to-all-start.2 = ((bf16[128,4,128]{2,0,1:T(8,128)(2,1)}), bf16[128,4,128]{2,0,1:T(8,128)(2,1)S(1)}, u32[]{:S(2)}, u32[]{:S(2)}) async-start(bf16[128,4,128]{2,0,1:T(8,128)(2,1)} %copy.96), calls=%async_computation.2 | async-start | bytes 262144 | tf_op jit(solution)/shard_map/all_to_all | solution.py:39
  18.9 4.4 %all-to-all-done.2 = bf16[128,4,128]{2,0,1:T(8,128)(2,1)S(1)} async-done(((bf16[128,4,128]{2,0,1:T(8,128)(2,1)}), bf16[128,4,128]{2,0,1:T(8,128)(2,1)S(1)}, u32[]{:S(2)}, u32[]{:S(2)}) %all-to-all-start.2) | async-done | bytes 131104 | tf_op jit(solution)/shard_map/all_to_all | solution.py:39
  23.4 3.6 %all-to-all-start.1 = ((bf16[128,32,128]{2,0,1:T(8,128)(2,1)}), bf16[128,32,128]{2,0,1:T(8,128)(2,1)S(1)}, u32[]{:S(2)}, u32[]{:S(2)}) async-start(bf16[128,32,128]{2,0,1:T(8,128)(2,1)} %copy.90), calls=%async_computation.1 | async-start | bytes 2097152 | tf_op jit(solution)/shard_map/all_to_all | solution.py:36
  27.0 12.9 %all-to-all-done.1 = bf16[128,32,128]{2,0,1:T(8,128)(2,1)S(1)} async-done(((bf16[128,32,128]{2,0,1:T(8,128)(2,1)}), bf16[128,32,128]{2,0,1:T(8,128)(2,1)S(1)}, u32[]{:S(2)}, u32[]{:S(2)}) %all-to-all-start.1) | async-done | bytes 1048608 | tf_op jit(solution)/shard_map/all_to_all | solution.py:36
  39.9 3.6 %all-to-all-start.5 = ((bf16[128,32,128]{2,0,1:T(8,128)(2,1)}), bf16[128,32,128]{2,0,1:T(8,128)(2,1)S(1)}, u32[]{:S(2)}, u32[]{:S(2)}) async-start(bf16[128,32,128]{2,0,1:T(8,128)(2,1)} %copy.108), calls=%async_computation.5 | async-start | bytes 2097152 | tf_op jit(solution)/shard_map/all_to_all | solution.py:37
  45.9 9.7 %all-to-all-done.5 = bf16[128,32,128]{2,0,1:T(8,128)(2,1)S(1)} async-done(((bf16[128,32,128]{2,0,1:T(8,128)(2,1)}), bf16[128,32,128]{2,0,1:T(8,128)(2,1)S(1)}, u32[]{:S(2)}, u32[]{:S(2)}) %all-to-all-start.5) | async-done | bytes 1048608 | tf_op jit(solution)/shard_map/all_to_all | solution.py:37
  55.6 5.9 %all-to-all-start.3 = ((bf16[2,16,32,2,128]{4,2,3,0,1:T(8,128)(2,1)}), bf16[2,16,32,2,128]{4,2,3,0,1:T(8,128)(2,1)}, u32[]{:S(2)}, u32[]{:S(2)}) async-start(bf16[2,16,32,2,128]{4,2,3,0,1:T(8,128)(2,1)} %select_bitcast_fusion), calls=%async_computation.3 | async-start | bytes 1048576 | tf_op jit(solution)/shard_map/all_to_all | solution.py:43
  62.3 2.3 %copy.110 = bf16[2,128,16,128]{3,2,1,0:T(8,128)(2,1)S(1)} copy(bf16[2,128,16,128]{3,1,2,0:T(8,128)(2,1)} %bitcast.255) | data formatting | bytes 2097152 | tf_op jit(solution)/shard_map/all_to_all | solution.py:37
  69.0 7.0 %all-to-all-done.3 = bf16[2,16,32,2,128]{4,2,3,0,1:T(8,128)(2,1)} async-done(((bf16[2,16,32,2,128]{4,2,3,0,1:T(8,128)(2,1)}), bf16[2,16,32,2,128]{4,2,3,0,1:T(8,128)(2,1)}, u32[]{:S(2)}, u32[]{:S(2)}) %all-to-all-start.3) | async-done | bytes 524320 | tf_op jit(solution)/shard_map/all_to_all | solution.py:43
  81.5 3.0 %copy.101 = f32[8,2,32,32,8]{3,4,2,1,0:T(8,128)} copy(f32[8,2,32,32,8]{3,2,4,1,0:T(8,128)S(1)} %fusion.57) | data formatting | bytes 1048576 | tf_op jit(solution)/shard_map/while | solution.py:88
  86.4 4.7 %while.43 = (s32[]{:T(128)}, f32[8,2,8,32]{3,2,1,0:T(8,128)S(1)}, f32[8,2,8,32]{3,2,1,0:T(8,128)}, s32[]{:T(128)}, pred[8,1]{0,1:T(4,128)(4,1)S(1)}, /*index=5*/f32[8,2,32,32,8]{3,4,2,1,0:T(8,128)}, s32[]{:T(128)}) while((s32[]{:T(128)}, f32[8,2,8,32]{3,2,1,0:T(8,128)S(1)}, f32[8,2,8,32]{3,2,1,0:T(8,128)}, s32[]{:T(128)}, ...), condition=%wide.region_7.9_spmd, body=%wide.region_4.8_spmd.sunk | while | flops 925698 | bytes 3489969 | solution.py:88
  92.0 3.5 %convolution_bitcast_fusion.1 = f32[8,32,2,8,128]{4,1,3,2,0:T(8,128)} fusion(f32[8,2,8,32,32]{3,4,2,1,0:T(8,128)} %copy-done.2, f32[8,2,8,32]{3,2,1,0:T(8,128)S(1)} %log_add_fusion, bf16[8,32,2,128,1]{3,1,0,2,4:T(8,128)(2,1)} %bitcast.260), kind=kOutput, calls=%fused_computation.52 | convolution fusion | flops 33816576 | bytes 2768896 | tf_op jit(solution)/shard_map/pkgqj,pjkd->pqkgd/dot_general | solution.py:94
  95.5 4.7 %while.44 = (s32[]{:T(128)}, f32[8,32,2,8,128]{4,1,3,2,0:T(8,128)}, s32[]{:T(128)}, pred[8,1]{0,1:T(4,128)(4,1)S(1)}, f32[8,2,32,32,8]{2,3,4,1,0:T(8,128)S(1)}, ...) while((s32[]{:T(128)}, f32[8,32,2,8,128]{4,1,3,2,0:T(8,128)}, s32[]{:T(128)}, ...), condition=%wide.region_9.11_spmd, body=%wide.region_8.10_spmd.sunk | while | flops 34603008 | bytes 4866141 | solution.py:108
  96.1 3.3 %bitcast_add_fusion.6 = f32[8,32,2,8,128]{4,1,3,2,0:T(8,128)} fusion(f32[8,32,2,8,128]{4,1,3,2,0:T(8,128)} %get-tuple-element.814, f32[8,2,32,32,8]{2,3,4,1,0:T(8,128)S(1)} %get-tuple-element.825, f32[8,2,8,32]{3,2,1,0:T(8,128)S(1)} %get-tuple-element.826, pred[8]{0:T(512)(128)(4,1)S(1)} %bitcast.277, bf16[8,32,2,128]{3,1,2,0:T(8,128)(2,1)S(1)} %get-tuple-element.827), kind=kOutput, calls=%fused_computation.9.clone.1 | convolution fusion | flops 34603008 | bytes 4866056 | tf_op jit(solution)/shard_map/while/body/pkgqj,pjkd->pqkgd/dot_general | solution.py:104
  100.2 3.1 %fusion.52 = f32[8,2,32,32,8]{3,2,4,1,0:T(8,128)} fusion(bf16[8,32,2,8,128]{4,3,2,1,0:T(8,128)(2,1)S(1)} %bitcast.243, bf16[8,32,2,128]{3,1,2,0:T(8,128)(2,1)S(1)} %get-tuple-element.868), kind=kOutput, calls=%fused_computation.76 | convolution fusion | flops 33554432 | bytes 1703936 | tf_op jit(solution)/shard_map/while/body/pqkgd,pjkd->pkgqj/dot_general | solution.py:118
  103.4 3.2 %multiply_reduce_fusion = (f32[8,32,2,8]{3,2,1,0:T(2,128)}, bf16[8,32,2,8,128]{4,3,2,1,0:T(8,128)(2,1)}) fusion(bf16[8,32,2,8,128]{4,3,2,1,0:T(8,128)(2,1)S(1)} %bitcast.244, f32[8,32,2,8,128]{4,1,3,2,0:T(8,128)S(1)} %copy-done.1), kind=kLoop, calls=%fused_computation.47 | loop fusion | flops 2093056 | bytes 4210688 | tf_op jit(solution)/shard_map/reduce_sum | solution.py:111
  107.6 3.3 %convolution_bitcast_fusion.4 = f32[1,8,32,2,128]{4,2,3,1,0:T(8,128)} fusion(f32[8,2,32,32,8]{3,2,4,1,0:T(8,128)} %copy-done.8, f32[8,2,8,32]{3,2,1,0:T(8,128)S(1)} %get-tuple-element.866, pred[8]{0:T(512)(128)(4,1)S(1)} %get-tuple-element.627, bf16[8,32,2,8,128]{4,3,2,1,0:T(8,128)(2,1)S(1)} %bitcast.245), kind=kOutput, calls=%fused_computation.56 | convolution fusion | flops 34078720 | bytes 1851400 | tf_op jit(solution)/shard_map/while/body/pkgqj,pqkgd->pjkd/dot_general | solution.py:129
  110.9 2.8 %fusion.28 = bf16[8,2,8,32,32]{3,4,2,1,0:T(8,128)(2,1)} fusion(f32[8,2,8,32,32]{3,4,2,1,0:T(8,128)S(1)} %copy-done.3, f32[8,2,8,32]{3,2,1,0:T(8,128)S(1)} %copy.113, f32[8,2,8,32]{3,2,1,0:T(8,128)S(1)} %get-tuple-element.866, bf16[8,32,2,8,128]{4,3,2,1,0:T(8,128)(2,1)S(1)} %bitcast.246, bf16[8,32,2,128,1]{3,1,0,2,4:T(8,128)(2,1)S(1)} %bitcast.261), kind=kOutput, calls=%fused_computation.42 | convolution fusion | flops 34078720 | bytes 1998848 | tf_op jit(solution)/shard_map/pqkgd,pjkd->pkgqj/dot_general | solution.py:118
  114.7 2.9 %copy.121 = f32[8,2,32,32,8]{2,3,4,1,0:T(8,128)} copy(f32[8,2,32,32,8]{3,2,4,1,0:T(8,128)} %fusion.52) | data formatting | bytes 1048576 | tf_op jit(solution)/shard_map/while | solution.py:154
  122.4 6.0 %while.45 = (s32[]{:T(128)}, f32[8,32,2,8,128]{4,1,3,2,0:T(8,128)}, f32[2,16,32,2,128]{4,3,2,1,0:T(2,128)S(1)}, s32[]{:T(128)}, pred[8,1]{0,1:T(4,128)(4,1)S(1)}...) while((s32[]{:T(128)}, f32[8,32,2,8,128]{4,1,3,2,0:T(8,128)}, ...), condition=%wide.region_12.14_spmd, body=%wide.region_11.13_spmd.sunk | while | flops 35127296 | bytes 12746905 | solution.py:154
  123.1 4.1 %bitcast_add_fusion.7 = f32[8,32,2,8,128]{4,1,3,2,0:T(8,128)} fusion(f32[8,32,2,8,128]{4,1,3,2,0:T(8,128)} %get-tuple-element.842, f32[8,2,32,32,8]{2,3,4,1,0:T(8,128)} %get-tuple-element.860, f32[8,2,32,32,8]{2,3,4,1,0:T(8,128)S(1)} %get-tuple-element.858, f32[8,2,8,32]{3,2,1,0:T(8,128)S(1)} %get-tuple-element.861, ...), kind=kOutput, calls=%fused_computation.20.clone.1 | convolution fusion | flops 34865152 | bytes 5406728 | tf_op jit(solution)/shard_map/while/body/pkgqj,pjkd->pqkgd/dot_general | solution.py:122
  128.4 4.0 %fusion.29 = bf16[8,32,2,8,128]{4,3,2,1,0:T(8,128)(2,1)} fusion(f32[8,32,2,8,128]{4,1,3,2,0:T(8,128)} %get-tuple-element.466), kind=kLoop, calls=%fused_computation.45 | loop fusion | flops 1048576 | bytes 3145728 | tf_op jit(solution)/shard_map/convert_element_type | solution.py:164
  132.4 3.6 %all-to-all-start.6 = ((bf16[256,16,128]{2,1,0:T(8,128)(2,1)}), bf16[256,16,128]{2,1,0:T(8,128)(2,1)S(1)}, u32[]{:S(2)}, u32[]{:S(2)}) async-start(bf16[256,16,128]{2,1,0:T(8,128)(2,1)} %bitcast.69), calls=%async_computation.6 | async-start | bytes 2097152 | tf_op jit(solution)/shard_map/all_to_all | solution.py:168
  136.1 13.9 %all-to-all-done.6 = bf16[256,16,128]{2,1,0:T(8,128)(2,1)S(1)} async-done(((bf16[256,16,128]{2,1,0:T(8,128)(2,1)}), bf16[256,16,128]{2,1,0:T(8,128)(2,1)S(1)}, u32[]{:S(2)}, u32[]{:S(2)}) %all-to-all-start.6) | async-done | bytes 1048608 | tf_op jit(solution)/shard_map/all_to_all | solution.py:168
  150.0 29.1 %all_to_all.124 = f32[2,16,32,2,128]{4,3,2,0,1:T(2,128)} all-to-all(f32[2,16,32,2,128]{4,3,2,0,1:T(2,128)S(1)} %copy.127), channel_id=1, replica_groups=mesh['grp'=16,'uly'=2] {'grp'}, dimensions={1} | all-to-all | bytes 2097152 | tf_op jit(solution)/shard_map/all_to_all | solution.py:158
  179.1 4.9 %all-to-all-start.4 = ((bf16[256,16,128]{2,1,0:T(8,128)(2,1)}), bf16[256,16,128]{2,1,0:T(8,128)(2,1)}, u32[]{:S(2)}, u32[]{:S(2)}) async-start(bf16[256,16,128]{2,1,0:T(8,128)(2,1)} %bitcast.252), calls=%async_computation.4 | async-start | bytes 2097152 | tf_op jit(solution)/shard_map/all_to_all | solution.py:167
  188.1 10.6 %all-to-all-done.4 = bf16[256,16,128]{2,1,0:T(8,128)(2,1)} async-done(((bf16[256,16,128]{2,1,0:T(8,128)(2,1)}), bf16[256,16,128]{2,1,0:T(8,128)(2,1)}, u32[]{:S(2)}, u32[]{:S(2)}) %all-to-all-start.4) | async-done | bytes 1048608 | tf_op jit(solution)/shard_map/all_to_all | solution.py:167
  198.7 3.4 %all-to-all-start.9 = ((bf16[256,2,128]{2,1,0:T(2,128)(2,1)}), bf16[256,2,128]{2,1,0:T(2,128)(2,1)S(1)}, u32[]{:S(2)}, u32[]{:S(2)}) async-start(bf16[256,2,128]{2,1,0:T(2,128)(2,1)} %copy.136), calls=%async_computation.9 | async-start | bytes 262144 | tf_op jit(solution)/shard_map/all_to_all | solution.py:172
  206.6 3.4 %all-to-all-start.8 = ((bf16[256,2,128]{2,1,0:T(2,128)(2,1)}), bf16[256,2,128]{2,1,0:T(2,128)(2,1)S(1)}, u32[]{:S(2)}, u32[]{:S(2)}) async-start(bf16[256,2,128]{2,1,0:T(2,128)(2,1)} %copy.131), calls=%async_computation.8 | async-start | bytes 262144 | tf_op jit(solution)/shard_map/all_to_all | solution.py:171
  211.1 2.4 %copy.107 = bf16[128,2,16,128]{3,2,1,0:T(8,128)(2,1)} copy(bf16[128,2,16,128]{3,2,0,1:T(8,128)(2,1)} %bitcast.44) | data formatting | bytes 2097152 | tf_op jit(solution)/shard_map/all_to_all | solution.py:167
  (125 shorter events, 45.9 us)
Async XLA Ops:
  0.6 13.4 %copy-start.24 = (bf16[128,32,128]{2,1,0:T(8,128)(2,1)S(1)}, bf16[128,32,128]{2,1,0:T(8,128)(2,1)}, u32[]{:S(2)}) copy-start(bf16[128,32,128]{2,1,0:T(8,128)(2,1)} %param.17) | copy-start | bytes 3145732
  2.3 13.1 %all-to-all-start = ((bf16[128,4,128]{2,0,1:T(8,128)(2,1)}), bf16[128,4,128]{2,0,1:T(8,128)(2,1)S(1)}, u32[]{:S(2)}, u32[]{:S(2)}) async-start(bf16[128,4,128]{2,0,1:T(8,128)(2,1)} %copy.88), calls=%async_computation | async-start | bytes 262144 | tf_op jit(solution)/shard_map/all_to_all | solution.py:38
  15.4 7.9 %all-to-all-start.2 = ((bf16[128,4,128]{2,0,1:T(8,128)(2,1)}), bf16[128,4,128]{2,0,1:T(8,128)(2,1)S(1)}, u32[]{:S(2)}, u32[]{:S(2)}) async-start(bf16[128,4,128]{2,0,1:T(8,128)(2,1)} %copy.96), calls=%async_computation.2 | async-start | bytes 262144 | tf_op jit(solution)/shard_map/all_to_all | solution.py:39
  18.9 21.0 %copy-start.27 = (s32[16]{0:T(128)}, s32[16]{0:T(128)S(1)}, u32[]{:S(2)}) copy-start(s32[16]{0:T(128)S(1)} %fusion.72) | copy-start | bytes 196
  23.4 16.6 %all-to-all-start.1 = ((bf16[128,32,128]{2,0,1:T(8,128)(2,1)}), bf16[128,32,128]{2,0,1:T(8,128)(2,1)S(1)}, u32[]{:S(2)}, u32[]{:S(2)}) async-start(bf16[128,32,128]{2,0,1:T(8,128)(2,1)} %copy.90), calls=%async_computation.1 | async-start | bytes 2097152 | tf_op jit(solution)/shard_map/all_to_all | solution.py:36
  39.9 15.7 %all-to-all-start.5 = ((bf16[128,32,128]{2,0,1:T(8,128)(2,1)}), bf16[128,32,128]{2,0,1:T(8,128)(2,1)S(1)}, u32[]{:S(2)}, u32[]{:S(2)}) async-start(bf16[128,32,128]{2,0,1:T(8,128)(2,1)} %copy.108), calls=%async_computation.5 | async-start | bytes 2097152 | tf_op jit(solution)/shard_map/all_to_all | solution.py:37
  44.2 20.4 %copy-start.19 = (bf16[2,128,2,128]{3,1,0,2:T(8,128)(2,1)}, bf16[2,128,2,128]{3,1,0,2:T(8,128)(2,1)S(1)}, u32[]{:S(2)}) copy-start(bf16[2,128,2,128]{3,1,0,2:T(8,128)(2,1)S(1)} %copy.89) | copy-start | bytes 393220
  44.2 11.4 %copy-start.21 = (bf16[2,128,2,128]{3,1,0,2:T(8,128)(2,1)}, bf16[2,128,2,128]{3,1,0,2:T(8,128)(2,1)S(1)}, u32[]{:S(2)}) copy-start(bf16[2,128,2,128]{3,1,0,2:T(8,128)(2,1)S(1)} %copy.97) | copy-start | bytes 393220
  55.6 6.7 %copy-start.16 = (bf16[128,32,128]{2,0,1:T(8,128)(2,1)}, bf16[128,32,128]{2,0,1:T(8,128)(2,1)S(1)}, u32[]{:S(2)}) copy-start(bf16[128,32,128]{2,0,1:T(8,128)(2,1)S(1)} %all-to-all-done.5) | copy-start | bytes 3145732
  55.6 20.4 %all-to-all-start.3 = ((bf16[2,16,32,2,128]{4,2,3,0,1:T(8,128)(2,1)}), bf16[2,16,32,2,128]{4,2,3,0,1:T(8,128)(2,1)}, u32[]{:S(2)}, u32[]{:S(2)}) async-start(bf16[2,16,32,2,128]{4,2,3,0,1:T(8,128)(2,1)} %select_bitcast_fusion), calls=%async_computation.3 | async-start | bytes 1048576 | tf_op jit(solution)/shard_map/all_to_all | solution.py:43
  62.3 16.1 %copy-start.10 = (bf16[2,128,16,128]{3,2,1,0:T(8,128)(2,1)}, bf16[2,128,16,128]{3,2,1,0:T(8,128)(2,1)S(1)}, u32[]{:S(2)}) copy-start(bf16[2,128,16,128]{3,2,1,0:T(8,128)(2,1)S(1)} %copy.92) | copy-start | bytes 3145732
  64.6 46.3 %copy-start.6 = (bf16[2,128,16,128]{3,2,1,0:T(8,128)(2,1)}, bf16[2,128,16,128]{3,2,1,0:T(8,128)(2,1)S(1)}, u32[]{:S(2)}) copy-start(bf16[2,128,16,128]{3,2,1,0:T(8,128)(2,1)S(1)} %copy.110) | copy-start | bytes 3145732
  87.0 2.8 %copy-start.17 = (f32[8,2,8,32]{3,2,1,0:T(8,128)S(1)}, f32[8,2,8,32]{3,2,1,0:T(8,128)}, u32[]{:S(2)}) copy-start(f32[8,2,8,32]{3,2,1,0:T(8,128)} %get-tuple-element.793) | copy-start | bytes 49156 | tf_op jit(solution)/shard_map/while
  100.2 3.1 %copy-start.1 = (f32[8,32,2,8,128]{4,1,3,2,0:T(8,128)S(1)}, f32[8,32,2,8,128]{4,1,3,2,0:T(8,128)}, u32[]{:S(2)}) copy-start(f32[8,32,2,8,128]{4,1,3,2,0:T(8,128)} %get-tuple-element.465) | copy-start | bytes 6291460
  107.6 3.3 %copy-start.3 = (f32[8,2,8,32,32]{3,4,2,1,0:T(8,128)S(1)}, f32[8,2,8,32,32]{3,4,2,1,0:T(8,128)}, u32[]{:S(2)}) copy-start(f32[8,2,8,32,32]{3,4,2,1,0:T(8,128)} %copy-done.2) | copy-start | bytes 1572868
  107.6 3.3 %copy-start.22 = (bf16[2,128,2,128]{3,1,0,2:T(8,128)(2,1)S(1)}, bf16[2,128,2,128]{3,1,0,2:T(8,128)(2,1)}, u32[]{:S(2)}) copy-start(bf16[2,128,2,128]{3,1,0,2:T(8,128)(2,1)} %copy-done.21) | copy-start | bytes 393220
  107.6 6.1 %copy-start.12 = (f32[8,2,32,32,8]{3,2,4,1,0:T(8,128)S(1)}, f32[8,2,32,32,8]{3,2,4,1,0:T(8,128)}, u32[]{:S(2)}) copy-start(f32[8,2,32,32,8]{3,2,4,1,0:T(8,128)} %fusion.52) | copy-start | bytes 1572868
  110.9 2.8 %copy-start.9 = (f32[8,2,32,32,8]{3,2,4,1,0:T(8,128)S(1)}, f32[8,2,32,32,8]{3,2,4,1,0:T(8,128)}, u32[]{:S(2)}) copy-start(f32[8,2,32,32,8]{3,2,4,1,0:T(8,128)} %copy-done.8) | copy-start | bytes 1572868
  110.9 2.8 %copy-start.11 = (bf16[2,128,16,128]{3,2,1,0:T(8,128)(2,1)S(1)}, bf16[2,128,16,128]{3,2,1,0:T(8,128)(2,1)}, u32[]{:S(2)}) copy-start(bf16[2,128,16,128]{3,2,1,0:T(8,128)(2,1)} %copy-done.10) | copy-start | bytes 3145732
  114.7 2.9 %copy-start.25 = (f32[1,8,32,2,128]{4,2,3,1,0:T(8,128)S(1)}, f32[1,8,32,2,128]{4,2,3,1,0:T(8,128)}, u32[]{:S(2)}) copy-start(f32[1,8,32,2,128]{4,2,3,1,0:T(8,128)} %convolution_bitcast_fusion.4) | copy-start | bytes 786436
  117.7 2.4 %copy-start.13 = (bf16[8,2,8,32,32]{3,4,2,1,0:T(8,128)(2,1)S(1)}, bf16[8,2,8,32,32]{3,4,2,1,0:T(8,128)(2,1)}, u32[]{:S(2)}) copy-start(bf16[8,2,8,32,32]{3,4,2,1,0:T(8,128)(2,1)} %fusion.28) | copy-start | bytes 786436
  123.0 4.1 %copy-start.5 = (f32[2,32,2,128,16]{3,2,1,4,0:T(2,128)S(1)}, f32[2,32,2,128,16]{3,2,1,4,0:T(2,128)}, u32[]{:S(2)}) copy-start(f32[2,32,2,128,16]{3,2,1,4,0:T(2,128)} %get-tuple-element.863) | copy-start | bytes 3145732 | tf_op jit(solution)/shard_map/while
  132.4 17.6 %all-to-all-start.6 = ((bf16[256,16,128]{2,1,0:T(8,128)(2,1)}), bf16[256,16,128]{2,1,0:T(8,128)(2,1)S(1)}, u32[]{:S(2)}, u32[]{:S(2)}) async-start(bf16[256,16,128]{2,1,0:T(8,128)(2,1)} %bitcast.69), calls=%async_computation.6 | async-start | bytes 2097152 | tf_op jit(solution)/shard_map/all_to_all | solution.py:168
  136.1 48.0 %copy-start.26 = (pred[16]{0:T(512)(128)(4,1)S(1)}, pred[16]{0:T(512)(128)(4,1)}, u32[]{:S(2)}) copy-start(pred[16]{0:T(512)(128)(4,1)} %get-tuple-element.620) | copy-start | bytes 52
  136.1 48.0 %copy-start.28 = (s32[16]{0:T(128)S(1)}, s32[16]{0:T(128)}, u32[]{:S(2)}) copy-start(s32[16]{0:T(128)} %copy-done.27) | copy-start | bytes 196
  150.0 29.1 %copy-start.14 = (bf16[256,16,128]{2,1,0:T(8,128)(2,1)}, bf16[256,16,128]{2,1,0:T(8,128)(2,1)S(1)}, u32[]{:S(2)}) copy-start(bf16[256,16,128]{2,1,0:T(8,128)(2,1)S(1)} %all-to-all-done.6) | copy-start | bytes 3145732
  179.1 7.4 %copy-start.4 = (f32[8,2,8,32,32]{3,4,2,1,0:T(8,128)S(1)}, f32[8,2,8,32,32]{3,4,2,1,0:T(8,128)}, u32[]{:S(2)}) copy-start(f32[8,2,8,32,32]{3,4,2,1,0:T(8,128)} %copy-done.2) | copy-start | bytes 1572868
  179.1 7.4 %copy-start.7 = (bf16[2,128,16,128]{3,2,1,0:T(8,128)(2,1)S(1)}, bf16[2,128,16,128]{3,2,1,0:T(8,128)(2,1)}, u32[]{:S(2)}) copy-start(bf16[2,128,16,128]{3,2,1,0:T(8,128)(2,1)} %copy-done.6) | copy-start | bytes 3145732
  179.1 19.6 %all-to-all-start.4 = ((bf16[256,16,128]{2,1,0:T(8,128)(2,1)}), bf16[256,16,128]{2,1,0:T(8,128)(2,1)}, u32[]{:S(2)}, u32[]{:S(2)}) async-start(bf16[256,16,128]{2,1,0:T(8,128)(2,1)} %bitcast.252), calls=%async_computation.4 | async-start | bytes 2097152 | tf_op jit(solution)/shard_map/all_to_all | solution.py:167
  187.3 22.6 %copy-start.15 = (bf16[256,16,128]{2,1,0:T(8,128)(2,1)S(1)}, bf16[256,16,128]{2,1,0:T(8,128)(2,1)}, u32[]{:S(2)}) copy-start(bf16[256,16,128]{2,1,0:T(8,128)(2,1)} %copy-done.14) | copy-start | bytes 3145732
  198.7 7.8 %all-to-all-start.9 = ((bf16[256,2,128]{2,1,0:T(2,128)(2,1)}), bf16[256,2,128]{2,1,0:T(2,128)(2,1)S(1)}, u32[]{:S(2)}, u32[]{:S(2)}) async-start(bf16[256,2,128]{2,1,0:T(2,128)(2,1)} %copy.136), calls=%async_computation.9 | async-start | bytes 262144 | tf_op jit(solution)/shard_map/all_to_all | solution.py:172
  206.6 7.8 %all-to-all-start.8 = ((bf16[256,2,128]{2,1,0:T(2,128)(2,1)}), bf16[256,2,128]{2,1,0:T(2,128)(2,1)S(1)}, u32[]{:S(2)}, u32[]{:S(2)}) async-start(bf16[256,2,128]{2,1,0:T(2,128)(2,1)} %copy.131), calls=%async_computation.8 | async-start | bytes 262144 | tf_op jit(solution)/shard_map/all_to_all | solution.py:171
  (6 other events, 8.7 us)
where the time goes:
time: 217 us; the launch traced here: 215 us
  waiting for transfers between devices  60.3 us (28%)
  starting transfers between devices  35.9 us (17%)
  local copies, waits for them, and re-layouts  35.3 us (16%)
  matrix products  32.2 us (15%)
  blocking collectives  29.1 us (13%)
  other arithmetic  17.1 us (8%)
  loops' own time  4.02 us (2%)
    all_to_all x1, blocking collectives, on_device(): lax.all_to_all(far_grads, 'grp', split_axis=1, concat_axis=1, tiled=True)  29.1 us
    all_to_all x1, waiting for transfers between devices, on_device(): lax.all_to_all(query_rows, 'uly', split_axis=0, concat_axis=1, tiled=True)  13.9 us
    all_to_all x1, waiting for transfers between devices, on_device(): lax.all_to_all(queries, 'uly', split_axis=1, concat_axis=0, tiled=True)  12.9 us
    unnamed x57, local copies, waits for them, and re-layouts  12.2 us
    all_to_all x1, waiting for transfers between devices, on_device(): lax.all_to_all(attended_rows, 'uly', split_axis=0, concat_axis=1, tiled=T...  10.6 us
    all_to_all x1, waiting for transfers between devices, on_device(): lax.all_to_all(output_cotangent, 'uly', split_axis=1, concat_axis=0, tile...  9.72 us
    all_to_all x1, waiting for transfers between devices, on_device(): lax.all_to_all(outgoing, 'grp', split_axis=1, concat_axis=1, tiled=True)  7.02 us
    dot_general x2, matrix products, backward(): jnp.einsum('pkgqj,pjkd->pqkgd', dscores, key_rows, preferred_element_type...  5.96 us
  transfers between devices with their start and end apart: 9, of which 8 were waited for; matrix products, arithmetic and copies ran while one was open for 13% of the time, Pallas kernels for 0%

commit v1 on v0

--- a/solution.py
+++ b/solution.py
@@ -1,10 +1,12 @@
 import jax
 import jax.numpy as jnp
 from jax import lax
+from jax.experimental import pallas as pl
+from jax.experimental.pallas import tpu as pltpu
 from jax.sharding import PartitionSpec as P
 
 
-def on_device(queries, keys, values, output_cotangent, block_lists, list_counts):
+def spread_blocks(queries, keys, values, output_cotangent, block_lists, list_counts):
     uly_count = lax.axis_size("uly")
     grp_count = lax.axis_size("grp")
     my_group = lax.axis_index("grp")
@@ -180,6 +182,190 @@
     return (attended, query_grad, key_gradient, value_gradient)
 
 
+HIDDEN = -1e30
+
+
+def attention_kernel(
+    source_ref, seen_ref, q_ref, g_ref, k_ref, v_ref, mine_ref, other_ref,
+    att_ref, dq_ref, dk_ref, dv_ref, far_mine_ref, far_other_ref, bias_ref,
+    *, heads, kv_heads, score_scale
+):
+    step = pl.program_id(0)
+    rows = q_ref.shape[0]
+    cols = k_ref.shape[0]
+    half = mine_ref.shape[2]
+
+    @pl.when(step == 0)
+    def _():
+        row = lax.broadcasted_iota(jnp.int32, (rows, cols), 0)
+        col = lax.broadcasted_iota(jnp.int32, (rows, cols), 1)
+        same = (row % heads) // (heads // kv_heads) == col % kv_heads
+        causal = col // kv_heads <= row // heads
+        bias_ref[:, :cols] = jnp.where(same & causal, 0.0, HIDDEN)
+        bias_ref[:, cols:] = jnp.where(same, 0.0, HIDDEN)
+
+    far_bias = jnp.where(seen_ref[step] > 0, 0.0, HIDDEN)
+    k_all = jnp.concatenate([k_ref[...], mine_ref[0, 0], other_ref[0, 0]], axis=0)
+    v_all = jnp.concatenate([v_ref[...], mine_ref[0, 1], other_ref[0, 1]], axis=0)
+    q = q_ref[...]
+    g = g_ref[...]
+    last = (((1,), (1,)), ((), ()))
+    first = (((0,), (0,)), ((), ()))
+    scores = lax.dot_general(q, k_all, last, preferred_element_type=jnp.float32) * score_scale
+    scores = scores + bias_ref[...]
+    scores = jnp.concatenate([scores[:, :cols], scores[:, cols:] + far_bias], axis=1)
+    highest = jnp.max(scores, axis=1, keepdims=True)
+    raised = jnp.exp(scores - highest)
+    total = jnp.sum(raised, axis=1, keepdims=True)
+    probs = raised * (1.0 / total)
+    weights = probs.astype(jnp.bfloat16)
+    attended = jnp.dot(weights, v_all, preferred_element_type=jnp.float32).astype(jnp.bfloat16)
+    att_ref[...] = attended
+    delta = jnp.sum(g.astype(jnp.float32) * attended.astype(jnp.float32), axis=1, keepdims=True)
+    dprobs = lax.dot_general(g, v_all, last, preferred_element_type=jnp.float32)
+    dscores = (probs * (dprobs - delta)).astype(jnp.bfloat16)
+    dq = jnp.dot(dscores, k_all, preferred_element_type=jnp.float32) * score_scale
+    dq_ref[...] = dq.astype(jnp.bfloat16)
+    dk = lax.dot_general(dscores, q, first, preferred_element_type=jnp.float32) * score_scale
+    dv = lax.dot_general(weights, g, first, preferred_element_type=jnp.float32)
+    dk_ref[...] = dk[:cols]
+    dv_ref[...] = dv[:cols]
+    far_mine_ref[0, 0] = dk[cols:cols + half].astype(jnp.bfloat16)
+    far_mine_ref[0, 1] = dv[cols:cols + half].astype(jnp.bfloat16)
+    far_other_ref[0, 0] = dk[cols + half:].astype(jnp.bfloat16)
+    far_other_ref[0, 1] = dv[cols + half:].astype(jnp.bfloat16)
+
+
+def whole_blocks(queries, keys, values, output_cotangent, block_lists, list_counts):
+    grp_count = lax.axis_size("grp")
+    uly_count = lax.axis_size("uly")
+    my_group = lax.axis_index("grp")
+    my_half = lax.axis_index("uly")
+    tokens, heads, width = queries.shape
+    kv_heads = keys.shape[1]
+    per_group = block_lists.shape[0] // grp_count
+    block_tok = tokens * uly_count // per_group
+    mine_blocks = tokens // block_tok
+    rows = block_tok * heads
+    cols = block_tok * kv_heads
+    half = cols // 2
+    score_scale = width ** (-0.5)
+    swap = [(0, 1), (1, 0)]
+
+    lists = block_lists.reshape(grp_count, per_group)
+    counted = (list_counts > 0).reshape(grp_count, per_group)
+    wanted = (lists // per_group == my_group) & counted
+    send_place = jnp.sum(jnp.where(wanted, lists % per_group, 0), axis=1)
+    sending = jnp.any(wanted, axis=1)
+    my_lists = lax.dynamic_index_in_dim(lists, my_group, 0, keepdims=False)
+    my_seen = lax.dynamic_index_in_dim(counted, my_group, 0, keepdims=False).astype(jnp.int32)
+    source = my_lists // per_group
+
+    def by_owner(vector):
+        both = vector.reshape(2, mine_blocks)
+        return (
+            lax.dynamic_index_in_dim(both, my_half, 0, keepdims=False),
+            lax.dynamic_index_in_dim(both, 1 - my_half, 0, keepdims=False),
+        )
+
+    source_own, source_sib = by_owner(source)
+    seen_own, seen_sib = by_owner(my_seen)
+    owner_first = jnp.where(
+        send_place // mine_blocks == my_half,
+        send_place % mine_blocks,
+        send_place % mine_blocks + mine_blocks,
+    )
+
+    parts = jnp.stack(
+        [keys.reshape(mine_blocks, 2, half, width), values.reshape(mine_blocks, 2, half, width)],
+        axis=2,
+    )
+    kept = lax.dynamic_index_in_dim(parts, my_half, 1, keepdims=False)
+    given = lax.dynamic_index_in_dim(parts, 1 - my_half, 1, keepdims=False)
+    gotten = lax.ppermute(given, "uly", swap)
+    outgoing = jnp.take(jnp.concatenate([kept, gotten]), owner_first, axis=0)
+    arrived = lax.all_to_all(outgoing, "grp", split_axis=0, concat_axis=0, tiled=True)
+    other = lax.ppermute(jnp.take(arrived, source_sib, axis=0), "uly", swap)
+
+    q2 = queries.reshape(tokens * heads, width)
+    g2 = output_cotangent.reshape(tokens * heads, width)
+    k2 = keys.reshape(tokens * kv_heads, width)
+    v2 = values.reshape(tokens * kv_heads, width)
+
+    def step_rows(i, *_):
+        return (i, 0)
+
+    def step_part(i, *_):
+        return (i, 0, 0, 0)
+
+    def from_source(i, source_ref, seen_ref):
+        return (source_ref[i], 0, 0, 0)
+
+    def far_spec(index_map):
+        return pl.BlockSpec((1, 2, half, width), index_map)
+
+    row_spec = pl.BlockSpec((rows, width), step_rows)
+    col_spec = pl.BlockSpec((cols, width), step_rows)
+    f32 = jnp.float32
+    bf16 = jnp.bfloat16
+    attended, dq, dk_near, dv_near, far_mine, far_other = pl.pallas_call(
+        lambda *refs: attention_kernel(
+            *refs, heads=heads, kv_heads=kv_heads, score_scale=score_scale
+        ),
+        grid_spec=pltpu.PrefetchScalarGridSpec(
+            num_scalar_prefetch=2,
+            grid=(mine_blocks,),
+            in_specs=[
+                row_spec, row_spec, col_spec, col_spec, far_spec(from_source), far_spec(step_part)
+            ],
+            out_specs=[
+                row_spec, row_spec, col_spec, col_spec, far_spec(step_part), far_spec(step_part)
+            ],
+            scratch_shapes=[pltpu.VMEM((rows, 2 * cols), f32)],
+        ),
+        out_shape=[
+            jax.ShapeDtypeStruct(q2.shape, bf16),
+            jax.ShapeDtypeStruct(q2.shape, bf16),
+            jax.ShapeDtypeStruct(k2.shape, f32),
+            jax.ShapeDtypeStruct(k2.shape, f32),
+            jax.ShapeDtypeStruct((mine_blocks, 2, half, width), bf16),
+            jax.ShapeDtypeStruct((mine_blocks, 2, half, width), bf16),
+        ],
+        compiler_params=pltpu.CompilerParams(vmem_limit_bytes=48 * 1024 * 1024),
+        name="attention",
+    )(source_own, seen_own, q2, g2, k2, v2, arrived, other)
+
+    from_sib = lax.ppermute(far_other, "uly", swap)
+    groups = jnp.arange(grp_count)
+    source_both = jnp.concatenate([source_own, source_sib])
+    asked = jnp.argmax(source_both[None, :] == groups[:, None], axis=1)
+    returning = jnp.take(jnp.concatenate([far_mine, from_sib]), asked, axis=0)
+    landed = lax.all_to_all(returning, "grp", split_axis=0, concat_axis=0, tiled=True)
+    routing = ((owner_first[:, None] == jnp.arange(per_group)[None, :]) & sending[:, None]).astype(
+        bf16
+    )
+    summed = jnp.einsum("sp,sxrd->pxrd", routing, landed, preferred_element_type=f32)
+    summed_own = summed[:mine_blocks]
+    back = lax.ppermute(summed[mine_blocks:].astype(bf16), "uly", swap)
+    first_half = jnp.where(my_half == 0, summed_own, back.astype(f32))
+    second_half = jnp.where(my_half == 0, back.astype(f32), summed_own)
+    far_sum = jnp.stack([first_half, second_half], axis=1)
+    near_shape = (mine_blocks, 2, half, width)
+    dk = (dk_near.reshape(near_shape) + far_sum[:, :, 0]).astype(bf16).reshape(keys.shape)
+    dv = (dv_near.reshape(near_shape) + far_sum[:, :, 1]).astype(bf16).reshape(keys.shape)
+    return (attended.reshape(queries.shape), dq.reshape(queries.shape), dk, dv)
+
+
+def on_device(queries, keys, values, output_cotangent, block_lists, list_counts):
+    uly_count = lax.axis_size("uly")
+    grp_count = lax.axis_size("grp")
+    blocks_all, remote = block_lists.shape
+    block_tok = queries.shape[0] * uly_count * grp_count // blocks_all
+    held_whole = queries.shape[0] % block_tok == 0
+    run = whole_blocks if held_whole and remote == 1 and uly_count == 2 else spread_blocks
+    return run(queries, keys, values, output_cotangent, block_lists, list_counts)
+
+
 def solution(mesh):
     placed = (
         P(("grp", "uly"), None, None),

time: 217 us -> 76.5 us (0.35)
  waiting for transfers between devices: 60.3 us -> 25.8 us
  matrix products: 32.2 us -> 0.39 us
  local copies, waits for them, and re-layouts: 35.3 us -> 3.66 us
  starting transfers between devices: 35.9 us -> 14 us
  other arithmetic: 17.1 us -> 5.54 us
  blocking collectives: 29.1 us -> 18.6 us
  Pallas kernels: 0 us -> 7.37 us
  loops' own time: 4.02 us -> 0 us
    all_to_all x9 -> x1, waiting for transfers between devices: 60.3 us -> 13.7 us  [whole_blocks(): lax.all_to_all(outgoing, 'grp', split_axis=0, concat_axis=0, tiled=True)]
    dot_general x14 -> x1, matrix products: 32.2 us -> 0.39 us  [whole_blocks(): jnp.einsum('sp,sxrd->pxrd', routing, landed, preferred_element_type=f32)]
    all_to_all x9 -> x1, starting transfers between devices: 35.9 us -> 6.26 us  [whole_blocks(): lax.all_to_all(outgoing, 'grp', split_axis=0, concat_axis=0, tiled=True)]
    ppermute x0 -> x4, waiting for transfers between devices: none -> 12 us  [the longest x1 3.9 us: whole_blocks(): back = lax.ppermute(summed[mine_blocks:].astype(bf16), 'uly', swap)]
    unnamed x57 -> x17, local copies, waits for them, and re-layouts: 12.2 us -> 1.34 us
    all_to_all x1, blocking collectives: 29.1 us -> 18.6 us  [whole_blocks(): lax.all_to_all(returning, 'grp', split_axis=0, concat_axis=0, tiled=True)]
    while x14 -> x0, local copies, waits for them, and re-layouts: 10.2 us -> none  [the longest x3 4.52 us: on_device(): lax.fori_loop(0, trip_count, grad_sweep, (query_sum, far_grads))]
    ppermute x0 -> x4, starting transfers between devices: none -> 7.72 us  [the longest x1 3.03 us: whole_blocks(): gotten = lax.ppermute(given, 'uly', swap)]
  transfers between devices with their start and end apart: 9 -> 5, of which waited for: 8 -> 5; matrix products, arithmetic and copies ran while one was open for 13% -> 3% of each run, Pallas kernels for 0% -> 0%
where the time goes in v1:
time: 76.5 us; the launch traced here: 76.2 us
  waiting for transfers between devices  25.8 us (34%)
  blocking collectives  18.6 us (24%)
  starting transfers between devices  14 us (18%)
  Pallas kernels  7.37 us (10%)
  other arithmetic  5.54 us (7%)
  local copies, waits for them, and re-layouts  3.66 us (5%)
  between operations  0.83 us (1%)
    all_to_all x1, blocking collectives, whole_blocks(): lax.all_to_all(returning, 'grp', split_axis=0, concat_axis=0, tiled=True)  18.6 us
    all_to_all x1, waiting for transfers between devices, whole_blocks(): lax.all_to_all(outgoing, 'grp', split_axis=0, concat_axis=0, tiled=True)  13.7 us
    pallas_call x1, Pallas kernels, whole_blocks(): pl.pallas_call(lambda *refs: attention_kernel(*refs, heads=heads, kv_head...  7.37 us
    all_to_all x1, starting transfers between devices, whole_blocks(): lax.all_to_all(outgoing, 'grp', split_axis=0, concat_axis=0, tiled=True)  6.26 us
    ppermute x1, waiting for transfers between devices, whole_blocks(): back = lax.ppermute(summed[mine_blocks:].astype(bf16), 'uly', swap)  3.9 us
    ppermute x1, waiting for transfers between devices, whole_blocks(): other = lax.ppermute(jnp.take(arrived, source_sib, axis=0), 'uly', swap)  3.8 us
    ppermute x1, waiting for transfers between devices, whole_blocks(): from_sib = lax.ppermute(far_other, 'uly', swap)  3.43 us
    ppermute x1, starting transfers between devices, whole_blocks(): gotten = lax.ppermute(given, 'uly', swap)  3.03 us
  transfers between devices with their start and end apart: 5, of which 5 were waited for; matrix products, arithmetic and copies ran while one was open for 3% of the time, Pallas kernels for 0%

profile of v1, /device:TPU:0, one launch (start us, length us, event | category | flops | bytes accessed | tf_op | source)
XLA Modules:
  0.0 76.2 jit_solution(1461367342172347223)
XLA Ops:
  0.6 1.0 %fusion.8 = (bf16[4,2,64,128]{3,2,0,1:T(8,128)(2,1)S(1)}, bf16[4,2,64,128]{3,2,0,1:T(8,128)(2,1)S(1)}) fusion(s32[]{:T(128)S(6)} %select_n.111, bf16[4,2,1,64,128]{4,3,1,0,2:T(8,128)(2,1)} %bitcast.39, bf16[4,2,1,64,128]{4,3,1,0,2:T(8,128)(2,1)} %bitcast.41, s32[]{:T(128)S(6)} %select_n.112), kind=kLoop, calls=%fused_computation.27 | loop fusion | flops 131072 | bytes 524296 | tf_op jit(solution)/shard_map/jit(dynamic_index_in_dim)/squeeze | solution.py:283
  1.6 3.0 %collective-permute-start = (bf16[4,2,64,128]{3,2,0,1:T(8,128)(2,1)S(1)}, bf16[4,2,64,128]{3,2,0,1:T(8,128)(2,1)S(1)}, u32[]{:S(2)}, u32[]{:S(2)}) collective-permute-start(bf16[4,2,64,128]{3,2,0,1:T(8,128)(2,1)S(1)} %get-tuple-element.30), channel_id=1, source_target_pairs={{0,1},{1,0},{2,3},{3,2},{4,5},{5,4},{6,7},{7,6},{8,9},{9,8},{10,11... | collective-permute-start | bytes 393224 | tf_op jit(solution)/shard_map/ppermute | solution.py:285
  4.6 0.7 copy-done.4
  5.3 0.1 reshape.123
  5.4 0.5 broadcast.212
  5.9 0.1 copy-done.5
  6.1 0.7 reduce.30
  6.7 0.1 reshape.122
  6.8 0.1 fusion.27
  6.9 0.1 fusion.11
  7.2 0.9 %collective-permute-done = bf16[4,2,64,128]{3,2,0,1:T(8,128)(2,1)S(1)} collective-permute-done((bf16[4,2,64,128]{3,2,0,1:T(8,128)(2,1)S(1)}, bf16[4,2,64,128]{3,2,0,1:T(8,128)(2,1)S(1)}, u32[]{:S(2)}, u32[]{:S(2)}) %collective-permute-start) | collective-permute-done | bytes 131104 | tf_op jit(solution)/shard_map/ppermute | solution.py:285
  8.2 0.6 gather_fusion.1
  8.8 0.9 %broadcast_select_fusion.1 = bf16[16,2,64,128]{3,2,1,0:T(8,128)(2,1)} fusion(bf16[16,2,64,128]{3,2,1,0:T(8,128)(2,1)S(1)} %gather_fusion.1, pred[16]{0:T(512)(128)(4,1)S(1)} %get-tuple-element.23), kind=kLoop, calls=%fused_computation.8 | loop fusion | flops 262144 | bytes 1048592 | tf_op jit(solution)/shard_map/jit(_take)/select_n | solution.py:286
  9.8 6.3 %all-to-all-start = ((bf16[16,2,64,128]{3,2,1,0:T(8,128)(2,1)}), bf16[16,2,64,128]{3,2,1,0:T(8,128)(2,1)S(1)}, u32[]{:S(2)}, u32[]{:S(2)}) async-start(bf16[16,2,64,128]{3,2,1,0:T(8,128)(2,1)} %broadcast_select_fusion.1), calls=%async_computation | async-start | bytes 1048576 | tf_op jit(solution)/shard_map/all_to_all | solution.py:287
  16.2 0.6 iota_reduce_fusion
  16.8 13.7 %all-to-all-done.refs_6_ = bf16[16,2,64,128]{3,2,1,0:T(8,128)(2,1)S(1)} async-done(((bf16[16,2,64,128]{3,2,1,0:T(8,128)(2,1)}), bf16[16,2,64,128]{3,2,1,0:T(8,128)(2,1)S(1)}, u32[]{:S(2)}, u32[]{:S(2)}) %all-to-all-start) | async-done | bytes 524320 | tf_op jit(solution)/shard_map/all_to_all | solution.py:287
  30.5 0.6 gather_fusion
  31.1 0.1 broadcast_select_fusion.2
  31.2 1.6 %collective-permute-start.1 = (bf16[4,2,64,128]{3,2,1,0:T(8,128)(2,1)S(1)}, bf16[4,2,64,128]{3,2,1,0:T(8,128)(2,1)S(1)}, u32[]{:S(2)}, u32[]{:S(2)}) collective-permute-start(bf16[4,2,64,128]{3,2,1,0:T(8,128)(2,1)S(1)} %broadcast_select_fusion.2), channel_id=1, source_target_pairs={{0,1},{1,0},{2,3},{3,2},{4,5},{5,4},{6,7},{7,6},{8,9},{9,8},{10,11... | collective-permute-start | bytes 393224 | tf_op jit(solution)/shard_map/ppermute | solution.py:288
  32.9 3.8 %collective-permute-done.1.refs_7_ = bf16[4,2,64,128]{3,2,1,0:T(8,128)(2,1)S(1)} collective-permute-done((bf16[4,2,64,128]{3,2,1,0:T(8,128)(2,1)S(1)}, bf16[4,2,64,128]{3,2,1,0:T(8,128)(2,1)S(1)}, u32[]{:S(2)}, u32[]{:S(2)}) %collective-permute-start.1) | collective-permute-done | bytes 131104 | tf_op jit(solution)/shard_map/ppermute | solution.py:288
  36.7 7.4 %attention.1 = (bf16[4096,128]{1,0:T(8,128)(2,1)}, bf16[4096,128]{1,0:T(8,128)(2,1)}, f32[512,128]{1,0:T(8,128)S(1)}, f32[512,128]{1,0:T(8,128)S(1)}, bf16[4,2,6...) custom-call(s32[4]{0:T(128)S(1)} %fusion.23.refs_0_, s32[4]{0:T(128)S(1)} %fusion.24.refs_1_, ...), custom_call_target="tpu_custom_call" | custom-call | tf_op jit(solution)/shard_map/attention/pallas_call | solution.py:311
  44.1 1.5 %collective-permute-start.2 = (bf16[4,2,64,128]{3,2,1,0:T(8,128)(2,1)S(1)}, bf16[4,2,64,128]{3,2,1,0:T(8,128)(2,1)S(1)}, u32[]{:S(2)}, u32[]{:S(2)}) collective-permute-start(bf16[4,2,64,128]{3,2,1,0:T(8,128)(2,1)S(1)} %get-tuple-element.16), channel_id=1, source_target_pairs={{0,1},{1,0},{2,3},{3,2},{4,5},{5,4},{6,7},{7,6},{8,9},{9,8},{10,11... | collective-permute-start | bytes 393224 | tf_op jit(solution)/shard_map/ppermute | solution.py:338
  45.6 3.4 %collective-permute-done.2 = bf16[4,2,64,128]{3,2,1,0:T(8,128)(2,1)S(1)} collective-permute-done((bf16[4,2,64,128]{3,2,1,0:T(8,128)(2,1)S(1)}, bf16[4,2,64,128]{3,2,1,0:T(8,128)(2,1)S(1)}, u32[]{:S(2)}, u32[]{:S(2)}) %collective-permute-start.2) | collective-permute-done | bytes 131104 | tf_op jit(solution)/shard_map/ppermute | solution.py:338
  49.1 0.6 gather_fusion.2
  49.7 0.1 broadcast_select_fusion
  49.8 18.6 %all_to_all.10 = bf16[16,2,64,128]{3,2,1,0:T(8,128)(2,1)S(1)} all-to-all(bf16[16,2,64,128]{3,2,1,0:T(8,128)(2,1)S(1)} %broadcast_select_fusion), channel_id=1, replica_groups=mesh['grp'=16,'uly'=2] {'grp'}, dimensions={0} | all-to-all | bytes 1048576 | tf_op jit(solution)/shard_map/all_to_all | solution.py:343
  68.5 0.4 fusion
  68.9 1.6 %collective-permute-start.3 = (bf16[4,2,64,128]{3,0,2,1:T(4,128)(2,1)S(1)}, bf16[4,2,64,128]{3,0,2,1:T(4,128)(2,1)S(1)}, u32[]{:S(2)}, u32[]{:S(2)}) collective-permute-start(bf16[4,2,64,128]{3,0,2,1:T(4,128)(2,1)S(1)} %slice.36), channel_id=1, source_target_pairs={{0,1},{1,0},{2,3},{3,2},{4,5},{5,4},{6,7},{7,6},{8,9},{9,8},{10,11... | collective-permute-start | bytes 393224 | tf_op jit(solution)/shard_map/ppermute | solution.py:349
  70.5 3.9 %collective-permute-done.3 = bf16[4,2,64,128]{3,0,2,1:T(4,128)(2,1)S(1)} collective-permute-done((bf16[4,2,64,128]{3,0,2,1:T(4,128)(2,1)S(1)}, bf16[4,2,64,128]{3,0,2,1:T(4,128)(2,1)S(1)}, u32[]{:S(2)}, u32[]{:S(2)}) %collective-permute-start.3) | collective-permute-done | bytes 131104 | tf_op jit(solution)/shard_map/ppermute | solution.py:349
  74.5 0.1 pad_maximum_fusion
  74.7 0.7 add_convert_fusion
  75.4 0.7 add_convert_fusion.1
  (37 shorter events, 0.6 us)
Async XLA Ops:
  1.6 6.5 %collective-permute-start = (bf16[4,2,64,128]{3,2,0,1:T(8,128)(2,1)S(1)}, bf16[4,2,64,128]{3,2,0,1:T(8,128)(2,1)S(1)}, u32[]{:S(2)}, u32[]{:S(2)}) collective-permute-start(bf16[4,2,64,128]{3,2,0,1:T(8,128)(2,1)S(1)} %get-tuple-element.30), channel_id=1, source_target_pairs={{0,1},{1,0},{2,3},{3,2},{4,5},{5,4},{6,7},{7,6},{8,9},{9,8},{10,11... | collective-permute-start | bytes 393224 | tf_op jit(solution)/shard_map/ppermute | solution.py:285
  4.6 0.7 copy-start.4
  5.4 0.7 copy-start.5
  8.8 27.8 %copy-start.1 = (bf16[128,32,128]{2,1,0:T(8,128)(2,1)S(1)}, bf16[128,32,128]{2,1,0:T(8,128)(2,1)}, u32[]{:S(2)}) copy-start(bf16[128,32,128]{2,1,0:T(8,128)(2,1)} %param.11) | copy-start | bytes 3145732
  9.7 26.9 %copy-start = (bf16[128,32,128]{2,1,0:T(8,128)(2,1)S(1)}, bf16[128,32,128]{2,1,0:T(8,128)(2,1)}, u32[]{:S(2)}) copy-start(bf16[128,32,128]{2,1,0:T(8,128)(2,1)} %param.8) | copy-start | bytes 3145732
  9.8 20.7 %all-to-all-start = ((bf16[16,2,64,128]{3,2,1,0:T(8,128)(2,1)}), bf16[16,2,64,128]{3,2,1,0:T(8,128)(2,1)S(1)}, u32[]{:S(2)}, u32[]{:S(2)}) async-start(bf16[16,2,64,128]{3,2,1,0:T(8,128)(2,1)} %broadcast_select_fusion.1), calls=%async_computation | async-start | bytes 1048576 | tf_op jit(solution)/shard_map/all_to_all | solution.py:287
  16.8 16.0 %copy-start.6 = (s32[16]{0:T(128)}, s32[16]{0:T(128)S(1)}, u32[]{:S(2)}) copy-start(s32[16]{0:T(128)S(1)} %get-tuple-element.17) | copy-start | bytes 196
  31.1 5.6 %copy-start.2 = (bf16[128,4,128]{2,1,0:T(4,128)(2,1)S(1)}, bf16[128,4,128]{2,1,0:T(4,128)(2,1)}, u32[]{:S(2)}) copy-start(bf16[128,4,128]{2,1,0:T(4,128)(2,1)} %param.9) | copy-start | bytes 393220
  31.1 5.6 %copy-start.3 = (bf16[128,4,128]{2,1,0:T(4,128)(2,1)S(1)}, bf16[128,4,128]{2,1,0:T(4,128)(2,1)}, u32[]{:S(2)}) copy-start(bf16[128,4,128]{2,1,0:T(4,128)(2,1)} %param.10) | copy-start | bytes 393220
  31.2 5.5 %collective-permute-start.1 = (bf16[4,2,64,128]{3,2,1,0:T(8,128)(2,1)S(1)}, bf16[4,2,64,128]{3,2,1,0:T(8,128)(2,1)S(1)}, u32[]{:S(2)}, u32[]{:S(2)}) collective-permute-start(bf16[4,2,64,128]{3,2,1,0:T(8,128)(2,1)S(1)} %broadcast_select_fusion.2), channel_id=1, source_target_pairs={{0,1},{1,0},{2,3},{3,2},{4,5},{5,4},{6,7},{7,6},{8,9},{9,8},{10,11... | collective-permute-start | bytes 393224 | tf_op jit(solution)/shard_map/ppermute | solution.py:288
  44.1 1.5 %copy-start.7 = (s32[16]{0:T(128)S(1)}, s32[16]{0:T(128)}, u32[]{:S(2)}) copy-start(s32[16]{0:T(128)} %copy-done.6) | copy-start | bytes 196
  44.1 5.0 %collective-permute-start.2 = (bf16[4,2,64,128]{3,2,1,0:T(8,128)(2,1)S(1)}, bf16[4,2,64,128]{3,2,1,0:T(8,128)(2,1)S(1)}, u32[]{:S(2)}, u32[]{:S(2)}) collective-permute-start(bf16[4,2,64,128]{3,2,1,0:T(8,128)(2,1)S(1)} %get-tuple-element.16), channel_id=1, source_target_pairs={{0,1},{1,0},{2,3},{3,2},{4,5},{5,4},{6,7},{7,6},{8,9},{9,8},{10,11... | collective-permute-start | bytes 393224 | tf_op jit(solution)/shard_map/ppermute | solution.py:338
  68.9 5.5 %collective-permute-start.3 = (bf16[4,2,64,128]{3,0,2,1:T(4,128)(2,1)S(1)}, bf16[4,2,64,128]{3,0,2,1:T(4,128)(2,1)S(1)}, u32[]{:S(2)}, u32[]{:S(2)}) collective-permute-start(bf16[4,2,64,128]{3,0,2,1:T(4,128)(2,1)S(1)} %slice.36), channel_id=1, source_target_pairs={{0,1},{1,0},{2,3},{3,2},{4,5},{5,4},{6,7},{7,6},{8,9},{9,8},{10,11... | collective-permute-start | bytes 393224 | tf_op jit(solution)/shard_map/ppermute | solution.py:349

commit v2 on v1

--- a/solution.py
+++ b/solution.py
@@ -183,24 +183,95 @@
 
 
 HIDDEN = -1e30
-
-
-def attention_kernel(
+LAST = (((1,), (1,)), ((), ()))
+FIRST = (((0,), (0,)), ((), ()))
+F32 = jnp.float32
+BF16 = jnp.bfloat16
+
+
+def dot_last(left, right):
+    return lax.dot_general(left, right, LAST, preferred_element_type=F32)
+
+
+def dot_first(left, right):
+    return lax.dot_general(left, right, FIRST, preferred_element_type=F32)
+
+
+def same_head(rows, cols, heads, kv_heads):
+    row = lax.broadcasted_iota(jnp.int32, (rows, cols), 0)
+    col = lax.broadcasted_iota(jnp.int32, (rows, cols), 1)
+    same = (row % heads) // (heads // kv_heads) == col % kv_heads
+    causal = col // kv_heads <= row // heads
+    return same, causal
+
+
+def near_kernel(q_ref, g_ref, k_ref, v_ref, stat_ref, bias_ref, *, heads, kv_heads, score_scale):
+    rows = q_ref.shape[0]
+    cols = k_ref.shape[0]
+
+    @pl.when(pl.program_id(0) == 0)
+    def _():
+        same, causal = same_head(rows, cols, heads, kv_heads)
+        bias_ref[...] = jnp.where(same & causal, 0.0, HIDDEN)
+
+    scores = dot_last(q_ref[...], k_ref[...]) * score_scale + bias_ref[...]
+    highest = jnp.max(scores, axis=1, keepdims=True)
+    raised = jnp.exp(scores - highest)
+    total = jnp.sum(raised, axis=1, keepdims=True)
+    delta = jnp.sum(raised * dot_last(g_ref[...], v_ref[...]), axis=1, keepdims=True)
+    lane = lax.broadcasted_iota(jnp.int32, stat_ref.shape, 1)
+    stat_ref[...] = jnp.where(lane == 0, highest, jnp.where(lane == 1, total, delta))
+
+
+def far_kernel(
+    source_ref, seen_ref, q_ref, g_ref, stat_ref, mine_ref, other_ref,
+    far_mine_ref, far_other_ref, bias_ref, *, heads, kv_heads, score_scale
+):
+    step = pl.program_id(0)
+    rows = q_ref.shape[0]
+    half = mine_ref.shape[2]
+
+    @pl.when(step == 0)
+    def _():
+        same, _ = same_head(rows, 2 * half, heads, kv_heads)
+        bias_ref[...] = jnp.where(same, 0.0, HIDDEN)
+
+    seen_bias = jnp.where(seen_ref[step] > 0, 0.0, HIDDEN)
+    q = q_ref[...]
+    g = g_ref[...]
+    k_far = jnp.concatenate([mine_ref[0, 0], other_ref[0, 0]], axis=0)
+    v_far = jnp.concatenate([mine_ref[0, 1], other_ref[0, 1]], axis=0)
+    stat = stat_ref[...]
+    scores = dot_last(q, k_far) * score_scale + (bias_ref[...] + seen_bias)
+    near_highest = stat[:, 0:1]
+    highest = jnp.maximum(near_highest, jnp.max(scores, axis=1, keepdims=True))
+    raised = jnp.exp(scores - highest)
+    shrink = jnp.exp(near_highest - highest)
+    dprobs = dot_last(g, v_far)
+    total = shrink * stat[:, 1:2] + jnp.sum(raised, axis=1, keepdims=True)
+    inverse = 1.0 / total
+    delta = (shrink * stat[:, 2:3] + jnp.sum(raised * dprobs, axis=1, keepdims=True)) * inverse
+    probs = raised * inverse
+    dscores = (probs * (dprobs - delta)).astype(BF16)
+    dk = (dot_first(dscores, q) * score_scale).astype(BF16)
+    dv = dot_first(probs.astype(BF16), g).astype(BF16)
+    far_mine_ref[0, 0] = dk[:half]
+    far_mine_ref[0, 1] = dv[:half]
+    far_other_ref[0, 0] = dk[half:]
+    far_other_ref[0, 1] = dv[half:]
+
+
+def local_kernel(
     source_ref, seen_ref, q_ref, g_ref, k_ref, v_ref, mine_ref, other_ref,
-    att_ref, dq_ref, dk_ref, dv_ref, far_mine_ref, far_other_ref, bias_ref,
-    *, heads, kv_heads, score_scale
+    att_ref, dq_ref, dk_ref, dv_ref, bias_ref, *, heads, kv_heads, score_scale
 ):
     step = pl.program_id(0)
     rows = q_ref.shape[0]
     cols = k_ref.shape[0]
-    half = mine_ref.shape[2]
 
     @pl.when(step == 0)
     def _():
-        row = lax.broadcasted_iota(jnp.int32, (rows, cols), 0)
-        col = lax.broadcasted_iota(jnp.int32, (rows, cols), 1)
-        same = (row % heads) // (heads // kv_heads) == col % kv_heads
-        causal = col // kv_heads <= row // heads
+        same, causal = same_head(rows, cols, heads, kv_heads)
         bias_ref[:, :cols] = jnp.where(same & causal, 0.0, HIDDEN)
         bias_ref[:, cols:] = jnp.where(same, 0.0, HIDDEN)
 
@@ -209,31 +280,25 @@
     v_all = jnp.concatenate([v_ref[...], mine_ref[0, 1], other_ref[0, 1]], axis=0)
     q = q_ref[...]
     g = g_ref[...]
-    last = (((1,), (1,)), ((), ()))
-    first = (((0,), (0,)), ((), ()))
-    scores = lax.dot_general(q, k_all, last, preferred_element_type=jnp.float32) * score_scale
-    scores = scores + bias_ref[...]
+    scores = dot_last(q, k_all) * score_scale + bias_ref[...]
     scores = jnp.concatenate([scores[:, :cols], scores[:, cols:] + far_bias], axis=1)
     highest = jnp.max(scores, axis=1, keepdims=True)
     raised = jnp.exp(scores - highest)
     total = jnp.sum(raised, axis=1, keepdims=True)
     probs = raised * (1.0 / total)
-    weights = probs.astype(jnp.bfloat16)
-    attended = jnp.dot(weights, v_all, preferred_element_type=jnp.float32).astype(jnp.bfloat16)
+    weights = probs.astype(BF16)
+    attended = jnp.dot(weights, v_all, preferred_element_type=F32).astype(BF16)
     att_ref[...] = attended
-    delta = jnp.sum(g.astype(jnp.float32) * attended.astype(jnp.float32), axis=1, keepdims=True)
-    dprobs = lax.dot_general(g, v_all, last, preferred_element_type=jnp.float32)
-    dscores = (probs * (dprobs - delta)).astype(jnp.bfloat16)
-    dq = jnp.dot(dscores, k_all, preferred_element_type=jnp.float32) * score_scale
-    dq_ref[...] = dq.astype(jnp.bfloat16)
-    dk = lax.dot_general(dscores, q, first, preferred_element_type=jnp.float32) * score_scale
-    dv = lax.dot_general(weights, g, first, preferred_element_type=jnp.float32)
-    dk_ref[...] = dk[:cols]
-    dv_ref[...] = dv[:cols]
-    far_mine_ref[0, 0] = dk[cols:cols + half].astype(jnp.bfloat16)
-    far_mine_ref[0, 1] = dv[cols:cols + half].astype(jnp.bfloat16)
-    far_other_ref[0, 0] = dk[cols + half:].astype(jnp.bfloat16)
-    far_other_ref[0, 1] = dv[cols + half:].astype(jnp.bfloat16)
+    delta = jnp.sum(g.astype(F32) * attended.astype(F32), axis=1, keepdims=True)
+    dscores = (probs * (dot_last(g, v_all) - delta)).astype(BF16)
+    dq = jnp.dot(dscores, k_all, preferred_element_type=F32) * score_scale
+    dq_ref[...] = dq.astype(BF16)
+    dk_ref[...] = dot_first(dscores[:, :cols], q) * score_scale
+    dv_ref[...] = dot_first(weights[:, :cols], g)
+
+
+def take_rows(array, index):
+    return array.at[index].get(mode="promise_in_bounds")
 
 
 def whole_blocks(queries, keys, values, output_cotangent, block_lists, list_counts):
@@ -249,7 +314,7 @@
     rows = block_tok * heads
     cols = block_tok * kv_heads
     half = cols // 2
-    score_scale = width ** (-0.5)
+    sizes = dict(heads=heads, kv_heads=kv_heads, score_scale=width ** (-0.5))
     swap = [(0, 1), (1, 0)]
 
     lists = block_lists.reshape(grp_count, per_group)
@@ -276,17 +341,6 @@
         send_place % mine_blocks + mine_blocks,
     )
 
-    parts = jnp.stack(
-        [keys.reshape(mine_blocks, 2, half, width), values.reshape(mine_blocks, 2, half, width)],
-        axis=2,
-    )
-    kept = lax.dynamic_index_in_dim(parts, my_half, 1, keepdims=False)
-    given = lax.dynamic_index_in_dim(parts, 1 - my_half, 1, keepdims=False)
-    gotten = lax.ppermute(given, "uly", swap)
-    outgoing = jnp.take(jnp.concatenate([kept, gotten]), owner_first, axis=0)
-    arrived = lax.all_to_all(outgoing, "grp", split_axis=0, concat_axis=0, tiled=True)
-    other = lax.ppermute(jnp.take(arrived, source_sib, axis=0), "uly", swap)
-
     q2 = queries.reshape(tokens * heads, width)
     g2 = output_cotangent.reshape(tokens * heads, width)
     k2 = keys.reshape(tokens * kv_heads, width)
@@ -306,53 +360,76 @@
 
     row_spec = pl.BlockSpec((rows, width), step_rows)
     col_spec = pl.BlockSpec((cols, width), step_rows)
-    f32 = jnp.float32
-    bf16 = jnp.bfloat16
-    attended, dq, dk_near, dv_near, far_mine, far_other = pl.pallas_call(
-        lambda *refs: attention_kernel(
-            *refs, heads=heads, kv_heads=kv_heads, score_scale=score_scale
-        ),
-        grid_spec=pltpu.PrefetchScalarGridSpec(
-            num_scalar_prefetch=2,
-            grid=(mine_blocks,),
-            in_specs=[
-                row_spec, row_spec, col_spec, col_spec, far_spec(from_source), far_spec(step_part)
-            ],
-            out_specs=[
-                row_spec, row_spec, col_spec, col_spec, far_spec(step_part), far_spec(step_part)
-            ],
-            scratch_shapes=[pltpu.VMEM((rows, 2 * cols), f32)],
-        ),
-        out_shape=[
-            jax.ShapeDtypeStruct(q2.shape, bf16),
-            jax.ShapeDtypeStruct(q2.shape, bf16),
-            jax.ShapeDtypeStruct(k2.shape, f32),
-            jax.ShapeDtypeStruct(k2.shape, f32),
-            jax.ShapeDtypeStruct((mine_blocks, 2, half, width), bf16),
-            jax.ShapeDtypeStruct((mine_blocks, 2, half, width), bf16),
-        ],
-        compiler_params=pltpu.CompilerParams(vmem_limit_bytes=48 * 1024 * 1024),
-        name="attention",
-    )(source_own, seen_own, q2, g2, k2, v2, arrived, other)
+    far_shape = jax.ShapeDtypeStruct((mine_blocks, 2, half, width), BF16)
+
+    def call(kernel, scalars, in_specs, out_specs, out_shape, bias_cols, name, operands):
+        return pl.pallas_call(
+            lambda *refs: kernel(*refs, **sizes),
+            grid_spec=pltpu.PrefetchScalarGridSpec(
+                num_scalar_prefetch=len(scalars),
+                grid=(mine_blocks,),
+                in_specs=in_specs,
+                out_specs=out_specs,
+                scratch_shapes=[pltpu.VMEM((rows, bias_cols), F32)],
+            ),
+            out_shape=out_shape,
+            compiler_params=pltpu.CompilerParams(vmem_limit_bytes=48 * 1024 * 1024),
+            name=name,
+        )(*scalars, *operands)
+
+    parts = jnp.stack(
+        [keys.reshape(mine_blocks, 2, half, width), values.reshape(mine_blocks, 2, half, width)],
+        axis=2,
+    )
+    kept = lax.dynamic_index_in_dim(parts, my_half, 1, keepdims=False)
+    given = lax.dynamic_index_in_dim(parts, 1 - my_half, 1, keepdims=False)
+    gotten = lax.ppermute(given, "uly", swap)
+    outgoing = take_rows(jnp.concatenate([kept, gotten]), owner_first)
+    outgoing, k2n = lax.optimization_barrier((outgoing, k2))
+    arrived = lax.all_to_all(outgoing, "grp", split_axis=0, concat_axis=0, tiled=True)
+    stats = call(
+        near_kernel, (), [row_spec, row_spec, col_spec, col_spec], row_spec,
+        jax.ShapeDtypeStruct((tokens * heads, width), F32), cols, "near", (q2, g2, k2n, v2),
+    )
+    arrived, stats = lax.optimization_barrier((arrived, stats))
+    other = lax.ppermute(take_rows(arrived, source_sib), "uly", swap)
+
+    far_mine, far_other = call(
+        far_kernel, (source_own, seen_own),
+        [row_spec, row_spec, row_spec, far_spec(from_source), far_spec(step_part)],
+        [far_spec(step_part), far_spec(step_part)], [far_shape, far_shape], cols, "far",
+        (q2, g2, stats, arrived, other),
+    )
 
     from_sib = lax.ppermute(far_other, "uly", swap)
     groups = jnp.arange(grp_count)
     source_both = jnp.concatenate([source_own, source_sib])
     asked = jnp.argmax(source_both[None, :] == groups[:, None], axis=1)
-    returning = jnp.take(jnp.concatenate([far_mine, from_sib]), asked, axis=0)
+    returning = take_rows(jnp.concatenate([far_mine, from_sib]), asked)
+    returning, k2l = lax.optimization_barrier((returning, k2))
     landed = lax.all_to_all(returning, "grp", split_axis=0, concat_axis=0, tiled=True)
+    row_shape = jax.ShapeDtypeStruct(q2.shape, BF16)
+    near_shape = jax.ShapeDtypeStruct(k2.shape, F32)
+    attended, dq, dk_near, dv_near = call(
+        local_kernel, (source_own, seen_own),
+        [row_spec, row_spec, col_spec, col_spec, far_spec(from_source), far_spec(step_part)],
+        [row_spec, row_spec, col_spec, col_spec],
+        [row_shape, row_shape, near_shape, near_shape], 2 * cols, "local",
+        (q2, g2, k2l, v2, arrived, other),
+    )
+    landed, dk_near = lax.optimization_barrier((landed, dk_near))
     routing = ((owner_first[:, None] == jnp.arange(per_group)[None, :]) & sending[:, None]).astype(
-        bf16
-    )
-    summed = jnp.einsum("sp,sxrd->pxrd", routing, landed, preferred_element_type=f32)
+        BF16
+    )
+    summed = jnp.einsum("sp,sxrd->pxrd", routing, landed, preferred_element_type=F32)
     summed_own = summed[:mine_blocks]
-    back = lax.ppermute(summed[mine_blocks:].astype(bf16), "uly", swap)
-    first_half = jnp.where(my_half == 0, summed_own, back.astype(f32))
-    second_half = jnp.where(my_half == 0, back.astype(f32), summed_own)
+    back = lax.ppermute(summed[mine_blocks:].astype(BF16), "uly", swap)
+    first_half = jnp.where(my_half == 0, summed_own, back.astype(F32))
+    second_half = jnp.where(my_half == 0, back.astype(F32), summed_own)
     far_sum = jnp.stack([first_half, second_half], axis=1)
-    near_shape = (mine_blocks, 2, half, width)
-    dk = (dk_near.reshape(near_shape) + far_sum[:, :, 0]).astype(bf16).reshape(keys.shape)
-    dv = (dv_near.reshape(near_shape) + far_sum[:, :, 1]).astype(bf16).reshape(keys.shape)
+    split = (mine_blocks, 2, half, width)
+    dk = (dk_near.reshape(split) + far_sum[:, :, 0]).astype(BF16).reshape(keys.shape)
+    dv = (dv_near.reshape(split) + far_sum[:, :, 1]).astype(BF16).reshape(keys.shape)
     return (attended.reshape(queries.shape), dq.reshape(queries.shape), dk, dv)
 
 

time: 76.5 us -> 81.6 us (1.067)
  blocking collectives: 18.6 us -> 0 us
  Pallas kernels: 7.37 us -> 18.7 us
  starting transfers between devices: 14 us -> 18.3 us
  local copies, waits for them, and re-layouts: 3.66 us -> 7.33 us
  waiting for transfers between devices: 25.8 us -> 28 us
  matrix products: 0.39 us -> 1.43 us
  other arithmetic: 5.54 us -> 6.48 us
    all_to_all x1 -> x0, blocking collectives: 18.6 us -> none  [whole_blocks(): lax.all_to_all(returning, 'grp', split_axis=0, concat_axis=0, tiled=True)]
    pallas_call x1 -> x3, Pallas kernels: 7.37 us -> 18.7 us  [call(): pl.pallas_call(lambda *refs: kernel(*refs, **sizes), grid_spec=pltpu.Pref...]
    all_to_all x0 -> x1, waiting for transfers between devices: none -> 6.93 us  [whole_blocks(): lax.all_to_all(returning, 'grp', split_axis=0, concat_axis=0, tiled=True)]
    all_to_all x0 -> x1, starting transfers between devices: none -> 4.43 us  [whole_blocks(): lax.all_to_all(returning, 'grp', split_axis=0, concat_axis=0, tiled=True)]
    all_to_all x1, waiting for transfers between devices: 13.7 us -> 10 us  [whole_blocks(): lax.all_to_all(outgoing, 'grp', split_axis=0, concat_axis=0, tiled=True)]
    unnamed x17 -> x15, local copies, waits for them, and re-layouts: 1.34 us -> 3.48 us
    gather x3, local copies, waits for them, and re-layouts: 1.87 us -> 3.4 us  [take_rows(): return array.at[index].get(mode='promise_in_bounds')]
    dot_general x1, matrix products: 0.39 us -> 1.43 us  [whole_blocks(): jnp.einsum('sp,sxrd->pxrd', routing, landed, preferred_element_type=F32)]
  transfers between devices with their start and end apart: 5 -> 6, of which waited for: 5 -> 6; matrix products, arithmetic and copies ran while one was open for 3% -> 6% of each run, Pallas kernels for 0% -> 12%
where the time goes in v2:
time: 81.6 us; the launch traced here: 81.1 us
  waiting for transfers between devices  28 us (34%)
  Pallas kernels  18.7 us (23%)
  starting transfers between devices  18.3 us (22%)
  local copies, waits for them, and re-layouts  7.33 us (9%)
  other arithmetic  6.48 us (8%)
  matrix products  1.43 us (2%)
  between operations  0.84 us (1%)
    pallas_call x3, Pallas kernels, call(): pl.pallas_call(lambda *refs: kernel(*refs, **sizes), grid_spec=pltpu.Pref...  18.7 us
    all_to_all x1, waiting for transfers between devices, whole_blocks(): lax.all_to_all(outgoing, 'grp', split_axis=0, concat_axis=0, tiled=True)  10 us
    all_to_all x1, waiting for transfers between devices, whole_blocks(): lax.all_to_all(returning, 'grp', split_axis=0, concat_axis=0, tiled=True)  6.93 us
    all_to_all x1, starting transfers between devices, whole_blocks(): lax.all_to_all(outgoing, 'grp', split_axis=0, concat_axis=0, tiled=True)  6.13 us
    all_to_all x1, starting transfers between devices, whole_blocks(): lax.all_to_all(returning, 'grp', split_axis=0, concat_axis=0, tiled=True)  4.43 us
    ppermute x1, waiting for transfers between devices, whole_blocks(): back = lax.ppermute(summed[mine_blocks:].astype(BF16), 'uly', swap)  3.9 us
    unnamed x15, local copies, waits for them, and re-layouts  3.48 us
    ppermute x1, waiting for transfers between devices, whole_blocks(): from_sib = lax.ppermute(far_other, 'uly', swap)  3.44 us
  transfers between devices with their start and end apart: 6, of which 6 were waited for; matrix products, arithmetic and copies ran while one was open for 6% of the time, Pallas kernels for 12%

profile of v2, /device:TPU:0, one launch (start us, length us, event | category | flops | bytes accessed | tf_op | source)
XLA Modules:
  0.0 81.1 jit_solution(4516498012312201249)
XLA Ops:
  0.7 1.1 %fusion.8 = (bf16[4,2,64,128]{3,2,0,1:T(8,128)(2,1)S(1)}, bf16[4,2,64,128]{3,2,0,1:T(8,128)(2,1)S(1)}) fusion(s32[]{:T(128)S(6)} %select_n.132, bf16[4,2,1,64,128]{4,3,1,0,2:T(8,128)(2,1)} %bitcast.54, bf16[4,2,1,64,128]{4,3,1,0,2:T(8,128)(2,1)} %bitcast.57, s32[]{:T(128)S(6)} %select_n.133), kind=kLoop, calls=%fused_computation.25 | loop fusion | flops 131072 | bytes 524296 | tf_op jit(solution)/shard_map/jit(dynamic_index_in_dim)/squeeze | solution.py:384
  1.8 3.0 %collective-permute-start = (bf16[4,2,64,128]{3,2,0,1:T(8,128)(2,1)S(1)}, bf16[4,2,64,128]{3,2,0,1:T(8,128)(2,1)S(1)}, u32[]{:S(2)}, u32[]{:S(2)}) collective-permute-start(bf16[4,2,64,128]{3,2,0,1:T(8,128)(2,1)S(1)} %get-tuple-element.41), channel_id=1, source_target_pairs={{0,1},{1,0},{2,3},{3,2},{4,5},{5,4},{6,7},{7,6},{8,9},{9,8},{10,11... | collective-permute-start | bytes 393224 | tf_op jit(solution)/shard_map/ppermute | solution.py:386
  4.8 0.7 broadcast_compare_fusion
  5.6 0.5 broadcast.258
  6.1 1.3 %reduce.30 = s32[128]{0:T(128)S(1)} reduce(s32[128,1]{0,1:T(1,128)} %param.10, s32[]{:T(128)} %broadcast.258), dimensions={1}, to_apply=%param.10.reduce_sub_computation.3 | reduce | bytes 1028 | tf_op args[4]
  7.5 0.1 fusion.28
  7.6 0.1 fusion.11
  7.8 0.5 collective-permute-done
  8.4 1.4 %gather_fusion = bf16[16,2,64,128]{3,2,1,0:T(8,128)(2,1)} fusion(bf16[8,2,64,128]{3,2,0,1:T(8,128)(2,1)S(1)} %pad_maximum_fusion.1, s32[1024]{0:T(1024)S(1)} %pad_clamp_fusion.2), kind=kCustom, calls=%fused_computation | custom fusion | bytes 1048640 | tf_op jit(solution)/shard_map/gather | solution.py:301
  9.8 6.1 %all-to-all-start = ((bf16[16,2,64,128]{3,2,1,0:T(8,128)(2,1)}), bf16[16,2,64,128]{3,2,1,0:T(8,128)(2,1)S(1)}, u32[]{:S(2)}, u32[]{:S(2)}) async-start(bf16[16,2,64,128]{3,2,1,0:T(8,128)(2,1)} %gather_fusion), calls=%async_computation | async-start | bytes 1048576 | tf_op jit(solution)/shard_map/all_to_all | solution.py:389
  16.2 2.8 %near.1.refs_4_ = f32[4096,128]{1,0:T(8,128)S(1)} custom-call(bf16[4096,128]{1,0:T(8,128)(2,1)S(1)} %bitcast.48, bf16[4096,128]{1,0:T(8,128)(2,1)S(1)} %bitcast.51, bf16[512,128]{1,0:T(8,128)(2,1)S(1)} %bitcast.55, bf16[512,128]{1,0:T(8,128)(2,1)S(1)} %bitcast.58), custom_call_target="tpu_custom_call" | custom-call | tf_op jit(solution)/shard_map/near/pallas_call | solution.py:366
  19.0 1.3 %copy-done.2 = f32[4096,128]{1,0:T(8,128)} copy-done((f32[4096,128]{1,0:T(8,128)}, f32[4096,128]{1,0:T(8,128)S(1)}, u32[]{:S(2)}) %copy-start.2) | copy-done | bytes 2097176
  20.4 10.0 %all-to-all-done.refs_5_.refs_6_ = bf16[16,2,64,128]{3,2,1,0:T(8,128)(2,1)S(1)} async-done(((bf16[16,2,64,128]{3,2,1,0:T(8,128)(2,1)}), bf16[16,2,64,128]{3,2,1,0:T(8,128)(2,1)S(1)}, u32[]{:S(2)}, u32[]{:S(2)}) %all-to-all-start) | async-done | bytes 524320 | tf_op jit(solution)/shard_map/all_to_all | solution.py:389
  30.4 0.6 gather_fusion.1
  31.0 1.6 %collective-permute-start.1 = (bf16[4,2,64,128]{3,2,1,0:T(8,128)(2,1)S(1)}, bf16[4,2,64,128]{3,2,1,0:T(8,128)(2,1)S(1)}, u32[]{:S(2)}, u32[]{:S(2)}) collective-permute-start(bf16[4,2,64,128]{3,2,1,0:T(8,128)(2,1)S(1)} %gather_fusion.1), channel_id=1, source_target_pairs={{0,1},{1,0},{2,3},{3,2},{4,5},{5,4},{6,7},{7,6},{8,9},{9,8},{10,11... | collective-permute-start | bytes 393224 | tf_op jit(solution)/shard_map/ppermute | solution.py:395
  32.5 0.6 iota_reduce_fusion
  33.2 3.2 %collective-permute-done.1.refs_6_.refs_7_ = bf16[4,2,64,128]{3,2,1,0:T(8,128)(2,1)S(1)} collective-permute-done((bf16[4,2,64,128]{3,2,1,0:T(8,128)(2,1)S(1)}, bf16[4,2,64,128]{3,2,1,0:T(8,128)(2,1)S(1)}, u32[]{:S(2)}, u32[]{:S(2)}) %collective-permute-start.1) | collective-permute-done | bytes 131104 | tf_op jit(solution)/shard_map/ppermute | solution.py:395
  36.4 1.6 %copy-done.3 = f32[4096,128]{1,0:T(8,128)S(1)} copy-done((f32[4096,128]{1,0:T(8,128)S(1)}, f32[4096,128]{1,0:T(8,128)}, u32[]{:S(2)}) %copy-start.3) | copy-done | bytes 2097176
  38.0 8.9 %far.1 = (bf16[4,2,64,128]{3,2,1,0:T(8,128)(2,1)S(1)}, bf16[4,2,64,128]{3,2,1,0:T(8,128)(2,1)S(1)}) custom-call(s32[4]{0:T(128)S(1)} %get-tuple-element.43.refs_0_, s32[4]{0:T(128)S(1)} %fusion.24.refs_1_, bf16[4096,128]{1,0:T(8,128)(2,1)S(1)} %bitcast.49, bf16[4096,128]{1,0:T(8,128)(2,1)S(1)} %bitcast.52, f32[4096,128]{1,0:T(8,128)S(1)} %copy-done.3, ...), custom_call_target="tpu_custom_call" | custom-call | tf_op jit(solution)/shard_map/far/pallas_call | solution.py:366
  47.0 1.6 %collective-permute-start.2 = (bf16[4,2,64,128]{3,2,1,0:T(8,128)(2,1)S(1)}, bf16[4,2,64,128]{3,2,1,0:T(8,128)(2,1)S(1)}, u32[]{:S(2)}, u32[]{:S(2)}) collective-permute-start(bf16[4,2,64,128]{3,2,1,0:T(8,128)(2,1)S(1)} %get-tuple-element.24), channel_id=1, source_target_pairs={{0,1},{1,0},{2,3},{3,2},{4,5},{5,4},{6,7},{7,6},{8,9},{9,8},{10,11... | collective-permute-start | bytes 393224 | tf_op jit(solution)/shard_map/ppermute | solution.py:404
  48.6 3.4 %collective-permute-done.2 = bf16[4,2,64,128]{3,2,1,0:T(8,128)(2,1)S(1)} collective-permute-done((bf16[4,2,64,128]{3,2,1,0:T(8,128)(2,1)S(1)}, bf16[4,2,64,128]{3,2,1,0:T(8,128)(2,1)S(1)}, u32[]{:S(2)}, u32[]{:S(2)}) %collective-permute-start.2) | collective-permute-done | bytes 131104 | tf_op jit(solution)/shard_map/ppermute | solution.py:404
  52.0 1.4 %gather_fusion.2 = bf16[16,2,64,128]{3,2,1,0:T(8,128)(2,1)} fusion(bf16[8,2,64,128]{3,2,1,0:T(8,128)(2,1)S(1)} %pad_maximum_fusion.2, s32[1024]{0:T(1024)S(1)} %pad_clamp_fusion), kind=kCustom, calls=%fused_computation.2 | custom fusion | bytes 1048640 | tf_op jit(solution)/shard_map/gather | solution.py:301
  53.4 4.4 %all-to-all-start.1 = ((bf16[16,2,64,128]{3,2,1,0:T(8,128)(2,1)}), bf16[16,2,64,128]{3,2,1,0:T(8,128)(2,1)}, u32[]{:S(2)}, u32[]{:S(2)}) async-start(bf16[16,2,64,128]{3,2,1,0:T(8,128)(2,1)} %gather_fusion.2), calls=%async_computation.1 | async-start | bytes 1048576 | tf_op jit(solution)/shard_map/all_to_all | solution.py:410
  57.9 0.7 compare_select_fusion.3
  58.6 6.9 %local.1 = (bf16[4096,128]{1,0:T(8,128)(2,1)}, bf16[4096,128]{1,0:T(8,128)(2,1)}, f32[512,128]{1,0:T(8,128)S(1)}, f32[512,128]{1,0:T(8,128)S(1)}) custom-call(s32[4]{0:T(128)S(1)} %get-tuple-element.43.refs_0_, s32[4]{0:T(128)S(1)} %fusion.24.refs_1_, bf16[4096,128]{1,0:T(8,128)(2,1)S(1)} %bitcast.50, bf16[4096,128]{1,0:T(8,128)(2,1)S(1)} %bitcast.53, ...), custom_call_target="tpu_custom_call" | custom-call | tf_op jit(solution)/shard_map/local/pallas_call | solution.py:366
  65.5 6.9 %all-to-all-done.1 = bf16[16,2,64,128]{3,2,1,0:T(8,128)(2,1)} async-done(((bf16[16,2,64,128]{3,2,1,0:T(8,128)(2,1)}), bf16[16,2,64,128]{3,2,1,0:T(8,128)(2,1)}, u32[]{:S(2)}, u32[]{:S(2)}) %all-to-all-start.1) | async-done | bytes 524320 | tf_op jit(solution)/shard_map/all_to_all | solution.py:410
  72.4 1.4 %fusion = f32[8,2,64,128]{3,0,2,1:T(8,128)S(1)} fusion(bf16[16,2,64,128]{3,2,1,0:T(8,128)(2,1)} %all-to-all-done.1, s32[16]{0:T(128)S(1)} %compare_select_fusion.3, pred[16]{0:T(512)(128)(4,1)S(1)} %get-tuple-element.34), kind=kOutput, calls=%fused_computation.5 | convolution fusion | flops 4194560 | bytes 1048656 | tf_op jit(solution)/shard_map/sp,sxrd->pxrd/dot_general | solution.py:424
  73.9 1.6 %collective-permute-start.3 = (bf16[4,2,64,128]{3,0,2,1:T(4,128)(2,1)S(1)}, bf16[4,2,64,128]{3,0,2,1:T(4,128)(2,1)S(1)}, u32[]{:S(2)}, u32[]{:S(2)}) collective-permute-start(bf16[4,2,64,128]{3,0,2,1:T(4,128)(2,1)S(1)} %slice.36), channel_id=1, source_target_pairs={{0,1},{1,0},{2,3},{3,2},{4,5},{5,4},{6,7},{7,6},{8,9},{9,8},{10,11... | collective-permute-start | bytes 393224 | tf_op jit(solution)/shard_map/ppermute | solution.py:426
  75.5 3.9 %collective-permute-done.3 = bf16[4,2,64,128]{3,0,2,1:T(4,128)(2,1)S(1)} collective-permute-done((bf16[4,2,64,128]{3,0,2,1:T(4,128)(2,1)S(1)}, bf16[4,2,64,128]{3,0,2,1:T(4,128)(2,1)S(1)}, u32[]{:S(2)}, u32[]{:S(2)}) %collective-permute-start.3) | collective-permute-done | bytes 131104 | tf_op jit(solution)/shard_map/ppermute | solution.py:426
  79.5 0.1 pad_maximum_fusion
  79.7 0.7 add_convert_fusion
  80.4 0.7 add_convert_fusion.1
  (33 shorter events, 0.8 us)
Async XLA Ops:
  0.6 15.5 %copy-start.4 = (bf16[128,4,128]{2,1,0:T(4,128)(2,1)S(1)}, bf16[128,4,128]{2,1,0:T(4,128)(2,1)}, u32[]{:S(2)}) copy-start(bf16[128,4,128]{2,1,0:T(4,128)(2,1)} %param.7) | copy-start | bytes 393220
  0.6 15.5 %copy-start.5 = (bf16[128,4,128]{2,1,0:T(4,128)(2,1)S(1)}, bf16[128,4,128]{2,1,0:T(4,128)(2,1)}, u32[]{:S(2)}) copy-start(bf16[128,4,128]{2,1,0:T(4,128)(2,1)} %param.8) | copy-start | bytes 393220
  0.7 15.5 %copy-start.1 = (bf16[128,32,128]{2,1,0:T(8,128)(2,1)S(1)}, bf16[128,32,128]{2,1,0:T(8,128)(2,1)}, u32[]{:S(2)}) copy-start(bf16[128,32,128]{2,1,0:T(8,128)(2,1)} %param.9) | copy-start | bytes 3145732
  0.7 15.5 %copy-start = (bf16[128,32,128]{2,1,0:T(8,128)(2,1)S(1)}, bf16[128,32,128]{2,1,0:T(8,128)(2,1)}, u32[]{:S(2)}) copy-start(bf16[128,32,128]{2,1,0:T(8,128)(2,1)} %param.6) | copy-start | bytes 3145732
  1.8 6.5 %collective-permute-start = (bf16[4,2,64,128]{3,2,0,1:T(8,128)(2,1)S(1)}, bf16[4,2,64,128]{3,2,0,1:T(8,128)(2,1)S(1)}, u32[]{:S(2)}, u32[]{:S(2)}) collective-permute-start(bf16[4,2,64,128]{3,2,0,1:T(8,128)(2,1)S(1)} %get-tuple-element.41), channel_id=1, source_target_pairs={{0,1},{1,0},{2,3},{3,2},{4,5},{5,4},{6,7},{7,6},{8,9},{9,8},{10,11... | collective-permute-start | bytes 393224 | tf_op jit(solution)/shard_map/ppermute | solution.py:386
  7.8 0.6 copy-start.6
  9.8 20.6 %all-to-all-start = ((bf16[16,2,64,128]{3,2,1,0:T(8,128)(2,1)}), bf16[16,2,64,128]{3,2,1,0:T(8,128)(2,1)S(1)}, u32[]{:S(2)}, u32[]{:S(2)}) async-start(bf16[16,2,64,128]{3,2,1,0:T(8,128)(2,1)} %gather_fusion), calls=%async_computation | async-start | bytes 1048576 | tf_op jit(solution)/shard_map/all_to_all | solution.py:389
  19.0 1.4 %copy-start.2 = (f32[4096,128]{1,0:T(8,128)}, f32[4096,128]{1,0:T(8,128)S(1)}, u32[]{:S(2)}) copy-start(f32[4096,128]{1,0:T(8,128)S(1)} %near.1.refs_4_) | copy-start | bytes 6291460
  31.0 5.5 %collective-permute-start.1 = (bf16[4,2,64,128]{3,2,1,0:T(8,128)(2,1)S(1)}, bf16[4,2,64,128]{3,2,1,0:T(8,128)(2,1)S(1)}, u32[]{:S(2)}, u32[]{:S(2)}) collective-permute-start(bf16[4,2,64,128]{3,2,1,0:T(8,128)(2,1)S(1)} %gather_fusion.1), channel_id=1, source_target_pairs={{0,1},{1,0},{2,3},{3,2},{4,5},{5,4},{6,7},{7,6},{8,9},{9,8},{10,11... | collective-permute-start | bytes 393224 | tf_op jit(solution)/shard_map/ppermute | solution.py:395
  36.4 1.6 %copy-start.3 = (f32[4096,128]{1,0:T(8,128)S(1)}, f32[4096,128]{1,0:T(8,128)}, u32[]{:S(2)}) copy-start(f32[4096,128]{1,0:T(8,128)} %copy-done.2) | copy-start | bytes 6291460
  47.0 5.0 %collective-permute-start.2 = (bf16[4,2,64,128]{3,2,1,0:T(8,128)(2,1)S(1)}, bf16[4,2,64,128]{3,2,1,0:T(8,128)(2,1)S(1)}, u32[]{:S(2)}, u32[]{:S(2)}) collective-permute-start(bf16[4,2,64,128]{3,2,1,0:T(8,128)(2,1)S(1)} %get-tuple-element.24), channel_id=1, source_target_pairs={{0,1},{1,0},{2,3},{3,2},{4,5},{5,4},{6,7},{7,6},{8,9},{9,8},{10,11... | collective-permute-start | bytes 393224 | tf_op jit(solution)/shard_map/ppermute | solution.py:404
  53.4 19.0 %all-to-all-start.1 = ((bf16[16,2,64,128]{3,2,1,0:T(8,128)(2,1)}), bf16[16,2,64,128]{3,2,1,0:T(8,128)(2,1)}, u32[]{:S(2)}, u32[]{:S(2)}) async-start(bf16[16,2,64,128]{3,2,1,0:T(8,128)(2,1)} %gather_fusion.2), calls=%async_computation.1 | async-start | bytes 1048576 | tf_op jit(solution)/shard_map/all_to_all | solution.py:410
  73.9 5.5 %collective-permute-start.3 = (bf16[4,2,64,128]{3,0,2,1:T(4,128)(2,1)S(1)}, bf16[4,2,64,128]{3,0,2,1:T(4,128)(2,1)S(1)}, u32[]{:S(2)}, u32[]{:S(2)}) collective-permute-start(bf16[4,2,64,128]{3,0,2,1:T(4,128)(2,1)S(1)} %slice.36), channel_id=1, source_target_pairs={{0,1},{1,0},{2,3},{3,2},{4,5},{5,4},{6,7},{7,6},{8,9},{9,8},{10,11... | collective-permute-start | bytes 393224 | tf_op jit(solution)/shard_map/ppermute | solution.py:426

commit v3 on v2

--- a/solution.py
+++ b/solution.py
@@ -1,3 +1,5 @@
+from functools import partial
+
 import jax
 import jax.numpy as jnp
 from jax import lax
@@ -205,60 +207,124 @@
     return same, causal
 
 
-def near_kernel(q_ref, g_ref, k_ref, v_ref, stat_ref, bias_ref, *, heads, kv_heads, score_scale):
-    rows = q_ref.shape[0]
-    cols = k_ref.shape[0]
-
-    @pl.when(pl.program_id(0) == 0)
-    def _():
-        same, causal = same_head(rows, cols, heads, kv_heads)
-        bias_ref[...] = jnp.where(same & causal, 0.0, HIDDEN)
-
-    scores = dot_last(q_ref[...], k_ref[...]) * score_scale + bias_ref[...]
-    highest = jnp.max(scores, axis=1, keepdims=True)
-    raised = jnp.exp(scores - highest)
-    total = jnp.sum(raised, axis=1, keepdims=True)
-    delta = jnp.sum(raised * dot_last(g_ref[...], v_ref[...]), axis=1, keepdims=True)
-    lane = lax.broadcasted_iota(jnp.int32, stat_ref.shape, 1)
-    stat_ref[...] = jnp.where(lane == 0, highest, jnp.where(lane == 1, total, delta))
+def head_major(cols, kv_heads):
+    row = lax.broadcasted_iota(jnp.int32, (cols, cols), 0)
+    col = lax.broadcasted_iota(jnp.int32, (cols, cols), 1)
+    place = cols // kv_heads
+    return jnp.where(col == (row % place) * kv_heads + row // place, 1.0, 0.0).astype(BF16)
+
+
+def reorder(one_hot, array):
+    return jnp.dot(one_hot, array, preferred_element_type=F32).astype(BF16)
+
+
+def own_head(scores, lane_head, kv_heads):
+    place = scores.shape[0] // kv_heads
+    kept = scores[:place]
+    for head in range(1, kv_heads):
+        kept = jnp.where(lane_head == head, scores[head * place:(head + 1) * place], kept)
+    return kept
+
+
+def all_heads(kept, lane_head, kv_heads):
+    none = jnp.zeros_like(kept)
+    return jnp.concatenate(
+        [jnp.where(lane_head == head, kept, none) for head in range(kv_heads)], axis=0
+    )
+
+
+def near_kernel(q_ref, g_ref, k_ref, v_ref, stat_ref, *, heads, kv_heads, score_scale):
+    blocks = stat_ref.shape[0]
+    rows = q_ref.shape[0] // blocks
+    cols = k_ref.shape[0] // blocks
+    place = cols // kv_heads
+    order = head_major(cols, kv_heads)
+    lane = lax.broadcasted_iota(jnp.int32, (1, rows), 1)
+    lane_head = lane % heads // (heads // kv_heads)
+    causal = lax.broadcasted_iota(jnp.int32, (place, rows), 0) <= lane // heads
+    for block in range(blocks):
+        span = slice(block * rows, (block + 1) * rows)
+        narrow = slice(block * cols, (block + 1) * cols)
+        k_near = reorder(order, k_ref[narrow])
+        v_near = reorder(order, v_ref[narrow])
+        scores = own_head(dot_last(k_near, q_ref[span]), lane_head, kv_heads) * score_scale
+        scores = jnp.where(causal, scores, HIDDEN)
+        highest = jnp.max(scores, axis=0, keepdims=True)
+        raised = jnp.exp(scores - highest)
+        dprobs = own_head(dot_last(v_near, g_ref[span]), lane_head, kv_heads)
+        stat_ref[block, 0:1] = highest
+        stat_ref[block, 1:2] = jnp.sum(raised, axis=0, keepdims=True)
+        stat_ref[block, 2:3] = jnp.sum(raised * dprobs, axis=0, keepdims=True)
 
 
 def far_kernel(
-    source_ref, seen_ref, q_ref, g_ref, stat_ref, mine_ref, other_ref,
-    far_mine_ref, far_other_ref, bias_ref, *, heads, kv_heads, score_scale
+    source_ref, seen_ref, q_ref, g_ref, stat_ref, arrived_ref, other_ref,
+    far_mine_ref, far_other_ref, *, heads, kv_heads, score_scale
 ):
-    step = pl.program_id(0)
-    rows = q_ref.shape[0]
-    half = mine_ref.shape[2]
-
-    @pl.when(step == 0)
-    def _():
-        same, _ = same_head(rows, 2 * half, heads, kv_heads)
-        bias_ref[...] = jnp.where(same, 0.0, HIDDEN)
-
-    seen_bias = jnp.where(seen_ref[step] > 0, 0.0, HIDDEN)
-    q = q_ref[...]
-    g = g_ref[...]
-    k_far = jnp.concatenate([mine_ref[0, 0], other_ref[0, 0]], axis=0)
-    v_far = jnp.concatenate([mine_ref[0, 1], other_ref[0, 1]], axis=0)
-    stat = stat_ref[...]
-    scores = dot_last(q, k_far) * score_scale + (bias_ref[...] + seen_bias)
-    near_highest = stat[:, 0:1]
-    highest = jnp.maximum(near_highest, jnp.max(scores, axis=1, keepdims=True))
-    raised = jnp.exp(scores - highest)
-    shrink = jnp.exp(near_highest - highest)
-    dprobs = dot_last(g, v_far)
-    total = shrink * stat[:, 1:2] + jnp.sum(raised, axis=1, keepdims=True)
-    inverse = 1.0 / total
-    delta = (shrink * stat[:, 2:3] + jnp.sum(raised * dprobs, axis=1, keepdims=True)) * inverse
-    probs = raised * inverse
-    dscores = (probs * (dprobs - delta)).astype(BF16)
-    dk = (dot_first(dscores, q) * score_scale).astype(BF16)
-    dv = dot_first(probs.astype(BF16), g).astype(BF16)
-    far_mine_ref[0, 0] = dk[:half]
-    far_mine_ref[0, 1] = dv[:half]
-    far_other_ref[0, 0] = dk[half:]
-    far_other_ref[0, 1] = dv[half:]
+    blocks = stat_ref.shape[0]
+    rows = q_ref.shape[0] // blocks
+    half = other_ref.shape[2]
+    order = head_major(2 * half, kv_heads)
+    lane = lax.broadcasted_iota(jnp.int32, (1, rows), 1)
+    lane_head = lane % heads // (heads // kv_heads)
+    for block in range(blocks):
+        span = slice(block * rows, (block + 1) * rows)
+        source = source_ref[block]
+        q = q_ref[span]
+        g = g_ref[span]
+        k_far = reorder(
+            order, jnp.concatenate([arrived_ref[source, 0], other_ref[block, 0]], axis=0)
+        )
+        v_far = reorder(
+            order, jnp.concatenate([arrived_ref[source, 1], other_ref[block, 1]], axis=0)
+        )
+        hidden = jnp.where(seen_ref[block] > 0, 0.0, HIDDEN)
+        scores = own_head(dot_last(k_far, q), lane_head, kv_heads) * score_scale + hidden
+        near_highest = stat_ref[block, 0:1]
+        highest = jnp.maximum(near_highest, jnp.max(scores, axis=0, keepdims=True))
+        raised = jnp.exp(scores - highest)
+        shrink = jnp.exp(near_highest - highest)
+        dprobs = own_head(dot_last(v_far, g), lane_head, kv_heads)
+        total = shrink * stat_ref[block, 1:2] + jnp.sum(raised, axis=0, keepdims=True)
+        inverse = 1.0 / total
+        delta = shrink * stat_ref[block, 2:3] + jnp.sum(raised * dprobs, axis=0, keepdims=True)
+        probs = raised * inverse
+        dscores = (probs * (dprobs - delta * inverse)).astype(BF16)
+        dk = jnp.dot(all_heads(dscores, lane_head, kv_heads), q, preferred_element_type=F32)
+        dv = jnp.dot(
+            all_heads(probs.astype(BF16), lane_head, kv_heads), g, preferred_element_type=F32
+        )
+        dk = dot_first(order, (dk * score_scale).astype(BF16)).astype(BF16)
+        dv = dot_first(order, dv.astype(BF16)).astype(BF16)
+        far_mine_ref[block, 0] = dk[:half]
+        far_mine_ref[block, 1] = dv[:half]
+        far_other_ref[block, 0] = dk[half:]
+        far_other_ref[block, 1] = dv[half:]
+
+
+def land_kernel(place_ref, sending_ref, landed_ref, own_ref, give_ref, sum_ref):
+    blocks = own_ref.shape[0]
+    sum_ref[...] = jnp.zeros_like(sum_ref)
+    for group in range(landed_ref.shape[0]):
+
+        @pl.when(sending_ref[group] > 0)
+        def _():
+            place = place_ref[group]
+            sum_ref[place] = sum_ref[place] + landed_ref[group].astype(F32)
+
+    own_ref[...] = sum_ref[:blocks]
+    give_ref[...] = sum_ref[blocks:].astype(BF16)
+
+
+def finish_kernel(half_ref, dk_near_ref, dv_near_ref, own_ref, back_ref, dk_ref, dv_ref):
+    blocks, _, half, _ = back_ref.shape
+    mine = half_ref[0]
+    for block in range(blocks):
+        for near_ref, out_ref, which in ((dk_near_ref, dk_ref, 0), (dv_near_ref, dv_ref, 1)):
+            for sums_ref, place in ((own_ref, mine), (back_ref, 1 - mine)):
+                span = pl.ds(pl.multiple_of(block * 2 * half + place * half, half), half)
+                far = sums_ref[block, which].astype(F32)
+                out_ref[span] = (near_ref[span] + far).astype(BF16)
 
 
 def local_kernel(
@@ -362,18 +428,17 @@
     col_spec = pl.BlockSpec((cols, width), step_rows)
     far_shape = jax.ShapeDtypeStruct((mine_blocks, 2, half, width), BF16)
 
-    def call(kernel, scalars, in_specs, out_specs, out_shape, bias_cols, name, operands):
+    limit = pltpu.CompilerParams(vmem_limit_bytes=24 * 1024 * 1024)
+
+    def call(kernel, scalars, operands, out_shape, name, scratch=()):
+        whole = pl.BlockSpec(memory_space=pltpu.VMEM)
         return pl.pallas_call(
-            lambda *refs: kernel(*refs, **sizes),
-            grid_spec=pltpu.PrefetchScalarGridSpec(
-                num_scalar_prefetch=len(scalars),
-                grid=(mine_blocks,),
-                in_specs=in_specs,
-                out_specs=out_specs,
-                scratch_shapes=[pltpu.VMEM((rows, bias_cols), F32)],
-            ),
+            kernel,
+            in_specs=[pl.BlockSpec(memory_space=pltpu.SMEM)] * len(scalars) + [whole] * len(operands),
+            out_specs=jax.tree.map(lambda _: whole, out_shape),
             out_shape=out_shape,
-            compiler_params=pltpu.CompilerParams(vmem_limit_bytes=48 * 1024 * 1024),
+            scratch_shapes=scratch,
+            compiler_params=limit,
             name=name,
         )(*scalars, *operands)
 
@@ -388,19 +453,16 @@
     outgoing, k2n = lax.optimization_barrier((outgoing, k2))
     arrived = lax.all_to_all(outgoing, "grp", split_axis=0, concat_axis=0, tiled=True)
     stats = call(
-        near_kernel, (), [row_spec, row_spec, col_spec, col_spec], row_spec,
-        jax.ShapeDtypeStruct((tokens * heads, width), F32), cols, "near", (q2, g2, k2n, v2),
+        partial(near_kernel, **sizes), (), (q2, g2, k2n, v2),
+        jax.ShapeDtypeStruct((mine_blocks, 8, rows), F32), "near",
     )
     arrived, stats = lax.optimization_barrier((arrived, stats))
     other = lax.ppermute(take_rows(arrived, source_sib), "uly", swap)
 
     far_mine, far_other = call(
-        far_kernel, (source_own, seen_own),
-        [row_spec, row_spec, row_spec, far_spec(from_source), far_spec(step_part)],
-        [far_spec(step_part), far_spec(step_part)], [far_shape, far_shape], cols, "far",
-        (q2, g2, stats, arrived, other),
-    )
-
+        partial(far_kernel, **sizes), (source_own, seen_own), (q2, g2, stats, arrived, other),
+        [far_shape, far_shape], "far",
+    )
     from_sib = lax.ppermute(far_other, "uly", swap)
     groups = jnp.arange(grp_count)
     source_both = jnp.concatenate([source_own, source_sib])
@@ -410,26 +472,35 @@
     landed = lax.all_to_all(returning, "grp", split_axis=0, concat_axis=0, tiled=True)
     row_shape = jax.ShapeDtypeStruct(q2.shape, BF16)
     near_shape = jax.ShapeDtypeStruct(k2.shape, F32)
-    attended, dq, dk_near, dv_near = call(
-        local_kernel, (source_own, seen_own),
-        [row_spec, row_spec, col_spec, col_spec, far_spec(from_source), far_spec(step_part)],
-        [row_spec, row_spec, col_spec, col_spec],
-        [row_shape, row_shape, near_shape, near_shape], 2 * cols, "local",
-        (q2, g2, k2l, v2, arrived, other),
-    )
+    attended, dq, dk_near, dv_near = pl.pallas_call(
+        partial(local_kernel, **sizes),
+        grid_spec=pltpu.PrefetchScalarGridSpec(
+            num_scalar_prefetch=2,
+            grid=(mine_blocks,),
+            in_specs=[
+                row_spec, row_spec, col_spec, col_spec, far_spec(from_source), far_spec(step_part)
+            ],
+            out_specs=[row_spec, row_spec, col_spec, col_spec],
+            scratch_shapes=[pltpu.VMEM((rows, 2 * cols), F32)],
+        ),
+        out_shape=[row_shape, row_shape, near_shape, near_shape],
+        compiler_params=limit,
+        name="local",
+    )(source_own, seen_own, q2, g2, k2l, v2, arrived, other)
     landed, dk_near = lax.optimization_barrier((landed, dk_near))
-    routing = ((owner_first[:, None] == jnp.arange(per_group)[None, :]) & sending[:, None]).astype(
-        BF16
-    )
-    summed = jnp.einsum("sp,sxrd->pxrd", routing, landed, preferred_element_type=F32)
-    summed_own = summed[:mine_blocks]
-    back = lax.ppermute(summed[mine_blocks:].astype(BF16), "uly", swap)
-    first_half = jnp.where(my_half == 0, summed_own, back.astype(F32))
-    second_half = jnp.where(my_half == 0, back.astype(F32), summed_own)
-    far_sum = jnp.stack([first_half, second_half], axis=1)
-    split = (mine_blocks, 2, half, width)
-    dk = (dk_near.reshape(split) + far_sum[:, :, 0]).astype(BF16).reshape(keys.shape)
-    dv = (dv_near.reshape(split) + far_sum[:, :, 1]).astype(BF16).reshape(keys.shape)
+    own, give = call(
+        land_kernel, (owner_first, sending.astype(jnp.int32)), (landed,),
+        [jax.ShapeDtypeStruct(far_shape.shape, F32), far_shape], "land",
+        [pltpu.VMEM((per_group, 2, half, width), F32)],
+    )
+    back = lax.ppermute(give, "uly", swap)
+    small = jax.ShapeDtypeStruct(k2.shape, BF16)
+    dk, dv = call(
+        finish_kernel, (my_half.reshape(1),), (dk_near, dv_near, own, back),
+        [small, small], "finish",
+    )
+    dk = dk.reshape(keys.shape)
+    dv = dv.reshape(keys.shape)
     return (attended.reshape(queries.shape), dq.reshape(queries.shape), dk, dv)
 
 

time: 81.6 us -> 72.3 us (0.89)
  Pallas kernels: 18.7 us -> 13 us
  other arithmetic: 6.48 us -> 2.72 us
  waiting for transfers between devices: 28 us -> 29.5 us
  matrix products: 1.43 us -> 0 us
    pallas_call x3 -> x5, Pallas kernels: 18.7 us -> 13 us  [the longest x1 6.93 us: whole_blocks(): pl.pallas_call(partial(local_kernel, **sizes), grid_spec=pltpu.PrefetchSc...]
    all_to_all x1, waiting for transfers between devices: 10 us -> 13 us  [whole_blocks(): lax.all_to_all(outgoing, 'grp', split_axis=0, concat_axis=0, tiled=True)]
    all_to_all x1, waiting for transfers between devices: 6.93 us -> 5.47 us  [whole_blocks(): lax.all_to_all(returning, 'grp', split_axis=0, concat_axis=0, tiled=True)]
    convert_element_type x2 -> x1, other arithmetic: 1.45 us -> 0.01 us  [whole_blocks(): sending.astype(jnp.int32)]
    dot_general x1 -> x0, matrix products: 1.43 us -> none  [whole_blocks(): jnp.einsum('sp,sxrd->pxrd', routing, landed, preferred_element_type=F32)]
    unnamed x15 -> x25, local copies, waits for them, and re-layouts: 3.48 us -> 3.86 us
  transfers between devices with their start and end apart: 6 -> 6, of which waited for: 6 -> 6; matrix products, arithmetic and copies ran while one was open for 6% -> 4% of each run, Pallas kernels for 12% -> 11%
where the time goes in v3:
time: 72.3 us; the launch traced here: 71.9 us
  waiting for transfers between devices  29.5 us (41%)
  starting transfers between devices  18.3 us (25%)
  Pallas kernels  13 us (18%)
  local copies, waits for them, and re-layouts  7.6 us (11%)
  other arithmetic  2.72 us (4%)
  between operations  0.81 us (1%)
    all_to_all x1, waiting for transfers between devices, whole_blocks(): lax.all_to_all(outgoing, 'grp', split_axis=0, concat_axis=0, tiled=True)  13 us
    pallas_call x1, Pallas kernels, whole_blocks(): pl.pallas_call(partial(local_kernel, **sizes), grid_spec=pltpu.PrefetchSc...  6.93 us
    all_to_all x1, starting transfers between devices, whole_blocks(): lax.all_to_all(outgoing, 'grp', split_axis=0, concat_axis=0, tiled=True)  6.13 us
    pallas_call x4, Pallas kernels, call(): pl.pallas_call(kernel, in_specs=[pl.BlockSpec(memory_space=pltpu.SMEM)] *...  6.03 us
    all_to_all x1, waiting for transfers between devices, whole_blocks(): lax.all_to_all(returning, 'grp', split_axis=0, concat_axis=0, tiled=True)  5.47 us
    all_to_all x1, starting transfers between devices, whole_blocks(): lax.all_to_all(returning, 'grp', split_axis=0, concat_axis=0, tiled=True)  4.38 us
    ppermute x1, waiting for transfers between devices, whole_blocks(): back = lax.ppermute(give, 'uly', swap)  3.89 us
    unnamed x25, local copies, waits for them, and re-layouts  3.86 us
  transfers between devices with their start and end apart: 6, of which 6 were waited for; matrix products, arithmetic and copies ran while one was open for 4% of the time, Pallas kernels for 11%

profile of v3, /device:TPU:0, one launch (start us, length us, event | category | flops | bytes accessed | tf_op | source)
XLA Modules:
  0.0 71.9 jit_solution(12403989268335897427)
XLA Ops:
  0.6 1.0 %fusion.3 = (bf16[4,2,64,128]{3,2,0,1:T(8,128)(2,1)S(1)}, bf16[4,2,64,128]{3,2,0,1:T(8,128)(2,1)S(1)}) fusion(s32[]{:T(128)S(6)} %select_n.104, bf16[4,2,1,64,128]{4,3,1,0,2:T(8,128)(2,1)} %bitcast.44, bf16[4,2,1,64,128]{4,3,1,0,2:T(8,128)(2,1)} %bitcast.47, s32[]{:T(128)S(6)} %select_n.105), kind=kLoop, calls=%fused_computation.12 | loop fusion | flops 131072 | bytes 524296 | tf_op jit(solution)/shard_map/jit(dynamic_index_in_dim)/squeeze | solution.py:449
  1.6 3.0 %collective-permute-start = (bf16[4,2,64,128]{3,2,0,1:T(8,128)(2,1)S(1)}, bf16[4,2,64,128]{3,2,0,1:T(8,128)(2,1)S(1)}, u32[]{:S(2)}, u32[]{:S(2)}) collective-permute-start(bf16[4,2,64,128]{3,2,0,1:T(8,128)(2,1)S(1)} %get-tuple-element.45), channel_id=1, source_target_pairs={{0,1},{1,0},{2,3},{3,2},{4,5},{5,4},{6,7},{7,6},{8,9},{9,8},{10,11... | collective-permute-start | bytes 393224 | tf_op jit(solution)/shard_map/ppermute | solution.py:451
  4.6 0.7 copy-done.10
  5.4 0.5 broadcast.220
  5.9 0.1 copy-done.11
  6.1 0.7 reduce.30
  6.8 0.1 fusion.18
  6.9 0.1 fusion.6
  7.1 0.5 copy-done.8
  7.6 0.5 collective-permute-done
  8.2 1.4 %gather_fusion = bf16[16,2,64,128]{3,2,1,0:T(8,128)(2,1)} fusion(bf16[8,2,64,128]{3,2,0,1:T(8,128)(2,1)S(1)} %pad_maximum_fusion, s32[1024]{0:T(1024)S(1)} %pad_clamp_fusion.2), kind=kCustom, calls=%fused_computation | custom fusion | bytes 1048640 | tf_op jit(solution)/shard_map/gather | solution.py:367
  9.6 6.1 %all-to-all-start = ((bf16[16,2,64,128]{3,2,1,0:T(8,128)(2,1)}), bf16[16,2,64,128]{3,2,1,0:T(8,128)(2,1)S(1)}, u32[]{:S(2)}, u32[]{:S(2)}) async-start(bf16[16,2,64,128]{3,2,1,0:T(8,128)(2,1)} %gather_fusion), calls=%async_computation | async-start | bytes 1048576 | tf_op jit(solution)/shard_map/all_to_all | solution.py:454
  16.0 1.2 %near.1.stat_ref = f32[4,8,1024]{2,1,0:T(8,128)S(1)} custom-call(bf16[4096,128]{1,0:T(8,128)(2,1)S(1)} %bitcast.38, bf16[4096,128]{1,0:T(8,128)(2,1)S(1)} %bitcast.41, bf16[512,128]{1,0:T(8,128)(2,1)S(1)} %bitcast.45, bf16[512,128]{1,0:T(8,128)(2,1)S(1)} %bitcast.48), custom_call_target="tpu_custom_call" | custom-call | tf_op jit(solution)/shard_map/near/pallas_call | solution.py:435
  17.3 13.0 %all-to-all-done.arrived_ref.mine_ref = bf16[16,2,64,128]{3,2,1,0:T(8,128)(2,1)S(1)} async-done(((bf16[16,2,64,128]{3,2,1,0:T(8,128)(2,1)}), bf16[16,2,64,128]{3,2,1,0:T(8,128)(2,1)S(1)}, u32[]{:S(2)}, u32[]{:S(2)}) %all-to-all-start) | async-done | bytes 524320 | tf_op jit(solution)/shard_map/all_to_all | solution.py:454
  30.2 0.6 gather_fusion.1
  30.8 1.6 %collective-permute-start.1 = (bf16[4,2,64,128]{3,2,1,0:T(8,128)(2,1)S(1)}, bf16[4,2,64,128]{3,2,1,0:T(8,128)(2,1)S(1)}, u32[]{:S(2)}, u32[]{:S(2)}) collective-permute-start(bf16[4,2,64,128]{3,2,1,0:T(8,128)(2,1)S(1)} %gather_fusion.1), channel_id=1, source_target_pairs={{0,1},{1,0},{2,3},{3,2},{4,5},{5,4},{6,7},{7,6},{8,9},{9,8},{10,11... | collective-permute-start | bytes 393224 | tf_op jit(solution)/shard_map/ppermute | solution.py:460
  32.4 0.6 iota_reduce_fusion
  33.1 3.2 %collective-permute-done.1.other_ref = bf16[4,2,64,128]{3,2,1,0:T(8,128)(2,1)S(1)} collective-permute-done((bf16[4,2,64,128]{3,2,1,0:T(8,128)(2,1)S(1)}, bf16[4,2,64,128]{3,2,1,0:T(8,128)(2,1)S(1)}, u32[]{:S(2)}, u32[]{:S(2)}) %collective-permute-start.1) | collective-permute-done | bytes 131104 | tf_op jit(solution)/shard_map/ppermute | solution.py:460
  36.3 3.3 %far.1 = (bf16[4,2,64,128]{3,2,1,0:T(8,128)(2,1)S(1)}, bf16[4,2,64,128]{3,2,1,0:T(8,128)(2,1)S(1)}) custom-call(s32[4]{0:T(128)S(1)} %get-tuple-element.47.source_ref, s32[4]{0:T(128)S(1)} %fusion.14.seen_ref, bf16[4096,128]{1,0:T(8,128)(2,1)S(1)} %bitcast.39, bf16[4096,128]{1,0:T(8,128)(2,1)S(1)} %bitcast.42, f32[4,8,1024]{2,1,0:T(8,128)S(1)} %near.1.stat_ref, ...), custom_call_target="tpu_custom_call" | custom-call | tf_op jit(solution)/shard_map/far/pallas_call | solution.py:435
  39.6 1.6 %collective-permute-start.2 = (bf16[4,2,64,128]{3,2,1,0:T(8,128)(2,1)S(1)}, bf16[4,2,64,128]{3,2,1,0:T(8,128)(2,1)S(1)}, u32[]{:S(2)}, u32[]{:S(2)}) collective-permute-start(bf16[4,2,64,128]{3,2,1,0:T(8,128)(2,1)S(1)} %get-tuple-element.28), channel_id=1, source_target_pairs={{0,1},{1,0},{2,3},{3,2},{4,5},{5,4},{6,7},{7,6},{8,9},{9,8},{10,11... | collective-permute-start | bytes 393224 | tf_op jit(solution)/shard_map/ppermute | solution.py:466
  41.2 3.4 %collective-permute-done.2 = bf16[4,2,64,128]{3,2,1,0:T(8,128)(2,1)S(1)} collective-permute-done((bf16[4,2,64,128]{3,2,1,0:T(8,128)(2,1)S(1)}, bf16[4,2,64,128]{3,2,1,0:T(8,128)(2,1)S(1)}, u32[]{:S(2)}, u32[]{:S(2)}) %collective-permute-start.2) | collective-permute-done | bytes 131104 | tf_op jit(solution)/shard_map/ppermute | solution.py:466
  44.6 1.4 %gather_fusion.2 = bf16[16,2,64,128]{3,2,1,0:T(8,128)(2,1)} fusion(bf16[8,2,64,128]{3,2,1,0:T(8,128)(2,1)S(1)} %pad_maximum_fusion.1, s32[1024]{0:T(1024)S(1)} %pad_clamp_fusion), kind=kCustom, calls=%fused_computation.2 | custom fusion | bytes 1048640 | tf_op jit(solution)/shard_map/gather | solution.py:367
  46.0 4.4 %all-to-all-start.1 = ((bf16[16,2,64,128]{3,2,1,0:T(8,128)(2,1)}), bf16[16,2,64,128]{3,2,1,0:T(8,128)(2,1)S(1)}, u32[]{:S(2)}, u32[]{:S(2)}) async-start(bf16[16,2,64,128]{3,2,1,0:T(8,128)(2,1)} %gather_fusion.2), calls=%async_computation.1 | async-start | bytes 1048576 | tf_op jit(solution)/shard_map/all_to_all | solution.py:472
  50.4 0.6 copy-done.9
  51.1 6.9 %local.1 = (bf16[4096,128]{1,0:T(8,128)(2,1)}, bf16[4096,128]{1,0:T(8,128)(2,1)}, f32[512,128]{1,0:T(8,128)S(1)}, f32[512,128]{1,0:T(8,128)S(1)}) custom-call(s32[4]{0:T(128)S(1)} %get-tuple-element.47.source_ref, s32[4]{0:T(128)S(1)} %fusion.14.seen_ref, bf16[4096,128]{1,0:T(8,128)(2,1)S(1)} %bitcast.40, bf16[4096,128]{1,0:T(8,128)(2,1)S(1)} %bitcast.43, ...), custom_call_target="tpu_custom_call" | custom-call | tf_op jit(solution)/shard_map/local/pallas_call | solution.py:475
  58.0 0.7 copy-done.4
  58.7 0.7 copy-done.6
  59.4 5.5 %all-to-all-done.1.landed_ref = bf16[16,2,64,128]{3,2,1,0:T(8,128)(2,1)S(1)} async-done(((bf16[16,2,64,128]{3,2,1,0:T(8,128)(2,1)}), bf16[16,2,64,128]{3,2,1,0:T(8,128)(2,1)S(1)}, u32[]{:S(2)}, u32[]{:S(2)}) %all-to-all-start.1) | async-done | bytes 524320 | tf_op jit(solution)/shard_map/all_to_all | solution.py:472
  64.9 0.8 %land.1 = (f32[4,2,64,128]{3,2,1,0:T(8,128)S(1)}, bf16[4,2,64,128]{3,2,1,0:T(8,128)(2,1)S(1)}) custom-call(s32[16]{0:T(128)S(1)} %compare_select_fusion.3.place_ref, s32[16]{0:T(128)S(1)} %convert_element_type.12.sending_ref, bf16[16,2,64,128]{3,2,1,0:T(8,128)(2,1)S(1)} %all-to-all-done.1.landed_ref), custom_call_target="tpu_custom_call" | custom-call | tf_op jit(solution)/shard_map/land/pallas_call | solution.py:435
  65.7 1.6 %collective-permute-start.3 = (bf16[4,2,64,128]{3,2,1,0:T(8,128)(2,1)S(1)}, bf16[4,2,64,128]{3,2,1,0:T(8,128)(2,1)S(1)}, u32[]{:S(2)}, u32[]{:S(2)}) collective-permute-start(bf16[4,2,64,128]{3,2,1,0:T(8,128)(2,1)S(1)} %get-tuple-element.39), channel_id=1, source_target_pairs={{0,1},{1,0},{2,3},{3,2},{4,5},{5,4},{6,7},{7,6},{8,9},{9,8},{10,11... | collective-permute-start | bytes 393224 | tf_op jit(solution)/shard_map/ppermute | solution.py:496
  67.2 3.9 %collective-permute-done.3.back_ref = bf16[4,2,64,128]{3,2,1,0:T(8,128)(2,1)S(1)} collective-permute-done((bf16[4,2,64,128]{3,2,1,0:T(8,128)(2,1)S(1)}, bf16[4,2,64,128]{3,2,1,0:T(8,128)(2,1)S(1)}, u32[]{:S(2)}, u32[]{:S(2)}) %collective-permute-start.3) | collective-permute-done | bytes 131104 | tf_op jit(solution)/shard_map/ppermute | solution.py:496
  71.1 0.7 %finish.1 = (bf16[512,128]{1,0:T(8,128)(2,1)}, bf16[512,128]{1,0:T(8,128)(2,1)}) custom-call(s32[1]{0:T(128)} %bitcast.17.half_ref, f32[512,128]{1,0:T(8,128)S(1)} %copy-done.5, f32[512,128]{1,0:T(8,128)S(1)} %copy-done.7, f32[4,2,64,128]{3,2,1,0:T(8,128)S(1)} %get-tuple-element.38.own_ref, bf16[4,2,64,128]{3,2,1,0:T(8,128)(2,1)S(1)} %collective-permute-done.3.back_ref), custom_call_target="tpu_custom_call" | custom-call | tf_op jit(solution)/shard_map/finish/pallas_call | solution.py:435
  (38 shorter events, 0.6 us)
Async XLA Ops:
  1.6 6.5 %collective-permute-start = (bf16[4,2,64,128]{3,2,0,1:T(8,128)(2,1)S(1)}, bf16[4,2,64,128]{3,2,0,1:T(8,128)(2,1)S(1)}, u32[]{:S(2)}, u32[]{:S(2)}) collective-permute-start(bf16[4,2,64,128]{3,2,0,1:T(8,128)(2,1)S(1)} %get-tuple-element.45), channel_id=1, source_target_pairs={{0,1},{1,0},{2,3},{3,2},{4,5},{5,4},{6,7},{7,6},{8,9},{9,8},{10,11... | collective-permute-start | bytes 393224 | tf_op jit(solution)/shard_map/ppermute | solution.py:451
  4.6 0.7 copy-start.10
  5.4 0.7 copy-start.11
  7.1 0.5 copy-start.8
  8.1 7.8 %copy-start.2 = (bf16[128,4,128]{2,1,0:T(4,128)(2,1)S(1)}, bf16[128,4,128]{2,1,0:T(4,128)(2,1)}, u32[]{:S(2)}) copy-start(bf16[128,4,128]{2,1,0:T(4,128)(2,1)} %param.7) | copy-start | bytes 393220
  8.1 7.8 %copy-start.3 = (bf16[128,4,128]{2,1,0:T(4,128)(2,1)S(1)}, bf16[128,4,128]{2,1,0:T(4,128)(2,1)}, u32[]{:S(2)}) copy-start(bf16[128,4,128]{2,1,0:T(4,128)(2,1)} %param.8) | copy-start | bytes 393220
  8.2 7.8 %copy-start = (bf16[128,32,128]{2,1,0:T(8,128)(2,1)S(1)}, bf16[128,32,128]{2,1,0:T(8,128)(2,1)}, u32[]{:S(2)}) copy-start(bf16[128,32,128]{2,1,0:T(8,128)(2,1)} %param.6) | copy-start | bytes 3145732
  8.2 7.8 %copy-start.1 = (bf16[128,32,128]{2,1,0:T(8,128)(2,1)S(1)}, bf16[128,32,128]{2,1,0:T(8,128)(2,1)}, u32[]{:S(2)}) copy-start(bf16[128,32,128]{2,1,0:T(8,128)(2,1)} %param.9) | copy-start | bytes 3145732
  9.6 20.6 %all-to-all-start = ((bf16[16,2,64,128]{3,2,1,0:T(8,128)(2,1)}), bf16[16,2,64,128]{3,2,1,0:T(8,128)(2,1)S(1)}, u32[]{:S(2)}, u32[]{:S(2)}) async-start(bf16[16,2,64,128]{3,2,1,0:T(8,128)(2,1)} %gather_fusion), calls=%async_computation | async-start | bytes 1048576 | tf_op jit(solution)/shard_map/all_to_all | solution.py:454
  30.8 5.5 %collective-permute-start.1 = (bf16[4,2,64,128]{3,2,1,0:T(8,128)(2,1)S(1)}, bf16[4,2,64,128]{3,2,1,0:T(8,128)(2,1)S(1)}, u32[]{:S(2)}, u32[]{:S(2)}) collective-permute-start(bf16[4,2,64,128]{3,2,1,0:T(8,128)(2,1)S(1)} %gather_fusion.1), channel_id=1, source_target_pairs={{0,1},{1,0},{2,3},{3,2},{4,5},{5,4},{6,7},{7,6},{8,9},{9,8},{10,11... | collective-permute-start | bytes 393224 | tf_op jit(solution)/shard_map/ppermute | solution.py:460
  39.6 5.0 %collective-permute-start.2 = (bf16[4,2,64,128]{3,2,1,0:T(8,128)(2,1)S(1)}, bf16[4,2,64,128]{3,2,1,0:T(8,128)(2,1)S(1)}, u32[]{:S(2)}, u32[]{:S(2)}) collective-permute-start(bf16[4,2,64,128]{3,2,1,0:T(8,128)(2,1)S(1)} %get-tuple-element.28), channel_id=1, source_target_pairs={{0,1},{1,0},{2,3},{3,2},{4,5},{5,4},{6,7},{7,6},{8,9},{9,8},{10,11... | collective-permute-start | bytes 393224 | tf_op jit(solution)/shard_map/ppermute | solution.py:466
  46.0 18.9 %all-to-all-start.1 = ((bf16[16,2,64,128]{3,2,1,0:T(8,128)(2,1)}), bf16[16,2,64,128]{3,2,1,0:T(8,128)(2,1)S(1)}, u32[]{:S(2)}, u32[]{:S(2)}) async-start(bf16[16,2,64,128]{3,2,1,0:T(8,128)(2,1)} %gather_fusion.2), calls=%async_computation.1 | async-start | bytes 1048576 | tf_op jit(solution)/shard_map/all_to_all | solution.py:472
  50.4 0.7 copy-start.9
  58.0 0.7 copy-start.4
  58.7 0.7 copy-start.6
  64.9 6.3 %copy-start.5 = (f32[512,128]{1,0:T(8,128)S(1)}, f32[512,128]{1,0:T(8,128)}, u32[]{:S(2)}) copy-start(f32[512,128]{1,0:T(8,128)} %copy-done.4) | copy-start | bytes 786436
  64.9 6.3 %copy-start.7 = (f32[512,128]{1,0:T(8,128)S(1)}, f32[512,128]{1,0:T(8,128)}, u32[]{:S(2)}) copy-start(f32[512,128]{1,0:T(8,128)} %copy-done.6) | copy-start | bytes 786436
  65.7 5.5 %collective-permute-start.3 = (bf16[4,2,64,128]{3,2,1,0:T(8,128)(2,1)S(1)}, bf16[4,2,64,128]{3,2,1,0:T(8,128)(2,1)S(1)}, u32[]{:S(2)}, u32[]{:S(2)}) collective-permute-start(bf16[4,2,64,128]{3,2,1,0:T(8,128)(2,1)S(1)} %get-tuple-element.39), channel_id=1, source_target_pairs={{0,1},{1,0},{2,3},{3,2},{4,5},{5,4},{6,7},{7,6},{8,9},{9,8},{10,11... | collective-permute-start | bytes 393224 | tf_op jit(solution)/shard_map/ppermute | solution.py:496

commit v4 on v3

--- a/solution.py
+++ b/solution.py
@@ -199,19 +199,13 @@
     return lax.dot_general(left, right, FIRST, preferred_element_type=F32)
 
 
-def same_head(rows, cols, heads, kv_heads):
-    row = lax.broadcasted_iota(jnp.int32, (rows, cols), 0)
-    col = lax.broadcasted_iota(jnp.int32, (rows, cols), 1)
-    same = (row % heads) // (heads // kv_heads) == col % kv_heads
-    causal = col // kv_heads <= row // heads
-    return same, causal
-
-
 def head_major(cols, kv_heads):
+    half = cols // 2
+    place = half // kv_heads
     row = lax.broadcasted_iota(jnp.int32, (cols, cols), 0)
     col = lax.broadcasted_iota(jnp.int32, (cols, cols), 1)
-    place = cols // kv_heads
-    return jnp.where(col == (row % place) * kv_heads + row // place, 1.0, 0.0).astype(BF16)
+    token = row // half * place + row % place
+    return jnp.where(col == token * kv_heads + row % half // place, 1.0, 0.0).astype(BF16)
 
 
 def reorder(one_hot, array):
@@ -233,98 +227,177 @@
     )
 
 
-def near_kernel(q_ref, g_ref, k_ref, v_ref, stat_ref, *, heads, kv_heads, score_scale):
-    blocks = stat_ref.shape[0]
-    rows = q_ref.shape[0] // blocks
-    cols = k_ref.shape[0] // blocks
-    place = cols // kv_heads
-    order = head_major(cols, kv_heads)
+def lanes(rows, heads, kv_heads):
     lane = lax.broadcasted_iota(jnp.int32, (1, rows), 1)
-    lane_head = lane % heads // (heads // kv_heads)
-    causal = lax.broadcasted_iota(jnp.int32, (place, rows), 0) <= lane // heads
+    return lane // heads, lane % heads // (heads // kv_heads)
+
+
+def pack_kernel(half_ref, k_ref, v_ref, kept_ref, given_ref, *, kv_heads):
+    blocks, _, half, _ = kept_ref.shape
+    mine = half_ref[0] == 0
+    order = head_major(2 * half, kv_heads)
     for block in range(blocks):
-        span = slice(block * rows, (block + 1) * rows)
-        narrow = slice(block * cols, (block + 1) * cols)
-        k_near = reorder(order, k_ref[narrow])
-        v_near = reorder(order, v_ref[narrow])
-        scores = own_head(dot_last(k_near, q_ref[span]), lane_head, kv_heads) * score_scale
-        scores = jnp.where(causal, scores, HIDDEN)
-        highest = jnp.max(scores, axis=0, keepdims=True)
-        raised = jnp.exp(scores - highest)
-        dprobs = own_head(dot_last(v_near, g_ref[span]), lane_head, kv_heads)
-        stat_ref[block, 0:1] = highest
-        stat_ref[block, 1:2] = jnp.sum(raised, axis=0, keepdims=True)
-        stat_ref[block, 2:3] = jnp.sum(raised * dprobs, axis=0, keepdims=True)
-
-
-def far_kernel(
-    source_ref, seen_ref, q_ref, g_ref, stat_ref, arrived_ref, other_ref,
-    far_mine_ref, far_other_ref, *, heads, kv_heads, score_scale
+        for which, ref in enumerate((k_ref, v_ref)):
+            ordered = reorder(order, ref[block * 2 * half:(block + 1) * 2 * half])
+            kept_ref[block, which] = jnp.where(mine, ordered[:half], ordered[half:])
+            given_ref[block, which] = jnp.where(mine, ordered[half:], ordered[:half])
+
+
+def outgoing_kernel(place_ref, sending_ref, blocks_ref, *refs, first):
+    out_ref, sems = refs[-2:]
+    blocks = blocks_ref.shape[0]
+    copies = []
+    for group in range(out_ref.shape[0]):
+        place = place_ref[group] - first
+        wanted = (sending_ref[group] > 0) & (place >= 0) & (place < blocks)
+        block = jnp.clip(place, 0, blocks - 1)
+        copies.append(
+            (wanted, pltpu.make_async_copy(blocks_ref.at[block], out_ref.at[group], sems.at[group]))
+        )
+    for wanted, copy in copies:
+        pl.when(wanted)(copy.start)
+    for wanted, copy in copies:
+        pl.when(wanted)(copy.wait)
+
+
+def returning_kernel(source_ref, blocks_ref, _, out_ref, sems):
+    copies = [
+        pltpu.make_async_copy(blocks_ref.at[block], out_ref.at[source_ref[block]], sems.at[block])
+        for block in range(blocks_ref.shape[0])
+    ]
+    for copy in copies:
+        copy.start()
+    for copy in copies:
+        copy.wait()
+
+
+def near_kernel(
+    half_ref, q_ref, g_ref, kept_ref, given_ref, stat_ref, *, heads, kv_heads, score_scale
 ):
     blocks = stat_ref.shape[0]
     rows = q_ref.shape[0] // blocks
-    half = other_ref.shape[2]
-    order = head_major(2 * half, kv_heads)
-    lane = lax.broadcasted_iota(jnp.int32, (1, rows), 1)
-    lane_head = lane % heads // (heads // kv_heads)
+    place = kept_ref.shape[2] // kv_heads
+    token, lane_head = lanes(rows, heads, kv_heads)
+    key = lax.broadcasted_iota(jnp.int32, (2 * place, rows), 0)
+    part = jnp.where(key < place, half_ref[0], 1 - half_ref[0])
+    causal = key % place + part * place <= token
     for block in range(blocks):
         span = slice(block * rows, (block + 1) * rows)
-        source = source_ref[block]
+        pieces = []
+        for which, ref in enumerate((q_ref, g_ref)):
+            both = jnp.concatenate([kept_ref[block, which], given_ref[block, which]], axis=0)
+            full = dot_last(both, ref[span])
+            half = full.shape[0] // 2
+            pieces.append(
+                jnp.concatenate(
+                    [
+                        own_head(full[:half], lane_head, kv_heads),
+                        own_head(full[half:], lane_head, kv_heads),
+                    ],
+                    axis=0,
+                )
+            )
+        scores = jnp.where(causal, pieces[0] * score_scale, HIDDEN)
+        highest = jnp.max(scores, axis=0, keepdims=True)
+        raised = jnp.exp(scores - highest)
+        stat_ref[block, 0:1] = highest
+        stat_ref[block, 1:2] = jnp.sum(raised, axis=0, keepdims=True)
+        stat_ref[block, 2:3] = jnp.sum(raised * pieces[1], axis=0, keepdims=True)
+
+
+def far_scores(part_ref, at, q, g, seen, lane_head, kv_heads, score_scale):
+    hidden = jnp.where(seen > 0, 0.0, HIDDEN)
+    scores = own_head(dot_last(part_ref[at, 0], q), lane_head, kv_heads) * score_scale + hidden
+    return scores, own_head(dot_last(part_ref[at, 1], g), lane_head, kv_heads)
+
+
+def merged(stat_ref, block, scores, dprobs):
+    before = stat_ref[block, 0:1]
+    highest = jnp.maximum(before, jnp.max(scores, axis=0, keepdims=True))
+    raised = jnp.exp(scores - highest)
+    shrink = jnp.exp(before - highest)
+    total = shrink * stat_ref[block, 1:2] + jnp.sum(raised, axis=0, keepdims=True)
+    delta = shrink * stat_ref[block, 2:3] + jnp.sum(raised * dprobs, axis=0, keepdims=True)
+    return highest, raised, total, delta
+
+
+def far_gradients(probs, dprobs, delta, q, g, lane_head, kv_heads, score_scale):
+    dscores = (probs * (dprobs - delta)).astype(BF16)
+    dk = jnp.dot(all_heads(dscores, lane_head, kv_heads), q, preferred_element_type=F32)
+    dv = jnp.dot(all_heads(probs.astype(BF16), lane_head, kv_heads), g, preferred_element_type=F32)
+    return (dk * score_scale).astype(BF16), dv.astype(BF16)
+
+
+def mid_kernel(
+    source_ref, seen_ref, q_ref, g_ref, stat_ref, arrived_ref, out_ref,
+    *, heads, kv_heads, score_scale
+):
+    blocks = stat_ref.shape[0]
+    rows = q_ref.shape[0] // blocks
+    _, lane_head = lanes(rows, heads, kv_heads)
+    for block in range(blocks):
+        span = slice(block * rows, (block + 1) * rows)
+        scores, dprobs = far_scores(
+            arrived_ref, source_ref[block], q_ref[span], g_ref[span], seen_ref[block],
+            lane_head, kv_heads, score_scale,
+        )
+        highest, _, total, delta = merged(stat_ref, block, scores, dprobs)
+        out_ref[block, 0:1] = highest
+        out_ref[block, 1:2] = total
+        out_ref[block, 2:3] = delta
+
+
+def far_kernel(
+    seen_ref, q_ref, g_ref, stat_ref, other_ref, grad_ref, out_ref,
+    *, heads, kv_heads, score_scale
+):
+    blocks = stat_ref.shape[0]
+    rows = q_ref.shape[0] // blocks
+    _, lane_head = lanes(rows, heads, kv_heads)
+    for block in range(blocks):
+        span = slice(block * rows, (block + 1) * rows)
         q = q_ref[span]
         g = g_ref[span]
-        k_far = reorder(
-            order, jnp.concatenate([arrived_ref[source, 0], other_ref[block, 0]], axis=0)
-        )
-        v_far = reorder(
-            order, jnp.concatenate([arrived_ref[source, 1], other_ref[block, 1]], axis=0)
-        )
-        hidden = jnp.where(seen_ref[block] > 0, 0.0, HIDDEN)
-        scores = own_head(dot_last(k_far, q), lane_head, kv_heads) * score_scale + hidden
-        near_highest = stat_ref[block, 0:1]
-        highest = jnp.maximum(near_highest, jnp.max(scores, axis=0, keepdims=True))
-        raised = jnp.exp(scores - highest)
-        shrink = jnp.exp(near_highest - highest)
-        dprobs = own_head(dot_last(v_far, g), lane_head, kv_heads)
-        total = shrink * stat_ref[block, 1:2] + jnp.sum(raised, axis=0, keepdims=True)
+        scores, dprobs = far_scores(
+            other_ref, block, q, g, seen_ref[block], lane_head, kv_heads, score_scale
+        )
+        highest, raised, total, delta = merged(stat_ref, block, scores, dprobs)
         inverse = 1.0 / total
-        delta = shrink * stat_ref[block, 2:3] + jnp.sum(raised * dprobs, axis=0, keepdims=True)
-        probs = raised * inverse
-        dscores = (probs * (dprobs - delta * inverse)).astype(BF16)
-        dk = jnp.dot(all_heads(dscores, lane_head, kv_heads), q, preferred_element_type=F32)
-        dv = jnp.dot(
-            all_heads(probs.astype(BF16), lane_head, kv_heads), g, preferred_element_type=F32
-        )
-        dk = dot_first(order, (dk * score_scale).astype(BF16)).astype(BF16)
-        dv = dot_first(order, dv.astype(BF16)).astype(BF16)
-        far_mine_ref[block, 0] = dk[:half]
-        far_mine_ref[block, 1] = dv[:half]
-        far_other_ref[block, 0] = dk[half:]
-        far_other_ref[block, 1] = dv[half:]
-
-
-def land_kernel(place_ref, sending_ref, landed_ref, own_ref, give_ref, sum_ref):
-    blocks = own_ref.shape[0]
-    sum_ref[...] = jnp.zeros_like(sum_ref)
-    for group in range(landed_ref.shape[0]):
-
-        @pl.when(sending_ref[group] > 0)
-        def _():
-            place = place_ref[group]
-            sum_ref[place] = sum_ref[place] + landed_ref[group].astype(F32)
-
-    own_ref[...] = sum_ref[:blocks]
-    give_ref[...] = sum_ref[blocks:].astype(BF16)
-
-
-def finish_kernel(half_ref, dk_near_ref, dv_near_ref, own_ref, back_ref, dk_ref, dv_ref):
-    blocks, _, half, _ = back_ref.shape
-    mine = half_ref[0]
+        delta = delta * inverse
+        grad_ref[block, 0], grad_ref[block, 1] = far_gradients(
+            raised * inverse, dprobs, delta, q, g, lane_head, kv_heads, score_scale
+        )
+        out_ref[block, 0:1] = highest
+        out_ref[block, 1:2] = inverse
+        out_ref[block, 2:3] = delta
+
+
+def mine_kernel(
+    source_ref, seen_ref, q_ref, g_ref, stat_ref, arrived_ref, out_ref, grad_ref, sems,
+    *, heads, kv_heads, score_scale
+):
+    blocks = stat_ref.shape[0]
+    rows = q_ref.shape[0] // blocks
+    _, lane_head = lanes(rows, heads, kv_heads)
+    copies = []
     for block in range(blocks):
-        for near_ref, out_ref, which in ((dk_near_ref, dk_ref, 0), (dv_near_ref, dv_ref, 1)):
-            for sums_ref, place in ((own_ref, mine), (back_ref, 1 - mine)):
-                span = pl.ds(pl.multiple_of(block * 2 * half + place * half, half), half)
-                far = sums_ref[block, which].astype(F32)
-                out_ref[span] = (near_ref[span] + far).astype(BF16)
+        span = slice(block * rows, (block + 1) * rows)
+        q = q_ref[span]
+        g = g_ref[span]
+        source = source_ref[block]
+        scores, dprobs = far_scores(
+            arrived_ref, source, q, g, seen_ref[block], lane_head, kv_heads, score_scale
+        )
+        probs = jnp.exp(scores - stat_ref[block, 0:1]) * stat_ref[block, 1:2]
+        grad_ref[block, 0], grad_ref[block, 1] = far_gradients(
+            probs, dprobs, stat_ref[block, 2:3], q, g, lane_head, kv_heads, score_scale
+        )
+        copies.append(
+            pltpu.make_async_copy(grad_ref.at[block], out_ref.at[source], sems.at[block])
+        )
+        copies[-1].start()
+    for copy in copies:
+        copy.wait()
 
 
 def local_kernel(
@@ -337,13 +410,21 @@
 
     @pl.when(step == 0)
     def _():
-        same, causal = same_head(rows, cols, heads, kv_heads)
+        half = cols // 2
+        place = half // kv_heads
+        row = lax.broadcasted_iota(jnp.int32, (rows, cols), 0)
+        col = lax.broadcasted_iota(jnp.int32, (rows, cols), 1)
+        same = row % heads // (heads // kv_heads) == col % half // place
+        causal = col // half * place + col % place <= row // heads
         bias_ref[:, :cols] = jnp.where(same & causal, 0.0, HIDDEN)
         bias_ref[:, cols:] = jnp.where(same, 0.0, HIDDEN)
 
     far_bias = jnp.where(seen_ref[step] > 0, 0.0, HIDDEN)
-    k_all = jnp.concatenate([k_ref[...], mine_ref[0, 0], other_ref[0, 0]], axis=0)
-    v_all = jnp.concatenate([v_ref[...], mine_ref[0, 1], other_ref[0, 1]], axis=0)
+    order = head_major(cols, kv_heads)
+    k_near = reorder(order, k_ref[...])
+    v_near = reorder(order, v_ref[...])
+    k_all = jnp.concatenate([k_near, mine_ref[0, 0], other_ref[0, 0]], axis=0)
+    v_all = jnp.concatenate([v_near, mine_ref[0, 1], other_ref[0, 1]], axis=0)
     q = q_ref[...]
     g = g_ref[...]
     scores = dot_last(q, k_all) * score_scale + bias_ref[...]
@@ -363,6 +444,35 @@
     dv_ref[...] = dot_first(weights[:, :cols], g)
 
 
+def landing_kernel(place_ref, sending_ref, landed_ref, out_ref, sum_ref, *, first):
+    blocks = sum_ref.shape[0]
+    sum_ref[...] = jnp.zeros_like(sum_ref)
+    for group in range(landed_ref.shape[0]):
+        place = place_ref[group] - first
+
+        @pl.when((sending_ref[group] > 0) & (place >= 0) & (place < blocks))
+        def _():
+            sum_ref[place] = sum_ref[place] + landed_ref[group].astype(F32)
+
+    out_ref[...] = sum_ref[...].astype(out_ref.dtype)
+
+
+def finish_kernel(
+    half_ref, dk_near_ref, dv_near_ref, own_ref, back_ref, dk_ref, dv_ref, *, kv_heads
+):
+    blocks, _, half, _ = back_ref.shape
+    mine = half_ref[0] == 0
+    order = head_major(2 * half, kv_heads)
+    for block in range(blocks):
+        span = slice(block * 2 * half, (block + 1) * 2 * half)
+        for near_ref, out_ref, which in ((dk_near_ref, dk_ref, 0), (dv_near_ref, dv_ref, 1)):
+            own = own_ref[block, which]
+            back = back_ref[block, which].astype(F32)
+            far = jnp.concatenate([jnp.where(mine, own, back), jnp.where(mine, back, own)], axis=0)
+            summed = (near_ref[span] + far).astype(BF16)
+            out_ref[span] = dot_first(order, summed).astype(BF16)
+
+
 def take_rows(array, index):
     return array.at[index].get(mode="promise_in_bounds")
 
@@ -387,7 +497,7 @@
     counted = (list_counts > 0).reshape(grp_count, per_group)
     wanted = (lists // per_group == my_group) & counted
     send_place = jnp.sum(jnp.where(wanted, lists % per_group, 0), axis=1)
-    sending = jnp.any(wanted, axis=1)
+    sending = jnp.any(wanted, axis=1).astype(jnp.int32)
     my_lists = lax.dynamic_index_in_dim(lists, my_group, 0, keepdims=False)
     my_seen = lax.dynamic_index_in_dim(counted, my_group, 0, keepdims=False).astype(jnp.int32)
     source = my_lists // per_group
@@ -400,18 +510,87 @@
         )
 
     source_own, source_sib = by_owner(source)
-    seen_own, seen_sib = by_owner(my_seen)
+    seen_own, _ = by_owner(my_seen)
     owner_first = jnp.where(
         send_place // mine_blocks == my_half,
         send_place % mine_blocks,
         send_place % mine_blocks + mine_blocks,
     )
+    half_id = my_half.reshape(1)
 
     q2 = queries.reshape(tokens * heads, width)
     g2 = output_cotangent.reshape(tokens * heads, width)
     k2 = keys.reshape(tokens * kv_heads, width)
     v2 = values.reshape(tokens * kv_heads, width)
 
+    part_shape = jax.ShapeDtypeStruct((mine_blocks, 2, half, width), BF16)
+    slot_shape = jax.ShapeDtypeStruct((grp_count, 2, half, width), BF16)
+    stat_shape = jax.ShapeDtypeStruct((mine_blocks, 8, rows), F32)
+    row_shape = jax.ShapeDtypeStruct(q2.shape, BF16)
+    near_shape = jax.ShapeDtypeStruct(k2.shape, F32)
+    small_shape = jax.ShapeDtypeStruct(k2.shape, BF16)
+    sum_scratch = [pltpu.VMEM((mine_blocks, 2, half, width), F32)]
+    slot_sems = [pltpu.SemaphoreType.DMA((grp_count,))]
+    limit = pltpu.CompilerParams(vmem_limit_bytes=24 * 1024 * 1024)
+    vmem = pl.BlockSpec(memory_space=pltpu.VMEM)
+    smem = pl.BlockSpec(memory_space=pltpu.SMEM)
+    anywhere = pl.BlockSpec(memory_space=pltpu.HBM)
+
+    def call(kernel, name, scalars, operands, out_shape, scratch=(), into=None, out_spec=vmem):
+        extra = () if into is None else (into,)
+        return pl.pallas_call(
+            kernel,
+            in_specs=[smem] * len(scalars) + [vmem] * len(operands) + [anywhere] * len(extra),
+            out_specs=jax.tree.map(lambda _: out_spec, out_shape),
+            out_shape=out_shape,
+            scratch_shapes=scratch,
+            input_output_aliases={len(scalars) + len(operands): 0} if extra else {},
+            compiler_params=limit,
+            name=name,
+        )(*scalars, *operands, *extra)
+
+    kept, given = call(
+        partial(pack_kernel, kv_heads=kv_heads), "pack", (half_id,), (k2, v2),
+        [part_shape, part_shape],
+    )
+    gotten = lax.ppermute(given, "uly", swap)
+    outgoing = call(
+        partial(outgoing_kernel, first=0), "send_own", (owner_first, sending), (kept,),
+        slot_shape, slot_sems, out_spec=anywhere,
+    )
+    outgoing = call(
+        partial(outgoing_kernel, first=mine_blocks), "send_sibling", (owner_first, sending),
+        (gotten,), slot_shape, slot_sems, into=outgoing, out_spec=anywhere,
+    )
+    outgoing, given = lax.optimization_barrier((outgoing, given))
+    arrived = lax.all_to_all(outgoing, "grp", split_axis=0, concat_axis=0, tiled=True)
+    stats = call(
+        partial(near_kernel, **sizes), "near", (half_id,), (q2, g2, kept, given), stat_shape
+    )
+    arrived, stats = lax.optimization_barrier((arrived, stats))
+    other = lax.ppermute(take_rows(arrived, source_sib), "uly", swap)
+    stats = call(
+        partial(mid_kernel, **sizes), "mid", (source_own, seen_own), (q2, g2, stats, arrived),
+        stat_shape,
+    )
+    far_other, stats = call(
+        partial(far_kernel, **sizes), "far", (seen_own,), (q2, g2, stats, other),
+        [part_shape, stat_shape],
+    )
+    from_sib = lax.ppermute(far_other, "uly", swap)
+    returning = call(
+        partial(mine_kernel, **sizes), "mine", (source_own, seen_own), (q2, g2, stats, arrived),
+        slot_shape,
+        [pltpu.VMEM(part_shape.shape, BF16), pltpu.SemaphoreType.DMA((mine_blocks,))],
+        out_spec=anywhere,
+    )
+    returning = call(
+        returning_kernel, "return_sibling", (source_sib,), (from_sib,), slot_shape,
+        [pltpu.SemaphoreType.DMA((mine_blocks,))], into=returning, out_spec=anywhere,
+    )
+    returning, k2l = lax.optimization_barrier((returning, k2))
+    landed = lax.all_to_all(returning, "grp", split_axis=0, concat_axis=0, tiled=True)
+
     def step_rows(i, *_):
         return (i, 0)
 
@@ -421,64 +600,17 @@
     def from_source(i, source_ref, seen_ref):
         return (source_ref[i], 0, 0, 0)
 
-    def far_spec(index_map):
-        return pl.BlockSpec((1, 2, half, width), index_map)
-
     row_spec = pl.BlockSpec((rows, width), step_rows)
     col_spec = pl.BlockSpec((cols, width), step_rows)
-    far_shape = jax.ShapeDtypeStruct((mine_blocks, 2, half, width), BF16)
-
-    limit = pltpu.CompilerParams(vmem_limit_bytes=24 * 1024 * 1024)
-
-    def call(kernel, scalars, operands, out_shape, name, scratch=()):
-        whole = pl.BlockSpec(memory_space=pltpu.VMEM)
-        return pl.pallas_call(
-            kernel,
-            in_specs=[pl.BlockSpec(memory_space=pltpu.SMEM)] * len(scalars) + [whole] * len(operands),
-            out_specs=jax.tree.map(lambda _: whole, out_shape),
-            out_shape=out_shape,
-            scratch_shapes=scratch,
-            compiler_params=limit,
-            name=name,
-        )(*scalars, *operands)
-
-    parts = jnp.stack(
-        [keys.reshape(mine_blocks, 2, half, width), values.reshape(mine_blocks, 2, half, width)],
-        axis=2,
-    )
-    kept = lax.dynamic_index_in_dim(parts, my_half, 1, keepdims=False)
-    given = lax.dynamic_index_in_dim(parts, 1 - my_half, 1, keepdims=False)
-    gotten = lax.ppermute(given, "uly", swap)
-    outgoing = take_rows(jnp.concatenate([kept, gotten]), owner_first)
-    outgoing, k2n = lax.optimization_barrier((outgoing, k2))
-    arrived = lax.all_to_all(outgoing, "grp", split_axis=0, concat_axis=0, tiled=True)
-    stats = call(
-        partial(near_kernel, **sizes), (), (q2, g2, k2n, v2),
-        jax.ShapeDtypeStruct((mine_blocks, 8, rows), F32), "near",
-    )
-    arrived, stats = lax.optimization_barrier((arrived, stats))
-    other = lax.ppermute(take_rows(arrived, source_sib), "uly", swap)
-
-    far_mine, far_other = call(
-        partial(far_kernel, **sizes), (source_own, seen_own), (q2, g2, stats, arrived, other),
-        [far_shape, far_shape], "far",
-    )
-    from_sib = lax.ppermute(far_other, "uly", swap)
-    groups = jnp.arange(grp_count)
-    source_both = jnp.concatenate([source_own, source_sib])
-    asked = jnp.argmax(source_both[None, :] == groups[:, None], axis=1)
-    returning = take_rows(jnp.concatenate([far_mine, from_sib]), asked)
-    returning, k2l = lax.optimization_barrier((returning, k2))
-    landed = lax.all_to_all(returning, "grp", split_axis=0, concat_axis=0, tiled=True)
-    row_shape = jax.ShapeDtypeStruct(q2.shape, BF16)
-    near_shape = jax.ShapeDtypeStruct(k2.shape, F32)
     attended, dq, dk_near, dv_near = pl.pallas_call(
         partial(local_kernel, **sizes),
         grid_spec=pltpu.PrefetchScalarGridSpec(
             num_scalar_prefetch=2,
             grid=(mine_blocks,),
             in_specs=[
-                row_spec, row_spec, col_spec, col_spec, far_spec(from_source), far_spec(step_part)
+                row_spec, row_spec, col_spec, col_spec,
+                pl.BlockSpec((1, 2, half, width), from_source),
+                pl.BlockSpec((1, 2, half, width), step_part),
             ],
             out_specs=[row_spec, row_spec, col_spec, col_spec],
             scratch_shapes=[pltpu.VMEM((rows, 2 * cols), F32)],
@@ -488,20 +620,23 @@
         name="local",
     )(source_own, seen_own, q2, g2, k2l, v2, arrived, other)
     landed, dk_near = lax.optimization_barrier((landed, dk_near))
-    own, give = call(
-        land_kernel, (owner_first, sending.astype(jnp.int32)), (landed,),
-        [jax.ShapeDtypeStruct(far_shape.shape, F32), far_shape], "land",
-        [pltpu.VMEM((per_group, 2, half, width), F32)],
+    give = call(
+        partial(landing_kernel, first=mine_blocks), "land_sibling", (owner_first, sending),
+        (landed,), part_shape, sum_scratch,
     )
     back = lax.ppermute(give, "uly", swap)
-    small = jax.ShapeDtypeStruct(k2.shape, BF16)
+    own = call(
+        partial(landing_kernel, first=0), "land_own", (owner_first, sending), (landed,),
+        jax.ShapeDtypeStruct(part_shape.shape, F32), sum_scratch,
+    )
     dk, dv = call(
-        finish_kernel, (my_half.reshape(1),), (dk_near, dv_near, own, back),
-        [small, small], "finish",
-    )
-    dk = dk.reshape(keys.shape)
-    dv = dv.reshape(keys.shape)
-    return (attended.reshape(queries.shape), dq.reshape(queries.shape), dk, dv)
+        partial(finish_kernel, kv_heads=kv_heads), "finish", (half_id,),
+        (dk_near, dv_near, own, back), [small_shape, small_shape],
+    )
+    return (
+        attended.reshape(queries.shape), dq.reshape(queries.shape),
+        dk.reshape(keys.shape), dv.reshape(keys.shape),
+    )
 
 
 def on_device(queries, keys, values, output_cotangent, block_lists, list_counts):

time: 72.3 us -> 72.8 us (level)
  Pallas kernels: 13 us -> 20.7 us
  waiting for transfers between devices: 29.5 us -> 25.7 us
  other arithmetic: 2.72 us -> 0.99 us
  local copies, waits for them, and re-layouts: 7.6 us -> 6.27 us
    pallas_call x4 -> x11, Pallas kernels: 6.03 us -> 13.3 us  [call(): pl.pallas_call(kernel, in_specs=[smem] * len(scalars) + [vmem] * len(oper...]
    gather x3 -> x1, local copies, waits for them, and re-layouts: 3.38 us -> 0.57 us  [take_rows(): return array.at[index].get(mode='promise_in_bounds')]
    ppermute x1, waiting for transfers between devices: 3.41 us -> 0.81 us  [whole_blocks(): from_sib = lax.ppermute(far_other, 'uly', swap)]
    unnamed x25 -> x27, local copies, waits for them, and re-layouts: 3.86 us -> 5.35 us
    squeeze x1 -> x0, other arithmetic: 0.97 us -> none  [whole_blocks(): kept = lax.dynamic_index_in_dim(parts, my_half, 1, keepdims=False)]
  transfers between devices with their start and end apart: 6 -> 6, of which waited for: 6 -> 5; matrix products, arithmetic and copies ran while one was open for 4% -> 3% of each run, Pallas kernels for 11% -> 20%
where the time goes in v4:
time: 72.8 us; the launch traced here: 72.5 us
  waiting for transfers between devices  25.7 us (35%)
  Pallas kernels  20.7 us (28%)
  starting transfers between devices  17.9 us (25%)
  local copies, waits for them, and re-layouts  6.27 us (9%)
  other arithmetic  0.99 us (1%)
  between operations  0.87 us (1%)
    all_to_all x1, waiting for transfers between devices, whole_blocks(): lax.all_to_all(outgoing, 'grp', split_axis=0, concat_axis=0, tiled=True)  13.5 us
    pallas_call x11, Pallas kernels, call(): pl.pallas_call(kernel, in_specs=[smem] * len(scalars) + [vmem] * len(oper...  13.3 us
    pallas_call x1, Pallas kernels, whole_blocks(): pl.pallas_call(partial(local_kernel, **sizes), grid_spec=pltpu.PrefetchSc...  7.46 us
    all_to_all x1, starting transfers between devices, whole_blocks(): lax.all_to_all(outgoing, 'grp', split_axis=0, concat_axis=0, tiled=True)  5.89 us
    all_to_all x1, waiting for transfers between devices, whole_blocks(): lax.all_to_all(returning, 'grp', split_axis=0, concat_axis=0, tiled=True)  5.57 us
    unnamed x27, local copies, waits for them, and re-layouts  5.35 us
    all_to_all x1, starting transfers between devices, whole_blocks(): lax.all_to_all(returning, 'grp', split_axis=0, concat_axis=0, tiled=True)  4.52 us
    ppermute x1, waiting for transfers between devices, whole_blocks(): back = lax.ppermute(give, 'uly', swap)  3.23 us
  transfers between devices with their start and end apart: 6, of which 5 were waited for; matrix products, arithmetic and copies ran while one was open for 3% of the time, Pallas kernels for 20%

profile of v4, /device:TPU:0, one launch (start us, length us, event | category | flops | bytes accessed | tf_op | source)
XLA Modules:
  0.0 72.5 jit_solution(11803491361787928341)
XLA Ops:
  0.6 0.9 %copy-done.3 = bf16[128,4,128]{2,1,0:T(4,128)(2,1)S(1)} copy-done((bf16[128,4,128]{2,1,0:T(4,128)(2,1)S(1)}, bf16[128,4,128]{2,1,0:T(4,128)(2,1)}, u32[]{:S(2)}) %copy-start.3) | copy-done | bytes 131096
  1.5 0.9 %copy-done.5 = bf16[128,4,128]{2,1,0:T(4,128)(2,1)S(1)} copy-done((bf16[128,4,128]{2,1,0:T(4,128)(2,1)S(1)}, bf16[128,4,128]{2,1,0:T(4,128)(2,1)}, u32[]{:S(2)}) %copy-start.5) | copy-done | bytes 131096
  2.4 0.2 pack.1
  2.7 3.0 %collective-permute-start = (bf16[4,2,64,128]{3,2,1,0:T(8,128)(2,1)S(1)}, bf16[4,2,64,128]{3,2,1,0:T(8,128)(2,1)S(1)}, u32[]{:S(2)}, u32[]{:S(2)}) collective-permute-start(bf16[4,2,64,128]{3,2,1,0:T(8,128)(2,1)S(1)} %get-tuple-element.25.given_ref), channel_id=1, source_target_pairs={{0,1},{1,0},{2,3},{3,2},{4,5},{5,4},{6,7},{7,6},{8,9},{9,8},{10,11... | collective-permute-start | bytes 393224 | tf_op jit(solution)/shard_map/ppermute | solution.py:556
  5.7 0.7 copy-done.11
  6.5 0.5 broadcast.102
  7.1 0.7 reduce.11
  8.2 1.4 %send_own.1.refs_0_ = bf16[16,2,64,128]{3,2,1,0:T(8,128)(2,1)} custom-call(s32[16]{0:T(128)S(1)} %compare_select_fusion.1.place_ref, s32[16]{0:T(128)S(1)} %convert_element_type.12.sending_ref, bf16[4,2,64,128]{3,2,1,0:T(8,128)(2,1)S(1)} %get-tuple-element.23.blocks_ref.kept_ref), custom_call_target="tpu_custom_call" | custom-call | tf_op jit(solution)/shard_map/send_own/pallas_call | solution.py:541
  9.6 1.3 %send_sibling.1 = bf16[16,2,64,128]{3,2,1,0:T(8,128)(2,1)} custom-call(s32[16]{0:T(128)S(1)} %compare_select_fusion.1.place_ref, s32[16]{0:T(128)S(1)} %convert_element_type.12.sending_ref, bf16[4,2,64,128]{3,2,1,0:T(8,128)(2,1)S(1)} %collective-permute-done.blocks_ref, bf16[16,2,64,128]{3,2,1,0:T(8,128)(2,1)} %send_own.1.refs_0_), custom_call_target="tpu_custom_call", output_to_operand_aliasing={{}: (3, {})} | custom-call | tf_op jit(solution)/shard_map/send_sibling/pallas_call | solution.py:541
  10.9 5.9 %all-to-all-start = ((bf16[16,2,64,128]{3,2,1,0:T(8,128)(2,1)}), bf16[16,2,64,128]{3,2,1,0:T(8,128)(2,1)S(1)}, u32[]{:S(2)}, u32[]{:S(2)}) async-start(bf16[16,2,64,128]{3,2,1,0:T(8,128)(2,1)} %send_sibling.1), calls=%async_computation | async-start | bytes 1048576 | tf_op jit(solution)/shard_map/all_to_all | solution.py:566
  17.1 0.7 %near.1.stat_ref = f32[4,8,1024]{2,1,0:T(8,128)S(1)} custom-call(s32[1]{0:T(128)} %bitcast.5.half_ref, bf16[4096,128]{1,0:T(8,128)(2,1)S(1)} %bitcast.20, bf16[4096,128]{1,0:T(8,128)(2,1)S(1)} %bitcast.25, bf16[4,2,64,128]{3,2,1,0:T(8,128)(2,1)S(1)} %get-tuple-element.23.blocks_ref.kept_ref, bf16[4,2,64,128]{3,2,1,0:T(8,128)(2,1)S(1)} %get-tuple-element.25.given_ref), custom_call_target="tpu_custom_call" | custom-call | tf_op jit(solution)/shard_map/near/pallas_call | solution.py:541
  17.8 13.5 %all-to-all-done.arrived_ref.mine_ref = bf16[16,2,64,128]{3,2,1,0:T(8,128)(2,1)S(1)} async-done(((bf16[16,2,64,128]{3,2,1,0:T(8,128)(2,1)}), bf16[16,2,64,128]{3,2,1,0:T(8,128)(2,1)S(1)}, u32[]{:S(2)}, u32[]{:S(2)}) %all-to-all-start) | async-done | bytes 524320 | tf_op jit(solution)/shard_map/all_to_all | solution.py:566
  31.3 0.6 gather_fusion
  31.9 1.5 %collective-permute-start.1 = (bf16[4,2,64,128]{3,2,1,0:T(8,128)(2,1)S(1)}, bf16[4,2,64,128]{3,2,1,0:T(8,128)(2,1)S(1)}, u32[]{:S(2)}, u32[]{:S(2)}) collective-permute-start(bf16[4,2,64,128]{3,2,1,0:T(8,128)(2,1)S(1)} %gather_fusion), channel_id=1, source_target_pairs={{0,1},{1,0},{2,3},{3,2},{4,5},{5,4},{6,7},{7,6},{8,9},{9,8},{10,11... | collective-permute-start | bytes 393224 | tf_op jit(solution)/shard_map/ppermute | solution.py:571
  33.4 1.4 %mid.1.stat_ref = f32[4,8,1024]{2,1,0:T(8,128)S(1)} custom-call(s32[4]{0:T(128)S(1)} %get-tuple-element.43.source_ref, s32[4]{0:T(128)S(1)} %fusion.8.seen_ref, bf16[4096,128]{1,0:T(8,128)(2,1)S(1)} %bitcast.21, bf16[4096,128]{1,0:T(8,128)(2,1)S(1)} %bitcast.26, f32[4,8,1024]{2,1,0:T(8,128)S(1)} %near.1.stat_ref, ...), custom_call_target="tpu_custom_call" | custom-call | tf_op jit(solution)/shard_map/mid/pallas_call | solution.py:541
  34.8 2.6 %collective-permute-done.1.other_ref = bf16[4,2,64,128]{3,2,1,0:T(8,128)(2,1)S(1)} collective-permute-done((bf16[4,2,64,128]{3,2,1,0:T(8,128)(2,1)S(1)}, bf16[4,2,64,128]{3,2,1,0:T(8,128)(2,1)S(1)}, u32[]{:S(2)}, u32[]{:S(2)}) %collective-permute-start.1) | collective-permute-done | bytes 131104 | tf_op jit(solution)/shard_map/ppermute | solution.py:571
  37.4 2.3 %far.1 = (bf16[4,2,64,128]{3,2,1,0:T(8,128)(2,1)S(1)}, f32[4,8,1024]{2,1,0:T(8,128)S(1)}) custom-call(s32[4]{0:T(128)S(1)} %fusion.8.seen_ref, bf16[4096,128]{1,0:T(8,128)(2,1)S(1)} %bitcast.22, bf16[4096,128]{1,0:T(8,128)(2,1)S(1)} %bitcast.27, f32[4,8,1024]{2,1,0:T(8,128)S(1)} %mid.1.stat_ref, bf16[4,2,64,128]{3,2,1,0:T(8,128)(2,1)S(1)} %collective-permute-done.1.other_ref), custom_call_target="tpu_custom_call" | custom-call | tf_op jit(solution)/shard_map/far/pallas_call | solution.py:541
  39.6 1.5 %collective-permute-start.2 = (bf16[4,2,64,128]{3,2,1,0:T(8,128)(2,1)S(1)}, bf16[4,2,64,128]{3,2,1,0:T(8,128)(2,1)S(1)}, u32[]{:S(2)}, u32[]{:S(2)}) collective-permute-start(bf16[4,2,64,128]{3,2,1,0:T(8,128)(2,1)S(1)} %get-tuple-element.28), channel_id=1, source_target_pairs={{0,1},{1,0},{2,3},{3,2},{4,5},{5,4},{6,7},{7,6},{8,9},{9,8},{10,11... | collective-permute-start | bytes 393224 | tf_op jit(solution)/shard_map/ppermute | solution.py:580
  41.2 2.7 %mine.1._ = bf16[16,2,64,128]{3,2,1,0:T(8,128)(2,1)S(1)} custom-call(s32[4]{0:T(128)S(1)} %get-tuple-element.43.source_ref, s32[4]{0:T(128)S(1)} %fusion.8.seen_ref, bf16[4096,128]{1,0:T(8,128)(2,1)S(1)} %bitcast.23, bf16[4096,128]{1,0:T(8,128)(2,1)S(1)} %bitcast.28, f32[4,8,1024]{2,1,0:T(8,128)S(1)} %get-tuple-element.29.stat_ref, ...), custom_call_target="tpu_custom_call" | custom-call | tf_op jit(solution)/shard_map/mine/pallas_call | solution.py:541
  43.9 0.8 %collective-permute-done.2.blocks_ref = bf16[4,2,64,128]{3,2,1,0:T(8,128)(2,1)S(1)} collective-permute-done((bf16[4,2,64,128]{3,2,1,0:T(8,128)(2,1)S(1)}, bf16[4,2,64,128]{3,2,1,0:T(8,128)(2,1)S(1)}, u32[]{:S(2)}, u32[]{:S(2)}) %collective-permute-start.2) | collective-permute-done | bytes 131104 | tf_op jit(solution)/shard_map/ppermute | solution.py:580
  44.7 0.8 %return_sibling.1 = bf16[16,2,64,128]{3,2,1,0:T(8,128)(2,1)S(1)} custom-call(s32[4]{0:T(128)S(1)} %get-tuple-element.42.source_ref, bf16[4,2,64,128]{3,2,1,0:T(8,128)(2,1)S(1)} %collective-permute-done.2.blocks_ref, bf16[16,2,64,128]{3,2,1,0:T(8,128)(2,1)S(1)} %mine.1._), custom_call_target="tpu_custom_call", output_to_operand_aliasing={{}: (2, {})} | custom-call | tf_op jit(solution)/shard_map/return_sibling/pallas_call | solution.py:541
  45.5 0.8 %copy-done.2 = bf16[16,2,64,128]{3,2,1,0:T(8,128)(2,1)} copy-done((bf16[16,2,64,128]{3,2,1,0:T(8,128)(2,1)}, bf16[16,2,64,128]{3,2,1,0:T(8,128)(2,1)S(1)}, u32[]{:S(2)}) %copy-start.2) | copy-done | bytes 524312
  46.2 4.5 %all-to-all-start.1 = ((bf16[16,2,64,128]{3,2,1,0:T(8,128)(2,1)}), bf16[16,2,64,128]{3,2,1,0:T(8,128)(2,1)S(1)}, u32[]{:S(2)}, u32[]{:S(2)}) async-start(bf16[16,2,64,128]{3,2,1,0:T(8,128)(2,1)} %copy-done.2), calls=%async_computation.1 | async-start | bytes 1048576 | tf_op jit(solution)/shard_map/all_to_all | solution.py:592
  50.8 7.5 %local.1 = (bf16[4096,128]{1,0:T(8,128)(2,1)}, bf16[4096,128]{1,0:T(8,128)(2,1)}, f32[512,128]{1,0:T(8,128)S(1)}, f32[512,128]{1,0:T(8,128)S(1)}) custom-call(s32[4]{0:T(128)S(1)} %get-tuple-element.43.source_ref, s32[4]{0:T(128)S(1)} %fusion.8.seen_ref, bf16[4096,128]{1,0:T(8,128)(2,1)S(1)} %bitcast.24, bf16[4096,128]{1,0:T(8,128)(2,1)S(1)} %bitcast.29, ...), custom_call_target="tpu_custom_call" | custom-call | tf_op jit(solution)/shard_map/local/pallas_call | solution.py:605
  58.3 0.7 copy-done.7
  59.0 0.7 copy-done.9
  59.7 5.6 %all-to-all-done.1.landed_ref = bf16[16,2,64,128]{3,2,1,0:T(8,128)(2,1)S(1)} async-done(((bf16[16,2,64,128]{3,2,1,0:T(8,128)(2,1)}), bf16[16,2,64,128]{3,2,1,0:T(8,128)(2,1)S(1)}, u32[]{:S(2)}, u32[]{:S(2)}) %all-to-all-start.1) | async-done | bytes 524320 | tf_op jit(solution)/shard_map/all_to_all | solution.py:592
  65.2 0.7 %land_sibling.1 = bf16[4,2,64,128]{3,2,1,0:T(8,128)(2,1)S(1)} custom-call(s32[16]{0:T(128)S(1)} %compare_select_fusion.1.place_ref, s32[16]{0:T(128)S(1)} %convert_element_type.12.sending_ref, bf16[16,2,64,128]{3,2,1,0:T(8,128)(2,1)S(1)} %all-to-all-done.1.landed_ref), custom_call_target="tpu_custom_call" | custom-call | tf_op jit(solution)/shard_map/land_sibling/pallas_call | solution.py:541
  66.0 1.5 %collective-permute-start.3 = (bf16[4,2,64,128]{3,2,1,0:T(8,128)(2,1)S(1)}, bf16[4,2,64,128]{3,2,1,0:T(8,128)(2,1)S(1)}, u32[]{:S(2)}, u32[]{:S(2)}) collective-permute-start(bf16[4,2,64,128]{3,2,1,0:T(8,128)(2,1)S(1)} %land_sibling.1), channel_id=1, source_target_pairs={{0,1},{1,0},{2,3},{3,2},{4,5},{5,4},{6,7},{7,6},{8,9},{9,8},{10,11... | collective-permute-start | bytes 393224 | tf_op jit(solution)/shard_map/ppermute | solution.py:627
  67.5 0.7 %land_own.1.own_ref = f32[4,2,64,128]{3,2,1,0:T(8,128)S(1)} custom-call(s32[16]{0:T(128)S(1)} %compare_select_fusion.1.place_ref, s32[16]{0:T(128)S(1)} %convert_element_type.12.sending_ref, bf16[16,2,64,128]{3,2,1,0:T(8,128)(2,1)S(1)} %all-to-all-done.1.landed_ref), custom_call_target="tpu_custom_call" | custom-call | tf_op jit(solution)/shard_map/land_own/pallas_call | solution.py:541
  68.3 3.2 %collective-permute-done.3.back_ref = bf16[4,2,64,128]{3,2,1,0:T(8,128)(2,1)S(1)} collective-permute-done((bf16[4,2,64,128]{3,2,1,0:T(8,128)(2,1)S(1)}, bf16[4,2,64,128]{3,2,1,0:T(8,128)(2,1)S(1)}, u32[]{:S(2)}, u32[]{:S(2)}) %collective-permute-start.3) | collective-permute-done | bytes 131104 | tf_op jit(solution)/shard_map/ppermute | solution.py:627
  71.5 1.0 %finish.1 = (bf16[512,128]{1,0:T(8,128)(2,1)}, bf16[512,128]{1,0:T(8,128)(2,1)}) custom-call(s32[1]{0:T(128)} %bitcast.5.half_ref, f32[512,128]{1,0:T(8,128)S(1)} %copy-done.8, f32[512,128]{1,0:T(8,128)S(1)} %copy-done.10, f32[4,2,64,128]{3,2,1,0:T(8,128)S(1)} %land_own.1.own_ref, bf16[4,2,64,128]{3,2,1,0:T(8,128)(2,1)S(1)} %collective-permute-done.3.back_ref), custom_call_target="tpu_custom_call" | custom-call | tf_op jit(solution)/shard_map/finish/pallas_call | solution.py:541
  (36 shorter events, 0.9 us)
Async XLA Ops:
  0.6 0.9 %copy-start.3 = (bf16[128,4,128]{2,1,0:T(4,128)(2,1)S(1)}, bf16[128,4,128]{2,1,0:T(4,128)(2,1)}, u32[]{:S(2)}) copy-start(bf16[128,4,128]{2,1,0:T(4,128)(2,1)} %param.7) | copy-start | bytes 393220
  1.5 0.9 %copy-start.5 = (bf16[128,4,128]{2,1,0:T(4,128)(2,1)S(1)}, bf16[128,4,128]{2,1,0:T(4,128)(2,1)}, u32[]{:S(2)}) copy-start(bf16[128,4,128]{2,1,0:T(4,128)(2,1)} %param.8) | copy-start | bytes 393220
  2.7 6.9 %collective-permute-start = (bf16[4,2,64,128]{3,2,1,0:T(8,128)(2,1)S(1)}, bf16[4,2,64,128]{3,2,1,0:T(8,128)(2,1)S(1)}, u32[]{:S(2)}, u32[]{:S(2)}) collective-permute-start(bf16[4,2,64,128]{3,2,1,0:T(8,128)(2,1)S(1)} %get-tuple-element.25.given_ref), channel_id=1, source_target_pairs={{0,1},{1,0},{2,3},{3,2},{4,5},{5,4},{6,7},{7,6},{8,9},{9,8},{10,11... | collective-permute-start | bytes 393224 | tf_op jit(solution)/shard_map/ppermute | solution.py:556
  5.7 0.7 copy-start.11
  6.5 0.7 copy-start.12
  9.6 7.5 %copy-start = (bf16[128,32,128]{2,1,0:T(8,128)(2,1)S(1)}, bf16[128,32,128]{2,1,0:T(8,128)(2,1)}, u32[]{:S(2)}) copy-start(bf16[128,32,128]{2,1,0:T(8,128)(2,1)} %param.6) | copy-start | bytes 3145732
  9.6 7.5 %copy-start.1 = (bf16[128,32,128]{2,1,0:T(8,128)(2,1)S(1)}, bf16[128,32,128]{2,1,0:T(8,128)(2,1)}, u32[]{:S(2)}) copy-start(bf16[128,32,128]{2,1,0:T(8,128)(2,1)} %param.9) | copy-start | bytes 3145732
  10.9 20.4 %all-to-all-start = ((bf16[16,2,64,128]{3,2,1,0:T(8,128)(2,1)}), bf16[16,2,64,128]{3,2,1,0:T(8,128)(2,1)S(1)}, u32[]{:S(2)}, u32[]{:S(2)}) async-start(bf16[16,2,64,128]{3,2,1,0:T(8,128)(2,1)} %send_sibling.1), calls=%async_computation | async-start | bytes 1048576 | tf_op jit(solution)/shard_map/all_to_all | solution.py:566
  31.9 5.5 %collective-permute-start.1 = (bf16[4,2,64,128]{3,2,1,0:T(8,128)(2,1)S(1)}, bf16[4,2,64,128]{3,2,1,0:T(8,128)(2,1)S(1)}, u32[]{:S(2)}, u32[]{:S(2)}) collective-permute-start(bf16[4,2,64,128]{3,2,1,0:T(8,128)(2,1)S(1)} %gather_fusion), channel_id=1, source_target_pairs={{0,1},{1,0},{2,3},{3,2},{4,5},{5,4},{6,7},{7,6},{8,9},{9,8},{10,11... | collective-permute-start | bytes 393224 | tf_op jit(solution)/shard_map/ppermute | solution.py:571
  39.6 5.0 %collective-permute-start.2 = (bf16[4,2,64,128]{3,2,1,0:T(8,128)(2,1)S(1)}, bf16[4,2,64,128]{3,2,1,0:T(8,128)(2,1)S(1)}, u32[]{:S(2)}, u32[]{:S(2)}) collective-permute-start(bf16[4,2,64,128]{3,2,1,0:T(8,128)(2,1)S(1)} %get-tuple-element.28), channel_id=1, source_target_pairs={{0,1},{1,0},{2,3},{3,2},{4,5},{5,4},{6,7},{7,6},{8,9},{9,8},{10,11... | collective-permute-start | bytes 393224 | tf_op jit(solution)/shard_map/ppermute | solution.py:580
  45.4 0.8 %copy-start.2 = (bf16[16,2,64,128]{3,2,1,0:T(8,128)(2,1)}, bf16[16,2,64,128]{3,2,1,0:T(8,128)(2,1)S(1)}, u32[]{:S(2)}) copy-start(bf16[16,2,64,128]{3,2,1,0:T(8,128)(2,1)S(1)} %return_sibling.1) | copy-start | bytes 1572868
  46.2 4.5 %copy-start.4 = (bf16[128,4,128]{2,1,0:T(4,128)(2,1)S(1)}, bf16[128,4,128]{2,1,0:T(4,128)(2,1)}, u32[]{:S(2)}) copy-start(bf16[128,4,128]{2,1,0:T(4,128)(2,1)} %param.7) | copy-start | bytes 393220
  46.2 4.5 %copy-start.6 = (bf16[128,4,128]{2,1,0:T(4,128)(2,1)S(1)}, bf16[128,4,128]{2,1,0:T(4,128)(2,1)}, u32[]{:S(2)}) copy-start(bf16[128,4,128]{2,1,0:T(4,128)(2,1)} %param.8) | copy-start | bytes 393220
  46.2 19.0 %all-to-all-start.1 = ((bf16[16,2,64,128]{3,2,1,0:T(8,128)(2,1)}), bf16[16,2,64,128]{3,2,1,0:T(8,128)(2,1)S(1)}, u32[]{:S(2)}, u32[]{:S(2)}) async-start(bf16[16,2,64,128]{3,2,1,0:T(8,128)(2,1)} %copy-done.2), calls=%async_computation.1 | async-start | bytes 1048576 | tf_op jit(solution)/shard_map/all_to_all | solution.py:592
  58.3 0.7 copy-start.7
  59.0 0.7 copy-start.9
  66.0 5.5 %copy-start.8 = (f32[512,128]{1,0:T(8,128)S(1)}, f32[512,128]{1,0:T(8,128)}, u32[]{:S(2)}) copy-start(f32[512,128]{1,0:T(8,128)} %copy-done.7) | copy-start | bytes 786436
  66.0 5.5 %copy-start.10 = (f32[512,128]{1,0:T(8,128)S(1)}, f32[512,128]{1,0:T(8,128)}, u32[]{:S(2)}) copy-start(f32[512,128]{1,0:T(8,128)} %copy-done.9) | copy-start | bytes 786436
  66.0 5.5 %collective-permute-start.3 = (bf16[4,2,64,128]{3,2,1,0:T(8,128)(2,1)S(1)}, bf16[4,2,64,128]{3,2,1,0:T(8,128)(2,1)S(1)}, u32[]{:S(2)}, u32[]{:S(2)}) collective-permute-start(bf16[4,2,64,128]{3,2,1,0:T(8,128)(2,1)S(1)} %land_sibling.1), channel_id=1, source_target_pairs={{0,1},{1,0},{2,3},{3,2},{4,5},{5,4},{6,7},{7,6},{8,9},{9,8},{10,11... | collective-permute-start | bytes 393224 | tf_op jit(solution)/shard_map/ppermute | solution.py:627

commit v5 on v4

--- a/solution.py
+++ b/solution.py
@@ -232,37 +232,69 @@
     return lane // heads, lane % heads // (heads // kv_heads)
 
 
-def pack_kernel(half_ref, k_ref, v_ref, kept_ref, given_ref, *, kv_heads):
+def plan_spans(grp_count, blocks):
+    return grp_count, 2 * grp_count, 2 * grp_count + blocks, 2 * grp_count + 2 * blocks
+
+
+def pack_kernel(
+    where_ref, lists_ref, counts_ref, k_hbm, v_hbm, plan_ref, kept_ref, given_ref,
+    k_ref, v_ref, sems, *, grp_count, kv_heads
+):
     blocks, _, half, _ = kept_ref.shape
-    mine = half_ref[0] == 0
+    copies = [
+        pltpu.make_async_copy(k_hbm, k_ref, sems.at[0]),
+        pltpu.make_async_copy(v_hbm, v_ref, sems.at[1]),
+    ]
+    for copy in copies:
+        copy.start()
+    group, mine = where_ref[0], where_ref[1]
+    per_group = 2 * blocks
+    low = group * per_group
+    sib_at, source_at, give_at, seen_at = plan_spans(grp_count, blocks)
+    for other in range(grp_count):
+        place = jnp.int32(-1)
+        for at in range(other * per_group, (other + 1) * per_group):
+            here = lists_ref[at] - low
+            wanted = (here >= 0) & (here < per_group) & (counts_ref[at] > 0)
+            place = jnp.where(wanted, here, place)
+        own = place - mine * blocks
+        sib = place - (1 - mine) * blocks
+        plan_ref[other] = jnp.where((own >= 0) & (own < blocks), own, -1)
+        plan_ref[sib_at + other] = jnp.where((sib >= 0) & (sib < blocks), sib, -1)
+    for block in range(blocks):
+        at = low + mine * blocks + block
+        plan_ref[source_at + block] = lax.div(lists_ref[at], per_group)
+        plan_ref[seen_at + block] = counts_ref[at]
+        at = low + (1 - mine) * blocks + block
+        plan_ref[give_at + block] = lax.div(lists_ref[at], per_group)
+    for copy in copies:
+        copy.wait()
+    first = mine == 0
     order = head_major(2 * half, kv_heads)
     for block in range(blocks):
         for which, ref in enumerate((k_ref, v_ref)):
             ordered = reorder(order, ref[block * 2 * half:(block + 1) * 2 * half])
-            kept_ref[block, which] = jnp.where(mine, ordered[:half], ordered[half:])
-            given_ref[block, which] = jnp.where(mine, ordered[half:], ordered[:half])
-
-
-def outgoing_kernel(place_ref, sending_ref, blocks_ref, *refs, first):
+            kept_ref[block, which] = jnp.where(first, ordered[:half], ordered[half:])
+            given_ref[block, which] = jnp.where(first, ordered[half:], ordered[:half])
+
+
+def outgoing_kernel(plan_ref, blocks_ref, *refs, first):
     out_ref, sems = refs[-2:]
-    blocks = blocks_ref.shape[0]
     copies = []
     for group in range(out_ref.shape[0]):
-        place = place_ref[group] - first
-        wanted = (sending_ref[group] > 0) & (place >= 0) & (place < blocks)
-        block = jnp.clip(place, 0, blocks - 1)
-        copies.append(
-            (wanted, pltpu.make_async_copy(blocks_ref.at[block], out_ref.at[group], sems.at[group]))
-        )
+        place = plan_ref[first + group]
+        source = blocks_ref.at[jnp.maximum(place, 0)]
+        copy = pltpu.make_async_copy(source, out_ref.at[group], sems.at[group])
+        copies.append((place >= 0, copy))
     for wanted, copy in copies:
         pl.when(wanted)(copy.start)
     for wanted, copy in copies:
         pl.when(wanted)(copy.wait)
 
 
-def returning_kernel(source_ref, blocks_ref, _, out_ref, sems):
+def returning_kernel(plan_ref, blocks_ref, _, out_ref, sems, *, give_at):
     copies = [
-        pltpu.make_async_copy(blocks_ref.at[block], out_ref.at[source_ref[block]], sems.at[block])
+        pltpu.make_async_copy(blocks_ref.at[block], out_ref.at[plan_ref[give_at + block]], sems.at[block])
         for block in range(blocks_ref.shape[0])
     ]
     for copy in copies:
@@ -272,14 +304,14 @@
 
 
 def near_kernel(
-    half_ref, q_ref, g_ref, kept_ref, given_ref, stat_ref, *, heads, kv_heads, score_scale
+    where_ref, q_ref, g_ref, kept_ref, given_ref, stat_ref, *, heads, kv_heads, score_scale
 ):
     blocks = stat_ref.shape[0]
     rows = q_ref.shape[0] // blocks
     place = kept_ref.shape[2] // kv_heads
     token, lane_head = lanes(rows, heads, kv_heads)
     key = lax.broadcasted_iota(jnp.int32, (2 * place, rows), 0)
-    part = jnp.where(key < place, half_ref[0], 1 - half_ref[0])
+    part = jnp.where(key < place, where_ref[1], 1 - where_ref[1])
     causal = key % place + part * place <= token
     for block in range(blocks):
         span = slice(block * rows, (block + 1) * rows)
@@ -329,8 +361,8 @@
 
 
 def mid_kernel(
-    source_ref, seen_ref, q_ref, g_ref, stat_ref, arrived_ref, out_ref,
-    *, heads, kv_heads, score_scale
+    plan_ref, q_ref, g_ref, stat_ref, arrived_ref, out_ref,
+    *, heads, kv_heads, score_scale, source_at, seen_at
 ):
     blocks = stat_ref.shape[0]
     rows = q_ref.shape[0] // blocks
@@ -338,8 +370,8 @@
     for block in range(blocks):
         span = slice(block * rows, (block + 1) * rows)
         scores, dprobs = far_scores(
-            arrived_ref, source_ref[block], q_ref[span], g_ref[span], seen_ref[block],
-            lane_head, kv_heads, score_scale,
+            arrived_ref, plan_ref[source_at + block], q_ref[span], g_ref[span],
+            plan_ref[seen_at + block],            lane_head, kv_heads, score_scale,
         )
         highest, _, total, delta = merged(stat_ref, block, scores, dprobs)
         out_ref[block, 0:1] = highest
@@ -348,8 +380,8 @@
 
 
 def far_kernel(
-    seen_ref, q_ref, g_ref, stat_ref, other_ref, grad_ref, out_ref,
-    *, heads, kv_heads, score_scale
+    plan_ref, q_ref, g_ref, stat_ref, other_ref, grad_ref, out_ref,
+    *, heads, kv_heads, score_scale, seen_at
 ):
     blocks = stat_ref.shape[0]
     rows = q_ref.shape[0] // blocks
@@ -359,7 +391,7 @@
         q = q_ref[span]
         g = g_ref[span]
         scores, dprobs = far_scores(
-            other_ref, block, q, g, seen_ref[block], lane_head, kv_heads, score_scale
+            other_ref, block, q, g, plan_ref[seen_at + block], lane_head, kv_heads, score_scale
         )
         highest, raised, total, delta = merged(stat_ref, block, scores, dprobs)
         inverse = 1.0 / total
@@ -373,8 +405,8 @@
 
 
 def mine_kernel(
-    source_ref, seen_ref, q_ref, g_ref, stat_ref, arrived_ref, out_ref, grad_ref, sems,
-    *, heads, kv_heads, score_scale
+    plan_ref, q_ref, g_ref, stat_ref, arrived_ref, out_ref, grad_ref, sems,
+    *, heads, kv_heads, score_scale, source_at, seen_at
 ):
     blocks = stat_ref.shape[0]
     rows = q_ref.shape[0] // blocks
@@ -384,9 +416,9 @@
         span = slice(block * rows, (block + 1) * rows)
         q = q_ref[span]
         g = g_ref[span]
-        source = source_ref[block]
+        source = plan_ref[source_at + block]
         scores, dprobs = far_scores(
-            arrived_ref, source, q, g, seen_ref[block], lane_head, kv_heads, score_scale
+            arrived_ref, source, q, g, plan_ref[seen_at + block], lane_head, kv_heads, score_scale
         )
         probs = jnp.exp(scores - stat_ref[block, 0:1]) * stat_ref[block, 1:2]
         grad_ref[block, 0], grad_ref[block, 1] = far_gradients(
@@ -401,8 +433,8 @@
 
 
 def local_kernel(
-    source_ref, seen_ref, q_ref, g_ref, k_ref, v_ref, mine_ref, other_ref,
-    att_ref, dq_ref, dk_ref, dv_ref, bias_ref, *, heads, kv_heads, score_scale
+    plan_ref, q_ref, g_ref, k_ref, v_ref, mine_ref, other_ref,
+    att_ref, dq_ref, dk_ref, dv_ref, bias_ref, *, heads, kv_heads, score_scale, seen_at
 ):
     step = pl.program_id(0)
     rows = q_ref.shape[0]
@@ -419,7 +451,7 @@
         bias_ref[:, :cols] = jnp.where(same & causal, 0.0, HIDDEN)
         bias_ref[:, cols:] = jnp.where(same, 0.0, HIDDEN)
 
-    far_bias = jnp.where(seen_ref[step] > 0, 0.0, HIDDEN)
+    far_bias = jnp.where(plan_ref[seen_at + step] > 0, 0.0, HIDDEN)
     order = head_major(cols, kv_heads)
     k_near = reorder(order, k_ref[...])
     v_near = reorder(order, v_ref[...])
@@ -444,13 +476,12 @@
     dv_ref[...] = dot_first(weights[:, :cols], g)
 
 
-def landing_kernel(place_ref, sending_ref, landed_ref, out_ref, sum_ref, *, first):
-    blocks = sum_ref.shape[0]
+def landing_kernel(plan_ref, landed_ref, out_ref, sum_ref, *, first):
     sum_ref[...] = jnp.zeros_like(sum_ref)
     for group in range(landed_ref.shape[0]):
-        place = place_ref[group] - first
-
-        @pl.when((sending_ref[group] > 0) & (place >= 0) & (place < blocks))
+        place = plan_ref[first + group]
+
+        @pl.when(place >= 0)
         def _():
             sum_ref[place] = sum_ref[place] + landed_ref[group].astype(F32)
 
@@ -458,10 +489,10 @@
 
 
 def finish_kernel(
-    half_ref, dk_near_ref, dv_near_ref, own_ref, back_ref, dk_ref, dv_ref, *, kv_heads
+    where_ref, dk_near_ref, dv_near_ref, own_ref, back_ref, dk_ref, dv_ref, *, kv_heads
 ):
     blocks, _, half, _ = back_ref.shape
-    mine = half_ref[0] == 0
+    mine = where_ref[1] == 0
     order = head_major(2 * half, kv_heads)
     for block in range(blocks):
         span = slice(block * 2 * half, (block + 1) * 2 * half)
@@ -493,30 +524,8 @@
     sizes = dict(heads=heads, kv_heads=kv_heads, score_scale=width ** (-0.5))
     swap = [(0, 1), (1, 0)]
 
-    lists = block_lists.reshape(grp_count, per_group)
-    counted = (list_counts > 0).reshape(grp_count, per_group)
-    wanted = (lists // per_group == my_group) & counted
-    send_place = jnp.sum(jnp.where(wanted, lists % per_group, 0), axis=1)
-    sending = jnp.any(wanted, axis=1).astype(jnp.int32)
-    my_lists = lax.dynamic_index_in_dim(lists, my_group, 0, keepdims=False)
-    my_seen = lax.dynamic_index_in_dim(counted, my_group, 0, keepdims=False).astype(jnp.int32)
-    source = my_lists // per_group
-
-    def by_owner(vector):
-        both = vector.reshape(2, mine_blocks)
-        return (
-            lax.dynamic_index_in_dim(both, my_half, 0, keepdims=False),
-            lax.dynamic_index_in_dim(both, 1 - my_half, 0, keepdims=False),
-        )
-
-    source_own, source_sib = by_owner(source)
-    seen_own, _ = by_owner(my_seen)
-    owner_first = jnp.where(
-        send_place // mine_blocks == my_half,
-        send_place % mine_blocks,
-        send_place % mine_blocks + mine_blocks,
-    )
-    half_id = my_half.reshape(1)
+    where = jnp.stack([my_group, my_half]).astype(jnp.int32)
+    sib_at, source_at, give_at, seen_at = plan_spans(grp_count, mine_blocks)
 
     q2 = queries.reshape(tokens * heads, width)
     g2 = output_cotangent.reshape(tokens * heads, width)
@@ -524,7 +533,7 @@
     v2 = values.reshape(tokens * kv_heads, width)
 
     part_shape = jax.ShapeDtypeStruct((mine_blocks, 2, half, width), BF16)
-    slot_shape = jax.ShapeDtypeStruct((grp_count, 2, half, width), BF16)
+    slot_shape = pltpu.HBM((grp_count, 2, half, width), BF16)
     stat_shape = jax.ShapeDtypeStruct((mine_blocks, 8, rows), F32)
     row_shape = jax.ShapeDtypeStruct(q2.shape, BF16)
     near_shape = jax.ShapeDtypeStruct(k2.shape, F32)
@@ -549,43 +558,59 @@
             name=name,
         )(*scalars, *operands, *extra)
 
-    kept, given = call(
-        partial(pack_kernel, kv_heads=kv_heads), "pack", (half_id,), (k2, v2),
-        [part_shape, part_shape],
+    plan, kept, given = pl.pallas_call(
+        partial(pack_kernel, grp_count=grp_count, kv_heads=kv_heads),
+        in_specs=[smem, smem, smem, anywhere, anywhere],
+        out_specs=[smem, vmem, vmem],
+        out_shape=[
+            jax.ShapeDtypeStruct((seen_at + mine_blocks,), jnp.int32), part_shape, part_shape
+        ],
+        scratch_shapes=[
+            pltpu.VMEM(k2.shape, BF16), pltpu.VMEM(k2.shape, BF16), pltpu.SemaphoreType.DMA((2,))
+        ],
+        compiler_params=limit,
+        name="pack",
+    )(
+        where,
+        pltpu.with_memory_space_constraint(block_lists.reshape(-1), pltpu.HBM),
+        pltpu.with_memory_space_constraint(list_counts, pltpu.HBM),
+        pltpu.with_memory_space_constraint(k2, pltpu.HBM),
+        pltpu.with_memory_space_constraint(v2, pltpu.HBM),
     )
     gotten = lax.ppermute(given, "uly", swap)
     outgoing = call(
-        partial(outgoing_kernel, first=0), "send_own", (owner_first, sending), (kept,),
+        partial(outgoing_kernel, first=0), "send_own", (plan,), (kept,),
         slot_shape, slot_sems, out_spec=anywhere,
     )
     outgoing = call(
-        partial(outgoing_kernel, first=mine_blocks), "send_sibling", (owner_first, sending),
-        (gotten,), slot_shape, slot_sems, into=outgoing, out_spec=anywhere,
+        partial(outgoing_kernel, first=sib_at), "send_sibling", (plan,), (gotten,),
+        slot_shape, slot_sems, into=outgoing, out_spec=anywhere,
     )
     outgoing, given = lax.optimization_barrier((outgoing, given))
     arrived = lax.all_to_all(outgoing, "grp", split_axis=0, concat_axis=0, tiled=True)
     stats = call(
-        partial(near_kernel, **sizes), "near", (half_id,), (q2, g2, kept, given), stat_shape
+        partial(near_kernel, **sizes), "near", (where,), (q2, g2, kept, given), stat_shape
     )
     arrived, stats = lax.optimization_barrier((arrived, stats))
-    other = lax.ppermute(take_rows(arrived, source_sib), "uly", swap)
+    give_rows = plan[give_at:give_at + mine_blocks]
+    other = lax.ppermute(take_rows(arrived, give_rows), "uly", swap)
     stats = call(
-        partial(mid_kernel, **sizes), "mid", (source_own, seen_own), (q2, g2, stats, arrived),
-        stat_shape,
+        partial(mid_kernel, source_at=source_at, seen_at=seen_at, **sizes), "mid", (plan,),
+        (q2, g2, stats, arrived), stat_shape,
     )
     far_other, stats = call(
-        partial(far_kernel, **sizes), "far", (seen_own,), (q2, g2, stats, other),
+        partial(far_kernel, seen_at=seen_at, **sizes), "far", (plan,), (q2, g2, stats, other),
         [part_shape, stat_shape],
     )
     from_sib = lax.ppermute(far_other, "uly", swap)
     returning = call(
-        partial(mine_kernel, **sizes), "mine", (source_own, seen_own), (q2, g2, stats, arrived),
-        slot_shape,
+        partial(mine_kernel, source_at=source_at, seen_at=seen_at, **sizes), "mine", (plan,),
+        (q2, g2, stats, arrived), slot_shape,
         [pltpu.VMEM(part_shape.shape, BF16), pltpu.SemaphoreType.DMA((mine_blocks,))],
         out_spec=anywhere,
     )
     returning = call(
-        returning_kernel, "return_sibling", (source_sib,), (from_sib,), slot_shape,
+        partial(returning_kernel, give_at=give_at), "return_sibling", (plan,), (from_sib,), slot_shape,
         [pltpu.SemaphoreType.DMA((mine_blocks,))], into=returning, out_spec=anywhere,
     )
     returning, k2l = lax.optimization_barrier((returning, k2))
@@ -597,15 +622,15 @@
     def step_part(i, *_):
         return (i, 0, 0, 0)
 
-    def from_source(i, source_ref, seen_ref):
-        return (source_ref[i], 0, 0, 0)
+    def from_source(i, plan_ref):
+        return (plan_ref[source_at + i], 0, 0, 0)
 
     row_spec = pl.BlockSpec((rows, width), step_rows)
     col_spec = pl.BlockSpec((cols, width), step_rows)
     attended, dq, dk_near, dv_near = pl.pallas_call(
-        partial(local_kernel, **sizes),
+        partial(local_kernel, seen_at=seen_at, **sizes),
         grid_spec=pltpu.PrefetchScalarGridSpec(
-            num_scalar_prefetch=2,
+            num_scalar_prefetch=1,
             grid=(mine_blocks,),
             in_specs=[
                 row_spec, row_spec, col_spec, col_spec,
@@ -618,19 +643,19 @@
         out_shape=[row_shape, row_shape, near_shape, near_shape],
         compiler_params=limit,
         name="local",
-    )(source_own, seen_own, q2, g2, k2l, v2, arrived, other)
+    )(plan, q2, g2, k2l, v2, arrived, other)
     landed, dk_near = lax.optimization_barrier((landed, dk_near))
     give = call(
-        partial(landing_kernel, first=mine_blocks), "land_sibling", (owner_first, sending),
-        (landed,), part_shape, sum_scratch,
+        partial(landing_kernel, first=sib_at), "land_sibling", (plan,), (landed,), part_shape,
+        sum_scratch,
     )
     back = lax.ppermute(give, "uly", swap)
     own = call(
-        partial(landing_kernel, first=0), "land_own", (owner_first, sending), (landed,),
+        partial(landing_kernel, first=0), "land_own", (plan,), (landed,),
         jax.ShapeDtypeStruct(part_shape.shape, F32), sum_scratch,
     )
     dk, dv = call(
-        partial(finish_kernel, kv_heads=kv_heads), "finish", (half_id,),
+        partial(finish_kernel, kv_heads=kv_heads), "finish", (where,),
         (dk_near, dv_near, own, back), [small_shape, small_shape],
     )
     return (

time: 72.8 us -> 73.2 us (level)
  local copies, waits for them, and re-layouts: 6.27 us -> 2 us
  Pallas kernels: 20.7 us -> 23.7 us
  waiting for transfers between devices: 25.7 us -> 27.8 us
  other arithmetic: 0.99 us -> 0.16 us
    unnamed x27 -> x16, local copies, waits for them, and re-layouts: 5.35 us -> 1.43 us
    ppermute x1, waiting for transfers between devices: 0.01 us -> 2.71 us  [whole_blocks(): gotten = lax.ppermute(given, 'uly', swap)]
    pallas_call x1 -> x2, Pallas kernels: 7.46 us -> 9.76 us  [the longest x1 7.5 us: whole_blocks(): pl.pallas_call(partial(local_kernel, seen_at=seen_at, **sizes), grid_spec...]
    pallas_call x11 -> x10, Pallas kernels: 13.3 us -> 14 us  [call(): pl.pallas_call(kernel, in_specs=[smem] * len(scalars) + [vmem] * len(oper...]
  transfers between devices with their start and end apart: 6 -> 6, of which waited for: 5 -> 6; matrix products, arithmetic and copies ran while one was open for 3% -> 0% of each run, Pallas kernels for 20% -> 20%
where the time goes in v5:
time: 73.2 us; the launch traced here: 72.9 us
  waiting for transfers between devices  27.8 us (38%)
  Pallas kernels  23.7 us (32%)
  starting transfers between devices  18.4 us (25%)
  local copies, waits for them, and re-layouts  2 us (3%)
  between operations  0.81 us (1%)
    pallas_call x10, Pallas kernels, call(): pl.pallas_call(kernel, in_specs=[smem] * len(scalars) + [vmem] * len(oper...  14 us
    all_to_all x1, waiting for transfers between devices, whole_blocks(): lax.all_to_all(outgoing, 'grp', split_axis=0, concat_axis=0, tiled=True)  13.1 us
    pallas_call x1, Pallas kernels, whole_blocks(): pl.pallas_call(partial(local_kernel, seen_at=seen_at, **sizes), grid_spec...  7.5 us
    all_to_all x1, starting transfers between devices, whole_blocks(): lax.all_to_all(outgoing, 'grp', split_axis=0, concat_axis=0, tiled=True)  6.15 us
    all_to_all x1, waiting for transfers between devices, whole_blocks(): lax.all_to_all(returning, 'grp', split_axis=0, concat_axis=0, tiled=True)  5.55 us
    all_to_all x1, starting transfers between devices, whole_blocks(): lax.all_to_all(returning, 'grp', split_axis=0, concat_axis=0, tiled=True)  4.52 us
    ppermute x1, waiting for transfers between devices, whole_blocks(): back = lax.ppermute(give, 'uly', swap)  3.21 us
    ppermute x1, starting transfers between devices, whole_blocks(): gotten = lax.ppermute(given, 'uly', swap)  3.03 us
  transfers between devices with their start and end apart: 6, of which 6 were waited for; matrix products, arithmetic and copies ran while one was open for 0% of the time, Pallas kernels for 20%

profile of v5, /device:TPU:0, one launch (start us, length us, event | category | flops | bytes accessed | tf_op | source)
XLA Modules:
  0.0 72.9 jit_solution(18071908091370910429)
XLA Ops:
  0.6 0.1 pad_add_fusion.where_ref
  0.7 2.3 %pack.1 = (s32[44]{0:T(128)S(1)}, bf16[4,2,64,128]{3,2,1,0:T(8,128)(2,1)S(1)}, bf16[4,2,64,128]{3,2,1,0:T(8,128)(2,1)S(1)}) custom-call(s32[2]{0:T(128)S(1)} %pad_add_fusion.where_ref, s32[128]{0:T(128)} %bitcast.25, s32[128]{0:T(128)} %counts_ref.1, bf16[512,128]{1,0:T(8,128)(2,1)} %bitcast.21, bf16[512,128]{1,0:T(8,128)(2,1)} %bitcast.23), custom_call_target="tpu_custom_call" | custom-call | tf_op jit(solution)/shard_map/pack/pallas_call | solution.py:561
  3.0 3.0 %collective-permute-start = (bf16[4,2,64,128]{3,2,1,0:T(8,128)(2,1)S(1)}, bf16[4,2,64,128]{3,2,1,0:T(8,128)(2,1)S(1)}, u32[]{:S(2)}, u32[]{:S(2)}) collective-permute-start(bf16[4,2,64,128]{3,2,1,0:T(8,128)(2,1)S(1)} %get-tuple-element.27.given_ref), channel_id=1, source_target_pairs={{0,1},{1,0},{2,3},{3,2},{4,5},{5,4},{6,7},{7,6},{8,9},{9,8},{10,11... | collective-permute-start | bytes 393224 | tf_op jit(solution)/shard_map/ppermute | solution.py:580
  6.0 0.8 %send_own.1.refs_0_ = bf16[16,2,64,128]{3,2,1,0:T(8,128)(2,1)} custom-call(s32[44]{0:T(128)S(1)} %get-tuple-element.23.plan_ref, bf16[4,2,64,128]{3,2,1,0:T(8,128)(2,1)S(1)} %get-tuple-element.25.blocks_ref.kept_ref), custom_call_target="tpu_custom_call" | custom-call | tf_op jit(solution)/shard_map/send_own/pallas_call | solution.py:550
  6.8 0.0 copy-start
  6.8 0.0 copy-start.1
  6.8 2.7 %collective-permute-done.blocks_ref = bf16[4,2,64,128]{3,2,1,0:T(8,128)(2,1)S(1)} collective-permute-done((bf16[4,2,64,128]{3,2,1,0:T(8,128)(2,1)S(1)}, bf16[4,2,64,128]{3,2,1,0:T(8,128)(2,1)S(1)}, u32[]{:S(2)}, u32[]{:S(2)}) %collective-permute-start) | collective-permute-done | bytes 131104 | tf_op jit(solution)/shard_map/ppermute | solution.py:580
  9.5 1.3 %send_sibling.1 = bf16[16,2,64,128]{3,2,1,0:T(8,128)(2,1)} custom-call(s32[44]{0:T(128)S(1)} %get-tuple-element.23.plan_ref, bf16[4,2,64,128]{3,2,1,0:T(8,128)(2,1)S(1)} %collective-permute-done.blocks_ref, bf16[16,2,64,128]{3,2,1,0:T(8,128)(2,1)} %send_own.1.refs_0_), custom_call_target="tpu_custom_call", output_to_operand_aliasing={{}: (2, {})} | custom-call | tf_op jit(solution)/shard_map/send_sibling/pallas_call | solution.py:550
  10.8 6.2 %all-to-all-start = ((bf16[16,2,64,128]{3,2,1,0:T(8,128)(2,1)}), bf16[16,2,64,128]{3,2,1,0:T(8,128)(2,1)S(1)}, u32[]{:S(2)}, u32[]{:S(2)}) async-start(bf16[16,2,64,128]{3,2,1,0:T(8,128)(2,1)} %send_sibling.1), calls=%async_computation | async-start | bytes 1048576 | tf_op jit(solution)/shard_map/all_to_all | solution.py:590
  17.0 0.1 compare_select_fusion
  17.1 1.3 %near.1.stat_ref = f32[4,8,1024]{2,1,0:T(8,128)S(1)} custom-call(s32[2]{0:T(128)S(1)} %pad_add_fusion.where_ref, bf16[4096,128]{1,0:T(8,128)(2,1)S(1)} %bitcast.11, bf16[4096,128]{1,0:T(8,128)(2,1)S(1)} %bitcast.16, bf16[4,2,64,128]{3,2,1,0:T(8,128)(2,1)S(1)} %get-tuple-element.25.blocks_ref.kept_ref, bf16[4,2,64,128]{3,2,1,0:T(8,128)(2,1)S(1)} %get-tuple-element.27.given_ref), custom_call_target="tpu_custom_call" | custom-call | tf_op jit(solution)/shard_map/near/pallas_call | solution.py:550
  18.4 13.1 %all-to-all-done.arrived_ref.mine_ref = bf16[16,2,64,128]{3,2,1,0:T(8,128)(2,1)S(1)} async-done(((bf16[16,2,64,128]{3,2,1,0:T(8,128)(2,1)}), bf16[16,2,64,128]{3,2,1,0:T(8,128)(2,1)S(1)}, u32[]{:S(2)}, u32[]{:S(2)}) %all-to-all-start) | async-done | bytes 524320 | tf_op jit(solution)/shard_map/all_to_all | solution.py:590
  31.5 0.6 gather_fusion
  32.1 1.6 %collective-permute-start.1 = (bf16[4,2,64,128]{3,2,1,0:T(8,128)(2,1)S(1)}, bf16[4,2,64,128]{3,2,1,0:T(8,128)(2,1)S(1)}, u32[]{:S(2)}, u32[]{:S(2)}) collective-permute-start(bf16[4,2,64,128]{3,2,1,0:T(8,128)(2,1)S(1)} %gather_fusion), channel_id=1, source_target_pairs={{0,1},{1,0},{2,3},{3,2},{4,5},{5,4},{6,7},{7,6},{8,9},{9,8},{10,11... | collective-permute-start | bytes 393224 | tf_op jit(solution)/shard_map/ppermute | solution.py:596
  33.6 1.4 %mid.1.stat_ref = f32[4,8,1024]{2,1,0:T(8,128)S(1)} custom-call(s32[44]{0:T(128)S(1)} %get-tuple-element.23.plan_ref, bf16[4096,128]{1,0:T(8,128)(2,1)S(1)} %bitcast.12, bf16[4096,128]{1,0:T(8,128)(2,1)S(1)} %bitcast.17, f32[4,8,1024]{2,1,0:T(8,128)S(1)} %near.1.stat_ref, bf16[16,2,64,128]{3,2,1,0:T(8,128)(2,1)S(1)} %all-to-all-done.arrived_ref.mine_ref), custom_call_target="tpu_custom_call" | custom-call | tf_op jit(solution)/shard_map/mid/pallas_call | solution.py:550
  35.0 2.5 %collective-permute-done.1.other_ref = bf16[4,2,64,128]{3,2,1,0:T(8,128)(2,1)S(1)} collective-permute-done((bf16[4,2,64,128]{3,2,1,0:T(8,128)(2,1)S(1)}, bf16[4,2,64,128]{3,2,1,0:T(8,128)(2,1)S(1)}, u32[]{:S(2)}, u32[]{:S(2)}) %collective-permute-start.1) | collective-permute-done | bytes 131104 | tf_op jit(solution)/shard_map/ppermute | solution.py:596
  37.5 2.3 %far.1 = (bf16[4,2,64,128]{3,2,1,0:T(8,128)(2,1)S(1)}, f32[4,8,1024]{2,1,0:T(8,128)S(1)}) custom-call(s32[44]{0:T(128)S(1)} %get-tuple-element.23.plan_ref, bf16[4096,128]{1,0:T(8,128)(2,1)S(1)} %bitcast.13, bf16[4096,128]{1,0:T(8,128)(2,1)S(1)} %bitcast.18, f32[4,8,1024]{2,1,0:T(8,128)S(1)} %mid.1.stat_ref, ...), custom_call_target="tpu_custom_call" | custom-call | tf_op jit(solution)/shard_map/far/pallas_call | solution.py:550
  39.8 1.6 %collective-permute-start.2 = (bf16[4,2,64,128]{3,2,1,0:T(8,128)(2,1)S(1)}, bf16[4,2,64,128]{3,2,1,0:T(8,128)(2,1)S(1)}, u32[]{:S(2)}, u32[]{:S(2)}) collective-permute-start(bf16[4,2,64,128]{3,2,1,0:T(8,128)(2,1)S(1)} %get-tuple-element.30), channel_id=1, source_target_pairs={{0,1},{1,0},{2,3},{3,2},{4,5},{5,4},{6,7},{7,6},{8,9},{9,8},{10,11... | collective-permute-start | bytes 393224 | tf_op jit(solution)/shard_map/ppermute | solution.py:605
  41.4 2.8 %mine.1._ = bf16[16,2,64,128]{3,2,1,0:T(8,128)(2,1)} custom-call(s32[44]{0:T(128)S(1)} %get-tuple-element.23.plan_ref, bf16[4096,128]{1,0:T(8,128)(2,1)S(1)} %bitcast.14, bf16[4096,128]{1,0:T(8,128)(2,1)S(1)} %bitcast.19, f32[4,8,1024]{2,1,0:T(8,128)S(1)} %get-tuple-element.31.stat_ref, bf16[16,2,64,128]{3,2,1,0:T(8,128)(2,1)S(1)} %all-to-all-done.arrived_ref.mine_ref), custom_call_target="tpu_custom_call" | custom-call | tf_op jit(solution)/shard_map/mine/pallas_call | solution.py:550
  44.2 0.7 collective-permute-done.2.blocks_ref
  44.9 1.2 %return_sibling.1 = bf16[16,2,64,128]{3,2,1,0:T(8,128)(2,1)} custom-call(s32[44]{0:T(128)S(1)} %get-tuple-element.23.plan_ref, bf16[4,2,64,128]{3,2,1,0:T(8,128)(2,1)S(1)} %collective-permute-done.2.blocks_ref, bf16[16,2,64,128]{3,2,1,0:T(8,128)(2,1)} %mine.1._), custom_call_target="tpu_custom_call", output_to_operand_aliasing={{}: (2, {})} | custom-call | tf_op jit(solution)/shard_map/return_sibling/pallas_call | solution.py:550
  46.1 0.0 copy-start.2
  46.1 4.5 %all-to-all-start.1 = ((bf16[16,2,64,128]{3,2,1,0:T(8,128)(2,1)}), bf16[16,2,64,128]{3,2,1,0:T(8,128)(2,1)S(1)}, u32[]{:S(2)}, u32[]{:S(2)}) async-start(bf16[16,2,64,128]{3,2,1,0:T(8,128)(2,1)} %return_sibling.1), calls=%async_computation.1 | async-start | bytes 1048576 | tf_op jit(solution)/shard_map/all_to_all | solution.py:617
  50.7 7.5 %local.1 = (bf16[4096,128]{1,0:T(8,128)(2,1)}, bf16[4096,128]{1,0:T(8,128)(2,1)}, f32[512,128]{1,0:T(8,128)S(1)}, f32[512,128]{1,0:T(8,128)S(1)}) custom-call(s32[44]{0:T(128)S(1)} %get-tuple-element.23.plan_ref, bf16[4096,128]{1,0:T(8,128)(2,1)S(1)} %bitcast.15, bf16[4096,128]{1,0:T(8,128)(2,1)S(1)} %bitcast.20, bf16[512,128]{1,0:T(8,128)(2,1)S(1)} %bitcast.22, ...), custom_call_target="tpu_custom_call" | custom-call | tf_op jit(solution)/shard_map/local/pallas_call | solution.py:630
  58.2 0.7 copy-done.4
  58.9 0.7 copy-done.6
  59.6 5.6 %all-to-all-done.1.landed_ref = bf16[16,2,64,128]{3,2,1,0:T(8,128)(2,1)S(1)} async-done(((bf16[16,2,64,128]{3,2,1,0:T(8,128)(2,1)}), bf16[16,2,64,128]{3,2,1,0:T(8,128)(2,1)S(1)}, u32[]{:S(2)}, u32[]{:S(2)}) %all-to-all-start.1) | async-done | bytes 524320 | tf_op jit(solution)/shard_map/all_to_all | solution.py:617
  65.1 0.7 land_sibling.1
  65.9 1.6 %collective-permute-start.3 = (bf16[4,2,64,128]{3,2,1,0:T(8,128)(2,1)S(1)}, bf16[4,2,64,128]{3,2,1,0:T(8,128)(2,1)S(1)}, u32[]{:S(2)}, u32[]{:S(2)}) collective-permute-start(bf16[4,2,64,128]{3,2,1,0:T(8,128)(2,1)S(1)} %land_sibling.1), channel_id=1, source_target_pairs={{0,1},{1,0},{2,3},{3,2},{4,5},{5,4},{6,7},{7,6},{8,9},{9,8},{10,11... | collective-permute-start | bytes 393224 | tf_op jit(solution)/shard_map/ppermute | solution.py:652
  67.4 0.7 land_own.1.own_ref
  68.1 3.2 %collective-permute-done.3.back_ref = bf16[4,2,64,128]{3,2,1,0:T(8,128)(2,1)S(1)} collective-permute-done((bf16[4,2,64,128]{3,2,1,0:T(8,128)(2,1)S(1)}, bf16[4,2,64,128]{3,2,1,0:T(8,128)(2,1)S(1)}, u32[]{:S(2)}, u32[]{:S(2)}) %collective-permute-start.3) | collective-permute-done | bytes 131104 | tf_op jit(solution)/shard_map/ppermute | solution.py:652
  71.3 1.5 %finish.1 = (bf16[512,128]{1,0:T(8,128)(2,1)}, bf16[512,128]{1,0:T(8,128)(2,1)}) custom-call(s32[2]{0:T(128)S(1)} %pad_add_fusion.where_ref, f32[512,128]{1,0:T(8,128)S(1)} %copy-done.5, f32[512,128]{1,0:T(8,128)S(1)} %copy-done.7, f32[4,2,64,128]{3,2,1,0:T(8,128)S(1)} %land_own.1.own_ref, bf16[4,2,64,128]{3,2,1,0:T(8,128)(2,1)S(1)} %collective-permute-done.3.back_ref), custom_call_target="tpu_custom_call" | custom-call | tf_op jit(solution)/shard_map/finish/pallas_call | solution.py:550
  (12 shorter events, 0.0 us)
Async XLA Ops:
  3.0 6.5 %collective-permute-start = (bf16[4,2,64,128]{3,2,1,0:T(8,128)(2,1)S(1)}, bf16[4,2,64,128]{3,2,1,0:T(8,128)(2,1)S(1)}, u32[]{:S(2)}, u32[]{:S(2)}) collective-permute-start(bf16[4,2,64,128]{3,2,1,0:T(8,128)(2,1)S(1)} %get-tuple-element.27.given_ref), channel_id=1, source_target_pairs={{0,1},{1,0},{2,3},{3,2},{4,5},{5,4},{6,7},{7,6},{8,9},{9,8},{10,11... | collective-permute-start | bytes 393224 | tf_op jit(solution)/shard_map/ppermute | solution.py:580
  6.8 10.3 %copy-start = (bf16[128,32,128]{2,1,0:T(8,128)(2,1)S(1)}, bf16[128,32,128]{2,1,0:T(8,128)(2,1)}, u32[]{:S(2)}) copy-start(bf16[128,32,128]{2,1,0:T(8,128)(2,1)} %param.6) | copy-start | bytes 3145732
  6.8 10.3 %copy-start.1 = (bf16[128,32,128]{2,1,0:T(8,128)(2,1)S(1)}, bf16[128,32,128]{2,1,0:T(8,128)(2,1)}, u32[]{:S(2)}) copy-start(bf16[128,32,128]{2,1,0:T(8,128)(2,1)} %param.9) | copy-start | bytes 3145732
  10.8 20.6 %all-to-all-start = ((bf16[16,2,64,128]{3,2,1,0:T(8,128)(2,1)}), bf16[16,2,64,128]{3,2,1,0:T(8,128)(2,1)S(1)}, u32[]{:S(2)}, u32[]{:S(2)}) async-start(bf16[16,2,64,128]{3,2,1,0:T(8,128)(2,1)} %send_sibling.1), calls=%async_computation | async-start | bytes 1048576 | tf_op jit(solution)/shard_map/all_to_all | solution.py:590
  32.1 5.5 %collective-permute-start.1 = (bf16[4,2,64,128]{3,2,1,0:T(8,128)(2,1)S(1)}, bf16[4,2,64,128]{3,2,1,0:T(8,128)(2,1)S(1)}, u32[]{:S(2)}, u32[]{:S(2)}) collective-permute-start(bf16[4,2,64,128]{3,2,1,0:T(8,128)(2,1)S(1)} %gather_fusion), channel_id=1, source_target_pairs={{0,1},{1,0},{2,3},{3,2},{4,5},{5,4},{6,7},{7,6},{8,9},{9,8},{10,11... | collective-permute-start | bytes 393224 | tf_op jit(solution)/shard_map/ppermute | solution.py:596
  39.8 5.0 %collective-permute-start.2 = (bf16[4,2,64,128]{3,2,1,0:T(8,128)(2,1)S(1)}, bf16[4,2,64,128]{3,2,1,0:T(8,128)(2,1)S(1)}, u32[]{:S(2)}, u32[]{:S(2)}) collective-permute-start(bf16[4,2,64,128]{3,2,1,0:T(8,128)(2,1)S(1)} %get-tuple-element.30), channel_id=1, source_target_pairs={{0,1},{1,0},{2,3},{3,2},{4,5},{5,4},{6,7},{7,6},{8,9},{9,8},{10,11... | collective-permute-start | bytes 393224 | tf_op jit(solution)/shard_map/ppermute | solution.py:605
  46.1 4.6 %copy-start.2 = (bf16[128,4,128]{2,1,0:T(4,128)(2,1)S(1)}, bf16[128,4,128]{2,1,0:T(4,128)(2,1)}, u32[]{:S(2)}) copy-start(bf16[128,4,128]{2,1,0:T(4,128)(2,1)} %param.7) | copy-start | bytes 393220
  46.1 4.5 %copy-start.3 = (bf16[128,4,128]{2,1,0:T(4,128)(2,1)S(1)}, bf16[128,4,128]{2,1,0:T(4,128)(2,1)}, u32[]{:S(2)}) copy-start(bf16[128,4,128]{2,1,0:T(4,128)(2,1)} %param.8) | copy-start | bytes 393220
  46.1 19.0 %all-to-all-start.1 = ((bf16[16,2,64,128]{3,2,1,0:T(8,128)(2,1)}), bf16[16,2,64,128]{3,2,1,0:T(8,128)(2,1)S(1)}, u32[]{:S(2)}, u32[]{:S(2)}) async-start(bf16[16,2,64,128]{3,2,1,0:T(8,128)(2,1)} %return_sibling.1), calls=%async_computation.1 | async-start | bytes 1048576 | tf_op jit(solution)/shard_map/all_to_all | solution.py:617
  58.2 0.7 copy-start.4
  58.9 0.7 copy-start.6
  65.8 5.5 %copy-start.5 = (f32[512,128]{1,0:T(8,128)S(1)}, f32[512,128]{1,0:T(8,128)}, u32[]{:S(2)}) copy-start(f32[512,128]{1,0:T(8,128)} %copy-done.4) | copy-start | bytes 786436
  65.9 5.5 %copy-start.7 = (f32[512,128]{1,0:T(8,128)S(1)}, f32[512,128]{1,0:T(8,128)}, u32[]{:S(2)}) copy-start(f32[512,128]{1,0:T(8,128)} %copy-done.6) | copy-start | bytes 786436
  65.9 5.5 %collective-permute-start.3 = (bf16[4,2,64,128]{3,2,1,0:T(8,128)(2,1)S(1)}, bf16[4,2,64,128]{3,2,1,0:T(8,128)(2,1)S(1)}, u32[]{:S(2)}, u32[]{:S(2)}) collective-permute-start(bf16[4,2,64,128]{3,2,1,0:T(8,128)(2,1)S(1)} %land_sibling.1), channel_id=1, source_target_pairs={{0,1},{1,0},{2,3},{3,2},{4,5},{5,4},{6,7},{7,6},{8,9},{9,8},{10,11... | collective-permute-start | bytes 393224 | tf_op jit(solution)/shard_map/ppermute | solution.py:652

commit v6 on v5

--- a/solution.py
+++ b/solution.py
@@ -236,18 +236,8 @@
     return grp_count, 2 * grp_count, 2 * grp_count + blocks, 2 * grp_count + 2 * blocks
 
 
-def pack_kernel(
-    where_ref, lists_ref, counts_ref, k_hbm, v_hbm, plan_ref, kept_ref, given_ref,
-    k_ref, v_ref, sems, *, grp_count, kv_heads
-):
-    blocks, _, half, _ = kept_ref.shape
-    copies = [
-        pltpu.make_async_copy(k_hbm, k_ref, sems.at[0]),
-        pltpu.make_async_copy(v_hbm, v_ref, sems.at[1]),
-    ]
-    for copy in copies:
-        copy.start()
-    group, mine = where_ref[0], where_ref[1]
+def plan_kernel(lists_ref, counts_ref, plan_ref, *, grp_count, blocks):
+    group, mine = lax.axis_index("grp"), lax.axis_index("uly")
     per_group = 2 * blocks
     low = group * per_group
     sib_at, source_at, give_at, seen_at = plan_spans(grp_count, blocks)
@@ -267,12 +257,21 @@
         plan_ref[seen_at + block] = counts_ref[at]
         at = low + (1 - mine) * blocks + block
         plan_ref[give_at + block] = lax.div(lists_ref[at], per_group)
+
+
+def pack_kernel(k_hbm, v_hbm, kept_ref, given_ref, k_ref, v_ref, sems, *, kv_heads):
+    blocks, _, half, _ = kept_ref.shape
+    copies = [
+        pltpu.make_async_copy(k_hbm, k_ref, sems.at[0]),
+        pltpu.make_async_copy(v_hbm, v_ref, sems.at[1]),
+    ]
     for copy in copies:
-        copy.wait()
-    first = mine == 0
+        copy.start()
+    first = lax.axis_index("uly") == 0
     order = head_major(2 * half, kv_heads)
-    for block in range(blocks):
-        for which, ref in enumerate((k_ref, v_ref)):
+    for which, ref in enumerate((k_ref, v_ref)):
+        copies[which].wait()
+        for block in range(blocks):
             ordered = reorder(order, ref[block * 2 * half:(block + 1) * 2 * half])
             kept_ref[block, which] = jnp.where(first, ordered[:half], ordered[half:])
             given_ref[block, which] = jnp.where(first, ordered[half:], ordered[:half])
@@ -304,14 +303,15 @@
 
 
 def near_kernel(
-    where_ref, q_ref, g_ref, kept_ref, given_ref, stat_ref, *, heads, kv_heads, score_scale
+    q_ref, g_ref, kept_ref, given_ref, stat_ref, *, heads, kv_heads, score_scale
 ):
     blocks = stat_ref.shape[0]
     rows = q_ref.shape[0] // blocks
     place = kept_ref.shape[2] // kv_heads
     token, lane_head = lanes(rows, heads, kv_heads)
     key = lax.broadcasted_iota(jnp.int32, (2 * place, rows), 0)
-    part = jnp.where(key < place, where_ref[1], 1 - where_ref[1])
+    mine = lax.axis_index("uly")
+    part = jnp.where(key < place, mine, 1 - mine)
     causal = key % place + part * place <= token
     for block in range(blocks):
         span = slice(block * rows, (block + 1) * rows)
@@ -489,10 +489,10 @@
 
 
 def finish_kernel(
-    where_ref, dk_near_ref, dv_near_ref, own_ref, back_ref, dk_ref, dv_ref, *, kv_heads
+    dk_near_ref, dv_near_ref, own_ref, back_ref, dk_ref, dv_ref, *, kv_heads
 ):
     blocks, _, half, _ = back_ref.shape
-    mine = where_ref[1] == 0
+    mine = lax.axis_index("uly") == 0
     order = head_major(2 * half, kv_heads)
     for block in range(blocks):
         span = slice(block * 2 * half, (block + 1) * 2 * half)
@@ -511,8 +511,6 @@
 def whole_blocks(queries, keys, values, output_cotangent, block_lists, list_counts):
     grp_count = lax.axis_size("grp")
     uly_count = lax.axis_size("uly")
-    my_group = lax.axis_index("grp")
-    my_half = lax.axis_index("uly")
     tokens, heads, width = queries.shape
     kv_heads = keys.shape[1]
     per_group = block_lists.shape[0] // grp_count
@@ -524,7 +522,6 @@
     sizes = dict(heads=heads, kv_heads=kv_heads, score_scale=width ** (-0.5))
     swap = [(0, 1), (1, 0)]
 
-    where = jnp.stack([my_group, my_half]).astype(jnp.int32)
     sib_at, source_at, give_at, seen_at = plan_spans(grp_count, mine_blocks)
 
     q2 = queries.reshape(tokens * heads, width)
@@ -558,25 +555,28 @@
             name=name,
         )(*scalars, *operands, *extra)
 
-    plan, kept, given = pl.pallas_call(
-        partial(pack_kernel, grp_count=grp_count, kv_heads=kv_heads),
-        in_specs=[smem, smem, smem, anywhere, anywhere],
-        out_specs=[smem, vmem, vmem],
-        out_shape=[
-            jax.ShapeDtypeStruct((seen_at + mine_blocks,), jnp.int32), part_shape, part_shape
-        ],
+    def in_hbm(array):
+        return pltpu.with_memory_space_constraint(array, pltpu.HBM)
+
+    kept, given = pl.pallas_call(
+        partial(pack_kernel, kv_heads=kv_heads),
+        in_specs=[anywhere, anywhere],
+        out_specs=[vmem, vmem],
+        out_shape=[part_shape, part_shape],
         scratch_shapes=[
             pltpu.VMEM(k2.shape, BF16), pltpu.VMEM(k2.shape, BF16), pltpu.SemaphoreType.DMA((2,))
         ],
         compiler_params=limit,
         name="pack",
-    )(
-        where,
-        pltpu.with_memory_space_constraint(block_lists.reshape(-1), pltpu.HBM),
-        pltpu.with_memory_space_constraint(list_counts, pltpu.HBM),
-        pltpu.with_memory_space_constraint(k2, pltpu.HBM),
-        pltpu.with_memory_space_constraint(v2, pltpu.HBM),
-    )
+    )(in_hbm(k2), in_hbm(v2))
+    plan = pl.pallas_call(
+        partial(plan_kernel, grp_count=grp_count, blocks=mine_blocks),
+        in_specs=[smem, smem],
+        out_specs=smem,
+        out_shape=pltpu.SMEM((seen_at + mine_blocks,), jnp.int32),
+        compiler_params=limit,
+        name="plan",
+    )(in_hbm(block_lists.reshape(-1)), in_hbm(list_counts))
     gotten = lax.ppermute(given, "uly", swap)
     outgoing = call(
         partial(outgoing_kernel, first=0), "send_own", (plan,), (kept,),
@@ -589,7 +589,7 @@
     outgoing, given = lax.optimization_barrier((outgoing, given))
     arrived = lax.all_to_all(outgoing, "grp", split_axis=0, concat_axis=0, tiled=True)
     stats = call(
-        partial(near_kernel, **sizes), "near", (where,), (q2, g2, kept, given), stat_shape
+        partial(near_kernel, **sizes), "near", (), (q2, g2, kept, given), stat_shape
     )
     arrived, stats = lax.optimization_barrier((arrived, stats))
     give_rows = plan[give_at:give_at + mine_blocks]
@@ -655,7 +655,7 @@
         jax.ShapeDtypeStruct(part_shape.shape, F32), sum_scratch,
     )
     dk, dv = call(
-        partial(finish_kernel, kv_heads=kv_heads), "finish", (where,),
+        partial(finish_kernel, kv_heads=kv_heads), "finish", (),
         (dk_near, dv_near, own, back), [small_shape, small_shape],
     )
     return (

time: 73.2 us -> 69.4 us (0.948)
  Pallas kernels: 23.7 us -> 18.4 us
  waiting for transfers between devices: 27.8 us -> 29.2 us
    pallas_call x10, Pallas kernels: 14 us -> 9.09 us  [call(): pl.pallas_call(kernel, in_specs=[smem] * len(scalars) + [vmem] * len(oper...]
    ppermute x1, waiting for transfers between devices: 2.71 us -> 1.57 us  [whole_blocks(): gotten = lax.ppermute(given, 'uly', swap)]
    pallas_call x1 -> x2, Pallas kernels: 2.26 us -> 2.39 us  [the longest x1 1.29 us: whole_blocks(): pl.pallas_call(partial(pack_kernel, kv_heads=kv_heads), in_specs=[anywher...]
  transfers between devices with their start and end apart: 6 -> 6, of which waited for: 6 -> 6; matrix products, arithmetic and copies ran while one was open for 0% -> 0% of each run, Pallas kernels for 20% -> 19%
where the time goes in v6:
time: 69.4 us; the launch traced here: 69.1 us
  waiting for transfers between devices  29.2 us (42%)
  starting transfers between devices  18.5 us (27%)
  Pallas kernels  18.4 us (27%)
  local copies, waits for them, and re-layouts  2 us (3%)
  between operations  0.81 us (1%)
    all_to_all x1, waiting for transfers between devices, whole_blocks(): lax.all_to_all(outgoing, 'grp', split_axis=0, concat_axis=0, tiled=True)  13.6 us
    pallas_call x10, Pallas kernels, call(): pl.pallas_call(kernel, in_specs=[smem] * len(scalars) + [vmem] * len(oper...  9.09 us
    pallas_call x1, Pallas kernels, whole_blocks(): pl.pallas_call(partial(local_kernel, seen_at=seen_at, **sizes), grid_spec...  6.92 us
    all_to_all x1, starting transfers between devices, whole_blocks(): lax.all_to_all(outgoing, 'grp', split_axis=0, concat_axis=0, tiled=True)  6.16 us
    all_to_all x1, waiting for transfers between devices, whole_blocks(): lax.all_to_all(returning, 'grp', split_axis=0, concat_axis=0, tiled=True)  6.14 us
    all_to_all x1, starting transfers between devices, whole_blocks(): lax.all_to_all(returning, 'grp', split_axis=0, concat_axis=0, tiled=True)  4.51 us
    ppermute x1, waiting for transfers between devices, whole_blocks(): back = lax.ppermute(give, 'uly', swap)  3.7 us
    ppermute x1, waiting for transfers between devices, whole_blocks(): other = lax.ppermute(take_rows(arrived, give_rows), 'uly', swap)  3.04 us
  transfers between devices with their start and end apart: 6, of which 6 were waited for; matrix products, arithmetic and copies ran while one was open for 0% of the time, Pallas kernels for 19%

profile of v6, /device:TPU:0, one launch (start us, length us, event | category | flops | bytes accessed | tf_op | source)
XLA Modules:
  0.0 69.1 jit_solution(16451181533324519934)
XLA Ops:
  0.6 1.3 %pack.1 = (bf16[4,2,64,128]{3,2,1,0:T(8,128)(2,1)S(1)}, bf16[4,2,64,128]{3,2,1,0:T(8,128)(2,1)S(1)}) custom-call(bf16[512,128]{1,0:T(8,128)(2,1)} %bitcast.19, bf16[512,128]{1,0:T(8,128)(2,1)} %bitcast.21), custom_call_target="tpu_custom_call" | custom-call | tf_op jit(solution)/shard_map/pack/pallas_call | solution.py:561
  1.9 3.0 %collective-permute-start = (bf16[4,2,64,128]{3,2,1,0:T(8,128)(2,1)S(1)}, bf16[4,2,64,128]{3,2,1,0:T(8,128)(2,1)S(1)}, u32[]{:S(2)}, u32[]{:S(2)}) collective-permute-start(bf16[4,2,64,128]{3,2,1,0:T(8,128)(2,1)S(1)} %get-tuple-element.25.given_ref), channel_id=1, source_target_pairs={{0,1},{1,0},{2,3},{3,2},{4,5},{5,4},{6,7},{7,6},{8,9},{9,8},{10,11... | collective-permute-start | bytes 393224 | tf_op jit(solution)/shard_map/ppermute | solution.py:580
  5.0 1.1 %plan.1.plan_ref = s32[44]{0:T(128)S(4)} custom-call(s32[128]{0:T(128)} %bitcast.27, s32[128]{0:T(128)} %counts_ref.1), custom_call_target="tpu_custom_call" | custom-call | tf_op jit(solution)/shard_map/plan/pallas_call | solution.py:572
  6.1 0.8 %send_own.1.refs_0_ = bf16[16,2,64,128]{3,2,1,0:T(8,128)(2,1)} custom-call(s32[44]{0:T(128)S(4)} %plan.1.plan_ref, bf16[4,2,64,128]{3,2,1,0:T(8,128)(2,1)S(1)} %get-tuple-element.23.blocks_ref.kept_ref), custom_call_target="tpu_custom_call" | custom-call | tf_op jit(solution)/shard_map/send_own/pallas_call | solution.py:547
  6.9 0.0 copy-start
  6.9 0.0 copy-start.1
  6.9 1.6 %collective-permute-done.blocks_ref = bf16[4,2,64,128]{3,2,1,0:T(8,128)(2,1)S(1)} collective-permute-done((bf16[4,2,64,128]{3,2,1,0:T(8,128)(2,1)S(1)}, bf16[4,2,64,128]{3,2,1,0:T(8,128)(2,1)S(1)}, u32[]{:S(2)}, u32[]{:S(2)}) %collective-permute-start) | collective-permute-done | bytes 131104 | tf_op jit(solution)/shard_map/ppermute | solution.py:580
  8.5 0.8 %send_sibling.1 = bf16[16,2,64,128]{3,2,1,0:T(8,128)(2,1)} custom-call(s32[44]{0:T(128)S(4)} %plan.1.plan_ref, bf16[4,2,64,128]{3,2,1,0:T(8,128)(2,1)S(1)} %collective-permute-done.blocks_ref, bf16[16,2,64,128]{3,2,1,0:T(8,128)(2,1)} %send_own.1.refs_0_), custom_call_target="tpu_custom_call", output_to_operand_aliasing={{}: (2, {})} | custom-call | tf_op jit(solution)/shard_map/send_sibling/pallas_call | solution.py:547
  9.2 6.2 %all-to-all-start = ((bf16[16,2,64,128]{3,2,1,0:T(8,128)(2,1)}), bf16[16,2,64,128]{3,2,1,0:T(8,128)(2,1)S(1)}, u32[]{:S(2)}, u32[]{:S(2)}) async-start(bf16[16,2,64,128]{3,2,1,0:T(8,128)(2,1)} %send_sibling.1), calls=%async_computation | async-start | bytes 1048576 | tf_op jit(solution)/shard_map/all_to_all | solution.py:590
  15.4 0.1 compare_select_fusion
  15.5 0.7 %near.1.stat_ref = f32[4,8,1024]{2,1,0:T(8,128)S(1)} custom-call(bf16[4096,128]{1,0:T(8,128)(2,1)S(1)} %bitcast.9, bf16[4096,128]{1,0:T(8,128)(2,1)S(1)} %bitcast.14, bf16[4,2,64,128]{3,2,1,0:T(8,128)(2,1)S(1)} %get-tuple-element.23.blocks_ref.kept_ref, bf16[4,2,64,128]{3,2,1,0:T(8,128)(2,1)S(1)} %get-tuple-element.25.given_ref), custom_call_target="tpu_custom_call" | custom-call | tf_op jit(solution)/shard_map/near/pallas_call | solution.py:547
  16.3 13.6 %all-to-all-done.arrived_ref.mine_ref = bf16[16,2,64,128]{3,2,1,0:T(8,128)(2,1)S(1)} async-done(((bf16[16,2,64,128]{3,2,1,0:T(8,128)(2,1)}), bf16[16,2,64,128]{3,2,1,0:T(8,128)(2,1)S(1)}, u32[]{:S(2)}, u32[]{:S(2)}) %all-to-all-start) | async-done | bytes 524320 | tf_op jit(solution)/shard_map/all_to_all | solution.py:590
  29.9 0.6 gather_fusion
  30.4 1.6 %collective-permute-start.1 = (bf16[4,2,64,128]{3,2,1,0:T(8,128)(2,1)S(1)}, bf16[4,2,64,128]{3,2,1,0:T(8,128)(2,1)S(1)}, u32[]{:S(2)}, u32[]{:S(2)}) collective-permute-start(bf16[4,2,64,128]{3,2,1,0:T(8,128)(2,1)S(1)} %gather_fusion), channel_id=1, source_target_pairs={{0,1},{1,0},{2,3},{3,2},{4,5},{5,4},{6,7},{7,6},{8,9},{9,8},{10,11... | collective-permute-start | bytes 393224 | tf_op jit(solution)/shard_map/ppermute | solution.py:596
  32.0 0.8 %mid.1.stat_ref = f32[4,8,1024]{2,1,0:T(8,128)S(1)} custom-call(s32[44]{0:T(128)S(4)} %plan.1.plan_ref, bf16[4096,128]{1,0:T(8,128)(2,1)S(1)} %bitcast.10, bf16[4096,128]{1,0:T(8,128)(2,1)S(1)} %bitcast.15, f32[4,8,1024]{2,1,0:T(8,128)S(1)} %near.1.stat_ref, bf16[16,2,64,128]{3,2,1,0:T(8,128)(2,1)S(1)} %all-to-all-done.arrived_ref.mine_ref), custom_call_target="tpu_custom_call" | custom-call | tf_op jit(solution)/shard_map/mid/pallas_call | solution.py:547
  32.9 3.0 %collective-permute-done.1.other_ref = bf16[4,2,64,128]{3,2,1,0:T(8,128)(2,1)S(1)} collective-permute-done((bf16[4,2,64,128]{3,2,1,0:T(8,128)(2,1)S(1)}, bf16[4,2,64,128]{3,2,1,0:T(8,128)(2,1)S(1)}, u32[]{:S(2)}, u32[]{:S(2)}) %collective-permute-start.1) | collective-permute-done | bytes 131104 | tf_op jit(solution)/shard_map/ppermute | solution.py:596
  35.9 1.7 %far.1 = (bf16[4,2,64,128]{3,2,1,0:T(8,128)(2,1)S(1)}, f32[4,8,1024]{2,1,0:T(8,128)S(1)}) custom-call(s32[44]{0:T(128)S(4)} %plan.1.plan_ref, bf16[4096,128]{1,0:T(8,128)(2,1)S(1)} %bitcast.11, bf16[4096,128]{1,0:T(8,128)(2,1)S(1)} %bitcast.16, f32[4,8,1024]{2,1,0:T(8,128)S(1)} %mid.1.stat_ref, bf16[4,2,64,128]{3,2,1,0:T(8,128)(2,1)S(1)} %collective-permute-done.1.other_ref), custom_call_target="tpu_custom_call" | custom-call | tf_op jit(solution)/shard_map/far/pallas_call | solution.py:547
  37.7 1.6 %collective-permute-start.2 = (bf16[4,2,64,128]{3,2,1,0:T(8,128)(2,1)S(1)}, bf16[4,2,64,128]{3,2,1,0:T(8,128)(2,1)S(1)}, u32[]{:S(2)}, u32[]{:S(2)}) collective-permute-start(bf16[4,2,64,128]{3,2,1,0:T(8,128)(2,1)S(1)} %get-tuple-element.28), channel_id=1, source_target_pairs={{0,1},{1,0},{2,3},{3,2},{4,5},{5,4},{6,7},{7,6},{8,9},{9,8},{10,11... | collective-permute-start | bytes 393224 | tf_op jit(solution)/shard_map/ppermute | solution.py:605
  39.2 2.2 %mine.1._ = bf16[16,2,64,128]{3,2,1,0:T(8,128)(2,1)} custom-call(s32[44]{0:T(128)S(4)} %plan.1.plan_ref, bf16[4096,128]{1,0:T(8,128)(2,1)S(1)} %bitcast.12, bf16[4096,128]{1,0:T(8,128)(2,1)S(1)} %bitcast.17, f32[4,8,1024]{2,1,0:T(8,128)S(1)} %get-tuple-element.29.stat_ref, bf16[16,2,64,128]{3,2,1,0:T(8,128)(2,1)S(1)} %all-to-all-done.arrived_ref.mine_ref), custom_call_target="tpu_custom_call" | custom-call | tf_op jit(solution)/shard_map/mine/pallas_call | solution.py:547
  41.5 1.2 %collective-permute-done.2.blocks_ref = bf16[4,2,64,128]{3,2,1,0:T(8,128)(2,1)S(1)} collective-permute-done((bf16[4,2,64,128]{3,2,1,0:T(8,128)(2,1)S(1)}, bf16[4,2,64,128]{3,2,1,0:T(8,128)(2,1)S(1)}, u32[]{:S(2)}, u32[]{:S(2)}) %collective-permute-start.2) | collective-permute-done | bytes 131104 | tf_op jit(solution)/shard_map/ppermute | solution.py:605
  42.7 0.7 return_sibling.1
  43.4 0.0 copy-start.2
  43.4 4.5 %all-to-all-start.1 = ((bf16[16,2,64,128]{3,2,1,0:T(8,128)(2,1)}), bf16[16,2,64,128]{3,2,1,0:T(8,128)(2,1)S(1)}, u32[]{:S(2)}, u32[]{:S(2)}) async-start(bf16[16,2,64,128]{3,2,1,0:T(8,128)(2,1)} %return_sibling.1), calls=%async_computation.1 | async-start | bytes 1048576 | tf_op jit(solution)/shard_map/all_to_all | solution.py:617
  48.0 6.9 %local.1 = (bf16[4096,128]{1,0:T(8,128)(2,1)}, bf16[4096,128]{1,0:T(8,128)(2,1)}, f32[512,128]{1,0:T(8,128)S(1)}, f32[512,128]{1,0:T(8,128)S(1)}) custom-call(s32[44]{0:T(128)S(4)} %plan.1.plan_ref, bf16[4096,128]{1,0:T(8,128)(2,1)S(1)} %bitcast.13, bf16[4096,128]{1,0:T(8,128)(2,1)S(1)} %bitcast.18, bf16[512,128]{1,0:T(8,128)(2,1)S(1)} %bitcast.20, ...), custom_call_target="tpu_custom_call" | custom-call | tf_op jit(solution)/shard_map/local/pallas_call | solution.py:630
  54.9 0.7 %copy-done.4 = f32[512,128]{1,0:T(8,128)} copy-done((f32[512,128]{1,0:T(8,128)}, f32[512,128]{1,0:T(8,128)S(1)}, u32[]{:S(2)}) %copy-start.4) | copy-done | bytes 262168
  55.6 0.7 %copy-done.6 = f32[512,128]{1,0:T(8,128)} copy-done((f32[512,128]{1,0:T(8,128)}, f32[512,128]{1,0:T(8,128)S(1)}, u32[]{:S(2)}) %copy-start.6) | copy-done | bytes 262168
  56.3 6.1 %all-to-all-done.1.landed_ref = bf16[16,2,64,128]{3,2,1,0:T(8,128)(2,1)S(1)} async-done(((bf16[16,2,64,128]{3,2,1,0:T(8,128)(2,1)}), bf16[16,2,64,128]{3,2,1,0:T(8,128)(2,1)S(1)}, u32[]{:S(2)}, u32[]{:S(2)}) %all-to-all-start.1) | async-done | bytes 524320 | tf_op jit(solution)/shard_map/all_to_all | solution.py:617
  62.4 0.2 land_sibling.1
  62.6 1.6 %collective-permute-start.3 = (bf16[4,2,64,128]{3,2,1,0:T(8,128)(2,1)S(1)}, bf16[4,2,64,128]{3,2,1,0:T(8,128)(2,1)S(1)}, u32[]{:S(2)}, u32[]{:S(2)}) collective-permute-start(bf16[4,2,64,128]{3,2,1,0:T(8,128)(2,1)S(1)} %land_sibling.1), channel_id=1, source_target_pairs={{0,1},{1,0},{2,3},{3,2},{4,5},{5,4},{6,7},{7,6},{8,9},{9,8},{10,11... | collective-permute-start | bytes 393224 | tf_op jit(solution)/shard_map/ppermute | solution.py:652
  64.2 0.2 land_own.1.own_ref
  64.4 3.7 %collective-permute-done.3.back_ref = bf16[4,2,64,128]{3,2,1,0:T(8,128)(2,1)S(1)} collective-permute-done((bf16[4,2,64,128]{3,2,1,0:T(8,128)(2,1)S(1)}, bf16[4,2,64,128]{3,2,1,0:T(8,128)(2,1)S(1)}, u32[]{:S(2)}, u32[]{:S(2)}) %collective-permute-start.3) | collective-permute-done | bytes 131104 | tf_op jit(solution)/shard_map/ppermute | solution.py:652
  68.1 1.0 %finish.1 = (bf16[512,128]{1,0:T(8,128)(2,1)}, bf16[512,128]{1,0:T(8,128)(2,1)}) custom-call(f32[512,128]{1,0:T(8,128)S(1)} %copy-done.5, f32[512,128]{1,0:T(8,128)S(1)} %copy-done.7, f32[4,2,64,128]{3,2,1,0:T(8,128)S(1)} %land_own.1.own_ref, bf16[4,2,64,128]{3,2,1,0:T(8,128)(2,1)S(1)} %collective-permute-done.3.back_ref), custom_call_target="tpu_custom_call" | custom-call | tf_op jit(solution)/shard_map/finish/pallas_call | solution.py:547
  (12 shorter events, 0.0 us)
Async XLA Ops:
  1.9 6.5 %collective-permute-start = (bf16[4,2,64,128]{3,2,1,0:T(8,128)(2,1)S(1)}, bf16[4,2,64,128]{3,2,1,0:T(8,128)(2,1)S(1)}, u32[]{:S(2)}, u32[]{:S(2)}) collective-permute-start(bf16[4,2,64,128]{3,2,1,0:T(8,128)(2,1)S(1)} %get-tuple-element.25.given_ref), channel_id=1, source_target_pairs={{0,1},{1,0},{2,3},{3,2},{4,5},{5,4},{6,7},{7,6},{8,9},{9,8},{10,11... | collective-permute-start | bytes 393224 | tf_op jit(solution)/shard_map/ppermute | solution.py:580
  6.9 8.7 %copy-start = (bf16[128,32,128]{2,1,0:T(8,128)(2,1)S(1)}, bf16[128,32,128]{2,1,0:T(8,128)(2,1)}, u32[]{:S(2)}) copy-start(bf16[128,32,128]{2,1,0:T(8,128)(2,1)} %param.6) | copy-start | bytes 3145732
  6.9 8.7 %copy-start.1 = (bf16[128,32,128]{2,1,0:T(8,128)(2,1)S(1)}, bf16[128,32,128]{2,1,0:T(8,128)(2,1)}, u32[]{:S(2)}) copy-start(bf16[128,32,128]{2,1,0:T(8,128)(2,1)} %param.9) | copy-start | bytes 3145732
  9.2 20.6 %all-to-all-start = ((bf16[16,2,64,128]{3,2,1,0:T(8,128)(2,1)}), bf16[16,2,64,128]{3,2,1,0:T(8,128)(2,1)S(1)}, u32[]{:S(2)}, u32[]{:S(2)}) async-start(bf16[16,2,64,128]{3,2,1,0:T(8,128)(2,1)} %send_sibling.1), calls=%async_computation | async-start | bytes 1048576 | tf_op jit(solution)/shard_map/all_to_all | solution.py:590
  30.4 5.5 %collective-permute-start.1 = (bf16[4,2,64,128]{3,2,1,0:T(8,128)(2,1)S(1)}, bf16[4,2,64,128]{3,2,1,0:T(8,128)(2,1)S(1)}, u32[]{:S(2)}, u32[]{:S(2)}) collective-permute-start(bf16[4,2,64,128]{3,2,1,0:T(8,128)(2,1)S(1)} %gather_fusion), channel_id=1, source_target_pairs={{0,1},{1,0},{2,3},{3,2},{4,5},{5,4},{6,7},{7,6},{8,9},{9,8},{10,11... | collective-permute-start | bytes 393224 | tf_op jit(solution)/shard_map/ppermute | solution.py:596
  37.7 5.0 %collective-permute-start.2 = (bf16[4,2,64,128]{3,2,1,0:T(8,128)(2,1)S(1)}, bf16[4,2,64,128]{3,2,1,0:T(8,128)(2,1)S(1)}, u32[]{:S(2)}, u32[]{:S(2)}) collective-permute-start(bf16[4,2,64,128]{3,2,1,0:T(8,128)(2,1)S(1)} %get-tuple-element.28), channel_id=1, source_target_pairs={{0,1},{1,0},{2,3},{3,2},{4,5},{5,4},{6,7},{7,6},{8,9},{9,8},{10,11... | collective-permute-start | bytes 393224 | tf_op jit(solution)/shard_map/ppermute | solution.py:605
  43.4 4.5 %copy-start.2 = (bf16[128,4,128]{2,1,0:T(4,128)(2,1)S(1)}, bf16[128,4,128]{2,1,0:T(4,128)(2,1)}, u32[]{:S(2)}) copy-start(bf16[128,4,128]{2,1,0:T(4,128)(2,1)} %param.7) | copy-start | bytes 393220
  43.4 4.5 %copy-start.3 = (bf16[128,4,128]{2,1,0:T(4,128)(2,1)S(1)}, bf16[128,4,128]{2,1,0:T(4,128)(2,1)}, u32[]{:S(2)}) copy-start(bf16[128,4,128]{2,1,0:T(4,128)(2,1)} %param.8) | copy-start | bytes 393220
  43.4 19.0 %all-to-all-start.1 = ((bf16[16,2,64,128]{3,2,1,0:T(8,128)(2,1)}), bf16[16,2,64,128]{3,2,1,0:T(8,128)(2,1)S(1)}, u32[]{:S(2)}, u32[]{:S(2)}) async-start(bf16[16,2,64,128]{3,2,1,0:T(8,128)(2,1)} %return_sibling.1), calls=%async_computation.1 | async-start | bytes 1048576 | tf_op jit(solution)/shard_map/all_to_all | solution.py:617
  54.9 0.7 %copy-start.4 = (f32[512,128]{1,0:T(8,128)}, f32[512,128]{1,0:T(8,128)S(1)}, u32[]{:S(2)}) copy-start(f32[512,128]{1,0:T(8,128)S(1)} %get-tuple-element.35.dk_near_ref) | copy-start | bytes 786436
  55.6 0.7 %copy-start.6 = (f32[512,128]{1,0:T(8,128)}, f32[512,128]{1,0:T(8,128)S(1)}, u32[]{:S(2)}) copy-start(f32[512,128]{1,0:T(8,128)S(1)} %get-tuple-element.36.dv_near_ref) | copy-start | bytes 786436
  62.6 5.5 %copy-start.5 = (f32[512,128]{1,0:T(8,128)S(1)}, f32[512,128]{1,0:T(8,128)}, u32[]{:S(2)}) copy-start(f32[512,128]{1,0:T(8,128)} %copy-done.4) | copy-start | bytes 786436
  62.6 5.5 %copy-start.7 = (f32[512,128]{1,0:T(8,128)S(1)}, f32[512,128]{1,0:T(8,128)}, u32[]{:S(2)}) copy-start(f32[512,128]{1,0:T(8,128)} %copy-done.6) | copy-start | bytes 786436
  62.6 5.5 %collective-permute-start.3 = (bf16[4,2,64,128]{3,2,1,0:T(8,128)(2,1)S(1)}, bf16[4,2,64,128]{3,2,1,0:T(8,128)(2,1)S(1)}, u32[]{:S(2)}, u32[]{:S(2)}) collective-permute-start(bf16[4,2,64,128]{3,2,1,0:T(8,128)(2,1)S(1)} %land_sibling.1), channel_id=1, source_target_pairs={{0,1},{1,0},{2,3},{3,2},{4,5},{5,4},{6,7},{7,6},{8,9},{9,8},{10,11... | collective-permute-start | bytes 393224 | tf_op jit(solution)/shard_map/ppermute | solution.py:652

commit v7 on v6

--- a/solution.py
+++ b/solution.py
@@ -291,9 +291,19 @@
         pl.when(wanted)(copy.wait)
 
 
+def giving_kernel(plan_ref, arrived_ref, *out_refs, give_at):
+    block = 0
+    for out_ref in out_refs:
+        for at in range(out_ref.shape[0]):
+            out_ref[at] = arrived_ref[plan_ref[give_at + block]]
+            block += 1
+
+
 def returning_kernel(plan_ref, blocks_ref, _, out_ref, sems, *, give_at):
     copies = [
-        pltpu.make_async_copy(blocks_ref.at[block], out_ref.at[plan_ref[give_at + block]], sems.at[block])
+        pltpu.make_async_copy(
+            blocks_ref.at[block], out_ref.at[plan_ref[give_at + block]], sems.at[block]
+        )
         for block in range(blocks_ref.shape[0])
     ]
     for copy in copies:
@@ -381,34 +391,35 @@
 
 def far_kernel(
     plan_ref, q_ref, g_ref, stat_ref, other_ref, grad_ref, out_ref,
-    *, heads, kv_heads, score_scale, seen_at
+    *, heads, kv_heads, score_scale, seen_at, first
 ):
-    blocks = stat_ref.shape[0]
-    rows = q_ref.shape[0] // blocks
+    rows = q_ref.shape[0] // stat_ref.shape[0]
     _, lane_head = lanes(rows, heads, kv_heads)
-    for block in range(blocks):
+    for at in range(other_ref.shape[0]):
+        block = first + at
         span = slice(block * rows, (block + 1) * rows)
         q = q_ref[span]
         g = g_ref[span]
         scores, dprobs = far_scores(
-            other_ref, block, q, g, plan_ref[seen_at + block], lane_head, kv_heads, score_scale
+            other_ref, at, q, g, plan_ref[seen_at + block], lane_head, kv_heads, score_scale
         )
         highest, raised, total, delta = merged(stat_ref, block, scores, dprobs)
         inverse = 1.0 / total
         delta = delta * inverse
-        grad_ref[block, 0], grad_ref[block, 1] = far_gradients(
+        grad_ref[at, 0], grad_ref[at, 1] = far_gradients(
             raised * inverse, dprobs, delta, q, g, lane_head, kv_heads, score_scale
         )
-        out_ref[block, 0:1] = highest
-        out_ref[block, 1:2] = inverse
-        out_ref[block, 2:3] = delta
+        out_ref[at, 0:1] = highest
+        out_ref[at, 1:2] = inverse
+        out_ref[at, 2:3] = delta
 
 
 def mine_kernel(
-    plan_ref, q_ref, g_ref, stat_ref, arrived_ref, out_ref, grad_ref, sems,
-    *, heads, kv_heads, score_scale, source_at, seen_at
+    plan_ref, q_ref, g_ref, arrived_ref, *refs, heads, kv_heads, score_scale, source_at, seen_at
 ):
-    blocks = stat_ref.shape[0]
+    stat_refs, (out_ref, grad_ref, sems) = refs[:-3], refs[-3:]
+    blocks = grad_ref.shape[0]
+    chunk = blocks // len(stat_refs)
     rows = q_ref.shape[0] // blocks
     _, lane_head = lanes(rows, heads, kv_heads)
     copies = []
@@ -416,13 +427,15 @@
         span = slice(block * rows, (block + 1) * rows)
         q = q_ref[span]
         g = g_ref[span]
+        stat_ref = stat_refs[block // chunk]
+        at = block % chunk
         source = plan_ref[source_at + block]
         scores, dprobs = far_scores(
             arrived_ref, source, q, g, plan_ref[seen_at + block], lane_head, kv_heads, score_scale
         )
-        probs = jnp.exp(scores - stat_ref[block, 0:1]) * stat_ref[block, 1:2]
+        probs = jnp.exp(scores - stat_ref[at, 0:1]) * stat_ref[at, 1:2]
         grad_ref[block, 0], grad_ref[block, 1] = far_gradients(
-            probs, dprobs, stat_ref[block, 2:3], q, g, lane_head, kv_heads, score_scale
+            probs, dprobs, stat_ref[at, 2:3], q, g, lane_head, kv_heads, score_scale
         )
         copies.append(
             pltpu.make_async_copy(grad_ref.at[block], out_ref.at[source], sems.at[block])
@@ -592,27 +605,45 @@
         partial(near_kernel, **sizes), "near", (), (q2, g2, kept, given), stat_shape
     )
     arrived, stats = lax.optimization_barrier((arrived, stats))
-    give_rows = plan[give_at:give_at + mine_blocks]
-    other = lax.ppermute(take_rows(arrived, give_rows), "uly", swap)
+    chunks = 2 if mine_blocks % 2 == 0 else 1
+    chunk = mine_blocks // chunks
+    chunk_shape = jax.ShapeDtypeStruct((chunk, 2, half, width), BF16)
+    giving = call(
+        partial(giving_kernel, give_at=give_at), "give", (plan,), (arrived,),
+        [chunk_shape] * chunks,
+    )
+    others = [lax.ppermute(part, "uly", swap) for part in giving]
     stats = call(
         partial(mid_kernel, source_at=source_at, seen_at=seen_at, **sizes), "mid", (plan,),
         (q2, g2, stats, arrived), stat_shape,
     )
-    far_other, stats = call(
-        partial(far_kernel, seen_at=seen_at, **sizes), "far", (plan,), (q2, g2, stats, other),
-        [part_shape, stat_shape],
-    )
-    from_sib = lax.ppermute(far_other, "uly", swap)
+    grads, final = [], []
+    for at, other in enumerate(others):
+        if grads:
+            other, grads[-1] = lax.optimization_barrier((other, grads[-1]))
+        grad, stat = call(
+            partial(far_kernel, seen_at=seen_at, first=at * chunk, **sizes), "far", (plan,),
+            (q2, g2, stats, other),
+            [chunk_shape, jax.ShapeDtypeStruct((chunk, 8, rows), F32)],
+        )
+        grads.append(grad)
+        final.append(stat)
+    from_sib = [lax.ppermute(part, "uly", swap) for part in grads]
+    if chunks > 1:
+        from_sib[0], final[-1] = lax.optimization_barrier((from_sib[0], final[-1]))
     returning = call(
         partial(mine_kernel, source_at=source_at, seen_at=seen_at, **sizes), "mine", (plan,),
-        (q2, g2, stats, arrived), slot_shape,
+        (q2, g2, arrived, *final), slot_shape,
         [pltpu.VMEM(part_shape.shape, BF16), pltpu.SemaphoreType.DMA((mine_blocks,))],
         out_spec=anywhere,
     )
-    returning = call(
-        partial(returning_kernel, give_at=give_at), "return_sibling", (plan,), (from_sib,), slot_shape,
-        [pltpu.SemaphoreType.DMA((mine_blocks,))], into=returning, out_spec=anywhere,
-    )
+    for at, part in enumerate(from_sib):
+        returning = call(
+            partial(returning_kernel, give_at=give_at + at * chunk), "return_sibling", (plan,),
+            (part,), slot_shape, [pltpu.SemaphoreType.DMA((chunk,))], into=returning,
+            out_spec=anywhere,
+        )
+    other = jnp.concatenate(others)
     returning, k2l = lax.optimization_barrier((returning, k2))
     landed = lax.all_to_all(returning, "grp", split_axis=0, concat_axis=0, tiled=True)
 

time: 69.4 us -> 69.2 us (level)
  Pallas kernels: 18.4 us -> 19.1 us
    ppermute x2 -> x4, starting transfers between devices: 3.17 us -> 4.18 us  [the longest x2 2.09 us: whole_blocks(): from_sib = [lax.ppermute(part, 'uly', swap) for part in grads]]
    all_to_all x1, starting transfers between devices: 4.51 us -> 3.58 us  [whole_blocks(): lax.all_to_all(returning, 'grp', split_axis=0, concat_axis=0, tiled=True)]
    pallas_call x10 -> x13, Pallas kernels: 9.09 us -> 9.81 us  [call(): pl.pallas_call(kernel, in_specs=[smem] * len(scalars) + [vmem] * len(oper...]
    ppermute x2 -> x4, waiting for transfers between devices: 4.25 us -> 3.86 us  [the longest x2 1.98 us: whole_blocks(): others = [lax.ppermute(part, 'uly', swap) for part in giving]]
    unnamed x16 -> x12, local copies, waits for them, and re-layouts: 1.43 us -> 1.65 us
  transfers between devices with their start and end apart: 6 -> 8, of which waited for: 6 -> 7; matrix products, arithmetic and copies ran while one was open for 0% -> 0% of each run, Pallas kernels for 19% -> 22%
where the time goes in v7:
time: 69.2 us; the launch traced here: 68.8 us
  waiting for transfers between devices  28.7 us (41%)
  Pallas kernels  19.1 us (28%)
  starting transfers between devices  18.6 us (27%)
  local copies, waits for them, and re-layouts  1.65 us (2%)
  between operations  0.82 us (1%)
    all_to_all x1, waiting for transfers between devices, whole_blocks(): lax.all_to_all(outgoing, 'grp', split_axis=0, concat_axis=0, tiled=True)  13.7 us
    pallas_call x13, Pallas kernels, call(): pl.pallas_call(kernel, in_specs=[smem] * len(scalars) + [vmem] * len(oper...  9.81 us
    pallas_call x1, Pallas kernels, whole_blocks(): pl.pallas_call(partial(local_kernel, seen_at=seen_at, **sizes), grid_spec...  6.87 us
    all_to_all x1, starting transfers between devices, whole_blocks(): lax.all_to_all(outgoing, 'grp', split_axis=0, concat_axis=0, tiled=True)  6.14 us
    all_to_all x1, waiting for transfers between devices, whole_blocks(): lax.all_to_all(returning, 'grp', split_axis=0, concat_axis=0, tiled=True)  5.88 us
    ppermute x1, waiting for transfers between devices, whole_blocks(): back = lax.ppermute(give, 'uly', swap)  3.65 us
    all_to_all x1, starting transfers between devices, whole_blocks(): lax.all_to_all(returning, 'grp', split_axis=0, concat_axis=0, tiled=True)  3.58 us
    ppermute x1, starting transfers between devices, whole_blocks(): gotten = lax.ppermute(given, 'uly', swap)  3.03 us
  transfers between devices with their start and end apart: 8, of which 7 were waited for; matrix products, arithmetic and copies ran while one was open for 0% of the time, Pallas kernels for 22%

profile of v7, /device:TPU:0, one launch (start us, length us, event | category | flops | bytes accessed | tf_op | source)
XLA Modules:
  0.0 68.8 jit_solution(16227047379887639610)
XLA Ops:
  0.6 1.3 %pack.1 = (bf16[4,2,64,128]{3,2,1,0:T(8,128)(2,1)S(1)}, bf16[4,2,64,128]{3,2,1,0:T(8,128)(2,1)S(1)}) custom-call(bf16[512,128]{1,0:T(8,128)(2,1)} %bitcast.21, bf16[512,128]{1,0:T(8,128)(2,1)} %bitcast.23), custom_call_target="tpu_custom_call" | custom-call | tf_op jit(solution)/shard_map/pack/pallas_call | solution.py:574
  1.9 3.0 %collective-permute-start = (bf16[4,2,64,128]{3,2,1,0:T(8,128)(2,1)S(1)}, bf16[4,2,64,128]{3,2,1,0:T(8,128)(2,1)S(1)}, u32[]{:S(2)}, u32[]{:S(2)}) collective-permute-start(bf16[4,2,64,128]{3,2,1,0:T(8,128)(2,1)S(1)} %get-tuple-element.33.given_ref), channel_id=1, source_target_pairs={{0,1},{1,0},{2,3},{3,2},{4,5},{5,4},{6,7},{7,6},{8,9},{9,8},{10,11... | collective-permute-start | bytes 393224 | tf_op jit(solution)/shard_map/ppermute | solution.py:593
  5.0 1.1 %plan.1.plan_ref = s32[44]{0:T(128)S(4)} custom-call(s32[128]{0:T(128)} %bitcast.29, s32[128]{0:T(128)} %counts_ref.1), custom_call_target="tpu_custom_call" | custom-call | tf_op jit(solution)/shard_map/plan/pallas_call | solution.py:585
  6.1 0.8 %send_own.1.refs_0_ = bf16[16,2,64,128]{3,2,1,0:T(8,128)(2,1)} custom-call(s32[44]{0:T(128)S(4)} %plan.1.plan_ref, bf16[4,2,64,128]{3,2,1,0:T(8,128)(2,1)S(1)} %get-tuple-element.31.blocks_ref.kept_ref), custom_call_target="tpu_custom_call" | custom-call | tf_op jit(solution)/shard_map/send_own/pallas_call | solution.py:560
  6.9 1.6 %collective-permute-done.blocks_ref = bf16[4,2,64,128]{3,2,1,0:T(8,128)(2,1)S(1)} collective-permute-done((bf16[4,2,64,128]{3,2,1,0:T(8,128)(2,1)S(1)}, bf16[4,2,64,128]{3,2,1,0:T(8,128)(2,1)S(1)}, u32[]{:S(2)}, u32[]{:S(2)}) %collective-permute-start) | collective-permute-done | bytes 131104 | tf_op jit(solution)/shard_map/ppermute | solution.py:593
  8.5 0.8 %send_sibling.1 = bf16[16,2,64,128]{3,2,1,0:T(8,128)(2,1)} custom-call(s32[44]{0:T(128)S(4)} %plan.1.plan_ref, bf16[4,2,64,128]{3,2,1,0:T(8,128)(2,1)S(1)} %collective-permute-done.blocks_ref, bf16[16,2,64,128]{3,2,1,0:T(8,128)(2,1)} %send_own.1.refs_0_), custom_call_target="tpu_custom_call", output_to_operand_aliasing={{}: (2, {})} | custom-call | tf_op jit(solution)/shard_map/send_sibling/pallas_call | solution.py:560
  9.2 6.1 %all-to-all-start = ((bf16[16,2,64,128]{3,2,1,0:T(8,128)(2,1)}), bf16[16,2,64,128]{3,2,1,0:T(8,128)(2,1)S(1)}, u32[]{:S(2)}, u32[]{:S(2)}) async-start(bf16[16,2,64,128]{3,2,1,0:T(8,128)(2,1)} %send_sibling.1), calls=%async_computation | async-start | bytes 1048576 | tf_op jit(solution)/shard_map/all_to_all | solution.py:603
  15.4 0.7 %near.1.stat_ref = f32[4,8,1024]{2,1,0:T(8,128)S(1)} custom-call(bf16[4096,128]{1,0:T(8,128)(2,1)S(1)} %bitcast.9, bf16[4096,128]{1,0:T(8,128)(2,1)S(1)} %bitcast.15, bf16[4,2,64,128]{3,2,1,0:T(8,128)(2,1)S(1)} %get-tuple-element.31.blocks_ref.kept_ref, bf16[4,2,64,128]{3,2,1,0:T(8,128)(2,1)S(1)} %get-tuple-element.33.given_ref), custom_call_target="tpu_custom_call" | custom-call | tf_op jit(solution)/shard_map/near/pallas_call | solution.py:560
  16.1 13.7 %all-to-all-done.arrived_ref.mine_ref = bf16[16,2,64,128]{3,2,1,0:T(8,128)(2,1)S(1)} async-done(((bf16[16,2,64,128]{3,2,1,0:T(8,128)(2,1)}), bf16[16,2,64,128]{3,2,1,0:T(8,128)(2,1)S(1)}, u32[]{:S(2)}, u32[]{:S(2)}) %all-to-all-start) | async-done | bytes 524320 | tf_op jit(solution)/shard_map/all_to_all | solution.py:603
  29.9 1.6 %collective-permute-start.2 = (bf16[2,2,64,128]{3,2,1,0:T(8,128)(2,1)S(1)}, bf16[2,2,64,128]{3,2,1,0:T(8,128)(2,1)S(1)}, u32[]{:S(2)}, u32[]{:S(2)}) collective-permute-start(bf16[2,2,64,128]{3,2,1,0:T(8,128)(2,1)S(1)} %get-tuple-element.37), channel_id=1, source_target_pairs={{0,1},{1,0},{2,3},{3,2},{4,5},{5,4},{6,7},{7,6},{8,9},{9,8},{10,11... | collective-permute-start | bytes 196616 | tf_op jit(solution)/shard_map/ppermute | solution.py:615
  31.4 0.5 collective-permute-start.1
  31.9 0.9 %mid.1.stat_ref = f32[4,8,1024]{2,1,0:T(8,128)S(1)} custom-call(s32[44]{0:T(128)S(4)} %plan.1.plan_ref, bf16[4096,128]{1,0:T(8,128)(2,1)S(1)} %bitcast.10, bf16[4096,128]{1,0:T(8,128)(2,1)S(1)} %bitcast.16, f32[4,8,1024]{2,1,0:T(8,128)S(1)} %near.1.stat_ref, bf16[16,2,64,128]{3,2,1,0:T(8,128)(2,1)S(1)} %all-to-all-done.arrived_ref.mine_ref), custom_call_target="tpu_custom_call" | custom-call | tf_op jit(solution)/shard_map/mid/pallas_call | solution.py:560
  32.8 1.8 %collective-permute-done.2.other_ref = bf16[2,2,64,128]{3,2,1,0:T(8,128)(2,1)S(1)} collective-permute-done((bf16[2,2,64,128]{3,2,1,0:T(8,128)(2,1)S(1)}, bf16[2,2,64,128]{3,2,1,0:T(8,128)(2,1)S(1)}, u32[]{:S(2)}, u32[]{:S(2)}) %collective-permute-start.2) | collective-permute-done | bytes 65568 | tf_op jit(solution)/shard_map/ppermute | solution.py:615
  34.6 0.9 %far.2 = (bf16[2,2,64,128]{3,2,1,0:T(8,128)(2,1)S(1)}, f32[2,8,1024]{2,1,0:T(8,128)S(1)}) custom-call(s32[44]{0:T(128)S(4)} %plan.1.plan_ref, bf16[4096,128]{1,0:T(8,128)(2,1)S(1)} %bitcast.11, bf16[4096,128]{1,0:T(8,128)(2,1)S(1)} %bitcast.17, f32[4,8,1024]{2,1,0:T(8,128)S(1)} %mid.1.stat_ref, bf16[2,2,64,128]{3,2,1,0:T(8,128)(2,1)S(1)} %collective-permute-done.2.other_ref), custom_call_target="tpu_custom_call" | custom-call | tf_op jit(solution)/shard_map/far/pallas_call | solution.py:560
  35.5 0.2 collective-permute-done.1.other_ref
  35.7 1.5 %collective-permute-start.4 = (bf16[2,2,64,128]{3,2,1,0:T(8,128)(2,1)S(1)}, bf16[2,2,64,128]{3,2,1,0:T(8,128)(2,1)S(1)}, u32[]{:S(2)}, u32[]{:S(2)}) collective-permute-start(bf16[2,2,64,128]{3,2,1,0:T(8,128)(2,1)S(1)} %get-tuple-element.41), channel_id=1, source_target_pairs={{0,1},{1,0},{2,3},{3,2},{4,5},{5,4},{6,7},{7,6},{8,9},{9,8},{10,11... | collective-permute-start | bytes 196616 | tf_op jit(solution)/shard_map/ppermute | solution.py:631
  37.2 0.9 %far.3 = (bf16[2,2,64,128]{3,2,1,0:T(8,128)(2,1)S(1)}, f32[2,8,1024]{2,1,0:T(8,128)S(1)}) custom-call(s32[44]{0:T(128)S(4)} %plan.1.plan_ref, bf16[4096,128]{1,0:T(8,128)(2,1)S(1)} %bitcast.12, bf16[4096,128]{1,0:T(8,128)(2,1)S(1)} %bitcast.18, f32[4,8,1024]{2,1,0:T(8,128)S(1)} %mid.1.stat_ref, bf16[2,2,64,128]{3,2,1,0:T(8,128)(2,1)S(1)} %collective-permute-done.1.other_ref), custom_call_target="tpu_custom_call" | custom-call | tf_op jit(solution)/shard_map/far/pallas_call | solution.py:560
  38.1 0.6 collective-permute-start.3
  38.7 1.9 %collective-permute-done.4.blocks_ref = bf16[2,2,64,128]{3,2,1,0:T(8,128)(2,1)S(1)} collective-permute-done((bf16[2,2,64,128]{3,2,1,0:T(8,128)(2,1)S(1)}, bf16[2,2,64,128]{3,2,1,0:T(8,128)(2,1)S(1)}, u32[]{:S(2)}, u32[]{:S(2)}) %collective-permute-start.4) | collective-permute-done | bytes 65568 | tf_op jit(solution)/shard_map/ppermute | solution.py:631
  40.6 2.2 %mine.1._ = bf16[16,2,64,128]{3,2,1,0:T(8,128)(2,1)} custom-call(s32[44]{0:T(128)S(4)} %plan.1.plan_ref, bf16[4096,128]{1,0:T(8,128)(2,1)S(1)} %bitcast.13, bf16[4096,128]{1,0:T(8,128)(2,1)S(1)} %bitcast.19, bf16[16,2,64,128]{3,2,1,0:T(8,128)(2,1)S(1)} %all-to-all-done.arrived_ref.mine_ref, f32[2,8,1024]{2,1,0:T(8,128)S(1)} %get-tuple-element.44.refs_0_, ...), custom_call_target="tpu_custom_call" | custom-call | tf_op jit(solution)/shard_map/mine/pallas_call | solution.py:560
  42.9 0.6 return_sibling.2._
  43.5 0.6 return_sibling.3
  44.2 3.6 %all-to-all-start.1 = ((bf16[16,2,64,128]{3,2,1,0:T(8,128)(2,1)}), bf16[16,2,64,128]{3,2,1,0:T(8,128)(2,1)S(1)}, u32[]{:S(2)}, u32[]{:S(2)}) async-start(bf16[16,2,64,128]{3,2,1,0:T(8,128)(2,1)} %return_sibling.3), calls=%async_computation.1 | async-start | bytes 1048576 | tf_op jit(solution)/shard_map/all_to_all | solution.py:648
  47.8 0.9 %copy-done.2 = bf16[128,4,128]{2,1,0:T(4,128)(2,1)S(1)} copy-done((bf16[128,4,128]{2,1,0:T(4,128)(2,1)S(1)}, bf16[128,4,128]{2,1,0:T(4,128)(2,1)}, u32[]{:S(2)}) %copy-start.2) | copy-done | bytes 131096
  48.7 6.9 %local.1 = (bf16[4096,128]{1,0:T(8,128)(2,1)}, bf16[4096,128]{1,0:T(8,128)(2,1)}, f32[512,128]{1,0:T(8,128)S(1)}, f32[512,128]{1,0:T(8,128)S(1)}) custom-call(s32[44]{0:T(128)S(4)} %plan.1.plan_ref, bf16[4096,128]{1,0:T(8,128)(2,1)S(1)} %bitcast.14, bf16[4096,128]{1,0:T(8,128)(2,1)S(1)} %bitcast.20, bf16[512,128]{1,0:T(8,128)(2,1)S(1)} %bitcast.22, ...), custom_call_target="tpu_custom_call" | custom-call | tf_op jit(solution)/shard_map/local/pallas_call | solution.py:661
  55.6 0.7 %copy-done.4 = f32[512,128]{1,0:T(8,128)} copy-done((f32[512,128]{1,0:T(8,128)}, f32[512,128]{1,0:T(8,128)S(1)}, u32[]{:S(2)}) %copy-start.4) | copy-done | bytes 262168
  56.3 5.9 %all-to-all-done.1.landed_ref = bf16[16,2,64,128]{3,2,1,0:T(8,128)(2,1)S(1)} async-done(((bf16[16,2,64,128]{3,2,1,0:T(8,128)(2,1)}), bf16[16,2,64,128]{3,2,1,0:T(8,128)(2,1)S(1)}, u32[]{:S(2)}, u32[]{:S(2)}) %all-to-all-start.1) | async-done | bytes 524320 | tf_op jit(solution)/shard_map/all_to_all | solution.py:648
  62.2 0.2 land_sibling.1
  62.4 1.7 %collective-permute-start.5 = (bf16[4,2,64,128]{3,2,1,0:T(8,128)(2,1)S(1)}, bf16[4,2,64,128]{3,2,1,0:T(8,128)(2,1)S(1)}, u32[]{:S(2)}, u32[]{:S(2)}) collective-permute-start(bf16[4,2,64,128]{3,2,1,0:T(8,128)(2,1)S(1)} %land_sibling.1), channel_id=1, source_target_pairs={{0,1},{1,0},{2,3},{3,2},{4,5},{5,4},{6,7},{7,6},{8,9},{9,8},{10,11... | collective-permute-start | bytes 393224 | tf_op jit(solution)/shard_map/ppermute | solution.py:683
  64.0 0.2 land_own.1.own_ref
  64.2 3.7 %collective-permute-done.5.back_ref = bf16[4,2,64,128]{3,2,1,0:T(8,128)(2,1)S(1)} collective-permute-done((bf16[4,2,64,128]{3,2,1,0:T(8,128)(2,1)S(1)}, bf16[4,2,64,128]{3,2,1,0:T(8,128)(2,1)S(1)}, u32[]{:S(2)}, u32[]{:S(2)}) %collective-permute-start.5) | collective-permute-done | bytes 131104 | tf_op jit(solution)/shard_map/ppermute | solution.py:683
  67.9 1.0 %finish.1 = (bf16[512,128]{1,0:T(8,128)(2,1)}, bf16[512,128]{1,0:T(8,128)(2,1)}) custom-call(f32[512,128]{1,0:T(8,128)S(1)} %get-tuple-element.51.dk_near_ref, f32[512,128]{1,0:T(8,128)S(1)} %copy-done.5, f32[4,2,64,128]{3,2,1,0:T(8,128)S(1)} %land_own.1.own_ref, bf16[4,2,64,128]{3,2,1,0:T(8,128)(2,1)S(1)} %collective-permute-done.5.back_ref), custom_call_target="tpu_custom_call" | custom-call | tf_op jit(solution)/shard_map/finish/pallas_call | solution.py:560
  (13 shorter events, 0.1 us)
Async XLA Ops:
  1.9 6.5 %collective-permute-start = (bf16[4,2,64,128]{3,2,1,0:T(8,128)(2,1)S(1)}, bf16[4,2,64,128]{3,2,1,0:T(8,128)(2,1)S(1)}, u32[]{:S(2)}, u32[]{:S(2)}) collective-permute-start(bf16[4,2,64,128]{3,2,1,0:T(8,128)(2,1)S(1)} %get-tuple-element.33.given_ref), channel_id=1, source_target_pairs={{0,1},{1,0},{2,3},{3,2},{4,5},{5,4},{6,7},{7,6},{8,9},{9,8},{10,11... | collective-permute-start | bytes 393224 | tf_op jit(solution)/shard_map/ppermute | solution.py:593
  6.9 8.5 %copy-start = (bf16[128,32,128]{2,1,0:T(8,128)(2,1)S(1)}, bf16[128,32,128]{2,1,0:T(8,128)(2,1)}, u32[]{:S(2)}) copy-start(bf16[128,32,128]{2,1,0:T(8,128)(2,1)} %param.6) | copy-start | bytes 3145732
  6.9 8.5 %copy-start.1 = (bf16[128,32,128]{2,1,0:T(8,128)(2,1)S(1)}, bf16[128,32,128]{2,1,0:T(8,128)(2,1)}, u32[]{:S(2)}) copy-start(bf16[128,32,128]{2,1,0:T(8,128)(2,1)} %param.9) | copy-start | bytes 3145732
  9.2 20.6 %all-to-all-start = ((bf16[16,2,64,128]{3,2,1,0:T(8,128)(2,1)}), bf16[16,2,64,128]{3,2,1,0:T(8,128)(2,1)S(1)}, u32[]{:S(2)}, u32[]{:S(2)}) async-start(bf16[16,2,64,128]{3,2,1,0:T(8,128)(2,1)} %send_sibling.1), calls=%async_computation | async-start | bytes 1048576 | tf_op jit(solution)/shard_map/all_to_all | solution.py:603
  29.9 4.7 %collective-permute-start.2 = (bf16[2,2,64,128]{3,2,1,0:T(8,128)(2,1)S(1)}, bf16[2,2,64,128]{3,2,1,0:T(8,128)(2,1)S(1)}, u32[]{:S(2)}, u32[]{:S(2)}) collective-permute-start(bf16[2,2,64,128]{3,2,1,0:T(8,128)(2,1)S(1)} %get-tuple-element.37), channel_id=1, source_target_pairs={{0,1},{1,0},{2,3},{3,2},{4,5},{5,4},{6,7},{7,6},{8,9},{9,8},{10,11... | collective-permute-start | bytes 196616 | tf_op jit(solution)/shard_map/ppermute | solution.py:615
  31.4 4.3 %collective-permute-start.1 = (bf16[2,2,64,128]{3,2,1,0:T(8,128)(2,1)S(1)}, bf16[2,2,64,128]{3,2,1,0:T(8,128)(2,1)S(1)}, u32[]{:S(2)}, u32[]{:S(2)}) collective-permute-start(bf16[2,2,64,128]{3,2,1,0:T(8,128)(2,1)S(1)} %get-tuple-element.36), channel_id=1, source_target_pairs={{0,1},{1,0},{2,3},{3,2},{4,5},{5,4},{6,7},{7,6},{8,9},{9,8},{10,11... | collective-permute-start | bytes 196616 | tf_op jit(solution)/shard_map/ppermute | solution.py:615
  35.7 4.9 %collective-permute-start.4 = (bf16[2,2,64,128]{3,2,1,0:T(8,128)(2,1)S(1)}, bf16[2,2,64,128]{3,2,1,0:T(8,128)(2,1)S(1)}, u32[]{:S(2)}, u32[]{:S(2)}) collective-permute-start(bf16[2,2,64,128]{3,2,1,0:T(8,128)(2,1)S(1)} %get-tuple-element.41), channel_id=1, source_target_pairs={{0,1},{1,0},{2,3},{3,2},{4,5},{5,4},{6,7},{7,6},{8,9},{9,8},{10,11... | collective-permute-start | bytes 196616 | tf_op jit(solution)/shard_map/ppermute | solution.py:631
  38.1 5.4 %collective-permute-start.3 = (bf16[2,2,64,128]{3,2,1,0:T(8,128)(2,1)S(1)}, bf16[2,2,64,128]{3,2,1,0:T(8,128)(2,1)S(1)}, u32[]{:S(2)}, u32[]{:S(2)}) collective-permute-start(bf16[2,2,64,128]{3,2,1,0:T(8,128)(2,1)S(1)} %get-tuple-element.40), channel_id=1, source_target_pairs={{0,1},{1,0},{2,3},{3,2},{4,5},{5,4},{6,7},{7,6},{8,9},{9,8},{10,11... | collective-permute-start | bytes 196616 | tf_op jit(solution)/shard_map/ppermute | solution.py:631
  44.2 18.0 %all-to-all-start.1 = ((bf16[16,2,64,128]{3,2,1,0:T(8,128)(2,1)}), bf16[16,2,64,128]{3,2,1,0:T(8,128)(2,1)S(1)}, u32[]{:S(2)}, u32[]{:S(2)}) async-start(bf16[16,2,64,128]{3,2,1,0:T(8,128)(2,1)} %return_sibling.3), calls=%async_computation.1 | async-start | bytes 1048576 | tf_op jit(solution)/shard_map/all_to_all | solution.py:648
  47.8 0.9 %copy-start.2 = (bf16[128,4,128]{2,1,0:T(4,128)(2,1)S(1)}, bf16[128,4,128]{2,1,0:T(4,128)(2,1)}, u32[]{:S(2)}) copy-start(bf16[128,4,128]{2,1,0:T(4,128)(2,1)} %param.7) | copy-start | bytes 393220
  47.8 1.0 %copy-start.3 = (bf16[128,4,128]{2,1,0:T(4,128)(2,1)S(1)}, bf16[128,4,128]{2,1,0:T(4,128)(2,1)}, u32[]{:S(2)}) copy-start(bf16[128,4,128]{2,1,0:T(4,128)(2,1)} %param.8) | copy-start | bytes 393220
  55.6 0.7 %copy-start.4 = (f32[512,128]{1,0:T(8,128)}, f32[512,128]{1,0:T(8,128)S(1)}, u32[]{:S(2)}) copy-start(f32[512,128]{1,0:T(8,128)S(1)} %get-tuple-element.52.dv_near_ref) | copy-start | bytes 786436
  62.4 5.5 %copy-start.5 = (f32[512,128]{1,0:T(8,128)S(1)}, f32[512,128]{1,0:T(8,128)}, u32[]{:S(2)}) copy-start(f32[512,128]{1,0:T(8,128)} %copy-done.4) | copy-start | bytes 786436
  62.4 5.5 %collective-permute-start.5 = (bf16[4,2,64,128]{3,2,1,0:T(8,128)(2,1)S(1)}, bf16[4,2,64,128]{3,2,1,0:T(8,128)(2,1)S(1)}, u32[]{:S(2)}, u32[]{:S(2)}) collective-permute-start(bf16[4,2,64,128]{3,2,1,0:T(8,128)(2,1)S(1)} %land_sibling.1), channel_id=1, source_target_pairs={{0,1},{1,0},{2,3},{3,2},{4,5},{5,4},{6,7},{7,6},{8,9},{9,8},{10,11... | collective-permute-start | bytes 393224 | tf_op jit(solution)/shard_map/ppermute | solution.py:683

commit v8 on v7

--- a/solution.py
+++ b/solution.py
@@ -299,15 +299,15 @@
             block += 1
 
 
-def returning_kernel(plan_ref, blocks_ref, _, out_ref, sems, *, give_at):
-    copies = [
-        pltpu.make_async_copy(
-            blocks_ref.at[block], out_ref.at[plan_ref[give_at + block]], sems.at[block]
-        )
-        for block in range(blocks_ref.shape[0])
-    ]
-    for copy in copies:
-        copy.start()
+def returning_kernel(plan_ref, *refs, give_at):
+    part_refs, (out_ref, sems) = refs[:-3], refs[-2:]
+    copies = []
+    for part_ref in part_refs:
+        for at in range(part_ref.shape[0]):
+            block = len(copies)
+            target = out_ref.at[plan_ref[give_at + block]]
+            copies.append(pltpu.make_async_copy(part_ref.at[at], target, sems.at[block]))
+            copies[-1].start()
     for copy in copies:
         copy.wait()
 
@@ -415,31 +415,26 @@
 
 
 def mine_kernel(
-    plan_ref, q_ref, g_ref, arrived_ref, *refs, heads, kv_heads, score_scale, source_at, seen_at
+    plan_ref, q_ref, g_ref, arrived_ref, stat_ref, *refs,
+    heads, kv_heads, score_scale, source_at, seen_at, rows, first
 ):
-    stat_refs, (out_ref, grad_ref, sems) = refs[:-3], refs[-3:]
-    blocks = grad_ref.shape[0]
-    chunk = blocks // len(stat_refs)
-    rows = q_ref.shape[0] // blocks
+    out_ref, grad_ref, sems = refs[-3:]
     _, lane_head = lanes(rows, heads, kv_heads)
     copies = []
-    for block in range(blocks):
+    for at in range(stat_ref.shape[0]):
+        block = first + at
         span = slice(block * rows, (block + 1) * rows)
         q = q_ref[span]
         g = g_ref[span]
-        stat_ref = stat_refs[block // chunk]
-        at = block % chunk
         source = plan_ref[source_at + block]
         scores, dprobs = far_scores(
             arrived_ref, source, q, g, plan_ref[seen_at + block], lane_head, kv_heads, score_scale
         )
         probs = jnp.exp(scores - stat_ref[at, 0:1]) * stat_ref[at, 1:2]
-        grad_ref[block, 0], grad_ref[block, 1] = far_gradients(
+        grad_ref[at, 0], grad_ref[at, 1] = far_gradients(
             probs, dprobs, stat_ref[at, 2:3], q, g, lane_head, kv_heads, score_scale
         )
-        copies.append(
-            pltpu.make_async_copy(grad_ref.at[block], out_ref.at[source], sems.at[block])
-        )
+        copies.append(pltpu.make_async_copy(grad_ref.at[at], out_ref.at[source], sems.at[at]))
         copies[-1].start()
     for copy in copies:
         copy.wait()
@@ -629,20 +624,23 @@
         grads.append(grad)
         final.append(stat)
     from_sib = [lax.ppermute(part, "uly", swap) for part in grads]
-    if chunks > 1:
-        from_sib[0], final[-1] = lax.optimization_barrier((from_sib[0], final[-1]))
+    returning = None
+    for at in reversed(range(chunks)):
+        if returning is not None:
+            from_sib[at], final[at] = lax.optimization_barrier((from_sib[at], final[at]))
+        returning = call(
+            partial(
+                mine_kernel, source_at=source_at, seen_at=seen_at, rows=rows, first=at * chunk,
+                **sizes,
+            ),
+            "mine", (plan,), (q2, g2, arrived, final[at]), slot_shape,
+            [pltpu.VMEM(chunk_shape.shape, BF16), pltpu.SemaphoreType.DMA((chunk,))],
+            into=returning, out_spec=anywhere,
+        )
     returning = call(
-        partial(mine_kernel, source_at=source_at, seen_at=seen_at, **sizes), "mine", (plan,),
-        (q2, g2, arrived, *final), slot_shape,
-        [pltpu.VMEM(part_shape.shape, BF16), pltpu.SemaphoreType.DMA((mine_blocks,))],
-        out_spec=anywhere,
-    )
-    for at, part in enumerate(from_sib):
-        returning = call(
-            partial(returning_kernel, give_at=give_at + at * chunk), "return_sibling", (plan,),
-            (part,), slot_shape, [pltpu.SemaphoreType.DMA((chunk,))], into=returning,
-            out_spec=anywhere,
-        )
+        partial(returning_kernel, give_at=give_at), "return_sibling", (plan,), from_sib,
+        slot_shape, [pltpu.SemaphoreType.DMA((mine_blocks,))], into=returning, out_spec=anywhere,
+    )
     other = jnp.concatenate(others)
     returning, k2l = lax.optimization_barrier((returning, k2))
     landed = lax.all_to_all(returning, "grp", split_axis=0, concat_axis=0, tiled=True)

time: 69.2 us -> 68.6 us (level)
  waiting for transfers between devices: 28.7 us -> 27.7 us
    ppermute x2, waiting for transfers between devices: 1.88 us -> 0.31 us  [whole_blocks(): from_sib = [lax.ppermute(part, 'uly', swap) for part in grads]]
    all_to_all x1, starting transfers between devices: 3.58 us -> 4.45 us  [whole_blocks(): lax.all_to_all(returning, 'grp', split_axis=0, concat_axis=0, tiled=True)]
    ppermute x1, starting transfers between devices: 1.65 us -> 0.89 us  [whole_blocks(): back = lax.ppermute(give, 'uly', swap)]
    ppermute x1, waiting for transfers between devices: 3.65 us -> 4.41 us  [whole_blocks(): back = lax.ppermute(give, 'uly', swap)]
where the time goes in v8:
time: 68.6 us; the launch traced here: 68.2 us
  waiting for transfers between devices  27.7 us (40%)
  Pallas kernels  19.2 us (28%)
  starting transfers between devices  18.8 us (27%)
  local copies, waits for them, and re-layouts  1.65 us (2%)
  between operations  0.81 us (1%)
    all_to_all x1, waiting for transfers between devices, whole_blocks(): lax.all_to_all(outgoing, 'grp', split_axis=0, concat_axis=0, tiled=True)  13.7 us
    pallas_call x13, Pallas kernels, call(): pl.pallas_call(kernel, in_specs=[smem] * len(scalars) + [vmem] * len(oper...  9.96 us
    pallas_call x1, Pallas kernels, whole_blocks(): pl.pallas_call(partial(local_kernel, seen_at=seen_at, **sizes), grid_spec...  6.87 us
    all_to_all x1, starting transfers between devices, whole_blocks(): lax.all_to_all(outgoing, 'grp', split_axis=0, concat_axis=0, tiled=True)  6.15 us
    all_to_all x1, waiting for transfers between devices, whole_blocks(): lax.all_to_all(returning, 'grp', split_axis=0, concat_axis=0, tiled=True)  5.92 us
    all_to_all x1, starting transfers between devices, whole_blocks(): lax.all_to_all(returning, 'grp', split_axis=0, concat_axis=0, tiled=True)  4.45 us
    ppermute x1, waiting for transfers between devices, whole_blocks(): back = lax.ppermute(give, 'uly', swap)  4.41 us
    ppermute x1, starting transfers between devices, whole_blocks(): gotten = lax.ppermute(given, 'uly', swap)  3.03 us
  transfers between devices with their start and end apart: 8, of which 7 were waited for; matrix products, arithmetic and copies ran while one was open for 0% of the time, Pallas kernels for 22%

profile of v8, /device:TPU:0, one launch (start us, length us, event | category | flops | bytes accessed | tf_op | source)
XLA Modules:
  0.0 68.2 jit_solution(16936785051339116708)
XLA Ops:
  0.6 1.3 %pack.1 = (bf16[4,2,64,128]{3,2,1,0:T(8,128)(2,1)S(1)}, bf16[4,2,64,128]{3,2,1,0:T(8,128)(2,1)S(1)}) custom-call(bf16[512,128]{1,0:T(8,128)(2,1)} %bitcast.23, bf16[512,128]{1,0:T(8,128)(2,1)} %bitcast.25), custom_call_target="tpu_custom_call" | custom-call | tf_op jit(solution)/shard_map/pack/pallas_call | solution.py:569
  1.9 3.0 %collective-permute-start = (bf16[4,2,64,128]{3,2,1,0:T(8,128)(2,1)S(1)}, bf16[4,2,64,128]{3,2,1,0:T(8,128)(2,1)S(1)}, u32[]{:S(2)}, u32[]{:S(2)}) collective-permute-start(bf16[4,2,64,128]{3,2,1,0:T(8,128)(2,1)S(1)} %get-tuple-element.33.given_ref), channel_id=1, source_target_pairs={{0,1},{1,0},{2,3},{3,2},{4,5},{5,4},{6,7},{7,6},{8,9},{9,8},{10,11... | collective-permute-start | bytes 393224 | tf_op jit(solution)/shard_map/ppermute | solution.py:588
  5.0 1.1 %plan.1.plan_ref = s32[44]{0:T(128)S(4)} custom-call(s32[128]{0:T(128)} %bitcast.31, s32[128]{0:T(128)} %counts_ref.1), custom_call_target="tpu_custom_call" | custom-call | tf_op jit(solution)/shard_map/plan/pallas_call | solution.py:580
  6.1 0.8 %send_own.1.refs_0_ = bf16[16,2,64,128]{3,2,1,0:T(8,128)(2,1)} custom-call(s32[44]{0:T(128)S(4)} %plan.1.plan_ref, bf16[4,2,64,128]{3,2,1,0:T(8,128)(2,1)S(1)} %get-tuple-element.31.blocks_ref.kept_ref), custom_call_target="tpu_custom_call" | custom-call | tf_op jit(solution)/shard_map/send_own/pallas_call | solution.py:555
  6.9 1.5 %collective-permute-done.blocks_ref = bf16[4,2,64,128]{3,2,1,0:T(8,128)(2,1)S(1)} collective-permute-done((bf16[4,2,64,128]{3,2,1,0:T(8,128)(2,1)S(1)}, bf16[4,2,64,128]{3,2,1,0:T(8,128)(2,1)S(1)}, u32[]{:S(2)}, u32[]{:S(2)}) %collective-permute-start) | collective-permute-done | bytes 131104 | tf_op jit(solution)/shard_map/ppermute | solution.py:588
  8.5 0.8 %send_sibling.1 = bf16[16,2,64,128]{3,2,1,0:T(8,128)(2,1)} custom-call(s32[44]{0:T(128)S(4)} %plan.1.plan_ref, bf16[4,2,64,128]{3,2,1,0:T(8,128)(2,1)S(1)} %collective-permute-done.blocks_ref, bf16[16,2,64,128]{3,2,1,0:T(8,128)(2,1)} %send_own.1.refs_0_), custom_call_target="tpu_custom_call", output_to_operand_aliasing={{}: (2, {})} | custom-call | tf_op jit(solution)/shard_map/send_sibling/pallas_call | solution.py:555
  9.2 6.2 %all-to-all-start = ((bf16[16,2,64,128]{3,2,1,0:T(8,128)(2,1)}), bf16[16,2,64,128]{3,2,1,0:T(8,128)(2,1)S(1)}, u32[]{:S(2)}, u32[]{:S(2)}) async-start(bf16[16,2,64,128]{3,2,1,0:T(8,128)(2,1)} %send_sibling.1), calls=%async_computation | async-start | bytes 1048576 | tf_op jit(solution)/shard_map/all_to_all | solution.py:598
  15.4 0.7 %near.1.stat_ref = f32[4,8,1024]{2,1,0:T(8,128)S(1)} custom-call(bf16[4096,128]{1,0:T(8,128)(2,1)S(1)} %bitcast.9, bf16[4096,128]{1,0:T(8,128)(2,1)S(1)} %bitcast.16, bf16[4,2,64,128]{3,2,1,0:T(8,128)(2,1)S(1)} %get-tuple-element.31.blocks_ref.kept_ref, bf16[4,2,64,128]{3,2,1,0:T(8,128)(2,1)S(1)} %get-tuple-element.33.given_ref), custom_call_target="tpu_custom_call" | custom-call | tf_op jit(solution)/shard_map/near/pallas_call | solution.py:555
  16.1 13.7 %all-to-all-done.arrived_ref.mine_ref = bf16[16,2,64,128]{3,2,1,0:T(8,128)(2,1)S(1)} async-done(((bf16[16,2,64,128]{3,2,1,0:T(8,128)(2,1)}), bf16[16,2,64,128]{3,2,1,0:T(8,128)(2,1)S(1)}, u32[]{:S(2)}, u32[]{:S(2)}) %all-to-all-start) | async-done | bytes 524320 | tf_op jit(solution)/shard_map/all_to_all | solution.py:598
  29.9 1.0 %collective-permute-start.2 = (bf16[2,2,64,128]{3,2,1,0:T(8,128)(2,1)S(1)}, bf16[2,2,64,128]{3,2,1,0:T(8,128)(2,1)S(1)}, u32[]{:S(2)}, u32[]{:S(2)}) collective-permute-start(bf16[2,2,64,128]{3,2,1,0:T(8,128)(2,1)S(1)} %get-tuple-element.37), channel_id=1, source_target_pairs={{0,1},{1,0},{2,3},{3,2},{4,5},{5,4},{6,7},{7,6},{8,9},{9,8},{10,11... | collective-permute-start | bytes 196616 | tf_op jit(solution)/shard_map/ppermute | solution.py:610
  30.8 1.1 %collective-permute-start.1 = (bf16[2,2,64,128]{3,2,1,0:T(8,128)(2,1)S(1)}, bf16[2,2,64,128]{3,2,1,0:T(8,128)(2,1)S(1)}, u32[]{:S(2)}, u32[]{:S(2)}) collective-permute-start(bf16[2,2,64,128]{3,2,1,0:T(8,128)(2,1)S(1)} %get-tuple-element.35), channel_id=1, source_target_pairs={{0,1},{1,0},{2,3},{3,2},{4,5},{5,4},{6,7},{7,6},{8,9},{9,8},{10,11... | collective-permute-start | bytes 196616 | tf_op jit(solution)/shard_map/ppermute | solution.py:610
  32.0 0.9 %mid.1.stat_ref = f32[4,8,1024]{2,1,0:T(8,128)S(1)} custom-call(s32[44]{0:T(128)S(4)} %plan.1.plan_ref, bf16[4096,128]{1,0:T(8,128)(2,1)S(1)} %bitcast.10, bf16[4096,128]{1,0:T(8,128)(2,1)S(1)} %bitcast.17, f32[4,8,1024]{2,1,0:T(8,128)S(1)} %near.1.stat_ref, bf16[16,2,64,128]{3,2,1,0:T(8,128)(2,1)S(1)} %all-to-all-done.arrived_ref.mine_ref), custom_call_target="tpu_custom_call" | custom-call | tf_op jit(solution)/shard_map/mid/pallas_call | solution.py:555
  32.8 1.8 %collective-permute-done.2.other_ref = bf16[2,2,64,128]{3,2,1,0:T(8,128)(2,1)S(1)} collective-permute-done((bf16[2,2,64,128]{3,2,1,0:T(8,128)(2,1)S(1)}, bf16[2,2,64,128]{3,2,1,0:T(8,128)(2,1)S(1)}, u32[]{:S(2)}, u32[]{:S(2)}) %collective-permute-start.2) | collective-permute-done | bytes 65568 | tf_op jit(solution)/shard_map/ppermute | solution.py:610
  34.6 0.9 %far.2 = (bf16[2,2,64,128]{3,2,1,0:T(8,128)(2,1)S(1)}, f32[2,8,1024]{2,1,0:T(8,128)S(1)}) custom-call(s32[44]{0:T(128)S(4)} %plan.1.plan_ref, bf16[4096,128]{1,0:T(8,128)(2,1)S(1)} %bitcast.11, bf16[4096,128]{1,0:T(8,128)(2,1)S(1)} %bitcast.18, f32[4,8,1024]{2,1,0:T(8,128)S(1)} %mid.1.stat_ref, bf16[2,2,64,128]{3,2,1,0:T(8,128)(2,1)S(1)} %collective-permute-done.2.other_ref), custom_call_target="tpu_custom_call" | custom-call | tf_op jit(solution)/shard_map/far/pallas_call | solution.py:555
  35.6 1.1 %collective-permute-start.3 = (bf16[2,2,64,128]{3,2,1,0:T(8,128)(2,1)S(1)}, bf16[2,2,64,128]{3,2,1,0:T(8,128)(2,1)S(1)}, u32[]{:S(2)}, u32[]{:S(2)}) collective-permute-start(bf16[2,2,64,128]{3,2,1,0:T(8,128)(2,1)S(1)} %get-tuple-element.39), channel_id=1, source_target_pairs={{0,1},{1,0},{2,3},{3,2},{4,5},{5,4},{6,7},{7,6},{8,9},{9,8},{10,11... | collective-permute-start | bytes 196616 | tf_op jit(solution)/shard_map/ppermute | solution.py:626
  36.7 0.9 %far.3 = (bf16[2,2,64,128]{3,2,1,0:T(8,128)(2,1)S(1)}, f32[2,8,1024]{2,1,0:T(8,128)S(1)}) custom-call(s32[44]{0:T(128)S(4)} %plan.1.plan_ref, bf16[4096,128]{1,0:T(8,128)(2,1)S(1)} %bitcast.12, bf16[4096,128]{1,0:T(8,128)(2,1)S(1)} %bitcast.19, f32[4,8,1024]{2,1,0:T(8,128)S(1)} %mid.1.stat_ref, bf16[2,2,64,128]{3,2,1,0:T(8,128)(2,1)S(1)} %collective-permute-done.1.other_ref), custom_call_target="tpu_custom_call" | custom-call | tf_op jit(solution)/shard_map/far/pallas_call | solution.py:555
  37.6 1.0 %collective-permute-start.4 = (bf16[2,2,64,128]{3,2,1,0:T(8,128)(2,1)S(1)}, bf16[2,2,64,128]{3,2,1,0:T(8,128)(2,1)S(1)}, u32[]{:S(2)}, u32[]{:S(2)}) collective-permute-start(bf16[2,2,64,128]{3,2,1,0:T(8,128)(2,1)S(1)} %get-tuple-element.43), channel_id=1, source_target_pairs={{0,1},{1,0},{2,3},{3,2},{4,5},{5,4},{6,7},{7,6},{8,9},{9,8},{10,11... | collective-permute-start | bytes 196616 | tf_op jit(solution)/shard_map/ppermute | solution.py:626
  38.7 1.5 %mine.2.refs_0_ = bf16[16,2,64,128]{3,2,1,0:T(8,128)(2,1)} custom-call(s32[44]{0:T(128)S(4)} %plan.1.plan_ref, bf16[4096,128]{1,0:T(8,128)(2,1)S(1)} %bitcast.13, bf16[4096,128]{1,0:T(8,128)(2,1)S(1)} %bitcast.20, bf16[16,2,64,128]{3,2,1,0:T(8,128)(2,1)S(1)} %all-to-all-done.arrived_ref.mine_ref, f32[2,8,1024]{2,1,0:T(8,128)S(1)} %get-tuple-element.45.stat_ref), custom_call_target="tpu_custom_call" | custom-call | tf_op jit(solution)/shard_map/mine/pallas_call | solution.py:555
  40.2 0.3 collective-permute-done.3.refs_0_
  40.4 1.5 %mine.3.refs_2_ = bf16[16,2,64,128]{3,2,1,0:T(8,128)(2,1)} custom-call(s32[44]{0:T(128)S(4)} %plan.1.plan_ref, bf16[4096,128]{1,0:T(8,128)(2,1)S(1)} %bitcast.14, bf16[4096,128]{1,0:T(8,128)(2,1)S(1)} %bitcast.21, bf16[16,2,64,128]{3,2,1,0:T(8,128)(2,1)S(1)} %all-to-all-done.arrived_ref.mine_ref, ...), custom_call_target="tpu_custom_call", output_to_operand_aliasing={{}: (5, {})} | custom-call | tf_op jit(solution)/shard_map/mine/pallas_call | solution.py:555
  42.0 0.7 %return_sibling.1 = bf16[16,2,64,128]{3,2,1,0:T(8,128)(2,1)} custom-call(s32[44]{0:T(128)S(4)} %plan.1.plan_ref, bf16[2,2,64,128]{3,2,1,0:T(8,128)(2,1)S(1)} %collective-permute-done.3.refs_0_, bf16[2,2,64,128]{3,2,1,0:T(8,128)(2,1)S(1)} %collective-permute-done.4.refs_1_, bf16[16,2,64,128]{3,2,1,0:T(8,128)(2,1)} %mine.3.refs_2_), custom_call_target="tpu_custom_call", output_to_operand_aliasing={{}: (3, {})} | custom-call | tf_op jit(solution)/shard_map/return_sibling/pallas_call | solution.py:555
  42.6 4.5 %all-to-all-start.1 = ((bf16[16,2,64,128]{3,2,1,0:T(8,128)(2,1)}), bf16[16,2,64,128]{3,2,1,0:T(8,128)(2,1)S(1)}, u32[]{:S(2)}, u32[]{:S(2)}) async-start(bf16[16,2,64,128]{3,2,1,0:T(8,128)(2,1)} %return_sibling.1), calls=%async_computation.1 | async-start | bytes 1048576 | tf_op jit(solution)/shard_map/all_to_all | solution.py:646
  47.2 0.9 %copy-done.2 = bf16[128,4,128]{2,1,0:T(4,128)(2,1)S(1)} copy-done((bf16[128,4,128]{2,1,0:T(4,128)(2,1)S(1)}, bf16[128,4,128]{2,1,0:T(4,128)(2,1)}, u32[]{:S(2)}) %copy-start.2) | copy-done | bytes 131096
  48.0 0.1 copy-done.3
  48.1 6.9 %local.1 = (bf16[4096,128]{1,0:T(8,128)(2,1)}, bf16[4096,128]{1,0:T(8,128)(2,1)}, f32[512,128]{1,0:T(8,128)S(1)}, f32[512,128]{1,0:T(8,128)S(1)}) custom-call(s32[44]{0:T(128)S(4)} %plan.1.plan_ref, bf16[4096,128]{1,0:T(8,128)(2,1)S(1)} %bitcast.15, bf16[4096,128]{1,0:T(8,128)(2,1)S(1)} %bitcast.22, bf16[512,128]{1,0:T(8,128)(2,1)S(1)} %bitcast.24, ...), custom_call_target="tpu_custom_call" | custom-call | tf_op jit(solution)/shard_map/local/pallas_call | solution.py:659
  55.0 0.7 %copy-done.4 = f32[512,128]{1,0:T(8,128)} copy-done((f32[512,128]{1,0:T(8,128)}, f32[512,128]{1,0:T(8,128)S(1)}, u32[]{:S(2)}) %copy-start.4) | copy-done | bytes 262168
  55.7 5.9 %all-to-all-done.1.landed_ref = bf16[16,2,64,128]{3,2,1,0:T(8,128)(2,1)S(1)} async-done(((bf16[16,2,64,128]{3,2,1,0:T(8,128)(2,1)}), bf16[16,2,64,128]{3,2,1,0:T(8,128)(2,1)S(1)}, u32[]{:S(2)}, u32[]{:S(2)}) %all-to-all-start.1) | async-done | bytes 524320 | tf_op jit(solution)/shard_map/all_to_all | solution.py:646
  61.6 0.2 land_sibling.1
  61.8 0.9 %collective-permute-start.5 = (bf16[4,2,64,128]{3,2,1,0:T(8,128)(2,1)S(1)}, bf16[4,2,64,128]{3,2,1,0:T(8,128)(2,1)S(1)}, u32[]{:S(2)}, u32[]{:S(2)}) collective-permute-start(bf16[4,2,64,128]{3,2,1,0:T(8,128)(2,1)S(1)} %land_sibling.1), channel_id=1, source_target_pairs={{0,1},{1,0},{2,3},{3,2},{4,5},{5,4},{6,7},{7,6},{8,9},{9,8},{10,11... | collective-permute-start | bytes 393224 | tf_op jit(solution)/shard_map/ppermute | solution.py:681
  62.7 0.2 land_own.1.own_ref
  62.8 4.4 %collective-permute-done.5.back_ref = bf16[4,2,64,128]{3,2,1,0:T(8,128)(2,1)S(1)} collective-permute-done((bf16[4,2,64,128]{3,2,1,0:T(8,128)(2,1)S(1)}, bf16[4,2,64,128]{3,2,1,0:T(8,128)(2,1)S(1)}, u32[]{:S(2)}, u32[]{:S(2)}) %collective-permute-start.5) | collective-permute-done | bytes 131104 | tf_op jit(solution)/shard_map/ppermute | solution.py:681
  67.2 1.0 %finish.1 = (bf16[512,128]{1,0:T(8,128)(2,1)}, bf16[512,128]{1,0:T(8,128)(2,1)}) custom-call(f32[512,128]{1,0:T(8,128)S(1)} %get-tuple-element.51.dk_near_ref, f32[512,128]{1,0:T(8,128)S(1)} %copy-done.5, f32[4,2,64,128]{3,2,1,0:T(8,128)S(1)} %land_own.1.own_ref, bf16[4,2,64,128]{3,2,1,0:T(8,128)(2,1)S(1)} %collective-permute-done.5.back_ref), custom_call_target="tpu_custom_call" | custom-call | tf_op jit(solution)/shard_map/finish/pallas_call | solution.py:555
  (13 shorter events, 0.1 us)
Async XLA Ops:
  1.9 6.5 %collective-permute-start = (bf16[4,2,64,128]{3,2,1,0:T(8,128)(2,1)S(1)}, bf16[4,2,64,128]{3,2,1,0:T(8,128)(2,1)S(1)}, u32[]{:S(2)}, u32[]{:S(2)}) collective-permute-start(bf16[4,2,64,128]{3,2,1,0:T(8,128)(2,1)S(1)} %get-tuple-element.33.given_ref), channel_id=1, source_target_pairs={{0,1},{1,0},{2,3},{3,2},{4,5},{5,4},{6,7},{7,6},{8,9},{9,8},{10,11... | collective-permute-start | bytes 393224 | tf_op jit(solution)/shard_map/ppermute | solution.py:588
  6.9 8.5 %copy-start = (bf16[128,32,128]{2,1,0:T(8,128)(2,1)S(1)}, bf16[128,32,128]{2,1,0:T(8,128)(2,1)}, u32[]{:S(2)}) copy-start(bf16[128,32,128]{2,1,0:T(8,128)(2,1)} %param.6) | copy-start | bytes 3145732
  6.9 8.5 %copy-start.1 = (bf16[128,32,128]{2,1,0:T(8,128)(2,1)S(1)}, bf16[128,32,128]{2,1,0:T(8,128)(2,1)}, u32[]{:S(2)}) copy-start(bf16[128,32,128]{2,1,0:T(8,128)(2,1)} %param.9) | copy-start | bytes 3145732
  9.2 20.6 %all-to-all-start = ((bf16[16,2,64,128]{3,2,1,0:T(8,128)(2,1)}), bf16[16,2,64,128]{3,2,1,0:T(8,128)(2,1)S(1)}, u32[]{:S(2)}, u32[]{:S(2)}) async-start(bf16[16,2,64,128]{3,2,1,0:T(8,128)(2,1)} %send_sibling.1), calls=%async_computation | async-start | bytes 1048576 | tf_op jit(solution)/shard_map/all_to_all | solution.py:598
  29.9 4.8 %collective-permute-start.2 = (bf16[2,2,64,128]{3,2,1,0:T(8,128)(2,1)S(1)}, bf16[2,2,64,128]{3,2,1,0:T(8,128)(2,1)S(1)}, u32[]{:S(2)}, u32[]{:S(2)}) collective-permute-start(bf16[2,2,64,128]{3,2,1,0:T(8,128)(2,1)S(1)} %get-tuple-element.37), channel_id=1, source_target_pairs={{0,1},{1,0},{2,3},{3,2},{4,5},{5,4},{6,7},{7,6},{8,9},{9,8},{10,11... | collective-permute-start | bytes 196616 | tf_op jit(solution)/shard_map/ppermute | solution.py:610
  30.8 4.8 %collective-permute-start.1 = (bf16[2,2,64,128]{3,2,1,0:T(8,128)(2,1)S(1)}, bf16[2,2,64,128]{3,2,1,0:T(8,128)(2,1)S(1)}, u32[]{:S(2)}, u32[]{:S(2)}) collective-permute-start(bf16[2,2,64,128]{3,2,1,0:T(8,128)(2,1)S(1)} %get-tuple-element.35), channel_id=1, source_target_pairs={{0,1},{1,0},{2,3},{3,2},{4,5},{5,4},{6,7},{7,6},{8,9},{9,8},{10,11... | collective-permute-start | bytes 196616 | tf_op jit(solution)/shard_map/ppermute | solution.py:610
  35.6 4.8 %collective-permute-start.3 = (bf16[2,2,64,128]{3,2,1,0:T(8,128)(2,1)S(1)}, bf16[2,2,64,128]{3,2,1,0:T(8,128)(2,1)S(1)}, u32[]{:S(2)}, u32[]{:S(2)}) collective-permute-start(bf16[2,2,64,128]{3,2,1,0:T(8,128)(2,1)S(1)} %get-tuple-element.39), channel_id=1, source_target_pairs={{0,1},{1,0},{2,3},{3,2},{4,5},{5,4},{6,7},{7,6},{8,9},{9,8},{10,11... | collective-permute-start | bytes 196616 | tf_op jit(solution)/shard_map/ppermute | solution.py:626
  37.6 4.3 %collective-permute-start.4 = (bf16[2,2,64,128]{3,2,1,0:T(8,128)(2,1)S(1)}, bf16[2,2,64,128]{3,2,1,0:T(8,128)(2,1)S(1)}, u32[]{:S(2)}, u32[]{:S(2)}) collective-permute-start(bf16[2,2,64,128]{3,2,1,0:T(8,128)(2,1)S(1)} %get-tuple-element.43), channel_id=1, source_target_pairs={{0,1},{1,0},{2,3},{3,2},{4,5},{5,4},{6,7},{7,6},{8,9},{9,8},{10,11... | collective-permute-start | bytes 196616 | tf_op jit(solution)/shard_map/ppermute | solution.py:626
  42.6 18.9 %all-to-all-start.1 = ((bf16[16,2,64,128]{3,2,1,0:T(8,128)(2,1)}), bf16[16,2,64,128]{3,2,1,0:T(8,128)(2,1)S(1)}, u32[]{:S(2)}, u32[]{:S(2)}) async-start(bf16[16,2,64,128]{3,2,1,0:T(8,128)(2,1)} %return_sibling.1), calls=%async_computation.1 | async-start | bytes 1048576 | tf_op jit(solution)/shard_map/all_to_all | solution.py:646
  47.1 0.9 %copy-start.2 = (bf16[128,4,128]{2,1,0:T(4,128)(2,1)S(1)}, bf16[128,4,128]{2,1,0:T(4,128)(2,1)}, u32[]{:S(2)}) copy-start(bf16[128,4,128]{2,1,0:T(4,128)(2,1)} %param.7) | copy-start | bytes 393220
  47.1 1.0 %copy-start.3 = (bf16[128,4,128]{2,1,0:T(4,128)(2,1)S(1)}, bf16[128,4,128]{2,1,0:T(4,128)(2,1)}, u32[]{:S(2)}) copy-start(bf16[128,4,128]{2,1,0:T(4,128)(2,1)} %param.8) | copy-start | bytes 393220
  55.0 0.7 %copy-start.4 = (f32[512,128]{1,0:T(8,128)}, f32[512,128]{1,0:T(8,128)S(1)}, u32[]{:S(2)}) copy-start(f32[512,128]{1,0:T(8,128)S(1)} %get-tuple-element.52.dv_near_ref) | copy-start | bytes 786436
  61.8 5.5 %copy-start.5 = (f32[512,128]{1,0:T(8,128)S(1)}, f32[512,128]{1,0:T(8,128)}, u32[]{:S(2)}) copy-start(f32[512,128]{1,0:T(8,128)} %copy-done.4) | copy-start | bytes 786436
  61.8 5.5 %collective-permute-start.5 = (bf16[4,2,64,128]{3,2,1,0:T(8,128)(2,1)S(1)}, bf16[4,2,64,128]{3,2,1,0:T(8,128)(2,1)S(1)}, u32[]{:S(2)}, u32[]{:S(2)}) collective-permute-start(bf16[4,2,64,128]{3,2,1,0:T(8,128)(2,1)S(1)} %land_sibling.1), channel_id=1, source_target_pairs={{0,1},{1,0},{2,3},{3,2},{4,5},{5,4},{6,7},{7,6},{8,9},{9,8},{10,11... | collective-permute-start | bytes 393224 | tf_op jit(solution)/shard_map/ppermute | solution.py:681

commit v9 on v8

--- a/solution.py
+++ b/solution.py
@@ -299,13 +299,13 @@
             block += 1
 
 
-def returning_kernel(plan_ref, *refs, give_at):
-    part_refs, (out_ref, sems) = refs[:-3], refs[-2:]
+def returning_kernel(plan_ref, *refs, source_at):
+    part_refs, (out_ref, sems) = refs[:-2], refs[-2:]
     copies = []
     for part_ref in part_refs:
         for at in range(part_ref.shape[0]):
             block = len(copies)
-            target = out_ref.at[plan_ref[give_at + block]]
+            target = out_ref.at[plan_ref[source_at + block]]
             copies.append(pltpu.make_async_copy(part_ref.at[at], target, sems.at[block]))
             copies[-1].start()
     for copy in copies:
@@ -415,29 +415,23 @@
 
 
 def mine_kernel(
-    plan_ref, q_ref, g_ref, arrived_ref, stat_ref, *refs,
-    heads, kv_heads, score_scale, source_at, seen_at, rows, first
+    plan_ref, q_ref, g_ref, arrived_ref, stat_ref, grad_ref,
+    *, heads, kv_heads, score_scale, source_at, seen_at, rows, first
 ):
-    out_ref, grad_ref, sems = refs[-3:]
     _, lane_head = lanes(rows, heads, kv_heads)
-    copies = []
     for at in range(stat_ref.shape[0]):
         block = first + at
         span = slice(block * rows, (block + 1) * rows)
         q = q_ref[span]
         g = g_ref[span]
-        source = plan_ref[source_at + block]
         scores, dprobs = far_scores(
-            arrived_ref, source, q, g, plan_ref[seen_at + block], lane_head, kv_heads, score_scale
+            arrived_ref, plan_ref[source_at + block], q, g, plan_ref[seen_at + block],
+            lane_head, kv_heads, score_scale,
         )
         probs = jnp.exp(scores - stat_ref[at, 0:1]) * stat_ref[at, 1:2]
         grad_ref[at, 0], grad_ref[at, 1] = far_gradients(
             probs, dprobs, stat_ref[at, 2:3], q, g, lane_head, kv_heads, score_scale
         )
-        copies.append(pltpu.make_async_copy(grad_ref.at[at], out_ref.at[source], sems.at[at]))
-        copies[-1].start()
-    for copy in copies:
-        copy.wait()
 
 
 def local_kernel(
@@ -607,15 +601,17 @@
         partial(giving_kernel, give_at=give_at), "give", (plan,), (arrived,),
         [chunk_shape] * chunks,
     )
-    others = [lax.ppermute(part, "uly", swap) for part in giving]
     stats = call(
         partial(mid_kernel, source_at=source_at, seen_at=seen_at, **sizes), "mid", (plan,),
         (q2, g2, stats, arrived), stat_shape,
     )
+    others = []
+    for part in giving:
+        if others:
+            part, stats = lax.optimization_barrier((part, stats))
+        others.append(lax.ppermute(part, "uly", swap))
     grads, final = [], []
     for at, other in enumerate(others):
-        if grads:
-            other, grads[-1] = lax.optimization_barrier((other, grads[-1]))
         grad, stat = call(
             partial(far_kernel, seen_at=seen_at, first=at * chunk, **sizes), "far", (plan,),
             (q2, g2, stats, other),
@@ -624,22 +620,20 @@
         grads.append(grad)
         final.append(stat)
     from_sib = [lax.ppermute(part, "uly", swap) for part in grads]
-    returning = None
+    mine = [None] * chunks
     for at in reversed(range(chunks)):
-        if returning is not None:
+        if at + 1 < chunks:
             from_sib[at], final[at] = lax.optimization_barrier((from_sib[at], final[at]))
-        returning = call(
+        mine[at] = call(
             partial(
                 mine_kernel, source_at=source_at, seen_at=seen_at, rows=rows, first=at * chunk,
                 **sizes,
             ),
-            "mine", (plan,), (q2, g2, arrived, final[at]), slot_shape,
-            [pltpu.VMEM(chunk_shape.shape, BF16), pltpu.SemaphoreType.DMA((chunk,))],
-            into=returning, out_spec=anywhere,
+            "mine", (plan,), (q2, g2, arrived, final[at]), chunk_shape,
         )
     returning = call(
-        partial(returning_kernel, give_at=give_at), "return_sibling", (plan,), from_sib,
-        slot_shape, [pltpu.SemaphoreType.DMA((mine_blocks,))], into=returning, out_spec=anywhere,
+        partial(returning_kernel, source_at=source_at), "return", (plan,), mine + from_sib,
+        slot_shape, [pltpu.SemaphoreType.DMA((per_group,))], out_spec=anywhere,
     )
     other = jnp.concatenate(others)
     returning, k2l = lax.optimization_barrier((returning, k2))

time: 68.6 us -> 68.7 us (level)
  waiting for transfers between devices: 27.7 us -> 30.1 us
  starting transfers between devices: 18.8 us -> 17.7 us
  Pallas kernels: 19.2 us -> 18.1 us
    ppermute x2, waiting for transfers between devices: 0.31 us -> 2.51 us  [whole_blocks(): from_sib = [lax.ppermute(part, 'uly', swap) for part in grads]]
    pallas_call x13, Pallas kernels: 9.96 us -> 8.84 us  [call(): pl.pallas_call(kernel, in_specs=[smem] * len(scalars) + [vmem] * len(oper...]
  transfers between devices with their start and end apart: 8 -> 8, of which waited for: 7 -> 7; matrix products, arithmetic and copies ran while one was open for 0% -> 0% of each run, Pallas kernels for 22% -> 21%
where the time goes in v9:
time: 68.7 us; the launch traced here: 68.3 us
  waiting for transfers between devices  30.1 us (44%)
  Pallas kernels  18.1 us (26%)
  starting transfers between devices  17.7 us (26%)
  local copies, waits for them, and re-layouts  1.65 us (2%)
  between operations  0.81 us (1%)
    all_to_all x1, waiting for transfers between devices, whole_blocks(): lax.all_to_all(outgoing, 'grp', split_axis=0, concat_axis=0, tiled=True)  13.7 us
    pallas_call x13, Pallas kernels, call(): pl.pallas_call(kernel, in_specs=[smem] * len(scalars) + [vmem] * len(oper...  8.84 us
    pallas_call x1, Pallas kernels, whole_blocks(): pl.pallas_call(partial(local_kernel, seen_at=seen_at, **sizes), grid_spec...  6.87 us
    all_to_all x1, starting transfers between devices, whole_blocks(): lax.all_to_all(outgoing, 'grp', split_axis=0, concat_axis=0, tiled=True)  6.14 us
    all_to_all x1, waiting for transfers between devices, whole_blocks(): lax.all_to_all(returning, 'grp', split_axis=0, concat_axis=0, tiled=True)  5.92 us
    ppermute x1, waiting for transfers between devices, whole_blocks(): back = lax.ppermute(give, 'uly', swap)  5.04 us
    all_to_all x1, starting transfers between devices, whole_blocks(): lax.all_to_all(returning, 'grp', split_axis=0, concat_axis=0, tiled=True)  3.97 us
    ppermute x1, starting transfers between devices, whole_blocks(): gotten = lax.ppermute(given, 'uly', swap)  3.03 us
  transfers between devices with their start and end apart: 8, of which 7 were waited for; matrix products, arithmetic and copies ran while one was open for 0% of the time, Pallas kernels for 21%

profile of v9, /device:TPU:0, one launch (start us, length us, event | category | flops | bytes accessed | tf_op | source)
XLA Modules:
  0.0 68.3 jit_solution(14830911392566151277)
XLA Ops:
  0.6 1.3 %pack.1 = (bf16[4,2,64,128]{3,2,1,0:T(8,128)(2,1)S(1)}, bf16[4,2,64,128]{3,2,1,0:T(8,128)(2,1)S(1)}) custom-call(bf16[512,128]{1,0:T(8,128)(2,1)} %bitcast.23, bf16[512,128]{1,0:T(8,128)(2,1)} %bitcast.25), custom_call_target="tpu_custom_call" | custom-call | tf_op jit(solution)/shard_map/pack/pallas_call | solution.py:563
  1.9 3.0 %collective-permute-start = (bf16[4,2,64,128]{3,2,1,0:T(8,128)(2,1)S(1)}, bf16[4,2,64,128]{3,2,1,0:T(8,128)(2,1)S(1)}, u32[]{:S(2)}, u32[]{:S(2)}) collective-permute-start(bf16[4,2,64,128]{3,2,1,0:T(8,128)(2,1)S(1)} %get-tuple-element.33.given_ref), channel_id=1, source_target_pairs={{0,1},{1,0},{2,3},{3,2},{4,5},{5,4},{6,7},{7,6},{8,9},{9,8},{10,11... | collective-permute-start | bytes 393224 | tf_op jit(solution)/shard_map/ppermute | solution.py:582
  5.0 1.1 %plan.1.plan_ref = s32[44]{0:T(128)S(4)} custom-call(s32[128]{0:T(128)} %bitcast.31, s32[128]{0:T(128)} %counts_ref.1), custom_call_target="tpu_custom_call" | custom-call | tf_op jit(solution)/shard_map/plan/pallas_call | solution.py:574
  6.1 0.8 %send_own.1.refs_0_ = bf16[16,2,64,128]{3,2,1,0:T(8,128)(2,1)} custom-call(s32[44]{0:T(128)S(4)} %plan.1.plan_ref, bf16[4,2,64,128]{3,2,1,0:T(8,128)(2,1)S(1)} %get-tuple-element.31.blocks_ref.kept_ref), custom_call_target="tpu_custom_call" | custom-call | tf_op jit(solution)/shard_map/send_own/pallas_call | solution.py:549
  6.9 1.5 %collective-permute-done.blocks_ref = bf16[4,2,64,128]{3,2,1,0:T(8,128)(2,1)S(1)} collective-permute-done((bf16[4,2,64,128]{3,2,1,0:T(8,128)(2,1)S(1)}, bf16[4,2,64,128]{3,2,1,0:T(8,128)(2,1)S(1)}, u32[]{:S(2)}, u32[]{:S(2)}) %collective-permute-start) | collective-permute-done | bytes 131104 | tf_op jit(solution)/shard_map/ppermute | solution.py:582
  8.5 0.8 %send_sibling.1 = bf16[16,2,64,128]{3,2,1,0:T(8,128)(2,1)} custom-call(s32[44]{0:T(128)S(4)} %plan.1.plan_ref, bf16[4,2,64,128]{3,2,1,0:T(8,128)(2,1)S(1)} %collective-permute-done.blocks_ref, bf16[16,2,64,128]{3,2,1,0:T(8,128)(2,1)} %send_own.1.refs_0_), custom_call_target="tpu_custom_call", output_to_operand_aliasing={{}: (2, {})} | custom-call | tf_op jit(solution)/shard_map/send_sibling/pallas_call | solution.py:549
  9.2 6.1 %all-to-all-start = ((bf16[16,2,64,128]{3,2,1,0:T(8,128)(2,1)}), bf16[16,2,64,128]{3,2,1,0:T(8,128)(2,1)S(1)}, u32[]{:S(2)}, u32[]{:S(2)}) async-start(bf16[16,2,64,128]{3,2,1,0:T(8,128)(2,1)} %send_sibling.1), calls=%async_computation | async-start | bytes 1048576 | tf_op jit(solution)/shard_map/all_to_all | solution.py:592
  15.4 0.7 %near.1.stat_ref = f32[4,8,1024]{2,1,0:T(8,128)S(1)} custom-call(bf16[4096,128]{1,0:T(8,128)(2,1)S(1)} %bitcast.9, bf16[4096,128]{1,0:T(8,128)(2,1)S(1)} %bitcast.16, bf16[4,2,64,128]{3,2,1,0:T(8,128)(2,1)S(1)} %get-tuple-element.31.blocks_ref.kept_ref, bf16[4,2,64,128]{3,2,1,0:T(8,128)(2,1)S(1)} %get-tuple-element.33.given_ref), custom_call_target="tpu_custom_call" | custom-call | tf_op jit(solution)/shard_map/near/pallas_call | solution.py:549
  16.1 13.7 %all-to-all-done.arrived_ref.mine_ref = bf16[16,2,64,128]{3,2,1,0:T(8,128)(2,1)S(1)} async-done(((bf16[16,2,64,128]{3,2,1,0:T(8,128)(2,1)}), bf16[16,2,64,128]{3,2,1,0:T(8,128)(2,1)S(1)}, u32[]{:S(2)}, u32[]{:S(2)}) %all-to-all-start) | async-done | bytes 524320 | tf_op jit(solution)/shard_map/all_to_all | solution.py:592
  29.9 1.6 %collective-permute-start.1 = (bf16[2,2,64,128]{3,2,1,0:T(8,128)(2,1)S(1)}, bf16[2,2,64,128]{3,2,1,0:T(8,128)(2,1)S(1)}, u32[]{:S(2)}, u32[]{:S(2)}) collective-permute-start(bf16[2,2,64,128]{3,2,1,0:T(8,128)(2,1)S(1)} %get-tuple-element.38), channel_id=1, source_target_pairs={{0,1},{1,0},{2,3},{3,2},{4,5},{5,4},{6,7},{7,6},{8,9},{9,8},{10,11... | collective-permute-start | bytes 196616 | tf_op jit(solution)/shard_map/ppermute | solution.py:612
  31.4 0.9 %mid.1.stat_ref = f32[4,8,1024]{2,1,0:T(8,128)S(1)} custom-call(s32[44]{0:T(128)S(4)} %plan.1.plan_ref, bf16[4096,128]{1,0:T(8,128)(2,1)S(1)} %bitcast.10, bf16[4096,128]{1,0:T(8,128)(2,1)S(1)} %bitcast.17, f32[4,8,1024]{2,1,0:T(8,128)S(1)} %near.1.stat_ref, bf16[16,2,64,128]{3,2,1,0:T(8,128)(2,1)S(1)} %all-to-all-done.arrived_ref.mine_ref), custom_call_target="tpu_custom_call" | custom-call | tf_op jit(solution)/shard_map/mid/pallas_call | solution.py:549
  32.3 0.6 collective-permute-start.3
  32.9 1.3 %collective-permute-done.1.other_ref = bf16[2,2,64,128]{3,2,1,0:T(8,128)(2,1)S(1)} collective-permute-done((bf16[2,2,64,128]{3,2,1,0:T(8,128)(2,1)S(1)}, bf16[2,2,64,128]{3,2,1,0:T(8,128)(2,1)S(1)}, u32[]{:S(2)}, u32[]{:S(2)}) %collective-permute-start.1) | collective-permute-done | bytes 65568 | tf_op jit(solution)/shard_map/ppermute | solution.py:612
  34.2 0.9 %far.2 = (bf16[2,2,64,128]{3,2,1,0:T(8,128)(2,1)S(1)}, f32[2,8,1024]{2,1,0:T(8,128)S(1)}) custom-call(s32[44]{0:T(128)S(4)} %plan.1.plan_ref, bf16[4096,128]{1,0:T(8,128)(2,1)S(1)} %bitcast.11, bf16[4096,128]{1,0:T(8,128)(2,1)S(1)} %bitcast.18, f32[4,8,1024]{2,1,0:T(8,128)S(1)} %mid.1.stat_ref, bf16[2,2,64,128]{3,2,1,0:T(8,128)(2,1)S(1)} %collective-permute-done.1.other_ref), custom_call_target="tpu_custom_call" | custom-call | tf_op jit(solution)/shard_map/far/pallas_call | solution.py:549
  35.1 2.1 %collective-permute-start.2 = (bf16[2,2,64,128]{3,2,1,0:T(8,128)(2,1)S(1)}, bf16[2,2,64,128]{3,2,1,0:T(8,128)(2,1)S(1)}, u32[]{:S(2)}, u32[]{:S(2)}) collective-permute-start(bf16[2,2,64,128]{3,2,1,0:T(8,128)(2,1)S(1)} %get-tuple-element.39), channel_id=1, source_target_pairs={{0,1},{1,0},{2,3},{3,2},{4,5},{5,4},{6,7},{7,6},{8,9},{9,8},{10,11... | collective-permute-start | bytes 196616 | tf_op jit(solution)/shard_map/ppermute | solution.py:622
  37.2 0.9 %far.3 = (bf16[2,2,64,128]{3,2,1,0:T(8,128)(2,1)S(1)}, f32[2,8,1024]{2,1,0:T(8,128)S(1)}) custom-call(s32[44]{0:T(128)S(4)} %plan.1.plan_ref, bf16[4096,128]{1,0:T(8,128)(2,1)S(1)} %bitcast.12, bf16[4096,128]{1,0:T(8,128)(2,1)S(1)} %bitcast.19, f32[4,8,1024]{2,1,0:T(8,128)S(1)} %mid.1.stat_ref, bf16[2,2,64,128]{3,2,1,0:T(8,128)(2,1)S(1)} %collective-permute-done.3.other_ref), custom_call_target="tpu_custom_call" | custom-call | tf_op jit(solution)/shard_map/far/pallas_call | solution.py:549
  38.1 0.1 collective-permute-start.4
  38.2 0.9 %mine.3.refs_1_ = bf16[2,2,64,128]{3,2,1,0:T(8,128)(2,1)S(1)} custom-call(s32[44]{0:T(128)S(4)} %plan.1.plan_ref, bf16[4096,128]{1,0:T(8,128)(2,1)S(1)} %bitcast.13, bf16[4096,128]{1,0:T(8,128)(2,1)S(1)} %bitcast.20, bf16[16,2,64,128]{3,2,1,0:T(8,128)(2,1)S(1)} %all-to-all-done.arrived_ref.mine_ref, f32[2,8,1024]{2,1,0:T(8,128)S(1)} %get-tuple-element.43.stat_ref), custom_call_target="tpu_custom_call" | custom-call | tf_op jit(solution)/shard_map/mine/pallas_call | solution.py:549
  39.1 0.9 %collective-permute-done.2.refs_2_ = bf16[2,2,64,128]{3,2,1,0:T(8,128)(2,1)S(1)} collective-permute-done((bf16[2,2,64,128]{3,2,1,0:T(8,128)(2,1)S(1)}, bf16[2,2,64,128]{3,2,1,0:T(8,128)(2,1)S(1)}, u32[]{:S(2)}, u32[]{:S(2)}) %collective-permute-start.2) | collective-permute-done | bytes 65568 | tf_op jit(solution)/shard_map/ppermute | solution.py:622
  40.0 0.9 %mine.2.refs_0_ = bf16[2,2,64,128]{3,2,1,0:T(8,128)(2,1)S(1)} custom-call(s32[44]{0:T(128)S(4)} %plan.1.plan_ref, bf16[4096,128]{1,0:T(8,128)(2,1)S(1)} %bitcast.14, bf16[4096,128]{1,0:T(8,128)(2,1)S(1)} %bitcast.21, bf16[16,2,64,128]{3,2,1,0:T(8,128)(2,1)S(1)} %all-to-all-done.arrived_ref.mine_ref, f32[2,8,1024]{2,1,0:T(8,128)S(1)} %get-tuple-element.41.stat_ref), custom_call_target="tpu_custom_call" | custom-call | tf_op jit(solution)/shard_map/mine/pallas_call | solution.py:549
  40.9 1.6 %collective-permute-done.4.refs_3_ = bf16[2,2,64,128]{3,2,1,0:T(8,128)(2,1)S(1)} collective-permute-done((bf16[2,2,64,128]{3,2,1,0:T(8,128)(2,1)S(1)}, bf16[2,2,64,128]{3,2,1,0:T(8,128)(2,1)S(1)}, u32[]{:S(2)}, u32[]{:S(2)}) %collective-permute-start.4) | collective-permute-done | bytes 65568 | tf_op jit(solution)/shard_map/ppermute | solution.py:622
  42.5 0.8 %return.1 = bf16[16,2,64,128]{3,2,1,0:T(8,128)(2,1)} custom-call(s32[44]{0:T(128)S(4)} %plan.1.plan_ref, bf16[2,2,64,128]{3,2,1,0:T(8,128)(2,1)S(1)} %mine.2.refs_0_, bf16[2,2,64,128]{3,2,1,0:T(8,128)(2,1)S(1)} %mine.3.refs_1_, bf16[2,2,64,128]{3,2,1,0:T(8,128)(2,1)S(1)} %collective-permute-done.2.refs_2_, ...), custom_call_target="tpu_custom_call" | custom-call | tf_op jit(solution)/shard_map/return/pallas_call | solution.py:549
  43.2 4.0 %all-to-all-start.1 = ((bf16[16,2,64,128]{3,2,1,0:T(8,128)(2,1)}), bf16[16,2,64,128]{3,2,1,0:T(8,128)(2,1)S(1)}, u32[]{:S(2)}, u32[]{:S(2)}) async-start(bf16[16,2,64,128]{3,2,1,0:T(8,128)(2,1)} %return.1), calls=%async_computation.1 | async-start | bytes 1048576 | tf_op jit(solution)/shard_map/all_to_all | solution.py:640
  47.3 0.9 %copy-done.2 = bf16[128,4,128]{2,1,0:T(4,128)(2,1)S(1)} copy-done((bf16[128,4,128]{2,1,0:T(4,128)(2,1)S(1)}, bf16[128,4,128]{2,1,0:T(4,128)(2,1)}, u32[]{:S(2)}) %copy-start.2) | copy-done | bytes 131096
  48.2 6.9 %local.1 = (bf16[4096,128]{1,0:T(8,128)(2,1)}, bf16[4096,128]{1,0:T(8,128)(2,1)}, f32[512,128]{1,0:T(8,128)S(1)}, f32[512,128]{1,0:T(8,128)S(1)}) custom-call(s32[44]{0:T(128)S(4)} %plan.1.plan_ref, bf16[4096,128]{1,0:T(8,128)(2,1)S(1)} %bitcast.15, bf16[4096,128]{1,0:T(8,128)(2,1)S(1)} %bitcast.22, bf16[512,128]{1,0:T(8,128)(2,1)S(1)} %bitcast.24, ...), custom_call_target="tpu_custom_call" | custom-call | tf_op jit(solution)/shard_map/local/pallas_call | solution.py:653
  55.1 0.7 %copy-done.4 = f32[512,128]{1,0:T(8,128)} copy-done((f32[512,128]{1,0:T(8,128)}, f32[512,128]{1,0:T(8,128)S(1)}, u32[]{:S(2)}) %copy-start.4) | copy-done | bytes 262168
  55.8 5.9 %all-to-all-done.1.landed_ref = bf16[16,2,64,128]{3,2,1,0:T(8,128)(2,1)S(1)} async-done(((bf16[16,2,64,128]{3,2,1,0:T(8,128)(2,1)}), bf16[16,2,64,128]{3,2,1,0:T(8,128)(2,1)S(1)}, u32[]{:S(2)}, u32[]{:S(2)}) %all-to-all-start.1) | async-done | bytes 524320 | tf_op jit(solution)/shard_map/all_to_all | solution.py:640
  61.7 0.2 land_sibling.1
  61.9 0.3 collective-permute-start.5
  62.1 0.2 land_own.1.own_ref
  62.3 5.0 %collective-permute-done.5.back_ref = bf16[4,2,64,128]{3,2,1,0:T(8,128)(2,1)S(1)} collective-permute-done((bf16[4,2,64,128]{3,2,1,0:T(8,128)(2,1)S(1)}, bf16[4,2,64,128]{3,2,1,0:T(8,128)(2,1)S(1)}, u32[]{:S(2)}, u32[]{:S(2)}) %collective-permute-start.5) | collective-permute-done | bytes 131104 | tf_op jit(solution)/shard_map/ppermute | solution.py:675
  67.4 1.0 %finish.1 = (bf16[512,128]{1,0:T(8,128)(2,1)}, bf16[512,128]{1,0:T(8,128)(2,1)}) custom-call(f32[512,128]{1,0:T(8,128)S(1)} %get-tuple-element.51.dk_near_ref, f32[512,128]{1,0:T(8,128)S(1)} %copy-done.5, f32[4,2,64,128]{3,2,1,0:T(8,128)S(1)} %land_own.1.own_ref, bf16[4,2,64,128]{3,2,1,0:T(8,128)(2,1)S(1)} %collective-permute-done.5.back_ref), custom_call_target="tpu_custom_call" | custom-call | tf_op jit(solution)/shard_map/finish/pallas_call | solution.py:549
  (13 shorter events, 0.1 us)
Async XLA Ops:
  1.9 6.5 %collective-permute-start = (bf16[4,2,64,128]{3,2,1,0:T(8,128)(2,1)S(1)}, bf16[4,2,64,128]{3,2,1,0:T(8,128)(2,1)S(1)}, u32[]{:S(2)}, u32[]{:S(2)}) collective-permute-start(bf16[4,2,64,128]{3,2,1,0:T(8,128)(2,1)S(1)} %get-tuple-element.33.given_ref), channel_id=1, source_target_pairs={{0,1},{1,0},{2,3},{3,2},{4,5},{5,4},{6,7},{7,6},{8,9},{9,8},{10,11... | collective-permute-start | bytes 393224 | tf_op jit(solution)/shard_map/ppermute | solution.py:582
  6.9 8.5 %copy-start = (bf16[128,32,128]{2,1,0:T(8,128)(2,1)S(1)}, bf16[128,32,128]{2,1,0:T(8,128)(2,1)}, u32[]{:S(2)}) copy-start(bf16[128,32,128]{2,1,0:T(8,128)(2,1)} %param.6) | copy-start | bytes 3145732
  6.9 8.5 %copy-start.1 = (bf16[128,32,128]{2,1,0:T(8,128)(2,1)S(1)}, bf16[128,32,128]{2,1,0:T(8,128)(2,1)}, u32[]{:S(2)}) copy-start(bf16[128,32,128]{2,1,0:T(8,128)(2,1)} %param.9) | copy-start | bytes 3145732
  9.2 20.6 %all-to-all-start = ((bf16[16,2,64,128]{3,2,1,0:T(8,128)(2,1)}), bf16[16,2,64,128]{3,2,1,0:T(8,128)(2,1)S(1)}, u32[]{:S(2)}, u32[]{:S(2)}) async-start(bf16[16,2,64,128]{3,2,1,0:T(8,128)(2,1)} %send_sibling.1), calls=%async_computation | async-start | bytes 1048576 | tf_op jit(solution)/shard_map/all_to_all | solution.py:592
  29.9 4.3 %collective-permute-start.1 = (bf16[2,2,64,128]{3,2,1,0:T(8,128)(2,1)S(1)}, bf16[2,2,64,128]{3,2,1,0:T(8,128)(2,1)S(1)}, u32[]{:S(2)}, u32[]{:S(2)}) collective-permute-start(bf16[2,2,64,128]{3,2,1,0:T(8,128)(2,1)S(1)} %get-tuple-element.38), channel_id=1, source_target_pairs={{0,1},{1,0},{2,3},{3,2},{4,5},{5,4},{6,7},{7,6},{8,9},{9,8},{10,11... | collective-permute-start | bytes 196616 | tf_op jit(solution)/shard_map/ppermute | solution.py:612
  32.3 4.9 %collective-permute-start.3 = (bf16[2,2,64,128]{3,2,1,0:T(8,128)(2,1)S(1)}, bf16[2,2,64,128]{3,2,1,0:T(8,128)(2,1)S(1)}, u32[]{:S(2)}, u32[]{:S(2)}) collective-permute-start(bf16[2,2,64,128]{3,2,1,0:T(8,128)(2,1)S(1)} %get-tuple-element.42), channel_id=1, source_target_pairs={{0,1},{1,0},{2,3},{3,2},{4,5},{5,4},{6,7},{7,6},{8,9},{9,8},{10,11... | collective-permute-start | bytes 196616 | tf_op jit(solution)/shard_map/ppermute | solution.py:612
  35.1 4.9 %collective-permute-start.2 = (bf16[2,2,64,128]{3,2,1,0:T(8,128)(2,1)S(1)}, bf16[2,2,64,128]{3,2,1,0:T(8,128)(2,1)S(1)}, u32[]{:S(2)}, u32[]{:S(2)}) collective-permute-start(bf16[2,2,64,128]{3,2,1,0:T(8,128)(2,1)S(1)} %get-tuple-element.39), channel_id=1, source_target_pairs={{0,1},{1,0},{2,3},{3,2},{4,5},{5,4},{6,7},{7,6},{8,9},{9,8},{10,11... | collective-permute-start | bytes 196616 | tf_op jit(solution)/shard_map/ppermute | solution.py:622
  38.1 4.3 %collective-permute-start.4 = (bf16[2,2,64,128]{3,2,1,0:T(8,128)(2,1)S(1)}, bf16[2,2,64,128]{3,2,1,0:T(8,128)(2,1)S(1)}, u32[]{:S(2)}, u32[]{:S(2)}) collective-permute-start(bf16[2,2,64,128]{3,2,1,0:T(8,128)(2,1)S(1)} %get-tuple-element.45), channel_id=1, source_target_pairs={{0,1},{1,0},{2,3},{3,2},{4,5},{5,4},{6,7},{7,6},{8,9},{9,8},{10,11... | collective-permute-start | bytes 196616 | tf_op jit(solution)/shard_map/ppermute | solution.py:622
  43.2 18.4 %all-to-all-start.1 = ((bf16[16,2,64,128]{3,2,1,0:T(8,128)(2,1)}), bf16[16,2,64,128]{3,2,1,0:T(8,128)(2,1)S(1)}, u32[]{:S(2)}, u32[]{:S(2)}) async-start(bf16[16,2,64,128]{3,2,1,0:T(8,128)(2,1)} %return.1), calls=%async_computation.1 | async-start | bytes 1048576 | tf_op jit(solution)/shard_map/all_to_all | solution.py:640
  47.2 0.9 %copy-start.2 = (bf16[128,4,128]{2,1,0:T(4,128)(2,1)S(1)}, bf16[128,4,128]{2,1,0:T(4,128)(2,1)}, u32[]{:S(2)}) copy-start(bf16[128,4,128]{2,1,0:T(4,128)(2,1)} %param.7) | copy-start | bytes 393220
  47.2 1.0 %copy-start.3 = (bf16[128,4,128]{2,1,0:T(4,128)(2,1)S(1)}, bf16[128,4,128]{2,1,0:T(4,128)(2,1)}, u32[]{:S(2)}) copy-start(bf16[128,4,128]{2,1,0:T(4,128)(2,1)} %param.8) | copy-start | bytes 393220
  55.1 0.7 %copy-start.4 = (f32[512,128]{1,0:T(8,128)}, f32[512,128]{1,0:T(8,128)S(1)}, u32[]{:S(2)}) copy-start(f32[512,128]{1,0:T(8,128)S(1)} %get-tuple-element.52.dv_near_ref) | copy-start | bytes 786436
  61.9 5.5 %copy-start.5 = (f32[512,128]{1,0:T(8,128)S(1)}, f32[512,128]{1,0:T(8,128)}, u32[]{:S(2)}) copy-start(f32[512,128]{1,0:T(8,128)} %copy-done.4) | copy-start | bytes 786436
  61.9 5.5 %collective-permute-start.5 = (bf16[4,2,64,128]{3,2,1,0:T(8,128)(2,1)S(1)}, bf16[4,2,64,128]{3,2,1,0:T(8,128)(2,1)S(1)}, u32[]{:S(2)}, u32[]{:S(2)}) collective-permute-start(bf16[4,2,64,128]{3,2,1,0:T(8,128)(2,1)S(1)} %land_sibling.1), channel_id=1, source_target_pairs={{0,1},{1,0},{2,3},{3,2},{4,5},{5,4},{6,7},{7,6},{8,9},{9,8},{10,11... | collective-permute-start | bytes 393224 | tf_op jit(solution)/shard_map/ppermute | solution.py:675

commit v10 on v9

--- a/solution.py
+++ b/solution.py
@@ -277,18 +277,18 @@
             given_ref[block, which] = jnp.where(first, ordered[half:], ordered[:half])
 
 
-def outgoing_kernel(plan_ref, blocks_ref, *refs, first):
-    out_ref, sems = refs[-2:]
-    copies = []
+def send_own_kernel(plan_ref, blocks_ref, out_ref):
+    for group in range(out_ref.shape[0]):
+        out_ref[group] = blocks_ref[jnp.maximum(plan_ref[group], 0)]
+
+
+def send_sibling_kernel(plan_ref, blocks_ref, _, out_ref, *, first):
     for group in range(out_ref.shape[0]):
         place = plan_ref[first + group]
-        source = blocks_ref.at[jnp.maximum(place, 0)]
-        copy = pltpu.make_async_copy(source, out_ref.at[group], sems.at[group])
-        copies.append((place >= 0, copy))
-    for wanted, copy in copies:
-        pl.when(wanted)(copy.start)
-    for wanted, copy in copies:
-        pl.when(wanted)(copy.wait)
+
+        @pl.when(place >= 0)
+        def _():
+            out_ref[group] = blocks_ref[place]
 
 
 def giving_kernel(plan_ref, arrived_ref, *out_refs, give_at):
@@ -315,36 +315,33 @@
 def near_kernel(
     q_ref, g_ref, kept_ref, given_ref, stat_ref, *, heads, kv_heads, score_scale
 ):
-    blocks = stat_ref.shape[0]
-    rows = q_ref.shape[0] // blocks
+    rows = q_ref.shape[0]
     place = kept_ref.shape[2] // kv_heads
     token, lane_head = lanes(rows, heads, kv_heads)
     key = lax.broadcasted_iota(jnp.int32, (2 * place, rows), 0)
     mine = lax.axis_index("uly")
     part = jnp.where(key < place, mine, 1 - mine)
     causal = key % place + part * place <= token
-    for block in range(blocks):
-        span = slice(block * rows, (block + 1) * rows)
-        pieces = []
-        for which, ref in enumerate((q_ref, g_ref)):
-            both = jnp.concatenate([kept_ref[block, which], given_ref[block, which]], axis=0)
-            full = dot_last(both, ref[span])
-            half = full.shape[0] // 2
-            pieces.append(
-                jnp.concatenate(
-                    [
-                        own_head(full[:half], lane_head, kv_heads),
-                        own_head(full[half:], lane_head, kv_heads),
-                    ],
-                    axis=0,
-                )
+    pieces = []
+    for which, ref in enumerate((q_ref, g_ref)):
+        both = jnp.concatenate([kept_ref[0, which], given_ref[0, which]], axis=0)
+        full = dot_last(both, ref[...])
+        half = full.shape[0] // 2
+        pieces.append(
+            jnp.concatenate(
+                [
+                    own_head(full[:half], lane_head, kv_heads),
+                    own_head(full[half:], lane_head, kv_heads),
+                ],
+                axis=0,
             )
-        scores = jnp.where(causal, pieces[0] * score_scale, HIDDEN)
-        highest = jnp.max(scores, axis=0, keepdims=True)
-        raised = jnp.exp(scores - highest)
-        stat_ref[block, 0:1] = highest
-        stat_ref[block, 1:2] = jnp.sum(raised, axis=0, keepdims=True)
-        stat_ref[block, 2:3] = jnp.sum(raised * pieces[1], axis=0, keepdims=True)
+        )
+    scores = jnp.where(causal, pieces[0] * score_scale, HIDDEN)
+    highest = jnp.max(scores, axis=0, keepdims=True)
+    raised = jnp.exp(scores - highest)
+    stat_ref[0, 0:1] = highest
+    stat_ref[0, 1:2] = jnp.sum(raised, axis=0, keepdims=True)
+    stat_ref[0, 2:3] = jnp.sum(raised * pieces[1], axis=0, keepdims=True)
 
 
 def far_scores(part_ref, at, q, g, seen, lane_head, kv_heads, score_scale):
@@ -532,13 +529,12 @@
     v2 = values.reshape(tokens * kv_heads, width)
 
     part_shape = jax.ShapeDtypeStruct((mine_blocks, 2, half, width), BF16)
-    slot_shape = pltpu.HBM((grp_count, 2, half, width), BF16)
+    slots = (grp_count, 2, half, width)
     stat_shape = jax.ShapeDtypeStruct((mine_blocks, 8, rows), F32)
     row_shape = jax.ShapeDtypeStruct(q2.shape, BF16)
     near_shape = jax.ShapeDtypeStruct(k2.shape, F32)
     small_shape = jax.ShapeDtypeStruct(k2.shape, BF16)
     sum_scratch = [pltpu.VMEM((mine_blocks, 2, half, width), F32)]
-    slot_sems = [pltpu.SemaphoreType.DMA((grp_count,))]
     limit = pltpu.CompilerParams(vmem_limit_bytes=24 * 1024 * 1024)
     vmem = pl.BlockSpec(memory_space=pltpu.VMEM)
     smem = pl.BlockSpec(memory_space=pltpu.SMEM)
@@ -548,7 +544,7 @@
         extra = () if into is None else (into,)
         return pl.pallas_call(
             kernel,
-            in_specs=[smem] * len(scalars) + [vmem] * len(operands) + [anywhere] * len(extra),
+            in_specs=[smem] * len(scalars) + [vmem] * (len(operands) + len(extra)),
             out_specs=jax.tree.map(lambda _: out_spec, out_shape),
             out_shape=out_shape,
             scratch_shapes=scratch,
@@ -556,6 +552,12 @@
             compiler_params=limit,
             name=name,
         )(*scalars, *operands, *extra)
+
+    def step_rows(i, *_):
+        return (i, 0)
+
+    def step_part(i, *_):
+        return (i, 0, 0, 0)
 
     def in_hbm(array):
         return pltpu.with_memory_space_constraint(array, pltpu.HBM)
@@ -580,20 +582,27 @@
         name="plan",
     )(in_hbm(block_lists.reshape(-1)), in_hbm(list_counts))
     gotten = lax.ppermute(given, "uly", swap)
+    row_spec = pl.BlockSpec((rows, width), step_rows)
+    part_spec = pl.BlockSpec((1, 2, half, width), step_part)
+    stats = pl.pallas_call(
+        partial(near_kernel, **sizes),
+        grid=(mine_blocks,),
+        in_specs=[row_spec, row_spec, part_spec, part_spec],
+        out_specs=pl.BlockSpec((1, 8, rows), lambda i: (i, 0, 0)),
+        out_shape=stat_shape,
+        compiler_params=limit,
+        name="near",
+    )(in_hbm(q2), in_hbm(g2), kept, given)
     outgoing = call(
-        partial(outgoing_kernel, first=0), "send_own", (plan,), (kept,),
-        slot_shape, slot_sems, out_spec=anywhere,
-    )
+        send_own_kernel, "send_own", (plan,), (kept,),
+        jax.ShapeDtypeStruct(slots, BF16),
+    )
+    gotten, stats = lax.optimization_barrier((gotten, stats))
     outgoing = call(
-        partial(outgoing_kernel, first=sib_at), "send_sibling", (plan,), (gotten,),
-        slot_shape, slot_sems, into=outgoing, out_spec=anywhere,
-    )
-    outgoing, given = lax.optimization_barrier((outgoing, given))
+        partial(send_sibling_kernel, first=sib_at), "send_sibling", (plan,), (gotten,),
+        jax.ShapeDtypeStruct(slots, BF16), into=outgoing,
+    )
     arrived = lax.all_to_all(outgoing, "grp", split_axis=0, concat_axis=0, tiled=True)
-    stats = call(
-        partial(near_kernel, **sizes), "near", (), (q2, g2, kept, given), stat_shape
-    )
-    arrived, stats = lax.optimization_barrier((arrived, stats))
     chunks = 2 if mine_blocks % 2 == 0 else 1
     chunk = mine_blocks // chunks
     chunk_shape = jax.ShapeDtypeStruct((chunk, 2, half, width), BF16)
@@ -633,22 +642,15 @@
         )
     returning = call(
         partial(returning_kernel, source_at=source_at), "return", (plan,), mine + from_sib,
-        slot_shape, [pltpu.SemaphoreType.DMA((per_group,))], out_spec=anywhere,
+        pltpu.HBM(slots, BF16), [pltpu.SemaphoreType.DMA((per_group,))], out_spec=anywhere,
     )
     other = jnp.concatenate(others)
     returning, k2l = lax.optimization_barrier((returning, k2))
     landed = lax.all_to_all(returning, "grp", split_axis=0, concat_axis=0, tiled=True)
 
-    def step_rows(i, *_):
-        return (i, 0)
-
-    def step_part(i, *_):
-        return (i, 0, 0, 0)
-
     def from_source(i, plan_ref):
         return (plan_ref[source_at + i], 0, 0, 0)
 
-    row_spec = pl.BlockSpec((rows, width), step_rows)
     col_spec = pl.BlockSpec((cols, width), step_rows)
     attended, dq, dk_near, dv_near = pl.pallas_call(
         partial(local_kernel, seen_at=seen_at, **sizes),
@@ -658,7 +660,7 @@
             in_specs=[
                 row_spec, row_spec, col_spec, col_spec,
                 pl.BlockSpec((1, 2, half, width), from_source),
-                pl.BlockSpec((1, 2, half, width), step_part),
+                part_spec,
             ],
             out_specs=[row_spec, row_spec, col_spec, col_spec],
             scratch_shapes=[pltpu.VMEM((rows, 2 * cols), F32)],

time: 68.7 us -> 67.6 us (0.984)
  blocking collectives: 0 us -> 20.3 us
  waiting for transfers between devices: 30.1 us -> 12.5 us
  starting transfers between devices: 17.7 us -> 12.9 us
  Pallas kernels: 18.1 us -> 19 us
    all_to_all x0 -> x1, blocking collectives: none -> 20.3 us  [whole_blocks(): lax.all_to_all(outgoing, 'grp', split_axis=0, concat_axis=0, tiled=True)]
    all_to_all x1 -> x0, waiting for transfers between devices: 13.7 us -> none  [whole_blocks(): lax.all_to_all(outgoing, 'grp', split_axis=0, concat_axis=0, tiled=True)]
    all_to_all x1 -> x0, starting transfers between devices: 6.14 us -> none  [whole_blocks(): lax.all_to_all(outgoing, 'grp', split_axis=0, concat_axis=0, tiled=True)]
    ppermute x1, waiting for transfers between devices: 1.55 us -> 0.01 us  [whole_blocks(): gotten = lax.ppermute(given, 'uly', swap)]
    ppermute x2, waiting for transfers between devices: 2.51 us -> 1.14 us  [whole_blocks(): from_sib = [lax.ppermute(part, 'uly', swap) for part in grads]]
    ppermute x1, starting transfers between devices: 0.25 us -> 1.43 us  [whole_blocks(): back = lax.ppermute(give, 'uly', swap)]
    ppermute x1, waiting for transfers between devices: 5.04 us -> 3.88 us  [whole_blocks(): back = lax.ppermute(give, 'uly', swap)]
    pallas_call x13, Pallas kernels: 8.84 us -> 9.77 us  [the longest x12 6.69 us: call(): pl.pallas_call(kernel, in_specs=[smem] * len(scalars) + [vmem] * (len(ope...]
  transfers between devices with their start and end apart: 8 -> 7, of which waited for: 7 -> 5; matrix products, arithmetic and copies ran while one was open for 0% -> 0% of each run, Pallas kernels for 21% -> 23%
where the time goes in v10:
time: 67.6 us; the launch traced here: 67.2 us
  blocking collectives  20.3 us (30%)
  Pallas kernels  19 us (28%)
  starting transfers between devices  12.9 us (19%)
  waiting for transfers between devices  12.5 us (18%)
  local copies, waits for them, and re-layouts  1.64 us (2%)
  between operations  0.8 us (1%)
    all_to_all x1, blocking collectives, whole_blocks(): lax.all_to_all(outgoing, 'grp', split_axis=0, concat_axis=0, tiled=True)  20.3 us
    pallas_call x1, Pallas kernels, whole_blocks(): pl.pallas_call(partial(local_kernel, seen_at=seen_at, **sizes), grid_spec...  6.87 us
    pallas_call x12, Pallas kernels, call(): pl.pallas_call(kernel, in_specs=[smem] * len(scalars) + [vmem] * (len(ope...  6.69 us
    all_to_all x1, waiting for transfers between devices, whole_blocks(): lax.all_to_all(returning, 'grp', split_axis=0, concat_axis=0, tiled=True)  5.93 us
    all_to_all x1, starting transfers between devices, whole_blocks(): lax.all_to_all(returning, 'grp', split_axis=0, concat_axis=0, tiled=True)  4.13 us
    ppermute x1, waiting for transfers between devices, whole_blocks(): back = lax.ppermute(give, 'uly', swap)  3.88 us
    pallas_call x1, Pallas kernels, whole_blocks(): pl.pallas_call(partial(near_kernel, **sizes), grid=(mine_blocks,), in_spe...  3.08 us
    ppermute x1, starting transfers between devices, whole_blocks(): gotten = lax.ppermute(given, 'uly', swap)  3.03 us
  transfers between devices with their start and end apart: 7, of which 5 were waited for; matrix products, arithmetic and copies ran while one was open for 0% of the time, Pallas kernels for 23%

profile of v10, /device:TPU:0, one launch (start us, length us, event | category | flops | bytes accessed | tf_op | source)
XLA Modules:
  0.0 67.2 jit_solution(1478472957443582932)
XLA Ops:
  0.6 1.3 %pack.1 = (bf16[4,2,64,128]{3,2,1,0:T(8,128)(2,1)S(1)}, bf16[4,2,64,128]{3,2,1,0:T(8,128)(2,1)S(1)}) custom-call(bf16[512,128]{1,0:T(8,128)(2,1)} %bitcast.23, bf16[512,128]{1,0:T(8,128)(2,1)} %bitcast.25), custom_call_target="tpu_custom_call" | custom-call | tf_op jit(solution)/shard_map/pack/pallas_call | solution.py:565
  1.9 3.0 %collective-permute-start = (bf16[4,2,64,128]{3,2,1,0:T(8,128)(2,1)S(1)}, bf16[4,2,64,128]{3,2,1,0:T(8,128)(2,1)S(1)}, u32[]{:S(2)}, u32[]{:S(2)}) collective-permute-start(bf16[4,2,64,128]{3,2,1,0:T(8,128)(2,1)S(1)} %get-tuple-element.28.given_ref), channel_id=1, source_target_pairs={{0,1},{1,0},{2,3},{3,2},{4,5},{5,4},{6,7},{7,6},{8,9},{9,8},{10,11... | collective-permute-start | bytes 393224 | tf_op jit(solution)/shard_map/ppermute | solution.py:584
  5.0 1.1 %plan.1.plan_ref = s32[44]{0:T(128)S(4)} custom-call(s32[128]{0:T(128)} %bitcast.31, s32[128]{0:T(128)} %counts_ref.1), custom_call_target="tpu_custom_call" | custom-call | tf_op jit(solution)/shard_map/plan/pallas_call | solution.py:576
  6.1 3.1 %near.1.stat_ref = f32[4,8,1024]{2,1,0:T(8,128)S(1)} custom-call(bf16[4096,128]{1,0:T(8,128)(2,1)} %bitcast.9, bf16[4096,128]{1,0:T(8,128)(2,1)} %bitcast.16, bf16[4,2,64,128]{3,2,1,0:T(8,128)(2,1)S(1)} %get-tuple-element.29.kept_ref.blocks_ref, bf16[4,2,64,128]{3,2,1,0:T(8,128)(2,1)S(1)} %get-tuple-element.28.given_ref), custom_call_target="tpu_custom_call" | custom-call | tf_op jit(solution)/shard_map/near/pallas_call | solution.py:587
  9.2 0.0 copy-start.1
  9.2 0.1 send_sibling.1
  9.4 20.3 %all_to_all.10.arrived_ref.mine_ref = bf16[16,2,64,128]{3,2,1,0:T(8,128)(2,1)S(1)} all-to-all(bf16[16,2,64,128]{3,2,1,0:T(8,128)(2,1)S(1)} %send_sibling.1), channel_id=1, replica_groups=mesh['grp'=16,'uly'=2] {'grp'}, dimensions={0} | all-to-all | bytes 1048576 | tf_op jit(solution)/shard_map/all_to_all | solution.py:605
  29.7 0.9 %collective-permute-start.1 = (bf16[2,2,64,128]{3,2,1,0:T(8,128)(2,1)S(1)}, bf16[2,2,64,128]{3,2,1,0:T(8,128)(2,1)S(1)}, u32[]{:S(2)}, u32[]{:S(2)}) collective-permute-start(bf16[2,2,64,128]{3,2,1,0:T(8,128)(2,1)S(1)} %get-tuple-element.34), channel_id=1, source_target_pairs={{0,1},{1,0},{2,3},{3,2},{4,5},{5,4},{6,7},{7,6},{8,9},{9,8},{10,11... | collective-permute-start | bytes 196616 | tf_op jit(solution)/shard_map/ppermute | solution.py:621
  30.6 0.9 %mid.1.stat_ref = f32[4,8,1024]{2,1,0:T(8,128)S(1)} custom-call(s32[44]{0:T(128)S(4)} %plan.1.plan_ref, bf16[4096,128]{1,0:T(8,128)(2,1)S(1)} %bitcast.10, bf16[4096,128]{1,0:T(8,128)(2,1)S(1)} %bitcast.17, f32[4,8,1024]{2,1,0:T(8,128)S(1)} %near.1.stat_ref, bf16[16,2,64,128]{3,2,1,0:T(8,128)(2,1)S(1)} %all_to_all.10.arrived_ref.mine_ref), custom_call_target="tpu_custom_call" | custom-call | tf_op jit(solution)/shard_map/mid/pallas_call | solution.py:545
  31.5 1.2 %collective-permute-start.3 = (bf16[2,2,64,128]{3,2,1,0:T(8,128)(2,1)S(1)}, bf16[2,2,64,128]{3,2,1,0:T(8,128)(2,1)S(1)}, u32[]{:S(2)}, u32[]{:S(2)}) collective-permute-start(bf16[2,2,64,128]{3,2,1,0:T(8,128)(2,1)S(1)} %get-tuple-element.38), channel_id=1, source_target_pairs={{0,1},{1,0},{2,3},{3,2},{4,5},{5,4},{6,7},{7,6},{8,9},{9,8},{10,11... | collective-permute-start | bytes 196616 | tf_op jit(solution)/shard_map/ppermute | solution.py:621
  32.7 1.5 %collective-permute-done.1.other_ref = bf16[2,2,64,128]{3,2,1,0:T(8,128)(2,1)S(1)} collective-permute-done((bf16[2,2,64,128]{3,2,1,0:T(8,128)(2,1)S(1)}, bf16[2,2,64,128]{3,2,1,0:T(8,128)(2,1)S(1)}, u32[]{:S(2)}, u32[]{:S(2)}) %collective-permute-start.1) | collective-permute-done | bytes 65568 | tf_op jit(solution)/shard_map/ppermute | solution.py:621
  34.3 0.9 %far.2 = (bf16[2,2,64,128]{3,2,1,0:T(8,128)(2,1)S(1)}, f32[2,8,1024]{2,1,0:T(8,128)S(1)}) custom-call(s32[44]{0:T(128)S(4)} %plan.1.plan_ref, bf16[4096,128]{1,0:T(8,128)(2,1)S(1)} %bitcast.11, bf16[4096,128]{1,0:T(8,128)(2,1)S(1)} %bitcast.18, f32[4,8,1024]{2,1,0:T(8,128)S(1)} %mid.1.stat_ref, bf16[2,2,64,128]{3,2,1,0:T(8,128)(2,1)S(1)} %collective-permute-done.1.other_ref), custom_call_target="tpu_custom_call" | custom-call | tf_op jit(solution)/shard_map/far/pallas_call | solution.py:545
  35.2 0.7 %collective-permute-start.2 = (bf16[2,2,64,128]{3,2,1,0:T(8,128)(2,1)S(1)}, bf16[2,2,64,128]{3,2,1,0:T(8,128)(2,1)S(1)}, u32[]{:S(2)}, u32[]{:S(2)}) collective-permute-start(bf16[2,2,64,128]{3,2,1,0:T(8,128)(2,1)S(1)} %get-tuple-element.35), channel_id=1, source_target_pairs={{0,1},{1,0},{2,3},{3,2},{4,5},{5,4},{6,7},{7,6},{8,9},{9,8},{10,11... | collective-permute-start | bytes 196616 | tf_op jit(solution)/shard_map/ppermute | solution.py:631
  35.9 0.9 %far.3 = (bf16[2,2,64,128]{3,2,1,0:T(8,128)(2,1)S(1)}, f32[2,8,1024]{2,1,0:T(8,128)S(1)}) custom-call(s32[44]{0:T(128)S(4)} %plan.1.plan_ref, bf16[4096,128]{1,0:T(8,128)(2,1)S(1)} %bitcast.12, bf16[4096,128]{1,0:T(8,128)(2,1)S(1)} %bitcast.19, f32[4,8,1024]{2,1,0:T(8,128)S(1)} %mid.1.stat_ref, bf16[2,2,64,128]{3,2,1,0:T(8,128)(2,1)S(1)} %collective-permute-done.3.other_ref), custom_call_target="tpu_custom_call" | custom-call | tf_op jit(solution)/shard_map/far/pallas_call | solution.py:545
  36.8 1.5 %collective-permute-start.4 = (bf16[2,2,64,128]{3,2,1,0:T(8,128)(2,1)S(1)}, bf16[2,2,64,128]{3,2,1,0:T(8,128)(2,1)S(1)}, u32[]{:S(2)}, u32[]{:S(2)}) collective-permute-start(bf16[2,2,64,128]{3,2,1,0:T(8,128)(2,1)S(1)} %get-tuple-element.41), channel_id=1, source_target_pairs={{0,1},{1,0},{2,3},{3,2},{4,5},{5,4},{6,7},{7,6},{8,9},{9,8},{10,11... | collective-permute-start | bytes 196616 | tf_op jit(solution)/shard_map/ppermute | solution.py:631
  38.3 0.9 %mine.3.refs_1_ = bf16[2,2,64,128]{3,2,1,0:T(8,128)(2,1)S(1)} custom-call(s32[44]{0:T(128)S(4)} %plan.1.plan_ref, bf16[4096,128]{1,0:T(8,128)(2,1)S(1)} %bitcast.13, bf16[4096,128]{1,0:T(8,128)(2,1)S(1)} %bitcast.20, bf16[16,2,64,128]{3,2,1,0:T(8,128)(2,1)S(1)} %all_to_all.10.arrived_ref.mine_ref, f32[2,8,1024]{2,1,0:T(8,128)S(1)} %get-tuple-element.39.stat_ref), custom_call_target="tpu_custom_call" | custom-call | tf_op jit(solution)/shard_map/mine/pallas_call | solution.py:545
  39.2 0.4 collective-permute-done.2.refs_2_
  39.6 0.9 %mine.2.refs_0_ = bf16[2,2,64,128]{3,2,1,0:T(8,128)(2,1)S(1)} custom-call(s32[44]{0:T(128)S(4)} %plan.1.plan_ref, bf16[4096,128]{1,0:T(8,128)(2,1)S(1)} %bitcast.14, bf16[4096,128]{1,0:T(8,128)(2,1)S(1)} %bitcast.21, bf16[16,2,64,128]{3,2,1,0:T(8,128)(2,1)S(1)} %all_to_all.10.arrived_ref.mine_ref, f32[2,8,1024]{2,1,0:T(8,128)S(1)} %get-tuple-element.37.stat_ref), custom_call_target="tpu_custom_call" | custom-call | tf_op jit(solution)/shard_map/mine/pallas_call | solution.py:545
  40.4 0.7 %collective-permute-done.4.refs_3_ = bf16[2,2,64,128]{3,2,1,0:T(8,128)(2,1)S(1)} collective-permute-done((bf16[2,2,64,128]{3,2,1,0:T(8,128)(2,1)S(1)}, bf16[2,2,64,128]{3,2,1,0:T(8,128)(2,1)S(1)}, u32[]{:S(2)}, u32[]{:S(2)}) %collective-permute-start.4) | collective-permute-done | bytes 65568 | tf_op jit(solution)/shard_map/ppermute | solution.py:631
  41.2 0.8 %return.1 = bf16[16,2,64,128]{3,2,1,0:T(8,128)(2,1)} custom-call(s32[44]{0:T(128)S(4)} %plan.1.plan_ref, bf16[2,2,64,128]{3,2,1,0:T(8,128)(2,1)S(1)} %mine.2.refs_0_, bf16[2,2,64,128]{3,2,1,0:T(8,128)(2,1)S(1)} %mine.3.refs_1_, bf16[2,2,64,128]{3,2,1,0:T(8,128)(2,1)S(1)} %collective-permute-done.2.refs_2_, ...), custom_call_target="tpu_custom_call" | custom-call | tf_op jit(solution)/shard_map/return/pallas_call | solution.py:545
  41.9 4.1 %all-to-all-start.1 = ((bf16[16,2,64,128]{3,2,1,0:T(8,128)(2,1)}), bf16[16,2,64,128]{3,2,1,0:T(8,128)(2,1)S(1)}, u32[]{:S(2)}, u32[]{:S(2)}) async-start(bf16[16,2,64,128]{3,2,1,0:T(8,128)(2,1)} %return.1), calls=%async_computation.1 | async-start | bytes 1048576 | tf_op jit(solution)/shard_map/all_to_all | solution.py:649
  46.1 0.0 copy-start.3
  46.1 0.9 %copy-done.2 = bf16[128,4,128]{2,1,0:T(4,128)(2,1)S(1)} copy-done((bf16[128,4,128]{2,1,0:T(4,128)(2,1)S(1)}, bf16[128,4,128]{2,1,0:T(4,128)(2,1)}, u32[]{:S(2)}) %copy-start.2) | copy-done | bytes 131096
  47.0 0.1 copy-done.3
  47.0 6.9 %local.1 = (bf16[4096,128]{1,0:T(8,128)(2,1)}, bf16[4096,128]{1,0:T(8,128)(2,1)}, f32[512,128]{1,0:T(8,128)S(1)}, f32[512,128]{1,0:T(8,128)S(1)}) custom-call(s32[44]{0:T(128)S(4)} %plan.1.plan_ref, bf16[4096,128]{1,0:T(8,128)(2,1)S(1)} %bitcast.15, bf16[4096,128]{1,0:T(8,128)(2,1)S(1)} %bitcast.22, bf16[512,128]{1,0:T(8,128)(2,1)S(1)} %bitcast.24, ...), custom_call_target="tpu_custom_call" | custom-call | tf_op jit(solution)/shard_map/local/pallas_call | solution.py:655
  53.9 0.7 %copy-done.4 = f32[512,128]{1,0:T(8,128)} copy-done((f32[512,128]{1,0:T(8,128)}, f32[512,128]{1,0:T(8,128)S(1)}, u32[]{:S(2)}) %copy-start.4) | copy-done | bytes 262168
  54.6 5.9 %all-to-all-done.1.landed_ref = bf16[16,2,64,128]{3,2,1,0:T(8,128)(2,1)S(1)} async-done(((bf16[16,2,64,128]{3,2,1,0:T(8,128)(2,1)}), bf16[16,2,64,128]{3,2,1,0:T(8,128)(2,1)S(1)}, u32[]{:S(2)}, u32[]{:S(2)}) %all-to-all-start.1) | async-done | bytes 524320 | tf_op jit(solution)/shard_map/all_to_all | solution.py:649
  60.5 0.2 land_sibling.1
  60.7 1.4 %collective-permute-start.5 = (bf16[4,2,64,128]{3,2,1,0:T(8,128)(2,1)S(1)}, bf16[4,2,64,128]{3,2,1,0:T(8,128)(2,1)S(1)}, u32[]{:S(2)}, u32[]{:S(2)}) collective-permute-start(bf16[4,2,64,128]{3,2,1,0:T(8,128)(2,1)S(1)} %land_sibling.1), channel_id=1, source_target_pairs={{0,1},{1,0},{2,3},{3,2},{4,5},{5,4},{6,7},{7,6},{8,9},{9,8},{10,11... | collective-permute-start | bytes 393224 | tf_op jit(solution)/shard_map/ppermute | solution.py:677
  62.2 0.2 land_own.1.own_ref
  62.3 3.9 %collective-permute-done.5.back_ref = bf16[4,2,64,128]{3,2,1,0:T(8,128)(2,1)S(1)} collective-permute-done((bf16[4,2,64,128]{3,2,1,0:T(8,128)(2,1)S(1)}, bf16[4,2,64,128]{3,2,1,0:T(8,128)(2,1)S(1)}, u32[]{:S(2)}, u32[]{:S(2)}) %collective-permute-start.5) | collective-permute-done | bytes 131104 | tf_op jit(solution)/shard_map/ppermute | solution.py:677
  66.2 1.0 %finish.1 = (bf16[512,128]{1,0:T(8,128)(2,1)}, bf16[512,128]{1,0:T(8,128)(2,1)}) custom-call(f32[512,128]{1,0:T(8,128)S(1)} %get-tuple-element.47.dk_near_ref, f32[512,128]{1,0:T(8,128)S(1)} %copy-done.5, f32[4,2,64,128]{3,2,1,0:T(8,128)S(1)} %land_own.1.own_ref, bf16[4,2,64,128]{3,2,1,0:T(8,128)(2,1)S(1)} %collective-permute-done.5.back_ref), custom_call_target="tpu_custom_call" | custom-call | tf_op jit(solution)/shard_map/finish/pallas_call | solution.py:545
  (12 shorter events, 0.1 us)
Async XLA Ops:
  1.9 7.3 %collective-permute-start = (bf16[4,2,64,128]{3,2,1,0:T(8,128)(2,1)S(1)}, bf16[4,2,64,128]{3,2,1,0:T(8,128)(2,1)S(1)}, u32[]{:S(2)}, u32[]{:S(2)}) collective-permute-start(bf16[4,2,64,128]{3,2,1,0:T(8,128)(2,1)S(1)} %get-tuple-element.28.given_ref), channel_id=1, source_target_pairs={{0,1},{1,0},{2,3},{3,2},{4,5},{5,4},{6,7},{7,6},{8,9},{9,8},{10,11... | collective-permute-start | bytes 393224 | tf_op jit(solution)/shard_map/ppermute | solution.py:584
  9.2 21.4 %copy-start.1 = (bf16[128,32,128]{2,1,0:T(8,128)(2,1)S(1)}, bf16[128,32,128]{2,1,0:T(8,128)(2,1)}, u32[]{:S(2)}) copy-start(bf16[128,32,128]{2,1,0:T(8,128)(2,1)} %param.9) | copy-start | bytes 3145732
  9.4 21.3 %copy-start = (bf16[128,32,128]{2,1,0:T(8,128)(2,1)S(1)}, bf16[128,32,128]{2,1,0:T(8,128)(2,1)}, u32[]{:S(2)}) copy-start(bf16[128,32,128]{2,1,0:T(8,128)(2,1)} %param.6) | copy-start | bytes 3145732
  29.7 4.6 %collective-permute-start.1 = (bf16[2,2,64,128]{3,2,1,0:T(8,128)(2,1)S(1)}, bf16[2,2,64,128]{3,2,1,0:T(8,128)(2,1)S(1)}, u32[]{:S(2)}, u32[]{:S(2)}) collective-permute-start(bf16[2,2,64,128]{3,2,1,0:T(8,128)(2,1)S(1)} %get-tuple-element.34), channel_id=1, source_target_pairs={{0,1},{1,0},{2,3},{3,2},{4,5},{5,4},{6,7},{7,6},{8,9},{9,8},{10,11... | collective-permute-start | bytes 196616 | tf_op jit(solution)/shard_map/ppermute | solution.py:621
  31.5 4.4 %collective-permute-start.3 = (bf16[2,2,64,128]{3,2,1,0:T(8,128)(2,1)S(1)}, bf16[2,2,64,128]{3,2,1,0:T(8,128)(2,1)S(1)}, u32[]{:S(2)}, u32[]{:S(2)}) collective-permute-start(bf16[2,2,64,128]{3,2,1,0:T(8,128)(2,1)S(1)} %get-tuple-element.38), channel_id=1, source_target_pairs={{0,1},{1,0},{2,3},{3,2},{4,5},{5,4},{6,7},{7,6},{8,9},{9,8},{10,11... | collective-permute-start | bytes 196616 | tf_op jit(solution)/shard_map/ppermute | solution.py:621
  35.2 4.4 %collective-permute-start.2 = (bf16[2,2,64,128]{3,2,1,0:T(8,128)(2,1)S(1)}, bf16[2,2,64,128]{3,2,1,0:T(8,128)(2,1)S(1)}, u32[]{:S(2)}, u32[]{:S(2)}) collective-permute-start(bf16[2,2,64,128]{3,2,1,0:T(8,128)(2,1)S(1)} %get-tuple-element.35), channel_id=1, source_target_pairs={{0,1},{1,0},{2,3},{3,2},{4,5},{5,4},{6,7},{7,6},{8,9},{9,8},{10,11... | collective-permute-start | bytes 196616 | tf_op jit(solution)/shard_map/ppermute | solution.py:631
  36.8 4.3 %collective-permute-start.4 = (bf16[2,2,64,128]{3,2,1,0:T(8,128)(2,1)S(1)}, bf16[2,2,64,128]{3,2,1,0:T(8,128)(2,1)S(1)}, u32[]{:S(2)}, u32[]{:S(2)}) collective-permute-start(bf16[2,2,64,128]{3,2,1,0:T(8,128)(2,1)S(1)} %get-tuple-element.41), channel_id=1, source_target_pairs={{0,1},{1,0},{2,3},{3,2},{4,5},{5,4},{6,7},{7,6},{8,9},{9,8},{10,11... | collective-permute-start | bytes 196616 | tf_op jit(solution)/shard_map/ppermute | solution.py:631
  41.9 18.6 %all-to-all-start.1 = ((bf16[16,2,64,128]{3,2,1,0:T(8,128)(2,1)}), bf16[16,2,64,128]{3,2,1,0:T(8,128)(2,1)S(1)}, u32[]{:S(2)}, u32[]{:S(2)}) async-start(bf16[16,2,64,128]{3,2,1,0:T(8,128)(2,1)} %return.1), calls=%async_computation.1 | async-start | bytes 1048576 | tf_op jit(solution)/shard_map/all_to_all | solution.py:649
  46.1 0.9 %copy-start.2 = (bf16[128,4,128]{2,1,0:T(4,128)(2,1)S(1)}, bf16[128,4,128]{2,1,0:T(4,128)(2,1)}, u32[]{:S(2)}) copy-start(bf16[128,4,128]{2,1,0:T(4,128)(2,1)} %param.7) | copy-start | bytes 393220
  46.1 1.0 %copy-start.3 = (bf16[128,4,128]{2,1,0:T(4,128)(2,1)S(1)}, bf16[128,4,128]{2,1,0:T(4,128)(2,1)}, u32[]{:S(2)}) copy-start(bf16[128,4,128]{2,1,0:T(4,128)(2,1)} %param.8) | copy-start | bytes 393220
  53.9 0.7 %copy-start.4 = (f32[512,128]{1,0:T(8,128)}, f32[512,128]{1,0:T(8,128)S(1)}, u32[]{:S(2)}) copy-start(f32[512,128]{1,0:T(8,128)S(1)} %get-tuple-element.48.dv_near_ref) | copy-start | bytes 786436
  60.7 5.5 %copy-start.5 = (f32[512,128]{1,0:T(8,128)S(1)}, f32[512,128]{1,0:T(8,128)}, u32[]{:S(2)}) copy-start(f32[512,128]{1,0:T(8,128)} %copy-done.4) | copy-start | bytes 786436
  60.7 5.5 %collective-permute-start.5 = (bf16[4,2,64,128]{3,2,1,0:T(8,128)(2,1)S(1)}, bf16[4,2,64,128]{3,2,1,0:T(8,128)(2,1)S(1)}, u32[]{:S(2)}, u32[]{:S(2)}) collective-permute-start(bf16[4,2,64,128]{3,2,1,0:T(8,128)(2,1)S(1)} %land_sibling.1), channel_id=1, source_target_pairs={{0,1},{1,0},{2,3},{3,2},{4,5},{5,4},{6,7},{7,6},{8,9},{9,8},{10,11... | collective-permute-start | bytes 393224 | tf_op jit(solution)/shard_map/ppermute | solution.py:677

commit v11 on v10

--- a/solution.py
+++ b/solution.py
@@ -206,6 +206,15 @@
     col = lax.broadcasted_iota(jnp.int32, (cols, cols), 1)
     token = row // half * place + row % place
     return jnp.where(col == token * kv_heads + row % half // place, 1.0, 0.0).astype(BF16)
+
+
+def half_order(cols, kv_heads, which):
+    half = cols // 2
+    place = half // kv_heads
+    row = lax.broadcasted_iota(jnp.int32, (half, cols), 0)
+    col = lax.broadcasted_iota(jnp.int32, (half, cols), 1)
+    token = which * place + row % place
+    return jnp.where(col == token * kv_heads + row // place, 1.0, 0.0).astype(BF16)
 
 
 def reorder(one_hot, array):
@@ -259,22 +268,19 @@
         plan_ref[give_at + block] = lax.div(lists_ref[at], per_group)
 
 
-def pack_kernel(k_hbm, v_hbm, kept_ref, given_ref, k_ref, v_ref, sems, *, kv_heads):
-    blocks, _, half, _ = kept_ref.shape
+def pack_kernel(k_hbm, v_hbm, k_ref, v_ref, given_ref, sems, *, kv_heads):
+    blocks, _, half, _ = given_ref.shape
     copies = [
         pltpu.make_async_copy(k_hbm, k_ref, sems.at[0]),
         pltpu.make_async_copy(v_hbm, v_ref, sems.at[1]),
     ]
     for copy in copies:
         copy.start()
-    first = lax.axis_index("uly") == 0
-    order = head_major(2 * half, kv_heads)
+    order = half_order(2 * half, kv_heads, 1 - lax.axis_index("uly"))
     for which, ref in enumerate((k_ref, v_ref)):
         copies[which].wait()
         for block in range(blocks):
-            ordered = reorder(order, ref[block * 2 * half:(block + 1) * 2 * half])
-            kept_ref[block, which] = jnp.where(first, ordered[:half], ordered[half:])
-            given_ref[block, which] = jnp.where(first, ordered[half:], ordered[:half])
+            given_ref[block, which] = reorder(order, ref[block * 2 * half:(block + 1) * 2 * half])
 
 
 def send_own_kernel(plan_ref, blocks_ref, out_ref):
@@ -313,35 +319,52 @@
 
 
 def near_kernel(
-    q_ref, g_ref, kept_ref, given_ref, stat_ref, *, heads, kv_heads, score_scale
+    q_hbm, g_hbm, k_ref, v_ref, given_ref, stat_ref, kept_ref, q_ref, g_ref, sems,
+    *, heads, kv_heads, score_scale
 ):
-    rows = q_ref.shape[0]
-    place = kept_ref.shape[2] // kv_heads
+    blocks = stat_ref.shape[0]
+    rows = q_ref.shape[0] // blocks
+    half = given_ref.shape[2]
+    place = half // kv_heads
+    copies = []
+    for block in range(blocks):
+        span = pl.ds(block * rows, rows)
+        for which, (source, target) in enumerate(((q_hbm, q_ref), (g_hbm, g_ref))):
+            sem = sems.at[which, block]
+            copies.append(pltpu.make_async_copy(source.at[span], target.at[span], sem))
+            copies[-1].start()
+    mine = lax.axis_index("uly")
+    order = half_order(2 * half, kv_heads, mine)
+    for block in range(blocks):
+        narrow = slice(block * 2 * half, (block + 1) * 2 * half)
+        kept_ref[block, 0] = reorder(order, k_ref[narrow])
+        kept_ref[block, 1] = reorder(order, v_ref[narrow])
     token, lane_head = lanes(rows, heads, kv_heads)
     key = lax.broadcasted_iota(jnp.int32, (2 * place, rows), 0)
-    mine = lax.axis_index("uly")
     part = jnp.where(key < place, mine, 1 - mine)
     causal = key % place + part * place <= token
-    pieces = []
-    for which, ref in enumerate((q_ref, g_ref)):
-        both = jnp.concatenate([kept_ref[0, which], given_ref[0, which]], axis=0)
-        full = dot_last(both, ref[...])
-        half = full.shape[0] // 2
-        pieces.append(
-            jnp.concatenate(
-                [
-                    own_head(full[:half], lane_head, kv_heads),
-                    own_head(full[half:], lane_head, kv_heads),
-                ],
-                axis=0,
+    for block in range(blocks):
+        span = slice(block * rows, (block + 1) * rows)
+        pieces = []
+        for which, ref in enumerate((q_ref, g_ref)):
+            copies[2 * block + which].wait()
+            both = jnp.concatenate([kept_ref[block, which], given_ref[block, which]], axis=0)
+            full = dot_last(both, ref[span])
+            pieces.append(
+                jnp.concatenate(
+                    [
+                        own_head(full[:half], lane_head, kv_heads),
+                        own_head(full[half:], lane_head, kv_heads),
+                    ],
+                    axis=0,
+                )
             )
-        )
-    scores = jnp.where(causal, pieces[0] * score_scale, HIDDEN)
-    highest = jnp.max(scores, axis=0, keepdims=True)
-    raised = jnp.exp(scores - highest)
-    stat_ref[0, 0:1] = highest
-    stat_ref[0, 1:2] = jnp.sum(raised, axis=0, keepdims=True)
-    stat_ref[0, 2:3] = jnp.sum(raised * pieces[1], axis=0, keepdims=True)
+        scores = jnp.where(causal, pieces[0] * score_scale, HIDDEN)
+        highest = jnp.max(scores, axis=0, keepdims=True)
+        raised = jnp.exp(scores - highest)
+        stat_ref[block, 0:1] = highest
+        stat_ref[block, 1:2] = jnp.sum(raised, axis=0, keepdims=True)
+        stat_ref[block, 2:3] = jnp.sum(raised * pieces[1], axis=0, keepdims=True)
 
 
 def far_scores(part_ref, at, q, g, seen, lane_head, kv_heads, score_scale):
@@ -562,14 +585,12 @@
     def in_hbm(array):
         return pltpu.with_memory_space_constraint(array, pltpu.HBM)
 
-    kept, given = pl.pallas_call(
+    k_here, v_here, given = pl.pallas_call(
         partial(pack_kernel, kv_heads=kv_heads),
         in_specs=[anywhere, anywhere],
-        out_specs=[vmem, vmem],
-        out_shape=[part_shape, part_shape],
-        scratch_shapes=[
-            pltpu.VMEM(k2.shape, BF16), pltpu.VMEM(k2.shape, BF16), pltpu.SemaphoreType.DMA((2,))
-        ],
+        out_specs=[vmem, vmem, vmem],
+        out_shape=[small_shape, small_shape, part_shape],
+        scratch_shapes=[pltpu.SemaphoreType.DMA((2,))],
         compiler_params=limit,
         name="pack",
     )(in_hbm(k2), in_hbm(v2))
@@ -584,15 +605,18 @@
     gotten = lax.ppermute(given, "uly", swap)
     row_spec = pl.BlockSpec((rows, width), step_rows)
     part_spec = pl.BlockSpec((1, 2, half, width), step_part)
-    stats = pl.pallas_call(
+    stats, kept = pl.pallas_call(
         partial(near_kernel, **sizes),
-        grid=(mine_blocks,),
-        in_specs=[row_spec, row_spec, part_spec, part_spec],
-        out_specs=pl.BlockSpec((1, 8, rows), lambda i: (i, 0, 0)),
-        out_shape=stat_shape,
+        in_specs=[anywhere, anywhere, vmem, vmem, vmem],
+        out_specs=[vmem, vmem],
+        out_shape=[stat_shape, part_shape],
+        scratch_shapes=[
+            pltpu.VMEM(q2.shape, BF16), pltpu.VMEM(q2.shape, BF16),
+            pltpu.SemaphoreType.DMA((2, mine_blocks)),
+        ],
         compiler_params=limit,
         name="near",
-    )(in_hbm(q2), in_hbm(g2), kept, given)
+    )(in_hbm(q2), in_hbm(g2), k_here, v_here, given)
     outgoing = call(
         send_own_kernel, "send_own", (plan,), (kept,),
         jax.ShapeDtypeStruct(slots, BF16),

time: 67.6 us -> 67.6 us (level)
  waiting for transfers between devices: 12.5 us -> 13.2 us
where the time goes in v11:
time: 67.6 us; the launch traced here: 67.4 us
  blocking collectives  20.3 us (30%)
  Pallas kernels  18.8 us (28%)
  waiting for transfers between devices  13.2 us (20%)
  starting transfers between devices  12.6 us (19%)
  local copies, waits for them, and re-layouts  1.65 us (2%)
  between operations  0.8 us (1%)
    all_to_all x1, blocking collectives, whole_blocks(): lax.all_to_all(outgoing, 'grp', split_axis=0, concat_axis=0, tiled=True)  20.3 us
    pallas_call x1, Pallas kernels, whole_blocks(): pl.pallas_call(partial(local_kernel, seen_at=seen_at, **sizes), grid_spec...  6.87 us
    pallas_call x12, Pallas kernels, call(): pl.pallas_call(kernel, in_specs=[smem] * len(scalars) + [vmem] * (len(ope...  6.69 us
    all_to_all x1, waiting for transfers between devices, whole_blocks(): lax.all_to_all(returning, 'grp', split_axis=0, concat_axis=0, tiled=True)  5.92 us
    ppermute x1, waiting for transfers between devices, whole_blocks(): back = lax.ppermute(give, 'uly', swap)  4.33 us
    all_to_all x1, starting transfers between devices, whole_blocks(): lax.all_to_all(returning, 'grp', split_axis=0, concat_axis=0, tiled=True)  4.25 us
    ppermute x1, starting transfers between devices, whole_blocks(): gotten = lax.ppermute(given, 'uly', swap)  3.03 us
    pallas_call x1, Pallas kernels, whole_blocks(): pl.pallas_call(partial(near_kernel, **sizes), in_specs=[anywhere, anywher...  2.94 us
  transfers between devices with their start and end apart: 7, of which 5 were waited for; matrix products, arithmetic and copies ran while one was open for 0% of the time, Pallas kernels for 23%

profile of v11, /device:TPU:0, one launch (start us, length us, event | category | flops | bytes accessed | tf_op | source)
XLA Modules:
  0.0 67.4 jit_solution(9863095790751080624)
XLA Ops:
  0.6 1.3 %pack.1 = (bf16[512,128]{1,0:T(8,128)(2,1)S(1)}, bf16[512,128]{1,0:T(8,128)(2,1)S(1)}, bf16[4,2,64,128]{3,2,1,0:T(8,128)(2,1)S(1)}) custom-call(bf16[512,128]{1,0:T(8,128)(2,1)} %bitcast.23, bf16[512,128]{1,0:T(8,128)(2,1)} %bitcast.25), custom_call_target="tpu_custom_call" | custom-call | tf_op jit(solution)/shard_map/pack/pallas_call | solution.py:588
  1.9 3.0 %collective-permute-start = (bf16[4,2,64,128]{3,2,1,0:T(8,128)(2,1)S(1)}, bf16[4,2,64,128]{3,2,1,0:T(8,128)(2,1)S(1)}, u32[]{:S(2)}, u32[]{:S(2)}) collective-permute-start(bf16[4,2,64,128]{3,2,1,0:T(8,128)(2,1)S(1)} %get-tuple-element.31.given_ref), channel_id=1, source_target_pairs={{0,1},{1,0},{2,3},{3,2},{4,5},{5,4},{6,7},{7,6},{8,9},{9,8},{10,11... | collective-permute-start | bytes 393224 | tf_op jit(solution)/shard_map/ppermute | solution.py:605
  4.9 1.1 %plan.1.plan_ref = s32[44]{0:T(128)S(4)} custom-call(s32[128]{0:T(128)} %bitcast.31, s32[128]{0:T(128)} %counts_ref.1), custom_call_target="tpu_custom_call" | custom-call | tf_op jit(solution)/shard_map/plan/pallas_call | solution.py:597
  6.0 2.9 %near.1 = (f32[4,8,1024]{2,1,0:T(8,128)S(1)}, bf16[4,2,64,128]{3,2,1,0:T(8,128)(2,1)S(1)}) custom-call(bf16[4096,128]{1,0:T(8,128)(2,1)} %bitcast.9, bf16[4096,128]{1,0:T(8,128)(2,1)} %bitcast.16, bf16[512,128]{1,0:T(8,128)(2,1)S(1)} %get-tuple-element.32.k_ref, bf16[512,128]{1,0:T(8,128)(2,1)S(1)} %get-tuple-element.33.v_ref, ...), custom_call_target="tpu_custom_call" | custom-call | tf_op jit(solution)/shard_map/near/pallas_call | solution.py:608
  9.0 0.0 copy-start.1
  9.1 0.1 send_sibling.1
  9.2 0.0 copy-start
  9.2 20.3 %all_to_all.10.arrived_ref.mine_ref = bf16[16,2,64,128]{3,2,1,0:T(8,128)(2,1)S(1)} all-to-all(bf16[16,2,64,128]{3,2,1,0:T(8,128)(2,1)S(1)} %send_sibling.1), channel_id=1, replica_groups=mesh['grp'=16,'uly'=2] {'grp'}, dimensions={0} | all-to-all | bytes 1048576 | tf_op jit(solution)/shard_map/all_to_all | solution.py:629
  29.5 1.1 %collective-permute-start.1 = (bf16[2,2,64,128]{3,2,1,0:T(8,128)(2,1)S(1)}, bf16[2,2,64,128]{3,2,1,0:T(8,128)(2,1)S(1)}, u32[]{:S(2)}, u32[]{:S(2)}) collective-permute-start(bf16[2,2,64,128]{3,2,1,0:T(8,128)(2,1)S(1)} %get-tuple-element.40), channel_id=1, source_target_pairs={{0,1},{1,0},{2,3},{3,2},{4,5},{5,4},{6,7},{7,6},{8,9},{9,8},{10,11... | collective-permute-start | bytes 196616 | tf_op jit(solution)/shard_map/ppermute | solution.py:645
  30.7 0.9 %mid.1.stat_ref = f32[4,8,1024]{2,1,0:T(8,128)S(1)} custom-call(s32[44]{0:T(128)S(4)} %plan.1.plan_ref, bf16[4096,128]{1,0:T(8,128)(2,1)S(1)} %bitcast.10, bf16[4096,128]{1,0:T(8,128)(2,1)S(1)} %bitcast.17, f32[4,8,1024]{2,1,0:T(8,128)S(1)} %get-tuple-element.38.stat_ref, bf16[16,2,64,128]{3,2,1,0:T(8,128)(2,1)S(1)} %all_to_all.10.arrived_ref.mine_ref), custom_call_target="tpu_custom_call" | custom-call | tf_op jit(solution)/shard_map/mid/pallas_call | solution.py:568
  31.5 1.0 %collective-permute-start.3 = (bf16[2,2,64,128]{3,2,1,0:T(8,128)(2,1)S(1)}, bf16[2,2,64,128]{3,2,1,0:T(8,128)(2,1)S(1)}, u32[]{:S(2)}, u32[]{:S(2)}) collective-permute-start(bf16[2,2,64,128]{3,2,1,0:T(8,128)(2,1)S(1)} %get-tuple-element.44), channel_id=1, source_target_pairs={{0,1},{1,0},{2,3},{3,2},{4,5},{5,4},{6,7},{7,6},{8,9},{9,8},{10,11... | collective-permute-start | bytes 196616 | tf_op jit(solution)/shard_map/ppermute | solution.py:645
  32.6 1.3 %collective-permute-done.1.other_ref = bf16[2,2,64,128]{3,2,1,0:T(8,128)(2,1)S(1)} collective-permute-done((bf16[2,2,64,128]{3,2,1,0:T(8,128)(2,1)S(1)}, bf16[2,2,64,128]{3,2,1,0:T(8,128)(2,1)S(1)}, u32[]{:S(2)}, u32[]{:S(2)}) %collective-permute-start.1) | collective-permute-done | bytes 65568 | tf_op jit(solution)/shard_map/ppermute | solution.py:645
  33.9 0.9 %far.2 = (bf16[2,2,64,128]{3,2,1,0:T(8,128)(2,1)S(1)}, f32[2,8,1024]{2,1,0:T(8,128)S(1)}) custom-call(s32[44]{0:T(128)S(4)} %plan.1.plan_ref, bf16[4096,128]{1,0:T(8,128)(2,1)S(1)} %bitcast.11, bf16[4096,128]{1,0:T(8,128)(2,1)S(1)} %bitcast.18, f32[4,8,1024]{2,1,0:T(8,128)S(1)} %mid.1.stat_ref, bf16[2,2,64,128]{3,2,1,0:T(8,128)(2,1)S(1)} %collective-permute-done.1.other_ref), custom_call_target="tpu_custom_call" | custom-call | tf_op jit(solution)/shard_map/far/pallas_call | solution.py:568
  34.8 1.2 %collective-permute-start.2 = (bf16[2,2,64,128]{3,2,1,0:T(8,128)(2,1)S(1)}, bf16[2,2,64,128]{3,2,1,0:T(8,128)(2,1)S(1)}, u32[]{:S(2)}, u32[]{:S(2)}) collective-permute-start(bf16[2,2,64,128]{3,2,1,0:T(8,128)(2,1)S(1)} %get-tuple-element.41), channel_id=1, source_target_pairs={{0,1},{1,0},{2,3},{3,2},{4,5},{5,4},{6,7},{7,6},{8,9},{9,8},{10,11... | collective-permute-start | bytes 196616 | tf_op jit(solution)/shard_map/ppermute | solution.py:655
  36.0 0.9 %far.3 = (bf16[2,2,64,128]{3,2,1,0:T(8,128)(2,1)S(1)}, f32[2,8,1024]{2,1,0:T(8,128)S(1)}) custom-call(s32[44]{0:T(128)S(4)} %plan.1.plan_ref, bf16[4096,128]{1,0:T(8,128)(2,1)S(1)} %bitcast.12, bf16[4096,128]{1,0:T(8,128)(2,1)S(1)} %bitcast.19, f32[4,8,1024]{2,1,0:T(8,128)S(1)} %mid.1.stat_ref, bf16[2,2,64,128]{3,2,1,0:T(8,128)(2,1)S(1)} %collective-permute-done.3.other_ref), custom_call_target="tpu_custom_call" | custom-call | tf_op jit(solution)/shard_map/far/pallas_call | solution.py:568
  36.9 1.0 %collective-permute-start.4 = (bf16[2,2,64,128]{3,2,1,0:T(8,128)(2,1)S(1)}, bf16[2,2,64,128]{3,2,1,0:T(8,128)(2,1)S(1)}, u32[]{:S(2)}, u32[]{:S(2)}) collective-permute-start(bf16[2,2,64,128]{3,2,1,0:T(8,128)(2,1)S(1)} %get-tuple-element.47), channel_id=1, source_target_pairs={{0,1},{1,0},{2,3},{3,2},{4,5},{5,4},{6,7},{7,6},{8,9},{9,8},{10,11... | collective-permute-start | bytes 196616 | tf_op jit(solution)/shard_map/ppermute | solution.py:655
  37.9 0.9 %mine.3.refs_1_ = bf16[2,2,64,128]{3,2,1,0:T(8,128)(2,1)S(1)} custom-call(s32[44]{0:T(128)S(4)} %plan.1.plan_ref, bf16[4096,128]{1,0:T(8,128)(2,1)S(1)} %bitcast.13, bf16[4096,128]{1,0:T(8,128)(2,1)S(1)} %bitcast.20, bf16[16,2,64,128]{3,2,1,0:T(8,128)(2,1)S(1)} %all_to_all.10.arrived_ref.mine_ref, f32[2,8,1024]{2,1,0:T(8,128)S(1)} %get-tuple-element.45.stat_ref), custom_call_target="tpu_custom_call" | custom-call | tf_op jit(solution)/shard_map/mine/pallas_call | solution.py:568
  38.8 0.8 %collective-permute-done.2.refs_2_ = bf16[2,2,64,128]{3,2,1,0:T(8,128)(2,1)S(1)} collective-permute-done((bf16[2,2,64,128]{3,2,1,0:T(8,128)(2,1)S(1)}, bf16[2,2,64,128]{3,2,1,0:T(8,128)(2,1)S(1)}, u32[]{:S(2)}, u32[]{:S(2)}) %collective-permute-start.2) | collective-permute-done | bytes 65568 | tf_op jit(solution)/shard_map/ppermute | solution.py:655
  39.5 0.9 %mine.2.refs_0_ = bf16[2,2,64,128]{3,2,1,0:T(8,128)(2,1)S(1)} custom-call(s32[44]{0:T(128)S(4)} %plan.1.plan_ref, bf16[4096,128]{1,0:T(8,128)(2,1)S(1)} %bitcast.14, bf16[4096,128]{1,0:T(8,128)(2,1)S(1)} %bitcast.21, bf16[16,2,64,128]{3,2,1,0:T(8,128)(2,1)S(1)} %all_to_all.10.arrived_ref.mine_ref, f32[2,8,1024]{2,1,0:T(8,128)S(1)} %get-tuple-element.43.stat_ref), custom_call_target="tpu_custom_call" | custom-call | tf_op jit(solution)/shard_map/mine/pallas_call | solution.py:568
  40.4 0.9 %collective-permute-done.4.refs_3_ = bf16[2,2,64,128]{3,2,1,0:T(8,128)(2,1)S(1)} collective-permute-done((bf16[2,2,64,128]{3,2,1,0:T(8,128)(2,1)S(1)}, bf16[2,2,64,128]{3,2,1,0:T(8,128)(2,1)S(1)}, u32[]{:S(2)}, u32[]{:S(2)}) %collective-permute-start.4) | collective-permute-done | bytes 65568 | tf_op jit(solution)/shard_map/ppermute | solution.py:655
  41.3 0.8 %return.1 = bf16[16,2,64,128]{3,2,1,0:T(8,128)(2,1)} custom-call(s32[44]{0:T(128)S(4)} %plan.1.plan_ref, bf16[2,2,64,128]{3,2,1,0:T(8,128)(2,1)S(1)} %mine.2.refs_0_, bf16[2,2,64,128]{3,2,1,0:T(8,128)(2,1)S(1)} %mine.3.refs_1_, bf16[2,2,64,128]{3,2,1,0:T(8,128)(2,1)S(1)} %collective-permute-done.2.refs_2_, ...), custom_call_target="tpu_custom_call" | custom-call | tf_op jit(solution)/shard_map/return/pallas_call | solution.py:568
  42.0 4.2 %all-to-all-start.1 = ((bf16[16,2,64,128]{3,2,1,0:T(8,128)(2,1)}), bf16[16,2,64,128]{3,2,1,0:T(8,128)(2,1)S(1)}, u32[]{:S(2)}, u32[]{:S(2)}) async-start(bf16[16,2,64,128]{3,2,1,0:T(8,128)(2,1)} %return.1), calls=%async_computation.1 | async-start | bytes 1048576 | tf_op jit(solution)/shard_map/all_to_all | solution.py:673
  46.3 0.9 %copy-done.2 = bf16[128,4,128]{2,1,0:T(4,128)(2,1)S(1)} copy-done((bf16[128,4,128]{2,1,0:T(4,128)(2,1)S(1)}, bf16[128,4,128]{2,1,0:T(4,128)(2,1)}, u32[]{:S(2)}) %copy-start.2) | copy-done | bytes 131096
  47.2 0.1 copy-done.3
  47.3 6.9 %local.1 = (bf16[4096,128]{1,0:T(8,128)(2,1)}, bf16[4096,128]{1,0:T(8,128)(2,1)}, f32[512,128]{1,0:T(8,128)S(1)}, f32[512,128]{1,0:T(8,128)S(1)}) custom-call(s32[44]{0:T(128)S(4)} %plan.1.plan_ref, bf16[4096,128]{1,0:T(8,128)(2,1)S(1)} %bitcast.15, bf16[4096,128]{1,0:T(8,128)(2,1)S(1)} %bitcast.22, bf16[512,128]{1,0:T(8,128)(2,1)S(1)} %bitcast.24, ...), custom_call_target="tpu_custom_call" | custom-call | tf_op jit(solution)/shard_map/local/pallas_call | solution.py:679
  54.1 0.7 %copy-done.4 = f32[512,128]{1,0:T(8,128)} copy-done((f32[512,128]{1,0:T(8,128)}, f32[512,128]{1,0:T(8,128)S(1)}, u32[]{:S(2)}) %copy-start.4) | copy-done | bytes 262168
  54.8 5.9 %all-to-all-done.1.landed_ref = bf16[16,2,64,128]{3,2,1,0:T(8,128)(2,1)S(1)} async-done(((bf16[16,2,64,128]{3,2,1,0:T(8,128)(2,1)}), bf16[16,2,64,128]{3,2,1,0:T(8,128)(2,1)S(1)}, u32[]{:S(2)}, u32[]{:S(2)}) %all-to-all-start.1) | async-done | bytes 524320 | tf_op jit(solution)/shard_map/all_to_all | solution.py:673
  60.8 0.2 land_sibling.1
  60.9 1.0 %collective-permute-start.5 = (bf16[4,2,64,128]{3,2,1,0:T(8,128)(2,1)S(1)}, bf16[4,2,64,128]{3,2,1,0:T(8,128)(2,1)S(1)}, u32[]{:S(2)}, u32[]{:S(2)}) collective-permute-start(bf16[4,2,64,128]{3,2,1,0:T(8,128)(2,1)S(1)} %land_sibling.1), channel_id=1, source_target_pairs={{0,1},{1,0},{2,3},{3,2},{4,5},{5,4},{6,7},{7,6},{8,9},{9,8},{10,11... | collective-permute-start | bytes 393224 | tf_op jit(solution)/shard_map/ppermute | solution.py:701
  61.9 0.2 land_own.1.own_ref
  62.1 4.3 %collective-permute-done.5.back_ref = bf16[4,2,64,128]{3,2,1,0:T(8,128)(2,1)S(1)} collective-permute-done((bf16[4,2,64,128]{3,2,1,0:T(8,128)(2,1)S(1)}, bf16[4,2,64,128]{3,2,1,0:T(8,128)(2,1)S(1)}, u32[]{:S(2)}, u32[]{:S(2)}) %collective-permute-start.5) | collective-permute-done | bytes 131104 | tf_op jit(solution)/shard_map/ppermute | solution.py:701
  66.4 1.0 %finish.1 = (bf16[512,128]{1,0:T(8,128)(2,1)}, bf16[512,128]{1,0:T(8,128)(2,1)}) custom-call(f32[512,128]{1,0:T(8,128)S(1)} %get-tuple-element.53.dk_near_ref, f32[512,128]{1,0:T(8,128)S(1)} %copy-done.5, f32[4,2,64,128]{3,2,1,0:T(8,128)S(1)} %land_own.1.own_ref, bf16[4,2,64,128]{3,2,1,0:T(8,128)(2,1)S(1)} %collective-permute-done.5.back_ref), custom_call_target="tpu_custom_call" | custom-call | tf_op jit(solution)/shard_map/finish/pallas_call | solution.py:568
  (12 shorter events, 0.1 us)
Async XLA Ops:
  1.9 7.1 %collective-permute-start = (bf16[4,2,64,128]{3,2,1,0:T(8,128)(2,1)S(1)}, bf16[4,2,64,128]{3,2,1,0:T(8,128)(2,1)S(1)}, u32[]{:S(2)}, u32[]{:S(2)}) collective-permute-start(bf16[4,2,64,128]{3,2,1,0:T(8,128)(2,1)S(1)} %get-tuple-element.31.given_ref), channel_id=1, source_target_pairs={{0,1},{1,0},{2,3},{3,2},{4,5},{5,4},{6,7},{7,6},{8,9},{9,8},{10,11... | collective-permute-start | bytes 393224 | tf_op jit(solution)/shard_map/ppermute | solution.py:605
  9.0 21.6 %copy-start.1 = (bf16[128,32,128]{2,1,0:T(8,128)(2,1)S(1)}, bf16[128,32,128]{2,1,0:T(8,128)(2,1)}, u32[]{:S(2)}) copy-start(bf16[128,32,128]{2,1,0:T(8,128)(2,1)} %param.9) | copy-start | bytes 3145732
  9.2 21.5 %copy-start = (bf16[128,32,128]{2,1,0:T(8,128)(2,1)S(1)}, bf16[128,32,128]{2,1,0:T(8,128)(2,1)}, u32[]{:S(2)}) copy-start(bf16[128,32,128]{2,1,0:T(8,128)(2,1)} %param.6) | copy-start | bytes 3145732
  29.5 4.3 %collective-permute-start.1 = (bf16[2,2,64,128]{3,2,1,0:T(8,128)(2,1)S(1)}, bf16[2,2,64,128]{3,2,1,0:T(8,128)(2,1)S(1)}, u32[]{:S(2)}, u32[]{:S(2)}) collective-permute-start(bf16[2,2,64,128]{3,2,1,0:T(8,128)(2,1)S(1)} %get-tuple-element.40), channel_id=1, source_target_pairs={{0,1},{1,0},{2,3},{3,2},{4,5},{5,4},{6,7},{7,6},{8,9},{9,8},{10,11... | collective-permute-start | bytes 196616 | tf_op jit(solution)/shard_map/ppermute | solution.py:645
  31.5 4.5 %collective-permute-start.3 = (bf16[2,2,64,128]{3,2,1,0:T(8,128)(2,1)S(1)}, bf16[2,2,64,128]{3,2,1,0:T(8,128)(2,1)S(1)}, u32[]{:S(2)}, u32[]{:S(2)}) collective-permute-start(bf16[2,2,64,128]{3,2,1,0:T(8,128)(2,1)S(1)} %get-tuple-element.44), channel_id=1, source_target_pairs={{0,1},{1,0},{2,3},{3,2},{4,5},{5,4},{6,7},{7,6},{8,9},{9,8},{10,11... | collective-permute-start | bytes 196616 | tf_op jit(solution)/shard_map/ppermute | solution.py:645
  34.8 4.7 %collective-permute-start.2 = (bf16[2,2,64,128]{3,2,1,0:T(8,128)(2,1)S(1)}, bf16[2,2,64,128]{3,2,1,0:T(8,128)(2,1)S(1)}, u32[]{:S(2)}, u32[]{:S(2)}) collective-permute-start(bf16[2,2,64,128]{3,2,1,0:T(8,128)(2,1)S(1)} %get-tuple-element.41), channel_id=1, source_target_pairs={{0,1},{1,0},{2,3},{3,2},{4,5},{5,4},{6,7},{7,6},{8,9},{9,8},{10,11... | collective-permute-start | bytes 196616 | tf_op jit(solution)/shard_map/ppermute | solution.py:655
  36.9 4.3 %collective-permute-start.4 = (bf16[2,2,64,128]{3,2,1,0:T(8,128)(2,1)S(1)}, bf16[2,2,64,128]{3,2,1,0:T(8,128)(2,1)S(1)}, u32[]{:S(2)}, u32[]{:S(2)}) collective-permute-start(bf16[2,2,64,128]{3,2,1,0:T(8,128)(2,1)S(1)} %get-tuple-element.47), channel_id=1, source_target_pairs={{0,1},{1,0},{2,3},{3,2},{4,5},{5,4},{6,7},{7,6},{8,9},{9,8},{10,11... | collective-permute-start | bytes 196616 | tf_op jit(solution)/shard_map/ppermute | solution.py:655
  42.0 18.7 %all-to-all-start.1 = ((bf16[16,2,64,128]{3,2,1,0:T(8,128)(2,1)}), bf16[16,2,64,128]{3,2,1,0:T(8,128)(2,1)S(1)}, u32[]{:S(2)}, u32[]{:S(2)}) async-start(bf16[16,2,64,128]{3,2,1,0:T(8,128)(2,1)} %return.1), calls=%async_computation.1 | async-start | bytes 1048576 | tf_op jit(solution)/shard_map/all_to_all | solution.py:673
  46.3 0.9 %copy-start.2 = (bf16[128,4,128]{2,1,0:T(4,128)(2,1)S(1)}, bf16[128,4,128]{2,1,0:T(4,128)(2,1)}, u32[]{:S(2)}) copy-start(bf16[128,4,128]{2,1,0:T(4,128)(2,1)} %param.7) | copy-start | bytes 393220
  46.3 1.0 %copy-start.3 = (bf16[128,4,128]{2,1,0:T(4,128)(2,1)S(1)}, bf16[128,4,128]{2,1,0:T(4,128)(2,1)}, u32[]{:S(2)}) copy-start(bf16[128,4,128]{2,1,0:T(4,128)(2,1)} %param.8) | copy-start | bytes 393220
  54.1 0.7 %copy-start.4 = (f32[512,128]{1,0:T(8,128)}, f32[512,128]{1,0:T(8,128)S(1)}, u32[]{:S(2)}) copy-start(f32[512,128]{1,0:T(8,128)S(1)} %get-tuple-element.54.dv_near_ref) | copy-start | bytes 786436
  60.9 5.5 %copy-start.5 = (f32[512,128]{1,0:T(8,128)S(1)}, f32[512,128]{1,0:T(8,128)}, u32[]{:S(2)}) copy-start(f32[512,128]{1,0:T(8,128)} %copy-done.4) | copy-start | bytes 786436
  60.9 5.5 %collective-permute-start.5 = (bf16[4,2,64,128]{3,2,1,0:T(8,128)(2,1)S(1)}, bf16[4,2,64,128]{3,2,1,0:T(8,128)(2,1)S(1)}, u32[]{:S(2)}, u32[]{:S(2)}) collective-permute-start(bf16[4,2,64,128]{3,2,1,0:T(8,128)(2,1)S(1)} %land_sibling.1), channel_id=1, source_target_pairs={{0,1},{1,0},{2,3},{3,2},{4,5},{5,4},{6,7},{7,6},{8,9},{9,8},{10,11... | collective-permute-start | bytes 393224 | tf_op jit(solution)/shard_map/ppermute | solution.py:701

commit v12 on v11

--- a/solution.py
+++ b/solution.py
@@ -283,9 +283,15 @@
             given_ref[block, which] = reorder(order, ref[block * 2 * half:(block + 1) * 2 * half])
 
 
-def send_own_kernel(plan_ref, blocks_ref, out_ref):
+def send_own_kernel(plan_ref, k_ref, v_ref, kept_ref, out_ref, *, kv_heads):
+    blocks, _, half, _ = kept_ref.shape
+    order = half_order(2 * half, kv_heads, lax.axis_index("uly"))
+    for block in range(blocks):
+        span = slice(block * 2 * half, (block + 1) * 2 * half)
+        kept_ref[block, 0] = reorder(order, k_ref[span])
+        kept_ref[block, 1] = reorder(order, v_ref[span])
     for group in range(out_ref.shape[0]):
-        out_ref[group] = blocks_ref[jnp.maximum(plan_ref[group], 0)]
+        out_ref[group] = kept_ref[jnp.maximum(plan_ref[group], 0)]
 
 
 def send_sibling_kernel(plan_ref, blocks_ref, _, out_ref, *, first):
@@ -319,26 +325,13 @@
 
 
 def near_kernel(
-    q_hbm, g_hbm, k_ref, v_ref, given_ref, stat_ref, kept_ref, q_ref, g_ref, sems,
-    *, heads, kv_heads, score_scale
+    q_ref, g_ref, kept_ref, given_ref, stat_ref, *, heads, kv_heads, score_scale
 ):
     blocks = stat_ref.shape[0]
     rows = q_ref.shape[0] // blocks
     half = given_ref.shape[2]
     place = half // kv_heads
-    copies = []
-    for block in range(blocks):
-        span = pl.ds(block * rows, rows)
-        for which, (source, target) in enumerate(((q_hbm, q_ref), (g_hbm, g_ref))):
-            sem = sems.at[which, block]
-            copies.append(pltpu.make_async_copy(source.at[span], target.at[span], sem))
-            copies[-1].start()
     mine = lax.axis_index("uly")
-    order = half_order(2 * half, kv_heads, mine)
-    for block in range(blocks):
-        narrow = slice(block * 2 * half, (block + 1) * 2 * half)
-        kept_ref[block, 0] = reorder(order, k_ref[narrow])
-        kept_ref[block, 1] = reorder(order, v_ref[narrow])
     token, lane_head = lanes(rows, heads, kv_heads)
     key = lax.broadcasted_iota(jnp.int32, (2 * place, rows), 0)
     part = jnp.where(key < place, mine, 1 - mine)
@@ -347,7 +340,6 @@
         span = slice(block * rows, (block + 1) * rows)
         pieces = []
         for which, ref in enumerate((q_ref, g_ref)):
-            copies[2 * block + which].wait()
             both = jnp.concatenate([kept_ref[block, which], given_ref[block, which]], axis=0)
             full = dot_last(both, ref[span])
             pieces.append(
@@ -605,28 +597,16 @@
     gotten = lax.ppermute(given, "uly", swap)
     row_spec = pl.BlockSpec((rows, width), step_rows)
     part_spec = pl.BlockSpec((1, 2, half, width), step_part)
-    stats, kept = pl.pallas_call(
-        partial(near_kernel, **sizes),
-        in_specs=[anywhere, anywhere, vmem, vmem, vmem],
-        out_specs=[vmem, vmem],
-        out_shape=[stat_shape, part_shape],
-        scratch_shapes=[
-            pltpu.VMEM(q2.shape, BF16), pltpu.VMEM(q2.shape, BF16),
-            pltpu.SemaphoreType.DMA((2, mine_blocks)),
-        ],
-        compiler_params=limit,
-        name="near",
-    )(in_hbm(q2), in_hbm(g2), k_here, v_here, given)
-    outgoing = call(
-        send_own_kernel, "send_own", (plan,), (kept,),
-        jax.ShapeDtypeStruct(slots, BF16),
-    )
-    gotten, stats = lax.optimization_barrier((gotten, stats))
+    kept, outgoing = call(
+        partial(send_own_kernel, kv_heads=kv_heads), "send_own", (plan,), (k_here, v_here),
+        [part_shape, jax.ShapeDtypeStruct(slots, BF16)],
+    )
     outgoing = call(
         partial(send_sibling_kernel, first=sib_at), "send_sibling", (plan,), (gotten,),
         jax.ShapeDtypeStruct(slots, BF16), into=outgoing,
     )
     arrived = lax.all_to_all(outgoing, "grp", split_axis=0, concat_axis=0, tiled=True)
+    kept, arrived = lax.optimization_barrier((kept, arrived))
     chunks = 2 if mine_blocks % 2 == 0 else 1
     chunk = mine_blocks // chunks
     chunk_shape = jax.ShapeDtypeStruct((chunk, 2, half, width), BF16)
@@ -634,6 +614,7 @@
         partial(giving_kernel, give_at=give_at), "give", (plan,), (arrived,),
         [chunk_shape] * chunks,
     )
+    stats = call(partial(near_kernel, **sizes), "near", (), (q2, g2, kept, given), stat_shape)
     stats = call(
         partial(mid_kernel, source_at=source_at, seen_at=seen_at, **sizes), "mid", (plan,),
         (q2, g2, stats, arrived), stat_shape,

time: 67.6 us -> 68.3 us (1.010)
  waiting for transfers between devices: 13.2 us -> 17.4 us
  Pallas kernels: 18.8 us -> 16.7 us
  starting transfers between devices: 12.6 us -> 10.9 us
    pallas_call x1 -> x0, Pallas kernels: 2.94 us -> none  [whole_blocks(): pl.pallas_call(partial(near_kernel, **sizes), in_specs=[anywhere, anywher...]
    ppermute x1, waiting for transfers between devices: 0.01 us -> 2.14 us  [whole_blocks(): gotten = lax.ppermute(given, 'uly', swap)]
    ppermute x2, waiting for transfers between devices: 1.64 us -> 2.51 us  [whole_blocks(): from_sib = [lax.ppermute(part, 'uly', swap) for part in grads]]
    pallas_call x12 -> x13, Pallas kernels: 6.69 us -> 7.51 us  [call(): pl.pallas_call(kernel, in_specs=[smem] * len(scalars) + [vmem] * (len(ope...]
  transfers between devices with their start and end apart: 7 -> 7, of which waited for: 5 -> 6; matrix products, arithmetic and copies ran while one was open for 0% -> 0% of each run, Pallas kernels for 23% -> 20%
where the time goes in v12:
time: 68.3 us; the launch traced here: 68 us
  blocking collectives  20.5 us (30%)
  waiting for transfers between devices  17.4 us (25%)
  Pallas kernels  16.7 us (24%)
  starting transfers between devices  10.9 us (16%)
  local copies, waits for them, and re-layouts  1.65 us (2%)
  between operations  0.77 us (1%)
    all_to_all x1, blocking collectives, whole_blocks(): lax.all_to_all(outgoing, 'grp', split_axis=0, concat_axis=0, tiled=True)  20.5 us
    pallas_call x13, Pallas kernels, call(): pl.pallas_call(kernel, in_specs=[smem] * len(scalars) + [vmem] * (len(ope...  7.51 us
    pallas_call x1, Pallas kernels, whole_blocks(): pl.pallas_call(partial(local_kernel, seen_at=seen_at, **sizes), grid_spec...  6.86 us
    all_to_all x1, waiting for transfers between devices, whole_blocks(): lax.all_to_all(returning, 'grp', split_axis=0, concat_axis=0, tiled=True)  5.93 us
    ppermute x1, waiting for transfers between devices, whole_blocks(): back = lax.ppermute(give, 'uly', swap)  4.96 us
    all_to_all x1, starting transfers between devices, whole_blocks(): lax.all_to_all(returning, 'grp', split_axis=0, concat_axis=0, tiled=True)  3.64 us
    ppermute x1, starting transfers between devices, whole_blocks(): gotten = lax.ppermute(given, 'uly', swap)  3.03 us
    ppermute x2, waiting for transfers between devices, whole_blocks(): from_sib = [lax.ppermute(part, 'uly', swap) for part in grads]  2.51 us
  transfers between devices with their start and end apart: 7, of which 6 were waited for; matrix products, arithmetic and copies ran while one was open for 0% of the time, Pallas kernels for 20%

profile of v12, /device:TPU:0, one launch (start us, length us, event | category | flops | bytes accessed | tf_op | source)
XLA Modules:
  0.0 68.0 jit_solution(13391160792219452132)
XLA Ops:
  0.6 1.3 %pack.1 = (bf16[512,128]{1,0:T(8,128)(2,1)S(1)}, bf16[512,128]{1,0:T(8,128)(2,1)S(1)}, bf16[4,2,64,128]{3,2,1,0:T(8,128)(2,1)S(1)}) custom-call(bf16[512,128]{1,0:T(8,128)(2,1)} %bitcast.23, bf16[512,128]{1,0:T(8,128)(2,1)} %bitcast.25), custom_call_target="tpu_custom_call" | custom-call | tf_op jit(solution)/shard_map/pack/pallas_call | solution.py:580
  1.9 3.0 %collective-permute-start = (bf16[4,2,64,128]{3,2,1,0:T(8,128)(2,1)S(1)}, bf16[4,2,64,128]{3,2,1,0:T(8,128)(2,1)S(1)}, u32[]{:S(2)}, u32[]{:S(2)}) collective-permute-start(bf16[4,2,64,128]{3,2,1,0:T(8,128)(2,1)S(1)} %get-tuple-element.34.given_ref), channel_id=1, source_target_pairs={{0,1},{1,0},{2,3},{3,2},{4,5},{5,4},{6,7},{7,6},{8,9},{9,8},{10,11... | collective-permute-start | bytes 393224 | tf_op jit(solution)/shard_map/ppermute | solution.py:597
  4.9 1.1 %plan.1.plan_ref = s32[44]{0:T(128)S(4)} custom-call(s32[128]{0:T(128)} %bitcast.31, s32[128]{0:T(128)} %counts_ref.1), custom_call_target="tpu_custom_call" | custom-call | tf_op jit(solution)/shard_map/plan/pallas_call | solution.py:589
  6.0 0.2 send_own.1
  6.3 2.1 %collective-permute-done.blocks_ref = bf16[4,2,64,128]{3,2,1,0:T(8,128)(2,1)S(1)} collective-permute-done((bf16[4,2,64,128]{3,2,1,0:T(8,128)(2,1)S(1)}, bf16[4,2,64,128]{3,2,1,0:T(8,128)(2,1)S(1)}, u32[]{:S(2)}, u32[]{:S(2)}) %collective-permute-start) | collective-permute-done | bytes 131104 | tf_op jit(solution)/shard_map/ppermute | solution.py:597
  8.4 20.5 %all_to_all.10.arrived_ref.mine_ref = bf16[16,2,64,128]{3,2,1,0:T(8,128)(2,1)S(1)} all-to-all(bf16[16,2,64,128]{3,2,1,0:T(8,128)(2,1)S(1)} %send_sibling.1), channel_id=1, replica_groups=mesh['grp'=16,'uly'=2] {'grp'}, dimensions={0} | all-to-all | bytes 1048576 | tf_op jit(solution)/shard_map/all_to_all | solution.py:608
  29.0 1.7 %collective-permute-start.1 = (bf16[2,2,64,128]{3,2,1,0:T(8,128)(2,1)S(1)}, bf16[2,2,64,128]{3,2,1,0:T(8,128)(2,1)S(1)}, u32[]{:S(2)}, u32[]{:S(2)}) collective-permute-start(bf16[2,2,64,128]{3,2,1,0:T(8,128)(2,1)S(1)} %get-tuple-element.40), channel_id=1, source_target_pairs={{0,1},{1,0},{2,3},{3,2},{4,5},{5,4},{6,7},{7,6},{8,9},{9,8},{10,11... | collective-permute-start | bytes 196616 | tf_op jit(solution)/shard_map/ppermute | solution.py:626
  30.6 0.7 %near.1.stat_ref = f32[4,8,1024]{2,1,0:T(8,128)S(1)} custom-call(bf16[4096,128]{1,0:T(8,128)(2,1)S(1)} %bitcast.9, bf16[4096,128]{1,0:T(8,128)(2,1)S(1)} %bitcast.16, bf16[4,2,64,128]{3,2,1,0:T(8,128)(2,1)S(1)} %get-tuple-element.38.kept_ref, bf16[4,2,64,128]{3,2,1,0:T(8,128)(2,1)S(1)} %get-tuple-element.34.given_ref), custom_call_target="tpu_custom_call" | custom-call | tf_op jit(solution)/shard_map/near/pallas_call | solution.py:560
  31.4 0.9 %mid.1.stat_ref = f32[4,8,1024]{2,1,0:T(8,128)S(1)} custom-call(s32[44]{0:T(128)S(4)} %plan.1.plan_ref, bf16[4096,128]{1,0:T(8,128)(2,1)S(1)} %bitcast.10, bf16[4096,128]{1,0:T(8,128)(2,1)S(1)} %bitcast.17, f32[4,8,1024]{2,1,0:T(8,128)S(1)} %near.1.stat_ref, bf16[16,2,64,128]{3,2,1,0:T(8,128)(2,1)S(1)} %all_to_all.10.arrived_ref.mine_ref), custom_call_target="tpu_custom_call" | custom-call | tf_op jit(solution)/shard_map/mid/pallas_call | solution.py:560
  32.2 0.5 collective-permute-start.3
  32.7 0.6 collective-permute-done.1.other_ref
  33.3 0.9 %far.2 = (bf16[2,2,64,128]{3,2,1,0:T(8,128)(2,1)S(1)}, f32[2,8,1024]{2,1,0:T(8,128)S(1)}) custom-call(s32[44]{0:T(128)S(4)} %plan.1.plan_ref, bf16[4096,128]{1,0:T(8,128)(2,1)S(1)} %bitcast.11, bf16[4096,128]{1,0:T(8,128)(2,1)S(1)} %bitcast.18, f32[4,8,1024]{2,1,0:T(8,128)S(1)} %mid.1.stat_ref, bf16[2,2,64,128]{3,2,1,0:T(8,128)(2,1)S(1)} %collective-permute-done.1.other_ref), custom_call_target="tpu_custom_call" | custom-call | tf_op jit(solution)/shard_map/far/pallas_call | solution.py:560
  34.2 1.7 %collective-permute-start.2 = (bf16[2,2,64,128]{3,2,1,0:T(8,128)(2,1)S(1)}, bf16[2,2,64,128]{3,2,1,0:T(8,128)(2,1)S(1)}, u32[]{:S(2)}, u32[]{:S(2)}) collective-permute-start(bf16[2,2,64,128]{3,2,1,0:T(8,128)(2,1)S(1)} %get-tuple-element.41), channel_id=1, source_target_pairs={{0,1},{1,0},{2,3},{3,2},{4,5},{5,4},{6,7},{7,6},{8,9},{9,8},{10,11... | collective-permute-start | bytes 196616 | tf_op jit(solution)/shard_map/ppermute | solution.py:636
  35.9 1.3 %collective-permute-done.3.other_ref = bf16[2,2,64,128]{3,2,1,0:T(8,128)(2,1)S(1)} collective-permute-done((bf16[2,2,64,128]{3,2,1,0:T(8,128)(2,1)S(1)}, bf16[2,2,64,128]{3,2,1,0:T(8,128)(2,1)S(1)}, u32[]{:S(2)}, u32[]{:S(2)}) %collective-permute-start.3) | collective-permute-done | bytes 65568 | tf_op jit(solution)/shard_map/ppermute | solution.py:626
  37.2 0.9 %far.3 = (bf16[2,2,64,128]{3,2,1,0:T(8,128)(2,1)S(1)}, f32[2,8,1024]{2,1,0:T(8,128)S(1)}) custom-call(s32[44]{0:T(128)S(4)} %plan.1.plan_ref, bf16[4096,128]{1,0:T(8,128)(2,1)S(1)} %bitcast.12, bf16[4096,128]{1,0:T(8,128)(2,1)S(1)} %bitcast.19, f32[4,8,1024]{2,1,0:T(8,128)S(1)} %mid.1.stat_ref, bf16[2,2,64,128]{3,2,1,0:T(8,128)(2,1)S(1)} %collective-permute-done.3.other_ref), custom_call_target="tpu_custom_call" | custom-call | tf_op jit(solution)/shard_map/far/pallas_call | solution.py:560
  38.1 0.1 collective-permute-start.4
  38.2 0.9 %mine.3.refs_1_ = bf16[2,2,64,128]{3,2,1,0:T(8,128)(2,1)S(1)} custom-call(s32[44]{0:T(128)S(4)} %plan.1.plan_ref, bf16[4096,128]{1,0:T(8,128)(2,1)S(1)} %bitcast.13, bf16[4096,128]{1,0:T(8,128)(2,1)S(1)} %bitcast.20, bf16[16,2,64,128]{3,2,1,0:T(8,128)(2,1)S(1)} %all_to_all.10.arrived_ref.mine_ref, f32[2,8,1024]{2,1,0:T(8,128)S(1)} %get-tuple-element.45.stat_ref), custom_call_target="tpu_custom_call" | custom-call | tf_op jit(solution)/shard_map/mine/pallas_call | solution.py:560
  39.1 0.9 %mine.2.refs_0_ = bf16[2,2,64,128]{3,2,1,0:T(8,128)(2,1)S(1)} custom-call(s32[44]{0:T(128)S(4)} %plan.1.plan_ref, bf16[4096,128]{1,0:T(8,128)(2,1)S(1)} %bitcast.14, bf16[4096,128]{1,0:T(8,128)(2,1)S(1)} %bitcast.21, bf16[16,2,64,128]{3,2,1,0:T(8,128)(2,1)S(1)} %all_to_all.10.arrived_ref.mine_ref, f32[2,8,1024]{2,1,0:T(8,128)S(1)} %get-tuple-element.43.stat_ref), custom_call_target="tpu_custom_call" | custom-call | tf_op jit(solution)/shard_map/mine/pallas_call | solution.py:560
  39.9 2.5 %collective-permute-done.4.refs_3_ = bf16[2,2,64,128]{3,2,1,0:T(8,128)(2,1)S(1)} collective-permute-done((bf16[2,2,64,128]{3,2,1,0:T(8,128)(2,1)S(1)}, bf16[2,2,64,128]{3,2,1,0:T(8,128)(2,1)S(1)}, u32[]{:S(2)}, u32[]{:S(2)}) %collective-permute-start.4) | collective-permute-done | bytes 65568 | tf_op jit(solution)/shard_map/ppermute | solution.py:636
  42.4 0.8 %return.1 = bf16[16,2,64,128]{3,2,1,0:T(8,128)(2,1)} custom-call(s32[44]{0:T(128)S(4)} %plan.1.plan_ref, bf16[2,2,64,128]{3,2,1,0:T(8,128)(2,1)S(1)} %mine.2.refs_0_, bf16[2,2,64,128]{3,2,1,0:T(8,128)(2,1)S(1)} %mine.3.refs_1_, bf16[2,2,64,128]{3,2,1,0:T(8,128)(2,1)S(1)} %collective-permute-done.2.refs_2_, ...), custom_call_target="tpu_custom_call" | custom-call | tf_op jit(solution)/shard_map/return/pallas_call | solution.py:560
  43.2 3.6 %all-to-all-start.1 = ((bf16[16,2,64,128]{3,2,1,0:T(8,128)(2,1)}), bf16[16,2,64,128]{3,2,1,0:T(8,128)(2,1)S(1)}, u32[]{:S(2)}, u32[]{:S(2)}) async-start(bf16[16,2,64,128]{3,2,1,0:T(8,128)(2,1)} %return.1), calls=%async_computation.1 | async-start | bytes 1048576 | tf_op jit(solution)/shard_map/all_to_all | solution.py:654
  46.9 0.0 copy-start.2
  46.9 0.9 %copy-done.2 = bf16[128,4,128]{2,1,0:T(4,128)(2,1)S(1)} copy-done((bf16[128,4,128]{2,1,0:T(4,128)(2,1)S(1)}, bf16[128,4,128]{2,1,0:T(4,128)(2,1)}, u32[]{:S(2)}) %copy-start.2) | copy-done | bytes 131096
  47.8 0.1 copy-done.3
  47.9 6.9 %local.1 = (bf16[4096,128]{1,0:T(8,128)(2,1)}, bf16[4096,128]{1,0:T(8,128)(2,1)}, f32[512,128]{1,0:T(8,128)S(1)}, f32[512,128]{1,0:T(8,128)S(1)}) custom-call(s32[44]{0:T(128)S(4)} %plan.1.plan_ref, bf16[4096,128]{1,0:T(8,128)(2,1)S(1)} %bitcast.15, bf16[4096,128]{1,0:T(8,128)(2,1)S(1)} %bitcast.22, bf16[512,128]{1,0:T(8,128)(2,1)S(1)} %bitcast.24, ...), custom_call_target="tpu_custom_call" | custom-call | tf_op jit(solution)/shard_map/local/pallas_call | solution.py:660
  54.7 0.7 %copy-done.4 = f32[512,128]{1,0:T(8,128)} copy-done((f32[512,128]{1,0:T(8,128)}, f32[512,128]{1,0:T(8,128)S(1)}, u32[]{:S(2)}) %copy-start.4) | copy-done | bytes 262168
  55.4 5.9 %all-to-all-done.1.landed_ref = bf16[16,2,64,128]{3,2,1,0:T(8,128)(2,1)S(1)} async-done(((bf16[16,2,64,128]{3,2,1,0:T(8,128)(2,1)}), bf16[16,2,64,128]{3,2,1,0:T(8,128)(2,1)S(1)}, u32[]{:S(2)}, u32[]{:S(2)}) %all-to-all-start.1) | async-done | bytes 524320 | tf_op jit(solution)/shard_map/all_to_all | solution.py:654
  61.4 0.2 land_sibling.1
  61.5 0.3 collective-permute-start.5
  61.9 0.2 land_own.1.own_ref
  62.1 5.0 %collective-permute-done.5.back_ref = bf16[4,2,64,128]{3,2,1,0:T(8,128)(2,1)S(1)} collective-permute-done((bf16[4,2,64,128]{3,2,1,0:T(8,128)(2,1)S(1)}, bf16[4,2,64,128]{3,2,1,0:T(8,128)(2,1)S(1)}, u32[]{:S(2)}, u32[]{:S(2)}) %collective-permute-start.5) | collective-permute-done | bytes 131104 | tf_op jit(solution)/shard_map/ppermute | solution.py:682
  67.0 1.0 %finish.1 = (bf16[512,128]{1,0:T(8,128)(2,1)}, bf16[512,128]{1,0:T(8,128)(2,1)}) custom-call(f32[512,128]{1,0:T(8,128)S(1)} %get-tuple-element.53.dk_near_ref, f32[512,128]{1,0:T(8,128)S(1)} %copy-done.5, f32[4,2,64,128]{3,2,1,0:T(8,128)S(1)} %land_own.1.own_ref, bf16[4,2,64,128]{3,2,1,0:T(8,128)(2,1)S(1)} %collective-permute-done.5.back_ref), custom_call_target="tpu_custom_call" | custom-call | tf_op jit(solution)/shard_map/finish/pallas_call | solution.py:560
  (12 shorter events, 0.0 us)
Async XLA Ops:
  1.9 6.5 %collective-permute-start = (bf16[4,2,64,128]{3,2,1,0:T(8,128)(2,1)S(1)}, bf16[4,2,64,128]{3,2,1,0:T(8,128)(2,1)S(1)}, u32[]{:S(2)}, u32[]{:S(2)}) collective-permute-start(bf16[4,2,64,128]{3,2,1,0:T(8,128)(2,1)S(1)} %get-tuple-element.34.given_ref), channel_id=1, source_target_pairs={{0,1},{1,0},{2,3},{3,2},{4,5},{5,4},{6,7},{7,6},{8,9},{9,8},{10,11... | collective-permute-start | bytes 393224 | tf_op jit(solution)/shard_map/ppermute | solution.py:597
  8.4 22.2 %copy-start.1 = (bf16[128,32,128]{2,1,0:T(8,128)(2,1)S(1)}, bf16[128,32,128]{2,1,0:T(8,128)(2,1)}, u32[]{:S(2)}) copy-start(bf16[128,32,128]{2,1,0:T(8,128)(2,1)} %param.9) | copy-start | bytes 3145732
  8.4 22.2 %copy-start = (bf16[128,32,128]{2,1,0:T(8,128)(2,1)S(1)}, bf16[128,32,128]{2,1,0:T(8,128)(2,1)}, u32[]{:S(2)}) copy-start(bf16[128,32,128]{2,1,0:T(8,128)(2,1)} %param.6) | copy-start | bytes 3145732
  29.0 4.3 %collective-permute-start.1 = (bf16[2,2,64,128]{3,2,1,0:T(8,128)(2,1)S(1)}, bf16[2,2,64,128]{3,2,1,0:T(8,128)(2,1)S(1)}, u32[]{:S(2)}, u32[]{:S(2)}) collective-permute-start(bf16[2,2,64,128]{3,2,1,0:T(8,128)(2,1)S(1)} %get-tuple-element.40), channel_id=1, source_target_pairs={{0,1},{1,0},{2,3},{3,2},{4,5},{5,4},{6,7},{7,6},{8,9},{9,8},{10,11... | collective-permute-start | bytes 196616 | tf_op jit(solution)/shard_map/ppermute | solution.py:626
  32.2 4.9 %collective-permute-start.3 = (bf16[2,2,64,128]{3,2,1,0:T(8,128)(2,1)S(1)}, bf16[2,2,64,128]{3,2,1,0:T(8,128)(2,1)S(1)}, u32[]{:S(2)}, u32[]{:S(2)}) collective-permute-start(bf16[2,2,64,128]{3,2,1,0:T(8,128)(2,1)S(1)} %get-tuple-element.44), channel_id=1, source_target_pairs={{0,1},{1,0},{2,3},{3,2},{4,5},{5,4},{6,7},{7,6},{8,9},{9,8},{10,11... | collective-permute-start | bytes 196616 | tf_op jit(solution)/shard_map/ppermute | solution.py:626
  34.2 4.8 %collective-permute-start.2 = (bf16[2,2,64,128]{3,2,1,0:T(8,128)(2,1)S(1)}, bf16[2,2,64,128]{3,2,1,0:T(8,128)(2,1)S(1)}, u32[]{:S(2)}, u32[]{:S(2)}) collective-permute-start(bf16[2,2,64,128]{3,2,1,0:T(8,128)(2,1)S(1)} %get-tuple-element.41), channel_id=1, source_target_pairs={{0,1},{1,0},{2,3},{3,2},{4,5},{5,4},{6,7},{7,6},{8,9},{9,8},{10,11... | collective-permute-start | bytes 196616 | tf_op jit(solution)/shard_map/ppermute | solution.py:636
  38.1 4.3 %collective-permute-start.4 = (bf16[2,2,64,128]{3,2,1,0:T(8,128)(2,1)S(1)}, bf16[2,2,64,128]{3,2,1,0:T(8,128)(2,1)S(1)}, u32[]{:S(2)}, u32[]{:S(2)}) collective-permute-start(bf16[2,2,64,128]{3,2,1,0:T(8,128)(2,1)S(1)} %get-tuple-element.47), channel_id=1, source_target_pairs={{0,1},{1,0},{2,3},{3,2},{4,5},{5,4},{6,7},{7,6},{8,9},{9,8},{10,11... | collective-permute-start | bytes 196616 | tf_op jit(solution)/shard_map/ppermute | solution.py:636
  43.2 18.1 %all-to-all-start.1 = ((bf16[16,2,64,128]{3,2,1,0:T(8,128)(2,1)}), bf16[16,2,64,128]{3,2,1,0:T(8,128)(2,1)S(1)}, u32[]{:S(2)}, u32[]{:S(2)}) async-start(bf16[16,2,64,128]{3,2,1,0:T(8,128)(2,1)} %return.1), calls=%async_computation.1 | async-start | bytes 1048576 | tf_op jit(solution)/shard_map/all_to_all | solution.py:654
  46.9 0.9 %copy-start.2 = (bf16[128,4,128]{2,1,0:T(4,128)(2,1)S(1)}, bf16[128,4,128]{2,1,0:T(4,128)(2,1)}, u32[]{:S(2)}) copy-start(bf16[128,4,128]{2,1,0:T(4,128)(2,1)} %param.7) | copy-start | bytes 393220
  46.9 1.0 %copy-start.3 = (bf16[128,4,128]{2,1,0:T(4,128)(2,1)S(1)}, bf16[128,4,128]{2,1,0:T(4,128)(2,1)}, u32[]{:S(2)}) copy-start(bf16[128,4,128]{2,1,0:T(4,128)(2,1)} %param.8) | copy-start | bytes 393220
  54.7 0.7 %copy-start.4 = (f32[512,128]{1,0:T(8,128)}, f32[512,128]{1,0:T(8,128)S(1)}, u32[]{:S(2)}) copy-start(f32[512,128]{1,0:T(8,128)S(1)} %get-tuple-element.54.dv_near_ref) | copy-start | bytes 786436
  61.5 5.5 %copy-start.5 = (f32[512,128]{1,0:T(8,128)S(1)}, f32[512,128]{1,0:T(8,128)}, u32[]{:S(2)}) copy-start(f32[512,128]{1,0:T(8,128)} %copy-done.4) | copy-start | bytes 786436
  61.5 5.5 %collective-permute-start.5 = (bf16[4,2,64,128]{3,2,1,0:T(8,128)(2,1)S(1)}, bf16[4,2,64,128]{3,2,1,0:T(8,128)(2,1)S(1)}, u32[]{:S(2)}, u32[]{:S(2)}) collective-permute-start(bf16[4,2,64,128]{3,2,1,0:T(8,128)(2,1)S(1)} %land_sibling.1), channel_id=1, source_target_pairs={{0,1},{1,0},{2,3},{3,2},{4,5},{5,4},{6,7},{7,6},{8,9},{9,8},{10,11... | collective-permute-start | bytes 393224 | tf_op jit(solution)/shard_map/ppermute | solution.py:682

commit v13 on v12

--- a/solution.py
+++ b/solution.py
@@ -615,15 +615,15 @@
         [chunk_shape] * chunks,
     )
     stats = call(partial(near_kernel, **sizes), "near", (), (q2, g2, kept, given), stat_shape)
-    stats = call(
-        partial(mid_kernel, source_at=source_at, seen_at=seen_at, **sizes), "mid", (plan,),
-        (q2, g2, stats, arrived), stat_shape,
-    )
     others = []
     for part in giving:
         if others:
             part, stats = lax.optimization_barrier((part, stats))
         others.append(lax.ppermute(part, "uly", swap))
+    stats = call(
+        partial(mid_kernel, source_at=source_at, seen_at=seen_at, **sizes), "mid", (plan,),
+        (q2, g2, stats, arrived), stat_shape,
+    )
     grads, final = [], []
     for at, other in enumerate(others):
         grad, stat = call(

time: 68.3 us -> 67.9 us (level)
  waiting for transfers between devices: 17.4 us -> 16.2 us
  starting transfers between devices: 10.9 us -> 11.8 us
    ppermute x2, waiting for transfers between devices: 1.86 us -> 0.59 us  [whole_blocks(): others.append(lax.ppermute(part, 'uly', swap))]
    ppermute x2, starting transfers between devices: 1.73 us -> 2.44 us  [whole_blocks(): from_sib = [lax.ppermute(part, 'uly', swap) for part in grads]]
where the time goes in v13:
time: 67.9 us; the launch traced here: 67.7 us
  blocking collectives  20.5 us (30%)
  Pallas kernels  16.7 us (25%)
  waiting for transfers between devices  16.2 us (24%)
  starting transfers between devices  11.8 us (17%)
  local copies, waits for them, and re-layouts  1.65 us (2%)
  between operations  0.76 us (1%)
    all_to_all x1, blocking collectives, whole_blocks(): lax.all_to_all(outgoing, 'grp', split_axis=0, concat_axis=0, tiled=True)  20.5 us
    pallas_call x13, Pallas kernels, call(): pl.pallas_call(kernel, in_specs=[smem] * len(scalars) + [vmem] * (len(ope...  7.48 us
    pallas_call x1, Pallas kernels, whole_blocks(): pl.pallas_call(partial(local_kernel, seen_at=seen_at, **sizes), grid_spec...  6.86 us
    all_to_all x1, waiting for transfers between devices, whole_blocks(): lax.all_to_all(returning, 'grp', split_axis=0, concat_axis=0, tiled=True)  5.93 us
    ppermute x1, waiting for transfers between devices, whole_blocks(): back = lax.ppermute(give, 'uly', swap)  5.05 us
    all_to_all x1, starting transfers between devices, whole_blocks(): lax.all_to_all(returning, 'grp', split_axis=0, concat_axis=0, tiled=True)  3.92 us
    ppermute x1, starting transfers between devices, whole_blocks(): gotten = lax.ppermute(given, 'uly', swap)  3.03 us
    ppermute x2, waiting for transfers between devices, whole_blocks(): from_sib = [lax.ppermute(part, 'uly', swap) for part in grads]  2.52 us
  transfers between devices with their start and end apart: 7, of which 6 were waited for; matrix products, arithmetic and copies ran while one was open for 0% of the time, Pallas kernels for 20%

profile of v13, /device:TPU:0, one launch (start us, length us, event | category | flops | bytes accessed | tf_op | source)
XLA Modules:
  0.0 67.7 jit_solution(10698611372560721122)
XLA Ops:
  0.6 1.3 %pack.1 = (bf16[512,128]{1,0:T(8,128)(2,1)S(1)}, bf16[512,128]{1,0:T(8,128)(2,1)S(1)}, bf16[4,2,64,128]{3,2,1,0:T(8,128)(2,1)S(1)}) custom-call(bf16[512,128]{1,0:T(8,128)(2,1)} %bitcast.23, bf16[512,128]{1,0:T(8,128)(2,1)} %bitcast.25), custom_call_target="tpu_custom_call" | custom-call | tf_op jit(solution)/shard_map/pack/pallas_call | solution.py:580
  1.9 3.0 %collective-permute-start = (bf16[4,2,64,128]{3,2,1,0:T(8,128)(2,1)S(1)}, bf16[4,2,64,128]{3,2,1,0:T(8,128)(2,1)S(1)}, u32[]{:S(2)}, u32[]{:S(2)}) collective-permute-start(bf16[4,2,64,128]{3,2,1,0:T(8,128)(2,1)S(1)} %get-tuple-element.34.given_ref), channel_id=1, source_target_pairs={{0,1},{1,0},{2,3},{3,2},{4,5},{5,4},{6,7},{7,6},{8,9},{9,8},{10,11... | collective-permute-start | bytes 393224 | tf_op jit(solution)/shard_map/ppermute | solution.py:597
  4.9 1.1 %plan.1.plan_ref = s32[44]{0:T(128)S(4)} custom-call(s32[128]{0:T(128)} %bitcast.31, s32[128]{0:T(128)} %counts_ref.1), custom_call_target="tpu_custom_call" | custom-call | tf_op jit(solution)/shard_map/plan/pallas_call | solution.py:589
  6.0 0.2 send_own.1
  6.3 2.1 %collective-permute-done.blocks_ref = bf16[4,2,64,128]{3,2,1,0:T(8,128)(2,1)S(1)} collective-permute-done((bf16[4,2,64,128]{3,2,1,0:T(8,128)(2,1)S(1)}, bf16[4,2,64,128]{3,2,1,0:T(8,128)(2,1)S(1)}, u32[]{:S(2)}, u32[]{:S(2)}) %collective-permute-start) | collective-permute-done | bytes 131104 | tf_op jit(solution)/shard_map/ppermute | solution.py:597
  8.4 20.5 %all_to_all.10.arrived_ref.mine_ref = bf16[16,2,64,128]{3,2,1,0:T(8,128)(2,1)S(1)} all-to-all(bf16[16,2,64,128]{3,2,1,0:T(8,128)(2,1)S(1)} %send_sibling.1), channel_id=1, replica_groups=mesh['grp'=16,'uly'=2] {'grp'}, dimensions={0} | all-to-all | bytes 1048576 | tf_op jit(solution)/shard_map/all_to_all | solution.py:608
  29.0 1.7 %collective-permute-start.1 = (bf16[2,2,64,128]{3,2,1,0:T(8,128)(2,1)S(1)}, bf16[2,2,64,128]{3,2,1,0:T(8,128)(2,1)S(1)}, u32[]{:S(2)}, u32[]{:S(2)}) collective-permute-start(bf16[2,2,64,128]{3,2,1,0:T(8,128)(2,1)S(1)} %get-tuple-element.40), channel_id=1, source_target_pairs={{0,1},{1,0},{2,3},{3,2},{4,5},{5,4},{6,7},{7,6},{8,9},{9,8},{10,11... | collective-permute-start | bytes 196616 | tf_op jit(solution)/shard_map/ppermute | solution.py:622
  30.6 0.7 %near.1.stat_ref = f32[4,8,1024]{2,1,0:T(8,128)S(1)} custom-call(bf16[4096,128]{1,0:T(8,128)(2,1)S(1)} %bitcast.9, bf16[4096,128]{1,0:T(8,128)(2,1)S(1)} %bitcast.16, bf16[4,2,64,128]{3,2,1,0:T(8,128)(2,1)S(1)} %get-tuple-element.38.kept_ref, bf16[4,2,64,128]{3,2,1,0:T(8,128)(2,1)S(1)} %get-tuple-element.34.given_ref), custom_call_target="tpu_custom_call" | custom-call | tf_op jit(solution)/shard_map/near/pallas_call | solution.py:560
  31.4 0.5 collective-permute-start.3
  31.8 0.9 %mid.1.stat_ref = f32[4,8,1024]{2,1,0:T(8,128)S(1)} custom-call(s32[44]{0:T(128)S(4)} %plan.1.plan_ref, bf16[4096,128]{1,0:T(8,128)(2,1)S(1)} %bitcast.10, bf16[4096,128]{1,0:T(8,128)(2,1)S(1)} %bitcast.17, f32[4,8,1024]{2,1,0:T(8,128)S(1)} %near.1.stat_ref, bf16[16,2,64,128]{3,2,1,0:T(8,128)(2,1)S(1)} %all_to_all.10.arrived_ref.mine_ref), custom_call_target="tpu_custom_call" | custom-call | tf_op jit(solution)/shard_map/mid/pallas_call | solution.py:560
  32.7 0.6 collective-permute-done.1.other_ref
  33.3 0.9 %far.2 = (bf16[2,2,64,128]{3,2,1,0:T(8,128)(2,1)S(1)}, f32[2,8,1024]{2,1,0:T(8,128)S(1)}) custom-call(s32[44]{0:T(128)S(4)} %plan.1.plan_ref, bf16[4096,128]{1,0:T(8,128)(2,1)S(1)} %bitcast.11, bf16[4096,128]{1,0:T(8,128)(2,1)S(1)} %bitcast.18, f32[4,8,1024]{2,1,0:T(8,128)S(1)} %mid.1.stat_ref, bf16[2,2,64,128]{3,2,1,0:T(8,128)(2,1)S(1)} %collective-permute-done.1.other_ref), custom_call_target="tpu_custom_call" | custom-call | tf_op jit(solution)/shard_map/far/pallas_call | solution.py:560
  34.2 2.4 %collective-permute-start.2 = (bf16[2,2,64,128]{3,2,1,0:T(8,128)(2,1)S(1)}, bf16[2,2,64,128]{3,2,1,0:T(8,128)(2,1)S(1)}, u32[]{:S(2)}, u32[]{:S(2)}) collective-permute-start(bf16[2,2,64,128]{3,2,1,0:T(8,128)(2,1)S(1)} %get-tuple-element.41), channel_id=1, source_target_pairs={{0,1},{1,0},{2,3},{3,2},{4,5},{5,4},{6,7},{7,6},{8,9},{9,8},{10,11... | collective-permute-start | bytes 196616 | tf_op jit(solution)/shard_map/ppermute | solution.py:636
  36.6 0.9 %far.3 = (bf16[2,2,64,128]{3,2,1,0:T(8,128)(2,1)S(1)}, f32[2,8,1024]{2,1,0:T(8,128)S(1)}) custom-call(s32[44]{0:T(128)S(4)} %plan.1.plan_ref, bf16[4096,128]{1,0:T(8,128)(2,1)S(1)} %bitcast.12, bf16[4096,128]{1,0:T(8,128)(2,1)S(1)} %bitcast.19, f32[4,8,1024]{2,1,0:T(8,128)S(1)} %mid.1.stat_ref, bf16[2,2,64,128]{3,2,1,0:T(8,128)(2,1)S(1)} %collective-permute-done.3.other_ref), custom_call_target="tpu_custom_call" | custom-call | tf_op jit(solution)/shard_map/far/pallas_call | solution.py:560
  37.5 0.1 collective-permute-start.4
  37.6 0.9 %mine.3.refs_1_ = bf16[2,2,64,128]{3,2,1,0:T(8,128)(2,1)S(1)} custom-call(s32[44]{0:T(128)S(4)} %plan.1.plan_ref, bf16[4096,128]{1,0:T(8,128)(2,1)S(1)} %bitcast.13, bf16[4096,128]{1,0:T(8,128)(2,1)S(1)} %bitcast.20, bf16[16,2,64,128]{3,2,1,0:T(8,128)(2,1)S(1)} %all_to_all.10.arrived_ref.mine_ref, f32[2,8,1024]{2,1,0:T(8,128)S(1)} %get-tuple-element.45.stat_ref), custom_call_target="tpu_custom_call" | custom-call | tf_op jit(solution)/shard_map/mine/pallas_call | solution.py:560
  38.5 1.0 %collective-permute-done.2.refs_2_ = bf16[2,2,64,128]{3,2,1,0:T(8,128)(2,1)S(1)} collective-permute-done((bf16[2,2,64,128]{3,2,1,0:T(8,128)(2,1)S(1)}, bf16[2,2,64,128]{3,2,1,0:T(8,128)(2,1)S(1)}, u32[]{:S(2)}, u32[]{:S(2)}) %collective-permute-start.2) | collective-permute-done | bytes 65568 | tf_op jit(solution)/shard_map/ppermute | solution.py:636
  39.5 0.9 %mine.2.refs_0_ = bf16[2,2,64,128]{3,2,1,0:T(8,128)(2,1)S(1)} custom-call(s32[44]{0:T(128)S(4)} %plan.1.plan_ref, bf16[4096,128]{1,0:T(8,128)(2,1)S(1)} %bitcast.14, bf16[4096,128]{1,0:T(8,128)(2,1)S(1)} %bitcast.21, bf16[16,2,64,128]{3,2,1,0:T(8,128)(2,1)S(1)} %all_to_all.10.arrived_ref.mine_ref, f32[2,8,1024]{2,1,0:T(8,128)S(1)} %get-tuple-element.43.stat_ref), custom_call_target="tpu_custom_call" | custom-call | tf_op jit(solution)/shard_map/mine/pallas_call | solution.py:560
  40.4 1.5 %collective-permute-done.4.refs_3_ = bf16[2,2,64,128]{3,2,1,0:T(8,128)(2,1)S(1)} collective-permute-done((bf16[2,2,64,128]{3,2,1,0:T(8,128)(2,1)S(1)}, bf16[2,2,64,128]{3,2,1,0:T(8,128)(2,1)S(1)}, u32[]{:S(2)}, u32[]{:S(2)}) %collective-permute-start.4) | collective-permute-done | bytes 65568 | tf_op jit(solution)/shard_map/ppermute | solution.py:636
  41.8 0.8 %return.1 = bf16[16,2,64,128]{3,2,1,0:T(8,128)(2,1)} custom-call(s32[44]{0:T(128)S(4)} %plan.1.plan_ref, bf16[2,2,64,128]{3,2,1,0:T(8,128)(2,1)S(1)} %mine.2.refs_0_, bf16[2,2,64,128]{3,2,1,0:T(8,128)(2,1)S(1)} %mine.3.refs_1_, bf16[2,2,64,128]{3,2,1,0:T(8,128)(2,1)S(1)} %collective-permute-done.2.refs_2_, ...), custom_call_target="tpu_custom_call" | custom-call | tf_op jit(solution)/shard_map/return/pallas_call | solution.py:560
  42.6 3.9 %all-to-all-start.1 = ((bf16[16,2,64,128]{3,2,1,0:T(8,128)(2,1)}), bf16[16,2,64,128]{3,2,1,0:T(8,128)(2,1)S(1)}, u32[]{:S(2)}, u32[]{:S(2)}) async-start(bf16[16,2,64,128]{3,2,1,0:T(8,128)(2,1)} %return.1), calls=%async_computation.1 | async-start | bytes 1048576 | tf_op jit(solution)/shard_map/all_to_all | solution.py:654
  46.6 0.0 copy-start.3
  46.6 0.9 %copy-done.2 = bf16[128,4,128]{2,1,0:T(4,128)(2,1)S(1)} copy-done((bf16[128,4,128]{2,1,0:T(4,128)(2,1)S(1)}, bf16[128,4,128]{2,1,0:T(4,128)(2,1)}, u32[]{:S(2)}) %copy-start.2) | copy-done | bytes 131096
  47.5 0.1 copy-done.3
  47.5 6.9 %local.1 = (bf16[4096,128]{1,0:T(8,128)(2,1)}, bf16[4096,128]{1,0:T(8,128)(2,1)}, f32[512,128]{1,0:T(8,128)S(1)}, f32[512,128]{1,0:T(8,128)S(1)}) custom-call(s32[44]{0:T(128)S(4)} %plan.1.plan_ref, bf16[4096,128]{1,0:T(8,128)(2,1)S(1)} %bitcast.15, bf16[4096,128]{1,0:T(8,128)(2,1)S(1)} %bitcast.22, bf16[512,128]{1,0:T(8,128)(2,1)S(1)} %bitcast.24, ...), custom_call_target="tpu_custom_call" | custom-call | tf_op jit(solution)/shard_map/local/pallas_call | solution.py:660
  54.4 0.7 %copy-done.4 = f32[512,128]{1,0:T(8,128)} copy-done((f32[512,128]{1,0:T(8,128)}, f32[512,128]{1,0:T(8,128)S(1)}, u32[]{:S(2)}) %copy-start.4) | copy-done | bytes 262168
  55.1 5.9 %all-to-all-done.1.landed_ref = bf16[16,2,64,128]{3,2,1,0:T(8,128)(2,1)S(1)} async-done(((bf16[16,2,64,128]{3,2,1,0:T(8,128)(2,1)}), bf16[16,2,64,128]{3,2,1,0:T(8,128)(2,1)S(1)}, u32[]{:S(2)}, u32[]{:S(2)}) %all-to-all-start.1) | async-done | bytes 524320 | tf_op jit(solution)/shard_map/all_to_all | solution.py:654
  61.0 0.2 land_sibling.1
  61.2 0.3 collective-permute-start.5
  61.5 0.2 land_own.1.own_ref
  61.6 5.1 %collective-permute-done.5.back_ref = bf16[4,2,64,128]{3,2,1,0:T(8,128)(2,1)S(1)} collective-permute-done((bf16[4,2,64,128]{3,2,1,0:T(8,128)(2,1)S(1)}, bf16[4,2,64,128]{3,2,1,0:T(8,128)(2,1)S(1)}, u32[]{:S(2)}, u32[]{:S(2)}) %collective-permute-start.5) | collective-permute-done | bytes 131104 | tf_op jit(solution)/shard_map/ppermute | solution.py:682
  66.7 1.0 %finish.1 = (bf16[512,128]{1,0:T(8,128)(2,1)}, bf16[512,128]{1,0:T(8,128)(2,1)}) custom-call(f32[512,128]{1,0:T(8,128)S(1)} %get-tuple-element.53.dk_near_ref, f32[512,128]{1,0:T(8,128)S(1)} %copy-done.5, f32[4,2,64,128]{3,2,1,0:T(8,128)S(1)} %land_own.1.own_ref, bf16[4,2,64,128]{3,2,1,0:T(8,128)(2,1)S(1)} %collective-permute-done.5.back_ref), custom_call_target="tpu_custom_call" | custom-call | tf_op jit(solution)/shard_map/finish/pallas_call | solution.py:560
  (12 shorter events, 0.0 us)
Async XLA Ops:
  1.9 6.5 %collective-permute-start = (bf16[4,2,64,128]{3,2,1,0:T(8,128)(2,1)S(1)}, bf16[4,2,64,128]{3,2,1,0:T(8,128)(2,1)S(1)}, u32[]{:S(2)}, u32[]{:S(2)}) collective-permute-start(bf16[4,2,64,128]{3,2,1,0:T(8,128)(2,1)S(1)} %get-tuple-element.34.given_ref), channel_id=1, source_target_pairs={{0,1},{1,0},{2,3},{3,2},{4,5},{5,4},{6,7},{7,6},{8,9},{9,8},{10,11... | collective-permute-start | bytes 393224 | tf_op jit(solution)/shard_map/ppermute | solution.py:597
  8.4 22.2 %copy-start.1 = (bf16[128,32,128]{2,1,0:T(8,128)(2,1)S(1)}, bf16[128,32,128]{2,1,0:T(8,128)(2,1)}, u32[]{:S(2)}) copy-start(bf16[128,32,128]{2,1,0:T(8,128)(2,1)} %param.9) | copy-start | bytes 3145732
  8.4 22.2 %copy-start = (bf16[128,32,128]{2,1,0:T(8,128)(2,1)S(1)}, bf16[128,32,128]{2,1,0:T(8,128)(2,1)}, u32[]{:S(2)}) copy-start(bf16[128,32,128]{2,1,0:T(8,128)(2,1)} %param.6) | copy-start | bytes 3145732
  29.0 4.3 %collective-permute-start.1 = (bf16[2,2,64,128]{3,2,1,0:T(8,128)(2,1)S(1)}, bf16[2,2,64,128]{3,2,1,0:T(8,128)(2,1)S(1)}, u32[]{:S(2)}, u32[]{:S(2)}) collective-permute-start(bf16[2,2,64,128]{3,2,1,0:T(8,128)(2,1)S(1)} %get-tuple-element.40), channel_id=1, source_target_pairs={{0,1},{1,0},{2,3},{3,2},{4,5},{5,4},{6,7},{7,6},{8,9},{9,8},{10,11... | collective-permute-start | bytes 196616 | tf_op jit(solution)/shard_map/ppermute | solution.py:622
  31.4 5.2 %collective-permute-start.3 = (bf16[2,2,64,128]{3,2,1,0:T(8,128)(2,1)S(1)}, bf16[2,2,64,128]{3,2,1,0:T(8,128)(2,1)S(1)}, u32[]{:S(2)}, u32[]{:S(2)}) collective-permute-start(bf16[2,2,64,128]{3,2,1,0:T(8,128)(2,1)S(1)} %get-tuple-element.44), channel_id=1, source_target_pairs={{0,1},{1,0},{2,3},{3,2},{4,5},{5,4},{6,7},{7,6},{8,9},{9,8},{10,11... | collective-permute-start | bytes 196616 | tf_op jit(solution)/shard_map/ppermute | solution.py:622
  34.2 5.3 %collective-permute-start.2 = (bf16[2,2,64,128]{3,2,1,0:T(8,128)(2,1)S(1)}, bf16[2,2,64,128]{3,2,1,0:T(8,128)(2,1)S(1)}, u32[]{:S(2)}, u32[]{:S(2)}) collective-permute-start(bf16[2,2,64,128]{3,2,1,0:T(8,128)(2,1)S(1)} %get-tuple-element.41), channel_id=1, source_target_pairs={{0,1},{1,0},{2,3},{3,2},{4,5},{5,4},{6,7},{7,6},{8,9},{9,8},{10,11... | collective-permute-start | bytes 196616 | tf_op jit(solution)/shard_map/ppermute | solution.py:636
  37.5 4.3 %collective-permute-start.4 = (bf16[2,2,64,128]{3,2,1,0:T(8,128)(2,1)S(1)}, bf16[2,2,64,128]{3,2,1,0:T(8,128)(2,1)S(1)}, u32[]{:S(2)}, u32[]{:S(2)}) collective-permute-start(bf16[2,2,64,128]{3,2,1,0:T(8,128)(2,1)S(1)} %get-tuple-element.47), channel_id=1, source_target_pairs={{0,1},{1,0},{2,3},{3,2},{4,5},{5,4},{6,7},{7,6},{8,9},{9,8},{10,11... | collective-permute-start | bytes 196616 | tf_op jit(solution)/shard_map/ppermute | solution.py:636
  42.6 18.4 %all-to-all-start.1 = ((bf16[16,2,64,128]{3,2,1,0:T(8,128)(2,1)}), bf16[16,2,64,128]{3,2,1,0:T(8,128)(2,1)S(1)}, u32[]{:S(2)}, u32[]{:S(2)}) async-start(bf16[16,2,64,128]{3,2,1,0:T(8,128)(2,1)} %return.1), calls=%async_computation.1 | async-start | bytes 1048576 | tf_op jit(solution)/shard_map/all_to_all | solution.py:654
  46.6 0.9 %copy-start.2 = (bf16[128,4,128]{2,1,0:T(4,128)(2,1)S(1)}, bf16[128,4,128]{2,1,0:T(4,128)(2,1)}, u32[]{:S(2)}) copy-start(bf16[128,4,128]{2,1,0:T(4,128)(2,1)} %param.7) | copy-start | bytes 393220
  46.6 1.0 %copy-start.3 = (bf16[128,4,128]{2,1,0:T(4,128)(2,1)S(1)}, bf16[128,4,128]{2,1,0:T(4,128)(2,1)}, u32[]{:S(2)}) copy-start(bf16[128,4,128]{2,1,0:T(4,128)(2,1)} %param.8) | copy-start | bytes 393220
  54.4 0.7 %copy-start.4 = (f32[512,128]{1,0:T(8,128)}, f32[512,128]{1,0:T(8,128)S(1)}, u32[]{:S(2)}) copy-start(f32[512,128]{1,0:T(8,128)S(1)} %get-tuple-element.54.dv_near_ref) | copy-start | bytes 786436
  61.2 5.5 %copy-start.5 = (f32[512,128]{1,0:T(8,128)S(1)}, f32[512,128]{1,0:T(8,128)}, u32[]{:S(2)}) copy-start(f32[512,128]{1,0:T(8,128)} %copy-done.4) | copy-start | bytes 786436
  61.2 5.5 %collective-permute-start.5 = (bf16[4,2,64,128]{3,2,1,0:T(8,128)(2,1)S(1)}, bf16[4,2,64,128]{3,2,1,0:T(8,128)(2,1)S(1)}, u32[]{:S(2)}, u32[]{:S(2)}) collective-permute-start(bf16[4,2,64,128]{3,2,1,0:T(8,128)(2,1)S(1)} %land_sibling.1), channel_id=1, source_target_pairs={{0,1},{1,0},{2,3},{3,2},{4,5},{5,4},{6,7},{7,6},{8,9},{9,8},{10,11... | collective-permute-start | bytes 393224 | tf_op jit(solution)/shard_map/ppermute | solution.py:682

commit v14 on v11

--- a/solution.py
+++ b/solution.py
@@ -245,7 +245,7 @@
     return grp_count, 2 * grp_count, 2 * grp_count + blocks, 2 * grp_count + 2 * blocks
 
 
-def plan_kernel(lists_ref, counts_ref, plan_ref, *, grp_count, blocks):
+def fill_plan(lists_ref, counts_ref, plan_ref, grp_count, blocks):
     group, mine = lax.axis_index("grp"), lax.axis_index("uly")
     per_group = 2 * blocks
     low = group * per_group
@@ -319,8 +319,8 @@
 
 
 def near_kernel(
-    q_hbm, g_hbm, k_ref, v_ref, given_ref, stat_ref, kept_ref, q_ref, g_ref, sems,
-    *, heads, kv_heads, score_scale
+    lists_ref, counts_ref, q_hbm, g_hbm, k_ref, v_ref, given_ref,
+    plan_ref, stat_ref, kept_ref, q_ref, g_ref, sems, *, heads, kv_heads, score_scale, grp_count
 ):
     blocks = stat_ref.shape[0]
     rows = q_ref.shape[0] // blocks
@@ -333,6 +333,7 @@
             sem = sems.at[which, block]
             copies.append(pltpu.make_async_copy(source.at[span], target.at[span], sem))
             copies[-1].start()
+    fill_plan(lists_ref, counts_ref, plan_ref, grp_count, blocks)
     mine = lax.axis_index("uly")
     order = half_order(2 * half, kv_heads, mine)
     for block in range(blocks):
@@ -594,29 +595,24 @@
         compiler_params=limit,
         name="pack",
     )(in_hbm(k2), in_hbm(v2))
-    plan = pl.pallas_call(
-        partial(plan_kernel, grp_count=grp_count, blocks=mine_blocks),
-        in_specs=[smem, smem],
-        out_specs=smem,
-        out_shape=pltpu.SMEM((seen_at + mine_blocks,), jnp.int32),
-        compiler_params=limit,
-        name="plan",
-    )(in_hbm(block_lists.reshape(-1)), in_hbm(list_counts))
     gotten = lax.ppermute(given, "uly", swap)
     row_spec = pl.BlockSpec((rows, width), step_rows)
     part_spec = pl.BlockSpec((1, 2, half, width), step_part)
-    stats, kept = pl.pallas_call(
-        partial(near_kernel, **sizes),
-        in_specs=[anywhere, anywhere, vmem, vmem, vmem],
-        out_specs=[vmem, vmem],
-        out_shape=[stat_shape, part_shape],
-        scratch_shapes=[
+    plan, stats, kept, q2, g2 = pl.pallas_call(
+        partial(near_kernel, grp_count=grp_count, **sizes),
+        in_specs=[smem, smem, anywhere, anywhere, vmem, vmem, vmem],
+        out_specs=[smem, vmem, vmem, vmem, vmem],
+        out_shape=[
+            pltpu.SMEM((seen_at + mine_blocks,), jnp.int32), stat_shape, part_shape,
             pltpu.VMEM(q2.shape, BF16), pltpu.VMEM(q2.shape, BF16),
-            pltpu.SemaphoreType.DMA((2, mine_blocks)),
         ],
+        scratch_shapes=[pltpu.SemaphoreType.DMA((2, mine_blocks))],
         compiler_params=limit,
         name="near",
-    )(in_hbm(q2), in_hbm(g2), k_here, v_here, given)
+    )(
+        in_hbm(block_lists.reshape(-1)), in_hbm(list_counts), in_hbm(q2), in_hbm(g2),
+        k_here, v_here, given,
+    )
     outgoing = call(
         send_own_kernel, "send_own", (plan,), (kept,),
         jax.ShapeDtypeStruct(slots, BF16),

time: 67.6 us -> 67.4 us (level)
    pallas_call x2 -> x1, Pallas kernels: 4.04 us -> 4.01 us  [whole_blocks(): pl.pallas_call(partial(near_kernel, grp_count=grp_count, **sizes), in_spe...]
    unnamed x12 -> x8, local copies, waits for them, and re-layouts: 1.65 us -> 1.64 us
where the time goes in v14:
time: 67.4 us; the launch traced here: 67.1 us
  blocking collectives  20.2 us (30%)
  Pallas kernels  18.9 us (28%)
  waiting for transfers between devices  12.9 us (19%)
  starting transfers between devices  12.7 us (19%)
  local copies, waits for them, and re-layouts  1.64 us (2%)
  between operations  0.77 us (1%)
    all_to_all x1, blocking collectives, whole_blocks(): lax.all_to_all(outgoing, 'grp', split_axis=0, concat_axis=0, tiled=True)  20.2 us
    pallas_call x1, Pallas kernels, whole_blocks(): pl.pallas_call(partial(local_kernel, seen_at=seen_at, **sizes), grid_spec...  6.86 us
    pallas_call x12, Pallas kernels, call(): pl.pallas_call(kernel, in_specs=[smem] * len(scalars) + [vmem] * (len(ope...  6.72 us
    all_to_all x1, waiting for transfers between devices, whole_blocks(): lax.all_to_all(returning, 'grp', split_axis=0, concat_axis=0, tiled=True)  5.93 us
    all_to_all x1, starting transfers between devices, whole_blocks(): lax.all_to_all(returning, 'grp', split_axis=0, concat_axis=0, tiled=True)  4.19 us
    ppermute x1, waiting for transfers between devices, whole_blocks(): back = lax.ppermute(give, 'uly', swap)  4.17 us
    pallas_call x1, Pallas kernels, whole_blocks(): pl.pallas_call(partial(near_kernel, grp_count=grp_count, **sizes), in_spe...  4.01 us
    ppermute x1, starting transfers between devices, whole_blocks(): gotten = lax.ppermute(given, 'uly', swap)  3.03 us
  transfers between devices with their start and end apart: 7, of which 5 were waited for; matrix products, arithmetic and copies ran while one was open for 0% of the time, Pallas kernels for 23%

profile of v14, /device:TPU:0, one launch (start us, length us, event | category | flops | bytes accessed | tf_op | source)
XLA Modules:
  0.0 67.1 jit_solution(14456381321011074088)
XLA Ops:
  0.6 1.3 %pack.1 = (bf16[512,128]{1,0:T(8,128)(2,1)S(1)}, bf16[512,128]{1,0:T(8,128)(2,1)S(1)}, bf16[4,2,64,128]{3,2,1,0:T(8,128)(2,1)S(1)}) custom-call(bf16[512,128]{1,0:T(8,128)(2,1)} %bitcast.9, bf16[512,128]{1,0:T(8,128)(2,1)} %bitcast.11), custom_call_target="tpu_custom_call" | custom-call | tf_op jit(solution)/shard_map/pack/pallas_call | solution.py:589
  1.9 3.0 %collective-permute-start = (bf16[4,2,64,128]{3,2,1,0:T(8,128)(2,1)S(1)}, bf16[4,2,64,128]{3,2,1,0:T(8,128)(2,1)S(1)}, u32[]{:S(2)}, u32[]{:S(2)}) collective-permute-start(bf16[4,2,64,128]{3,2,1,0:T(8,128)(2,1)S(1)} %get-tuple-element.36.given_ref), channel_id=1, source_target_pairs={{0,1},{1,0},{2,3},{3,2},{4,5},{5,4},{6,7},{7,6},{8,9},{9,8},{10,11... | collective-permute-start | bytes 393224 | tf_op jit(solution)/shard_map/ppermute | solution.py:598
  4.9 4.0 %near.1 = (s32[44]{0:T(128)S(4)}, f32[4,8,1024]{2,1,0:T(8,128)S(1)}, bf16[4,2,64,128]{3,2,1,0:T(8,128)(2,1)S(1)}, bf16[4096,128]{1,0:T(8,128)(2,1)S(1)}, bf16[4096,128]{1,0:T(8,128)(2,1)S(1)}) custom-call(s32[128]{0:T(128)} %bitcast.15, s32[128]{0:T(128)} %counts_ref.1, bf16[4096,128]{1,0:T(8,128)(2,1)} %bitcast.13, bf16[4096,128]{1,0:T(8,128)(2,1)} %bitcast.14, ...), custom_call_target="tpu_custom_call" | custom-call | tf_op jit(solution)/shard_map/near/pallas_call | solution.py:601
  9.0 0.0 collective-permute-done.blocks_ref
  9.0 0.1 send_sibling.1
  9.2 20.2 %all_to_all.10.arrived_ref.mine_ref = bf16[16,2,64,128]{3,2,1,0:T(8,128)(2,1)S(1)} all-to-all(bf16[16,2,64,128]{3,2,1,0:T(8,128)(2,1)S(1)} %send_sibling.1), channel_id=1, replica_groups=mesh['grp'=16,'uly'=2] {'grp'}, dimensions={0} | all-to-all | bytes 1048576 | tf_op jit(solution)/shard_map/all_to_all | solution.py:625
  29.4 1.1 %collective-permute-start.1 = (bf16[2,2,64,128]{3,2,1,0:T(8,128)(2,1)S(1)}, bf16[2,2,64,128]{3,2,1,0:T(8,128)(2,1)S(1)}, u32[]{:S(2)}, u32[]{:S(2)}) collective-permute-start(bf16[2,2,64,128]{3,2,1,0:T(8,128)(2,1)S(1)} %get-tuple-element.46), channel_id=1, source_target_pairs={{0,1},{1,0},{2,3},{3,2},{4,5},{5,4},{6,7},{7,6},{8,9},{9,8},{10,11... | collective-permute-start | bytes 196616 | tf_op jit(solution)/shard_map/ppermute | solution.py:641
  30.4 0.8 %mid.1.stat_ref = f32[4,8,1024]{2,1,0:T(8,128)S(1)} custom-call(s32[44]{0:T(128)S(4)} %get-tuple-element.37.plan_ref, bf16[4096,128]{1,0:T(8,128)(2,1)S(1)} %get-tuple-element.38.q_ref, bf16[4096,128]{1,0:T(8,128)(2,1)S(1)} %get-tuple-element.39.g_ref, f32[4,8,1024]{2,1,0:T(8,128)S(1)} %get-tuple-element.44.stat_ref, ...), custom_call_target="tpu_custom_call" | custom-call | tf_op jit(solution)/shard_map/mid/pallas_call | solution.py:569
  31.3 1.1 %collective-permute-start.3 = (bf16[2,2,64,128]{3,2,1,0:T(8,128)(2,1)S(1)}, bf16[2,2,64,128]{3,2,1,0:T(8,128)(2,1)S(1)}, u32[]{:S(2)}, u32[]{:S(2)}) collective-permute-start(bf16[2,2,64,128]{3,2,1,0:T(8,128)(2,1)S(1)} %get-tuple-element.50), channel_id=1, source_target_pairs={{0,1},{1,0},{2,3},{3,2},{4,5},{5,4},{6,7},{7,6},{8,9},{9,8},{10,11... | collective-permute-start | bytes 196616 | tf_op jit(solution)/shard_map/ppermute | solution.py:641
  32.4 1.4 %collective-permute-done.1.other_ref = bf16[2,2,64,128]{3,2,1,0:T(8,128)(2,1)S(1)} collective-permute-done((bf16[2,2,64,128]{3,2,1,0:T(8,128)(2,1)S(1)}, bf16[2,2,64,128]{3,2,1,0:T(8,128)(2,1)S(1)}, u32[]{:S(2)}, u32[]{:S(2)}) %collective-permute-start.1) | collective-permute-done | bytes 65568 | tf_op jit(solution)/shard_map/ppermute | solution.py:641
  33.7 0.9 %far.2 = (bf16[2,2,64,128]{3,2,1,0:T(8,128)(2,1)S(1)}, f32[2,8,1024]{2,1,0:T(8,128)S(1)}) custom-call(s32[44]{0:T(128)S(4)} %get-tuple-element.37.plan_ref, bf16[4096,128]{1,0:T(8,128)(2,1)S(1)} %get-tuple-element.38.q_ref, bf16[4096,128]{1,0:T(8,128)(2,1)S(1)} %get-tuple-element.39.g_ref, f32[4,8,1024]{2,1,0:T(8,128)S(1)} %mid.1.stat_ref, ...), custom_call_target="tpu_custom_call" | custom-call | tf_op jit(solution)/shard_map/far/pallas_call | solution.py:569
  34.7 1.0 %collective-permute-start.2 = (bf16[2,2,64,128]{3,2,1,0:T(8,128)(2,1)S(1)}, bf16[2,2,64,128]{3,2,1,0:T(8,128)(2,1)S(1)}, u32[]{:S(2)}, u32[]{:S(2)}) collective-permute-start(bf16[2,2,64,128]{3,2,1,0:T(8,128)(2,1)S(1)} %get-tuple-element.47), channel_id=1, source_target_pairs={{0,1},{1,0},{2,3},{3,2},{4,5},{5,4},{6,7},{7,6},{8,9},{9,8},{10,11... | collective-permute-start | bytes 196616 | tf_op jit(solution)/shard_map/ppermute | solution.py:651
  35.7 0.9 %far.3 = (bf16[2,2,64,128]{3,2,1,0:T(8,128)(2,1)S(1)}, f32[2,8,1024]{2,1,0:T(8,128)S(1)}) custom-call(s32[44]{0:T(128)S(4)} %get-tuple-element.37.plan_ref, bf16[4096,128]{1,0:T(8,128)(2,1)S(1)} %get-tuple-element.38.q_ref, bf16[4096,128]{1,0:T(8,128)(2,1)S(1)} %get-tuple-element.39.g_ref, f32[4,8,1024]{2,1,0:T(8,128)S(1)} %mid.1.stat_ref, ...), custom_call_target="tpu_custom_call" | custom-call | tf_op jit(solution)/shard_map/far/pallas_call | solution.py:569
  36.6 1.1 %collective-permute-start.4 = (bf16[2,2,64,128]{3,2,1,0:T(8,128)(2,1)S(1)}, bf16[2,2,64,128]{3,2,1,0:T(8,128)(2,1)S(1)}, u32[]{:S(2)}, u32[]{:S(2)}) collective-permute-start(bf16[2,2,64,128]{3,2,1,0:T(8,128)(2,1)S(1)} %get-tuple-element.53), channel_id=1, source_target_pairs={{0,1},{1,0},{2,3},{3,2},{4,5},{5,4},{6,7},{7,6},{8,9},{9,8},{10,11... | collective-permute-start | bytes 196616 | tf_op jit(solution)/shard_map/ppermute | solution.py:651
  37.8 0.9 %mine.3.refs_1_ = bf16[2,2,64,128]{3,2,1,0:T(8,128)(2,1)S(1)} custom-call(s32[44]{0:T(128)S(4)} %get-tuple-element.37.plan_ref, bf16[4096,128]{1,0:T(8,128)(2,1)S(1)} %get-tuple-element.38.q_ref, bf16[4096,128]{1,0:T(8,128)(2,1)S(1)} %get-tuple-element.39.g_ref, bf16[16,2,64,128]{3,2,1,0:T(8,128)(2,1)S(1)} %all_to_all.10.arrived_ref.mine_ref, ...), custom_call_target="tpu_custom_call" | custom-call | tf_op jit(solution)/shard_map/mine/pallas_call | solution.py:569
  38.6 0.6 collective-permute-done.2.refs_2_
  39.3 0.9 %mine.2.refs_0_ = bf16[2,2,64,128]{3,2,1,0:T(8,128)(2,1)S(1)} custom-call(s32[44]{0:T(128)S(4)} %get-tuple-element.37.plan_ref, bf16[4096,128]{1,0:T(8,128)(2,1)S(1)} %get-tuple-element.38.q_ref, bf16[4096,128]{1,0:T(8,128)(2,1)S(1)} %get-tuple-element.39.g_ref, bf16[16,2,64,128]{3,2,1,0:T(8,128)(2,1)S(1)} %all_to_all.10.arrived_ref.mine_ref, ...), custom_call_target="tpu_custom_call" | custom-call | tf_op jit(solution)/shard_map/mine/pallas_call | solution.py:569
  40.1 0.8 %collective-permute-done.4.refs_3_ = bf16[2,2,64,128]{3,2,1,0:T(8,128)(2,1)S(1)} collective-permute-done((bf16[2,2,64,128]{3,2,1,0:T(8,128)(2,1)S(1)}, bf16[2,2,64,128]{3,2,1,0:T(8,128)(2,1)S(1)}, u32[]{:S(2)}, u32[]{:S(2)}) %collective-permute-start.4) | collective-permute-done | bytes 65568 | tf_op jit(solution)/shard_map/ppermute | solution.py:651
  40.9 0.8 %return.1 = bf16[16,2,64,128]{3,2,1,0:T(8,128)(2,1)} custom-call(s32[44]{0:T(128)S(4)} %get-tuple-element.37.plan_ref, bf16[2,2,64,128]{3,2,1,0:T(8,128)(2,1)S(1)} %mine.2.refs_0_, bf16[2,2,64,128]{3,2,1,0:T(8,128)(2,1)S(1)} %mine.3.refs_1_, bf16[2,2,64,128]{3,2,1,0:T(8,128)(2,1)S(1)} %collective-permute-done.2.refs_2_, ...), custom_call_target="tpu_custom_call" | custom-call | tf_op jit(solution)/shard_map/return/pallas_call | solution.py:569
  41.7 4.2 %all-to-all-start.1 = ((bf16[16,2,64,128]{3,2,1,0:T(8,128)(2,1)}), bf16[16,2,64,128]{3,2,1,0:T(8,128)(2,1)S(1)}, u32[]{:S(2)}, u32[]{:S(2)}) async-start(bf16[16,2,64,128]{3,2,1,0:T(8,128)(2,1)} %return.1), calls=%async_computation.1 | async-start | bytes 1048576 | tf_op jit(solution)/shard_map/all_to_all | solution.py:669
  45.9 0.0 copy-start
  46.0 0.0 copy-start.1
  46.0 0.9 %copy-done = bf16[128,4,128]{2,1,0:T(4,128)(2,1)S(1)} copy-done((bf16[128,4,128]{2,1,0:T(4,128)(2,1)S(1)}, bf16[128,4,128]{2,1,0:T(4,128)(2,1)}, u32[]{:S(2)}) %copy-start) | copy-done | bytes 131096
  46.8 0.1 copy-done.1
  46.9 6.9 %local.1 = (bf16[4096,128]{1,0:T(8,128)(2,1)}, bf16[4096,128]{1,0:T(8,128)(2,1)}, f32[512,128]{1,0:T(8,128)S(1)}, f32[512,128]{1,0:T(8,128)S(1)}) custom-call(s32[44]{0:T(128)S(4)} %get-tuple-element.37.plan_ref, bf16[4096,128]{1,0:T(8,128)(2,1)S(1)} %get-tuple-element.38.q_ref, bf16[4096,128]{1,0:T(8,128)(2,1)S(1)} %get-tuple-element.39.g_ref, ...), custom_call_target="tpu_custom_call" | custom-call | tf_op jit(solution)/shard_map/local/pallas_call | solution.py:675
  53.8 0.7 %copy-done.2 = f32[512,128]{1,0:T(8,128)} copy-done((f32[512,128]{1,0:T(8,128)}, f32[512,128]{1,0:T(8,128)S(1)}, u32[]{:S(2)}) %copy-start.2) | copy-done | bytes 262168
  54.5 5.9 %all-to-all-done.1.landed_ref = bf16[16,2,64,128]{3,2,1,0:T(8,128)(2,1)S(1)} async-done(((bf16[16,2,64,128]{3,2,1,0:T(8,128)(2,1)}), bf16[16,2,64,128]{3,2,1,0:T(8,128)(2,1)S(1)}, u32[]{:S(2)}, u32[]{:S(2)}) %all-to-all-start.1) | async-done | bytes 524320 | tf_op jit(solution)/shard_map/all_to_all | solution.py:669
  60.4 0.2 land_sibling.1
  60.6 1.1 %collective-permute-start.5 = (bf16[4,2,64,128]{3,2,1,0:T(8,128)(2,1)S(1)}, bf16[4,2,64,128]{3,2,1,0:T(8,128)(2,1)S(1)}, u32[]{:S(2)}, u32[]{:S(2)}) collective-permute-start(bf16[4,2,64,128]{3,2,1,0:T(8,128)(2,1)S(1)} %land_sibling.1), channel_id=1, source_target_pairs={{0,1},{1,0},{2,3},{3,2},{4,5},{5,4},{6,7},{7,6},{8,9},{9,8},{10,11... | collective-permute-start | bytes 393224 | tf_op jit(solution)/shard_map/ppermute | solution.py:697
  61.7 0.2 land_own.1.own_ref
  61.9 4.2 %collective-permute-done.5.back_ref = bf16[4,2,64,128]{3,2,1,0:T(8,128)(2,1)S(1)} collective-permute-done((bf16[4,2,64,128]{3,2,1,0:T(8,128)(2,1)S(1)}, bf16[4,2,64,128]{3,2,1,0:T(8,128)(2,1)S(1)}, u32[]{:S(2)}, u32[]{:S(2)}) %collective-permute-start.5) | collective-permute-done | bytes 131104 | tf_op jit(solution)/shard_map/ppermute | solution.py:697
  66.1 1.0 %finish.1 = (bf16[512,128]{1,0:T(8,128)(2,1)}, bf16[512,128]{1,0:T(8,128)(2,1)}) custom-call(f32[512,128]{1,0:T(8,128)S(1)} %get-tuple-element.59.dk_near_ref, f32[512,128]{1,0:T(8,128)S(1)} %copy-done.3, f32[4,2,64,128]{3,2,1,0:T(8,128)S(1)} %land_own.1.own_ref, bf16[4,2,64,128]{3,2,1,0:T(8,128)(2,1)S(1)} %collective-permute-done.5.back_ref), custom_call_target="tpu_custom_call" | custom-call | tf_op jit(solution)/shard_map/finish/pallas_call | solution.py:569
  (7 shorter events, 0.1 us)
Async XLA Ops:
  1.9 7.1 %collective-permute-start = (bf16[4,2,64,128]{3,2,1,0:T(8,128)(2,1)S(1)}, bf16[4,2,64,128]{3,2,1,0:T(8,128)(2,1)S(1)}, u32[]{:S(2)}, u32[]{:S(2)}) collective-permute-start(bf16[4,2,64,128]{3,2,1,0:T(8,128)(2,1)S(1)} %get-tuple-element.36.given_ref), channel_id=1, source_target_pairs={{0,1},{1,0},{2,3},{3,2},{4,5},{5,4},{6,7},{7,6},{8,9},{9,8},{10,11... | collective-permute-start | bytes 393224 | tf_op jit(solution)/shard_map/ppermute | solution.py:598
  29.4 4.4 %collective-permute-start.1 = (bf16[2,2,64,128]{3,2,1,0:T(8,128)(2,1)S(1)}, bf16[2,2,64,128]{3,2,1,0:T(8,128)(2,1)S(1)}, u32[]{:S(2)}, u32[]{:S(2)}) collective-permute-start(bf16[2,2,64,128]{3,2,1,0:T(8,128)(2,1)S(1)} %get-tuple-element.46), channel_id=1, source_target_pairs={{0,1},{1,0},{2,3},{3,2},{4,5},{5,4},{6,7},{7,6},{8,9},{9,8},{10,11... | collective-permute-start | bytes 196616 | tf_op jit(solution)/shard_map/ppermute | solution.py:641
  31.3 4.4 %collective-permute-start.3 = (bf16[2,2,64,128]{3,2,1,0:T(8,128)(2,1)S(1)}, bf16[2,2,64,128]{3,2,1,0:T(8,128)(2,1)S(1)}, u32[]{:S(2)}, u32[]{:S(2)}) collective-permute-start(bf16[2,2,64,128]{3,2,1,0:T(8,128)(2,1)S(1)} %get-tuple-element.50), channel_id=1, source_target_pairs={{0,1},{1,0},{2,3},{3,2},{4,5},{5,4},{6,7},{7,6},{8,9},{9,8},{10,11... | collective-permute-start | bytes 196616 | tf_op jit(solution)/shard_map/ppermute | solution.py:641
  34.7 4.6 %collective-permute-start.2 = (bf16[2,2,64,128]{3,2,1,0:T(8,128)(2,1)S(1)}, bf16[2,2,64,128]{3,2,1,0:T(8,128)(2,1)S(1)}, u32[]{:S(2)}, u32[]{:S(2)}) collective-permute-start(bf16[2,2,64,128]{3,2,1,0:T(8,128)(2,1)S(1)} %get-tuple-element.47), channel_id=1, source_target_pairs={{0,1},{1,0},{2,3},{3,2},{4,5},{5,4},{6,7},{7,6},{8,9},{9,8},{10,11... | collective-permute-start | bytes 196616 | tf_op jit(solution)/shard_map/ppermute | solution.py:651
  36.6 4.3 %collective-permute-start.4 = (bf16[2,2,64,128]{3,2,1,0:T(8,128)(2,1)S(1)}, bf16[2,2,64,128]{3,2,1,0:T(8,128)(2,1)S(1)}, u32[]{:S(2)}, u32[]{:S(2)}) collective-permute-start(bf16[2,2,64,128]{3,2,1,0:T(8,128)(2,1)S(1)} %get-tuple-element.53), channel_id=1, source_target_pairs={{0,1},{1,0},{2,3},{3,2},{4,5},{5,4},{6,7},{7,6},{8,9},{9,8},{10,11... | collective-permute-start | bytes 196616 | tf_op jit(solution)/shard_map/ppermute | solution.py:651
  41.7 18.7 %all-to-all-start.1 = ((bf16[16,2,64,128]{3,2,1,0:T(8,128)(2,1)}), bf16[16,2,64,128]{3,2,1,0:T(8,128)(2,1)S(1)}, u32[]{:S(2)}, u32[]{:S(2)}) async-start(bf16[16,2,64,128]{3,2,1,0:T(8,128)(2,1)} %return.1), calls=%async_computation.1 | async-start | bytes 1048576 | tf_op jit(solution)/shard_map/all_to_all | solution.py:669
  45.9 0.9 %copy-start = (bf16[128,4,128]{2,1,0:T(4,128)(2,1)S(1)}, bf16[128,4,128]{2,1,0:T(4,128)(2,1)}, u32[]{:S(2)}) copy-start(bf16[128,4,128]{2,1,0:T(4,128)(2,1)} %param.7) | copy-start | bytes 393220
  46.0 1.0 %copy-start.1 = (bf16[128,4,128]{2,1,0:T(4,128)(2,1)S(1)}, bf16[128,4,128]{2,1,0:T(4,128)(2,1)}, u32[]{:S(2)}) copy-start(bf16[128,4,128]{2,1,0:T(4,128)(2,1)} %param.8) | copy-start | bytes 393220
  53.8 0.7 %copy-start.2 = (f32[512,128]{1,0:T(8,128)}, f32[512,128]{1,0:T(8,128)S(1)}, u32[]{:S(2)}) copy-start(f32[512,128]{1,0:T(8,128)S(1)} %get-tuple-element.60.dv_near_ref) | copy-start | bytes 786436
  60.6 5.5 %copy-start.3 = (f32[512,128]{1,0:T(8,128)S(1)}, f32[512,128]{1,0:T(8,128)}, u32[]{:S(2)}) copy-start(f32[512,128]{1,0:T(8,128)} %copy-done.2) | copy-start | bytes 786436
  60.6 5.5 %collective-permute-start.5 = (bf16[4,2,64,128]{3,2,1,0:T(8,128)(2,1)S(1)}, bf16[4,2,64,128]{3,2,1,0:T(8,128)(2,1)S(1)}, u32[]{:S(2)}, u32[]{:S(2)}) collective-permute-start(bf16[4,2,64,128]{3,2,1,0:T(8,128)(2,1)S(1)} %land_sibling.1), channel_id=1, source_target_pairs={{0,1},{1,0},{2,3},{3,2},{4,5},{5,4},{6,7},{7,6},{8,9},{9,8},{10,11... | collective-permute-start | bytes 393224 | tf_op jit(solution)/shard_map/ppermute | solution.py:697

commit v15 on v13

--- a/solution.py
+++ b/solution.py
@@ -607,7 +607,7 @@
     )
     arrived = lax.all_to_all(outgoing, "grp", split_axis=0, concat_axis=0, tiled=True)
     kept, arrived = lax.optimization_barrier((kept, arrived))
-    chunks = 2 if mine_blocks % 2 == 0 else 1
+    chunks = 1
     chunk = mine_blocks // chunks
     chunk_shape = jax.ShapeDtypeStruct((chunk, 2, half, width), BF16)
     giving = call(

time: 67.9 us -> 68 us (level)
  starting transfers between devices: 11.8 us -> 12.8 us
    ppermute x2 -> x1, waiting for transfers between devices: 0.59 us -> 2.16 us  [whole_blocks(): others.append(lax.ppermute(part, 'uly', swap))]
    ppermute x1, starting transfers between devices: 0.26 us -> 1.73 us  [whole_blocks(): back = lax.ppermute(give, 'uly', swap)]
    ppermute x1, waiting for transfers between devices: 5.05 us -> 3.58 us  [whole_blocks(): back = lax.ppermute(give, 'uly', swap)]
    ppermute x2 -> x1, waiting for transfers between devices: 2.52 us -> 1.71 us  [whole_blocks(): from_sib = [lax.ppermute(part, 'uly', swap) for part in grads]]
    ppermute x2 -> x1, starting transfers between devices: 2.44 us -> 1.73 us  [whole_blocks(): from_sib = [lax.ppermute(part, 'uly', swap) for part in grads]]
    ppermute x2 -> x1, starting transfers between devices: 2.16 us -> 1.73 us  [whole_blocks(): others.append(lax.ppermute(part, 'uly', swap))]
    unnamed x12 -> x16, local copies, waits for them, and re-layouts: 1.65 us -> 1.43 us
    pallas_call x13 -> x11, Pallas kernels: 7.48 us -> 7.34 us  [call(): pl.pallas_call(kernel, in_specs=[smem] * len(scalars) + [vmem] * (len(ope...]
  transfers between devices with their start and end apart: 7 -> 5, of which waited for: 6 -> 5; matrix products, arithmetic and copies ran while one was open for 0% -> 0% of each run, Pallas kernels for 20% -> 17%
where the time goes in v15:
time: 68 us; the launch traced here: 67.7 us
  blocking collectives  20.4 us (30%)
  Pallas kernels  16.6 us (24%)
  waiting for transfers between devices  15.7 us (23%)
  starting transfers between devices  12.8 us (19%)
  local copies, waits for them, and re-layouts  1.43 us (2%)
  between operations  0.78 us (1%)
    all_to_all x1, blocking collectives, whole_blocks(): lax.all_to_all(outgoing, 'grp', split_axis=0, concat_axis=0, tiled=True)  20.4 us
    pallas_call x11, Pallas kernels, call(): pl.pallas_call(kernel, in_specs=[smem] * len(scalars) + [vmem] * (len(ope...  7.34 us
    pallas_call x1, Pallas kernels, whole_blocks(): pl.pallas_call(partial(local_kernel, seen_at=seen_at, **sizes), grid_spec...  6.91 us
    all_to_all x1, waiting for transfers between devices, whole_blocks(): lax.all_to_all(returning, 'grp', split_axis=0, concat_axis=0, tiled=True)  6.13 us
    all_to_all x1, starting transfers between devices, whole_blocks(): lax.all_to_all(returning, 'grp', split_axis=0, concat_axis=0, tiled=True)  4.54 us
    ppermute x1, waiting for transfers between devices, whole_blocks(): back = lax.ppermute(give, 'uly', swap)  3.58 us
    ppermute x1, starting transfers between devices, whole_blocks(): gotten = lax.ppermute(given, 'uly', swap)  3.03 us
    ppermute x1, waiting for transfers between devices, whole_blocks(): others.append(lax.ppermute(part, 'uly', swap))  2.16 us
  transfers between devices with their start and end apart: 5, of which 5 were waited for; matrix products, arithmetic and copies ran while one was open for 0% of the time, Pallas kernels for 17%

profile of v15, /device:TPU:0, one launch (start us, length us, event | category | flops | bytes accessed | tf_op | source)
XLA Modules:
  0.0 67.7 jit_solution(4397582191146463494)
XLA Ops:
  0.6 1.3 %pack.1 = (bf16[512,128]{1,0:T(8,128)(2,1)S(1)}, bf16[512,128]{1,0:T(8,128)(2,1)S(1)}, bf16[4,2,64,128]{3,2,1,0:T(8,128)(2,1)S(1)}) custom-call(bf16[512,128]{1,0:T(8,128)(2,1)} %bitcast.19, bf16[512,128]{1,0:T(8,128)(2,1)} %bitcast.21), custom_call_target="tpu_custom_call" | custom-call | tf_op jit(solution)/shard_map/pack/pallas_call | solution.py:580
  1.9 3.0 %collective-permute-start = (bf16[4,2,64,128]{3,2,1,0:T(8,128)(2,1)S(1)}, bf16[4,2,64,128]{3,2,1,0:T(8,128)(2,1)S(1)}, u32[]{:S(2)}, u32[]{:S(2)}) collective-permute-start(bf16[4,2,64,128]{3,2,1,0:T(8,128)(2,1)S(1)} %get-tuple-element.26.given_ref), channel_id=1, source_target_pairs={{0,1},{1,0},{2,3},{3,2},{4,5},{5,4},{6,7},{7,6},{8,9},{9,8},{10,11... | collective-permute-start | bytes 393224 | tf_op jit(solution)/shard_map/ppermute | solution.py:597
  4.9 1.1 %plan.1.plan_ref = s32[44]{0:T(128)S(4)} custom-call(s32[128]{0:T(128)} %bitcast.27, s32[128]{0:T(128)} %counts_ref.1), custom_call_target="tpu_custom_call" | custom-call | tf_op jit(solution)/shard_map/plan/pallas_call | solution.py:589
  6.0 0.2 send_own.1
  6.3 2.1 %collective-permute-done.blocks_ref = bf16[4,2,64,128]{3,2,1,0:T(8,128)(2,1)S(1)} collective-permute-done((bf16[4,2,64,128]{3,2,1,0:T(8,128)(2,1)S(1)}, bf16[4,2,64,128]{3,2,1,0:T(8,128)(2,1)S(1)}, u32[]{:S(2)}, u32[]{:S(2)}) %collective-permute-start) | collective-permute-done | bytes 131104 | tf_op jit(solution)/shard_map/ppermute | solution.py:597
  8.4 0.1 send_sibling.1
  8.5 0.0 copy-start
  8.5 20.4 %all_to_all.10.arrived_ref.mine_ref = bf16[16,2,64,128]{3,2,1,0:T(8,128)(2,1)S(1)} all-to-all(bf16[16,2,64,128]{3,2,1,0:T(8,128)(2,1)S(1)} %send_sibling.1), channel_id=1, replica_groups=mesh['grp'=16,'uly'=2] {'grp'}, dimensions={0} | all-to-all | bytes 1048576 | tf_op jit(solution)/shard_map/all_to_all | solution.py:608
  29.0 1.7 %collective-permute-start.1 = (bf16[4,2,64,128]{3,2,1,0:T(8,128)(2,1)S(1)}, bf16[4,2,64,128]{3,2,1,0:T(8,128)(2,1)S(1)}, u32[]{:S(2)}, u32[]{:S(2)}) collective-permute-start(bf16[4,2,64,128]{3,2,1,0:T(8,128)(2,1)S(1)} %give.1), channel_id=1, source_target_pairs={{0,1},{1,0},{2,3},{3,2},{4,5},{5,4},{6,7},{7,6},{8,9},{9,8},{10,11... | collective-permute-start | bytes 393224 | tf_op jit(solution)/shard_map/ppermute | solution.py:622
  30.7 0.0 copy-done.1
  30.7 0.7 %near.1.stat_ref = f32[4,8,1024]{2,1,0:T(8,128)S(1)} custom-call(bf16[4096,128]{1,0:T(8,128)(2,1)S(1)} %bitcast.9, bf16[4096,128]{1,0:T(8,128)(2,1)S(1)} %bitcast.14, bf16[4,2,64,128]{3,2,1,0:T(8,128)(2,1)S(1)} %get-tuple-element.29.kept_ref, bf16[4,2,64,128]{3,2,1,0:T(8,128)(2,1)S(1)} %get-tuple-element.26.given_ref), custom_call_target="tpu_custom_call" | custom-call | tf_op jit(solution)/shard_map/near/pallas_call | solution.py:560
  31.4 0.9 %mid.1.stat_ref = f32[4,8,1024]{2,1,0:T(8,128)S(1)} custom-call(s32[44]{0:T(128)S(4)} %plan.1.plan_ref, bf16[4096,128]{1,0:T(8,128)(2,1)S(1)} %bitcast.10, bf16[4096,128]{1,0:T(8,128)(2,1)S(1)} %bitcast.15, f32[4,8,1024]{2,1,0:T(8,128)S(1)} %near.1.stat_ref, bf16[16,2,64,128]{3,2,1,0:T(8,128)(2,1)S(1)} %all_to_all.10.arrived_ref.mine_ref), custom_call_target="tpu_custom_call" | custom-call | tf_op jit(solution)/shard_map/mid/pallas_call | solution.py:560
  32.3 2.2 %collective-permute-done.1.other_ref = bf16[4,2,64,128]{3,2,1,0:T(8,128)(2,1)S(1)} collective-permute-done((bf16[4,2,64,128]{3,2,1,0:T(8,128)(2,1)S(1)}, bf16[4,2,64,128]{3,2,1,0:T(8,128)(2,1)S(1)}, u32[]{:S(2)}, u32[]{:S(2)}) %collective-permute-start.1) | collective-permute-done | bytes 131104 | tf_op jit(solution)/shard_map/ppermute | solution.py:622
  34.4 1.7 %far.1 = (bf16[4,2,64,128]{3,2,1,0:T(8,128)(2,1)S(1)}, f32[4,8,1024]{2,1,0:T(8,128)S(1)}) custom-call(s32[44]{0:T(128)S(4)} %plan.1.plan_ref, bf16[4096,128]{1,0:T(8,128)(2,1)S(1)} %bitcast.11, bf16[4096,128]{1,0:T(8,128)(2,1)S(1)} %bitcast.16, f32[4,8,1024]{2,1,0:T(8,128)S(1)} %mid.1.stat_ref, bf16[4,2,64,128]{3,2,1,0:T(8,128)(2,1)S(1)} %collective-permute-done.1.other_ref), custom_call_target="tpu_custom_call" | custom-call | tf_op jit(solution)/shard_map/far/pallas_call | solution.py:560
  36.2 1.7 %collective-permute-start.2 = (bf16[4,2,64,128]{3,2,1,0:T(8,128)(2,1)S(1)}, bf16[4,2,64,128]{3,2,1,0:T(8,128)(2,1)S(1)}, u32[]{:S(2)}, u32[]{:S(2)}) collective-permute-start(bf16[4,2,64,128]{3,2,1,0:T(8,128)(2,1)S(1)} %get-tuple-element.31), channel_id=1, source_target_pairs={{0,1},{1,0},{2,3},{3,2},{4,5},{5,4},{6,7},{7,6},{8,9},{9,8},{10,11... | collective-permute-start | bytes 393224 | tf_op jit(solution)/shard_map/ppermute | solution.py:636
  37.9 1.6 %mine.1.refs_0_ = bf16[4,2,64,128]{3,2,1,0:T(8,128)(2,1)S(1)} custom-call(s32[44]{0:T(128)S(4)} %plan.1.plan_ref, bf16[4096,128]{1,0:T(8,128)(2,1)S(1)} %bitcast.12, bf16[4096,128]{1,0:T(8,128)(2,1)S(1)} %bitcast.17, bf16[16,2,64,128]{3,2,1,0:T(8,128)(2,1)S(1)} %all_to_all.10.arrived_ref.mine_ref, f32[4,8,1024]{2,1,0:T(8,128)S(1)} %get-tuple-element.30.stat_ref), custom_call_target="tpu_custom_call" | custom-call | tf_op jit(solution)/shard_map/mine/pallas_call | solution.py:560
  39.5 1.7 %collective-permute-done.2.refs_1_ = bf16[4,2,64,128]{3,2,1,0:T(8,128)(2,1)S(1)} collective-permute-done((bf16[4,2,64,128]{3,2,1,0:T(8,128)(2,1)S(1)}, bf16[4,2,64,128]{3,2,1,0:T(8,128)(2,1)S(1)}, u32[]{:S(2)}, u32[]{:S(2)}) %collective-permute-start.2) | collective-permute-done | bytes 131104 | tf_op jit(solution)/shard_map/ppermute | solution.py:636
  41.2 0.8 %return.1 = bf16[16,2,64,128]{3,2,1,0:T(8,128)(2,1)} custom-call(s32[44]{0:T(128)S(4)} %plan.1.plan_ref, bf16[4,2,64,128]{3,2,1,0:T(8,128)(2,1)S(1)} %mine.1.refs_0_, bf16[4,2,64,128]{3,2,1,0:T(8,128)(2,1)S(1)} %collective-permute-done.2.refs_1_), custom_call_target="tpu_custom_call" | custom-call | tf_op jit(solution)/shard_map/return/pallas_call | solution.py:560
  42.0 0.0 copy-start.2
  42.0 0.0 copy-start.3
  42.0 4.5 %all-to-all-start.1 = ((bf16[16,2,64,128]{3,2,1,0:T(8,128)(2,1)}), bf16[16,2,64,128]{3,2,1,0:T(8,128)(2,1)S(1)}, u32[]{:S(2)}, u32[]{:S(2)}) async-start(bf16[16,2,64,128]{3,2,1,0:T(8,128)(2,1)} %return.1), calls=%async_computation.1 | async-start | bytes 1048576 | tf_op jit(solution)/shard_map/all_to_all | solution.py:654
  46.6 6.9 %local.1 = (bf16[4096,128]{1,0:T(8,128)(2,1)}, bf16[4096,128]{1,0:T(8,128)(2,1)}, f32[512,128]{1,0:T(8,128)S(1)}, f32[512,128]{1,0:T(8,128)S(1)}) custom-call(s32[44]{0:T(128)S(4)} %plan.1.plan_ref, bf16[4096,128]{1,0:T(8,128)(2,1)S(1)} %bitcast.13, bf16[4096,128]{1,0:T(8,128)(2,1)S(1)} %bitcast.18, bf16[512,128]{1,0:T(8,128)(2,1)S(1)} %bitcast.20, ...), custom_call_target="tpu_custom_call" | custom-call | tf_op jit(solution)/shard_map/local/pallas_call | solution.py:660
  53.5 0.7 %copy-done.4 = f32[512,128]{1,0:T(8,128)} copy-done((f32[512,128]{1,0:T(8,128)}, f32[512,128]{1,0:T(8,128)S(1)}, u32[]{:S(2)}) %copy-start.4) | copy-done | bytes 262168
  54.2 0.7 %copy-done.6 = f32[512,128]{1,0:T(8,128)} copy-done((f32[512,128]{1,0:T(8,128)}, f32[512,128]{1,0:T(8,128)S(1)}, u32[]{:S(2)}) %copy-start.6) | copy-done | bytes 262168
  54.9 6.1 %all-to-all-done.1.landed_ref = bf16[16,2,64,128]{3,2,1,0:T(8,128)(2,1)S(1)} async-done(((bf16[16,2,64,128]{3,2,1,0:T(8,128)(2,1)}), bf16[16,2,64,128]{3,2,1,0:T(8,128)(2,1)S(1)}, u32[]{:S(2)}, u32[]{:S(2)}) %all-to-all-start.1) | async-done | bytes 524320 | tf_op jit(solution)/shard_map/all_to_all | solution.py:654
  61.1 0.2 land_sibling.1
  61.2 0.0 copy-start.5
  61.2 0.0 copy-start.7
  61.3 1.7 %collective-permute-start.3 = (bf16[4,2,64,128]{3,2,1,0:T(8,128)(2,1)S(1)}, bf16[4,2,64,128]{3,2,1,0:T(8,128)(2,1)S(1)}, u32[]{:S(2)}, u32[]{:S(2)}) collective-permute-start(bf16[4,2,64,128]{3,2,1,0:T(8,128)(2,1)S(1)} %land_sibling.1), channel_id=1, source_target_pairs={{0,1},{1,0},{2,3},{3,2},{4,5},{5,4},{6,7},{7,6},{8,9},{9,8},{10,11... | collective-permute-start | bytes 393224 | tf_op jit(solution)/shard_map/ppermute | solution.py:682
  63.0 0.2 land_own.1.own_ref
  63.2 3.6 %collective-permute-done.3.back_ref = bf16[4,2,64,128]{3,2,1,0:T(8,128)(2,1)S(1)} collective-permute-done((bf16[4,2,64,128]{3,2,1,0:T(8,128)(2,1)S(1)}, bf16[4,2,64,128]{3,2,1,0:T(8,128)(2,1)S(1)}, u32[]{:S(2)}, u32[]{:S(2)}) %collective-permute-start.3) | collective-permute-done | bytes 131104 | tf_op jit(solution)/shard_map/ppermute | solution.py:682
  66.8 1.0 %finish.1 = (bf16[512,128]{1,0:T(8,128)(2,1)}, bf16[512,128]{1,0:T(8,128)(2,1)}) custom-call(f32[512,128]{1,0:T(8,128)S(1)} %copy-done.5, f32[512,128]{1,0:T(8,128)S(1)} %copy-done.7, f32[4,2,64,128]{3,2,1,0:T(8,128)S(1)} %land_own.1.own_ref, bf16[4,2,64,128]{3,2,1,0:T(8,128)(2,1)S(1)} %collective-permute-done.3.back_ref), custom_call_target="tpu_custom_call" | custom-call | tf_op jit(solution)/shard_map/finish/pallas_call | solution.py:560
  (9 shorter events, 0.0 us)
Async XLA Ops:
  1.9 6.5 %collective-permute-start = (bf16[4,2,64,128]{3,2,1,0:T(8,128)(2,1)S(1)}, bf16[4,2,64,128]{3,2,1,0:T(8,128)(2,1)S(1)}, u32[]{:S(2)}, u32[]{:S(2)}) collective-permute-start(bf16[4,2,64,128]{3,2,1,0:T(8,128)(2,1)S(1)} %get-tuple-element.26.given_ref), channel_id=1, source_target_pairs={{0,1},{1,0},{2,3},{3,2},{4,5},{5,4},{6,7},{7,6},{8,9},{9,8},{10,11... | collective-permute-start | bytes 393224 | tf_op jit(solution)/shard_map/ppermute | solution.py:597
  8.4 22.3 %copy-start.1 = (bf16[128,32,128]{2,1,0:T(8,128)(2,1)S(1)}, bf16[128,32,128]{2,1,0:T(8,128)(2,1)}, u32[]{:S(2)}) copy-start(bf16[128,32,128]{2,1,0:T(8,128)(2,1)} %param.9) | copy-start | bytes 3145732
  8.5 22.2 %copy-start = (bf16[128,32,128]{2,1,0:T(8,128)(2,1)S(1)}, bf16[128,32,128]{2,1,0:T(8,128)(2,1)}, u32[]{:S(2)}) copy-start(bf16[128,32,128]{2,1,0:T(8,128)(2,1)} %param.6) | copy-start | bytes 3145732
  29.0 5.5 %collective-permute-start.1 = (bf16[4,2,64,128]{3,2,1,0:T(8,128)(2,1)S(1)}, bf16[4,2,64,128]{3,2,1,0:T(8,128)(2,1)S(1)}, u32[]{:S(2)}, u32[]{:S(2)}) collective-permute-start(bf16[4,2,64,128]{3,2,1,0:T(8,128)(2,1)S(1)} %give.1), channel_id=1, source_target_pairs={{0,1},{1,0},{2,3},{3,2},{4,5},{5,4},{6,7},{7,6},{8,9},{9,8},{10,11... | collective-permute-start | bytes 393224 | tf_op jit(solution)/shard_map/ppermute | solution.py:622
  36.2 5.0 %collective-permute-start.2 = (bf16[4,2,64,128]{3,2,1,0:T(8,128)(2,1)S(1)}, bf16[4,2,64,128]{3,2,1,0:T(8,128)(2,1)S(1)}, u32[]{:S(2)}, u32[]{:S(2)}) collective-permute-start(bf16[4,2,64,128]{3,2,1,0:T(8,128)(2,1)S(1)} %get-tuple-element.31), channel_id=1, source_target_pairs={{0,1},{1,0},{2,3},{3,2},{4,5},{5,4},{6,7},{7,6},{8,9},{9,8},{10,11... | collective-permute-start | bytes 393224 | tf_op jit(solution)/shard_map/ppermute | solution.py:636
  42.0 4.6 %copy-start.2 = (bf16[128,4,128]{2,1,0:T(4,128)(2,1)S(1)}, bf16[128,4,128]{2,1,0:T(4,128)(2,1)}, u32[]{:S(2)}) copy-start(bf16[128,4,128]{2,1,0:T(4,128)(2,1)} %param.7) | copy-start | bytes 393220
  42.0 4.6 %copy-start.3 = (bf16[128,4,128]{2,1,0:T(4,128)(2,1)S(1)}, bf16[128,4,128]{2,1,0:T(4,128)(2,1)}, u32[]{:S(2)}) copy-start(bf16[128,4,128]{2,1,0:T(4,128)(2,1)} %param.8) | copy-start | bytes 393220
  42.0 19.0 %all-to-all-start.1 = ((bf16[16,2,64,128]{3,2,1,0:T(8,128)(2,1)}), bf16[16,2,64,128]{3,2,1,0:T(8,128)(2,1)S(1)}, u32[]{:S(2)}, u32[]{:S(2)}) async-start(bf16[16,2,64,128]{3,2,1,0:T(8,128)(2,1)} %return.1), calls=%async_computation.1 | async-start | bytes 1048576 | tf_op jit(solution)/shard_map/all_to_all | solution.py:654
  53.5 0.7 %copy-start.4 = (f32[512,128]{1,0:T(8,128)}, f32[512,128]{1,0:T(8,128)S(1)}, u32[]{:S(2)}) copy-start(f32[512,128]{1,0:T(8,128)S(1)} %get-tuple-element.37.dk_near_ref) | copy-start | bytes 786436
  54.2 0.7 %copy-start.6 = (f32[512,128]{1,0:T(8,128)}, f32[512,128]{1,0:T(8,128)S(1)}, u32[]{:S(2)}) copy-start(f32[512,128]{1,0:T(8,128)S(1)} %get-tuple-element.38.dv_near_ref) | copy-start | bytes 786436
  61.2 5.5 %copy-start.5 = (f32[512,128]{1,0:T(8,128)S(1)}, f32[512,128]{1,0:T(8,128)}, u32[]{:S(2)}) copy-start(f32[512,128]{1,0:T(8,128)} %copy-done.4) | copy-start | bytes 786436
  61.2 5.5 %copy-start.7 = (f32[512,128]{1,0:T(8,128)S(1)}, f32[512,128]{1,0:T(8,128)}, u32[]{:S(2)}) copy-start(f32[512,128]{1,0:T(8,128)} %copy-done.6) | copy-start | bytes 786436
  61.3 5.5 %collective-permute-start.3 = (bf16[4,2,64,128]{3,2,1,0:T(8,128)(2,1)S(1)}, bf16[4,2,64,128]{3,2,1,0:T(8,128)(2,1)S(1)}, u32[]{:S(2)}, u32[]{:S(2)}) collective-permute-start(bf16[4,2,64,128]{3,2,1,0:T(8,128)(2,1)S(1)} %land_sibling.1), channel_id=1, source_target_pairs={{0,1},{1,0},{2,3},{3,2},{4,5},{5,4},{6,7},{7,6},{8,9},{9,8},{10,11... | collective-permute-start | bytes 393224 | tf_op jit(solution)/shard_map/ppermute | solution.py:682

commit v16 on v10

--- a/solution.py
+++ b/solution.py
@@ -206,6 +206,13 @@
     col = lax.broadcasted_iota(jnp.int32, (cols, cols), 1)
     token = row // half * place + row % place
     return jnp.where(col == token * kv_heads + row % half // place, 1.0, 0.0).astype(BF16)
+
+
+def token_major(half, kv_heads):
+    place = half // kv_heads
+    row = lax.broadcasted_iota(jnp.int32, (half, half), 0)
+    col = lax.broadcasted_iota(jnp.int32, (half, half), 1)
+    return jnp.where(col == row % kv_heads * place + row // kv_heads, 1.0, 0.0).astype(BF16)
 
 
 def reorder(one_hot, array):
@@ -261,17 +268,19 @@
 
 def pack_kernel(k_hbm, v_hbm, kept_ref, given_ref, k_ref, v_ref, sems, *, kv_heads):
     blocks, _, half, _ = kept_ref.shape
-    copies = [
-        pltpu.make_async_copy(k_hbm, k_ref, sems.at[0]),
-        pltpu.make_async_copy(v_hbm, v_ref, sems.at[1]),
-    ]
-    for copy in copies:
-        copy.start()
+    arrays = ((k_hbm, k_ref), (v_hbm, v_ref))
+    copies = []
+    for block in range(blocks):
+        span = pl.ds(block * 2 * half, 2 * half)
+        for which, (source, target) in enumerate(arrays):
+            sem = sems.at[which, block]
+            copies.append(pltpu.make_async_copy(source.at[span], target.at[span], sem))
+            copies[-1].start()
     first = lax.axis_index("uly") == 0
     order = head_major(2 * half, kv_heads)
-    for which, ref in enumerate((k_ref, v_ref)):
-        copies[which].wait()
-        for block in range(blocks):
+    for block in range(blocks):
+        for which, (_, ref) in enumerate(arrays):
+            copies[2 * block + which].wait()
             ordered = reorder(order, ref[block * 2 * half:(block + 1) * 2 * half])
             kept_ref[block, which] = jnp.where(first, ordered[:half], ordered[half:])
             given_ref[block, which] = jnp.where(first, ordered[half:], ordered[:half])
@@ -487,20 +496,40 @@
     out_ref[...] = sum_ref[...].astype(out_ref.dtype)
 
 
+def own_half_kernel(
+    plan_ref, landed_ref, dk_near_ref, dv_near_ref, out_ref, sum_ref, *, kv_heads
+):
+    sum_ref[...] = jnp.zeros_like(sum_ref)
+    for group in range(landed_ref.shape[0]):
+        place = plan_ref[group]
+
+        @pl.when(place >= 0)
+        def _():
+            sum_ref[place] = sum_ref[place] + landed_ref[group].astype(F32)
+
+    blocks, _, half, _ = out_ref.shape
+    order = token_major(half, kv_heads)
+    mine = lax.axis_index("uly")
+    for block in range(blocks):
+        span = pl.ds(pl.multiple_of((2 * block + mine) * half, half), half)
+        for which, near_ref in enumerate((dk_near_ref, dv_near_ref)):
+            summed = (near_ref[span] + sum_ref[block, which]).astype(BF16)
+            out_ref[block, which] = reorder(order, summed)
+
+
 def finish_kernel(
     dk_near_ref, dv_near_ref, own_ref, back_ref, dk_ref, dv_ref, *, kv_heads
 ):
     blocks, _, half, _ = back_ref.shape
-    mine = lax.axis_index("uly") == 0
-    order = head_major(2 * half, kv_heads)
-    for block in range(blocks):
-        span = slice(block * 2 * half, (block + 1) * 2 * half)
-        for near_ref, out_ref, which in ((dk_near_ref, dk_ref, 0), (dv_near_ref, dv_ref, 1)):
-            own = own_ref[block, which]
-            back = back_ref[block, which].astype(F32)
-            far = jnp.concatenate([jnp.where(mine, own, back), jnp.where(mine, back, own)], axis=0)
-            summed = (near_ref[span] + far).astype(BF16)
-            out_ref[span] = dot_first(order, summed).astype(BF16)
+    order = token_major(half, kv_heads)
+    mine = lax.axis_index("uly")
+    for which, (near_ref, out_ref) in enumerate(((dk_near_ref, dk_ref), (dv_near_ref, dv_ref))):
+        for block in range(blocks):
+            here = pl.ds(pl.multiple_of((2 * block + mine) * half, half), half)
+            there = pl.ds(pl.multiple_of((2 * block + 1 - mine) * half, half), half)
+            summed = (near_ref[there] + back_ref[block, which].astype(F32)).astype(BF16)
+            out_ref[here] = own_ref[block, which]
+            out_ref[there] = reorder(order, summed)
 
 
 def take_rows(array, index):
@@ -568,7 +597,8 @@
         out_specs=[vmem, vmem],
         out_shape=[part_shape, part_shape],
         scratch_shapes=[
-            pltpu.VMEM(k2.shape, BF16), pltpu.VMEM(k2.shape, BF16), pltpu.SemaphoreType.DMA((2,))
+            pltpu.VMEM(k2.shape, BF16), pltpu.VMEM(k2.shape, BF16),
+            pltpu.SemaphoreType.DMA((2, mine_blocks)),
         ],
         compiler_params=limit,
         name="pack",
@@ -676,8 +706,8 @@
     )
     back = lax.ppermute(give, "uly", swap)
     own = call(
-        partial(landing_kernel, first=0), "land_own", (plan,), (landed,),
-        jax.ShapeDtypeStruct(part_shape.shape, F32), sum_scratch,
+        partial(own_half_kernel, kv_heads=kv_heads), "land_own", (plan,),
+        (landed, dk_near, dv_near), part_shape, sum_scratch,
     )
     dk, dv = call(
         partial(finish_kernel, kv_heads=kv_heads), "finish", (),

time: 67.6 us -> 68.3 us (1.010)
  Pallas kernels: 19 us -> 19.8 us
    pallas_call x1, Pallas kernels: 1.29 us -> 2.03 us  [whole_blocks(): pl.pallas_call(partial(pack_kernel, kv_heads=kv_heads), in_specs=[anywher...]
where the time goes in v16:
time: 68.3 us; the launch traced here: 67.9 us
  blocking collectives  20.3 us (30%)
  Pallas kernels  19.8 us (29%)
  starting transfers between devices  12.9 us (19%)
  waiting for transfers between devices  12.4 us (18%)
  local copies, waits for them, and re-layouts  1.64 us (2%)
  between operations  0.79 us (1%)
    all_to_all x1, blocking collectives, whole_blocks(): lax.all_to_all(outgoing, 'grp', split_axis=0, concat_axis=0, tiled=True)  20.3 us
    pallas_call x1, Pallas kernels, whole_blocks(): pl.pallas_call(partial(local_kernel, seen_at=seen_at, **sizes), grid_spec...  6.87 us
    pallas_call x12, Pallas kernels, call(): pl.pallas_call(kernel, in_specs=[smem] * len(scalars) + [vmem] * (len(ope...  6.75 us
    all_to_all x1, waiting for transfers between devices, whole_blocks(): lax.all_to_all(returning, 'grp', split_axis=0, concat_axis=0, tiled=True)  5.93 us
    all_to_all x1, starting transfers between devices, whole_blocks(): lax.all_to_all(returning, 'grp', split_axis=0, concat_axis=0, tiled=True)  4.14 us
    ppermute x1, waiting for transfers between devices, whole_blocks(): back = lax.ppermute(give, 'uly', swap)  3.77 us
    pallas_call x1, Pallas kernels, whole_blocks(): pl.pallas_call(partial(near_kernel, **sizes), grid=(mine_blocks,), in_spe...  3.08 us
    ppermute x1, starting transfers between devices, whole_blocks(): gotten = lax.ppermute(given, 'uly', swap)  3.03 us
  transfers between devices with their start and end apart: 7, of which 5 were waited for; matrix products, arithmetic and copies ran while one was open for 0% of the time, Pallas kernels for 23%

profile of v16, /device:TPU:0, one launch (start us, length us, event | category | flops | bytes accessed | tf_op | source)
XLA Modules:
  0.0 67.9 jit_solution(3911938677323261691)
XLA Ops:
  0.6 2.0 %pack.1 = (bf16[4,2,64,128]{3,2,1,0:T(8,128)(2,1)S(1)}, bf16[4,2,64,128]{3,2,1,0:T(8,128)(2,1)S(1)}) custom-call(bf16[512,128]{1,0:T(8,128)(2,1)} %bitcast.23, bf16[512,128]{1,0:T(8,128)(2,1)} %bitcast.25), custom_call_target="tpu_custom_call" | custom-call | tf_op jit(solution)/shard_map/pack/pallas_call | solution.py:594
  2.7 3.0 %collective-permute-start = (bf16[4,2,64,128]{3,2,1,0:T(8,128)(2,1)S(1)}, bf16[4,2,64,128]{3,2,1,0:T(8,128)(2,1)S(1)}, u32[]{:S(2)}, u32[]{:S(2)}) collective-permute-start(bf16[4,2,64,128]{3,2,1,0:T(8,128)(2,1)S(1)} %get-tuple-element.28.given_ref), channel_id=1, source_target_pairs={{0,1},{1,0},{2,3},{3,2},{4,5},{5,4},{6,7},{7,6},{8,9},{9,8},{10,11... | collective-permute-start | bytes 393224 | tf_op jit(solution)/shard_map/ppermute | solution.py:614
  5.7 1.1 %plan.1.plan_ref = s32[44]{0:T(128)S(4)} custom-call(s32[128]{0:T(128)} %bitcast.31, s32[128]{0:T(128)} %counts_ref.1), custom_call_target="tpu_custom_call" | custom-call | tf_op jit(solution)/shard_map/plan/pallas_call | solution.py:606
  6.9 3.1 %near.1.stat_ref = f32[4,8,1024]{2,1,0:T(8,128)S(1)} custom-call(bf16[4096,128]{1,0:T(8,128)(2,1)} %bitcast.9, bf16[4096,128]{1,0:T(8,128)(2,1)} %bitcast.16, bf16[4,2,64,128]{3,2,1,0:T(8,128)(2,1)S(1)} %get-tuple-element.29.kept_ref.blocks_ref, bf16[4,2,64,128]{3,2,1,0:T(8,128)(2,1)S(1)} %get-tuple-element.28.given_ref), custom_call_target="tpu_custom_call" | custom-call | tf_op jit(solution)/shard_map/near/pallas_call | solution.py:617
  10.0 0.1 send_sibling.1
  10.1 0.0 copy-start
  10.1 20.3 %all_to_all.10.arrived_ref.mine_ref = bf16[16,2,64,128]{3,2,1,0:T(8,128)(2,1)S(1)} all-to-all(bf16[16,2,64,128]{3,2,1,0:T(8,128)(2,1)S(1)} %send_sibling.1), channel_id=1, replica_groups=mesh['grp'=16,'uly'=2] {'grp'}, dimensions={0} | all-to-all | bytes 1048576 | tf_op jit(solution)/shard_map/all_to_all | solution.py:635
  30.5 1.0 %collective-permute-start.1 = (bf16[2,2,64,128]{3,2,1,0:T(8,128)(2,1)S(1)}, bf16[2,2,64,128]{3,2,1,0:T(8,128)(2,1)S(1)}, u32[]{:S(2)}, u32[]{:S(2)}) collective-permute-start(bf16[2,2,64,128]{3,2,1,0:T(8,128)(2,1)S(1)} %get-tuple-element.34), channel_id=1, source_target_pairs={{0,1},{1,0},{2,3},{3,2},{4,5},{5,4},{6,7},{7,6},{8,9},{9,8},{10,11... | collective-permute-start | bytes 196616 | tf_op jit(solution)/shard_map/ppermute | solution.py:651
  31.4 0.9 %mid.1.stat_ref = f32[4,8,1024]{2,1,0:T(8,128)S(1)} custom-call(s32[44]{0:T(128)S(4)} %plan.1.plan_ref, bf16[4096,128]{1,0:T(8,128)(2,1)S(1)} %bitcast.10, bf16[4096,128]{1,0:T(8,128)(2,1)S(1)} %bitcast.17, f32[4,8,1024]{2,1,0:T(8,128)S(1)} %near.1.stat_ref, bf16[16,2,64,128]{3,2,1,0:T(8,128)(2,1)S(1)} %all_to_all.10.arrived_ref.mine_ref), custom_call_target="tpu_custom_call" | custom-call | tf_op jit(solution)/shard_map/mid/pallas_call | solution.py:574
  32.3 1.2 %collective-permute-start.3 = (bf16[2,2,64,128]{3,2,1,0:T(8,128)(2,1)S(1)}, bf16[2,2,64,128]{3,2,1,0:T(8,128)(2,1)S(1)}, u32[]{:S(2)}, u32[]{:S(2)}) collective-permute-start(bf16[2,2,64,128]{3,2,1,0:T(8,128)(2,1)S(1)} %get-tuple-element.38), channel_id=1, source_target_pairs={{0,1},{1,0},{2,3},{3,2},{4,5},{5,4},{6,7},{7,6},{8,9},{9,8},{10,11... | collective-permute-start | bytes 196616 | tf_op jit(solution)/shard_map/ppermute | solution.py:651
  33.5 1.5 %collective-permute-done.1.other_ref = bf16[2,2,64,128]{3,2,1,0:T(8,128)(2,1)S(1)} collective-permute-done((bf16[2,2,64,128]{3,2,1,0:T(8,128)(2,1)S(1)}, bf16[2,2,64,128]{3,2,1,0:T(8,128)(2,1)S(1)}, u32[]{:S(2)}, u32[]{:S(2)}) %collective-permute-start.1) | collective-permute-done | bytes 65568 | tf_op jit(solution)/shard_map/ppermute | solution.py:651
  35.0 0.9 %far.2 = (bf16[2,2,64,128]{3,2,1,0:T(8,128)(2,1)S(1)}, f32[2,8,1024]{2,1,0:T(8,128)S(1)}) custom-call(s32[44]{0:T(128)S(4)} %plan.1.plan_ref, bf16[4096,128]{1,0:T(8,128)(2,1)S(1)} %bitcast.11, bf16[4096,128]{1,0:T(8,128)(2,1)S(1)} %bitcast.18, f32[4,8,1024]{2,1,0:T(8,128)S(1)} %mid.1.stat_ref, bf16[2,2,64,128]{3,2,1,0:T(8,128)(2,1)S(1)} %collective-permute-done.1.other_ref), custom_call_target="tpu_custom_call" | custom-call | tf_op jit(solution)/shard_map/far/pallas_call | solution.py:574
  35.9 0.8 %collective-permute-start.2 = (bf16[2,2,64,128]{3,2,1,0:T(8,128)(2,1)S(1)}, bf16[2,2,64,128]{3,2,1,0:T(8,128)(2,1)S(1)}, u32[]{:S(2)}, u32[]{:S(2)}) collective-permute-start(bf16[2,2,64,128]{3,2,1,0:T(8,128)(2,1)S(1)} %get-tuple-element.35), channel_id=1, source_target_pairs={{0,1},{1,0},{2,3},{3,2},{4,5},{5,4},{6,7},{7,6},{8,9},{9,8},{10,11... | collective-permute-start | bytes 196616 | tf_op jit(solution)/shard_map/ppermute | solution.py:661
  36.7 0.9 %far.3 = (bf16[2,2,64,128]{3,2,1,0:T(8,128)(2,1)S(1)}, f32[2,8,1024]{2,1,0:T(8,128)S(1)}) custom-call(s32[44]{0:T(128)S(4)} %plan.1.plan_ref, bf16[4096,128]{1,0:T(8,128)(2,1)S(1)} %bitcast.12, bf16[4096,128]{1,0:T(8,128)(2,1)S(1)} %bitcast.19, f32[4,8,1024]{2,1,0:T(8,128)S(1)} %mid.1.stat_ref, bf16[2,2,64,128]{3,2,1,0:T(8,128)(2,1)S(1)} %collective-permute-done.3.other_ref), custom_call_target="tpu_custom_call" | custom-call | tf_op jit(solution)/shard_map/far/pallas_call | solution.py:574
  37.6 1.4 %collective-permute-start.4 = (bf16[2,2,64,128]{3,2,1,0:T(8,128)(2,1)S(1)}, bf16[2,2,64,128]{3,2,1,0:T(8,128)(2,1)S(1)}, u32[]{:S(2)}, u32[]{:S(2)}) collective-permute-start(bf16[2,2,64,128]{3,2,1,0:T(8,128)(2,1)S(1)} %get-tuple-element.41), channel_id=1, source_target_pairs={{0,1},{1,0},{2,3},{3,2},{4,5},{5,4},{6,7},{7,6},{8,9},{9,8},{10,11... | collective-permute-start | bytes 196616 | tf_op jit(solution)/shard_map/ppermute | solution.py:661
  39.0 0.9 %mine.3.refs_1_ = bf16[2,2,64,128]{3,2,1,0:T(8,128)(2,1)S(1)} custom-call(s32[44]{0:T(128)S(4)} %plan.1.plan_ref, bf16[4096,128]{1,0:T(8,128)(2,1)S(1)} %bitcast.13, bf16[4096,128]{1,0:T(8,128)(2,1)S(1)} %bitcast.20, bf16[16,2,64,128]{3,2,1,0:T(8,128)(2,1)S(1)} %all_to_all.10.arrived_ref.mine_ref, f32[2,8,1024]{2,1,0:T(8,128)S(1)} %get-tuple-element.39.stat_ref), custom_call_target="tpu_custom_call" | custom-call | tf_op jit(solution)/shard_map/mine/pallas_call | solution.py:574
  39.9 0.5 collective-permute-done.2.refs_2_
  40.3 0.9 %mine.2.refs_0_ = bf16[2,2,64,128]{3,2,1,0:T(8,128)(2,1)S(1)} custom-call(s32[44]{0:T(128)S(4)} %plan.1.plan_ref, bf16[4096,128]{1,0:T(8,128)(2,1)S(1)} %bitcast.14, bf16[4096,128]{1,0:T(8,128)(2,1)S(1)} %bitcast.21, bf16[16,2,64,128]{3,2,1,0:T(8,128)(2,1)S(1)} %all_to_all.10.arrived_ref.mine_ref, f32[2,8,1024]{2,1,0:T(8,128)S(1)} %get-tuple-element.37.stat_ref), custom_call_target="tpu_custom_call" | custom-call | tf_op jit(solution)/shard_map/mine/pallas_call | solution.py:574
  41.2 0.8 %collective-permute-done.4.refs_3_ = bf16[2,2,64,128]{3,2,1,0:T(8,128)(2,1)S(1)} collective-permute-done((bf16[2,2,64,128]{3,2,1,0:T(8,128)(2,1)S(1)}, bf16[2,2,64,128]{3,2,1,0:T(8,128)(2,1)S(1)}, u32[]{:S(2)}, u32[]{:S(2)}) %collective-permute-start.4) | collective-permute-done | bytes 65568 | tf_op jit(solution)/shard_map/ppermute | solution.py:661
  42.0 0.8 %return.1 = bf16[16,2,64,128]{3,2,1,0:T(8,128)(2,1)} custom-call(s32[44]{0:T(128)S(4)} %plan.1.plan_ref, bf16[2,2,64,128]{3,2,1,0:T(8,128)(2,1)S(1)} %mine.2.refs_0_, bf16[2,2,64,128]{3,2,1,0:T(8,128)(2,1)S(1)} %mine.3.refs_1_, bf16[2,2,64,128]{3,2,1,0:T(8,128)(2,1)S(1)} %collective-permute-done.2.refs_2_, ...), custom_call_target="tpu_custom_call" | custom-call | tf_op jit(solution)/shard_map/return/pallas_call | solution.py:574
  42.7 4.1 %all-to-all-start.1 = ((bf16[16,2,64,128]{3,2,1,0:T(8,128)(2,1)}), bf16[16,2,64,128]{3,2,1,0:T(8,128)(2,1)S(1)}, u32[]{:S(2)}, u32[]{:S(2)}) async-start(bf16[16,2,64,128]{3,2,1,0:T(8,128)(2,1)} %return.1), calls=%async_computation.1 | async-start | bytes 1048576 | tf_op jit(solution)/shard_map/all_to_all | solution.py:679
  46.9 0.0 copy-start.4
  46.9 0.9 %copy-done.4 = bf16[128,4,128]{2,1,0:T(4,128)(2,1)S(1)} copy-done((bf16[128,4,128]{2,1,0:T(4,128)(2,1)S(1)}, bf16[128,4,128]{2,1,0:T(4,128)(2,1)}, u32[]{:S(2)}) %copy-start.4) | copy-done | bytes 131096
  47.8 0.1 copy-done.5
  47.8 6.9 %local.1 = (bf16[4096,128]{1,0:T(8,128)(2,1)}, bf16[4096,128]{1,0:T(8,128)(2,1)}, f32[512,128]{1,0:T(8,128)S(1)}, f32[512,128]{1,0:T(8,128)S(1)}) custom-call(s32[44]{0:T(128)S(4)} %plan.1.plan_ref, bf16[4096,128]{1,0:T(8,128)(2,1)S(1)} %bitcast.15, bf16[4096,128]{1,0:T(8,128)(2,1)S(1)} %bitcast.22, bf16[512,128]{1,0:T(8,128)(2,1)S(1)} %bitcast.24, ...), custom_call_target="tpu_custom_call" | custom-call | tf_op jit(solution)/shard_map/local/pallas_call | solution.py:685
  54.7 0.7 %copy-done.2 = f32[512,128]{1,0:T(8,128)} copy-done((f32[512,128]{1,0:T(8,128)}, f32[512,128]{1,0:T(8,128)S(1)}, u32[]{:S(2)}) %copy-start.2) | copy-done | bytes 262168
  55.4 5.9 %all-to-all-done.1.landed_ref = bf16[16,2,64,128]{3,2,1,0:T(8,128)(2,1)S(1)} async-done(((bf16[16,2,64,128]{3,2,1,0:T(8,128)(2,1)}), bf16[16,2,64,128]{3,2,1,0:T(8,128)(2,1)S(1)}, u32[]{:S(2)}, u32[]{:S(2)}) %all-to-all-start.1) | async-done | bytes 524320 | tf_op jit(solution)/shard_map/all_to_all | solution.py:679
  61.3 0.2 land_sibling.1
  61.5 1.4 %collective-permute-start.5 = (bf16[4,2,64,128]{3,2,1,0:T(8,128)(2,1)S(1)}, bf16[4,2,64,128]{3,2,1,0:T(8,128)(2,1)S(1)}, u32[]{:S(2)}, u32[]{:S(2)}) collective-permute-start(bf16[4,2,64,128]{3,2,1,0:T(8,128)(2,1)S(1)} %land_sibling.1), channel_id=1, source_target_pairs={{0,1},{1,0},{2,3},{3,2},{4,5},{5,4},{6,7},{7,6},{8,9},{9,8},{10,11... | collective-permute-start | bytes 393224 | tf_op jit(solution)/shard_map/ppermute | solution.py:707
  62.9 0.3 land_own.1.own_ref
  63.2 3.8 %collective-permute-done.5.back_ref = bf16[4,2,64,128]{3,2,1,0:T(8,128)(2,1)S(1)} collective-permute-done((bf16[4,2,64,128]{3,2,1,0:T(8,128)(2,1)S(1)}, bf16[4,2,64,128]{3,2,1,0:T(8,128)(2,1)S(1)}, u32[]{:S(2)}, u32[]{:S(2)}) %collective-permute-start.5) | collective-permute-done | bytes 131104 | tf_op jit(solution)/shard_map/ppermute | solution.py:707
  67.0 0.9 %finish.1 = (bf16[512,128]{1,0:T(8,128)(2,1)}, bf16[512,128]{1,0:T(8,128)(2,1)}) custom-call(f32[512,128]{1,0:T(8,128)S(1)} %get-tuple-element.47.dk_near_ref, f32[512,128]{1,0:T(8,128)S(1)} %copy-done.3, bf16[4,2,64,128]{3,2,1,0:T(8,128)(2,1)S(1)} %land_own.1.own_ref, bf16[4,2,64,128]{3,2,1,0:T(8,128)(2,1)S(1)} %collective-permute-done.5.back_ref), custom_call_target="tpu_custom_call" | custom-call | tf_op jit(solution)/shard_map/finish/pallas_call | solution.py:574
  (12 shorter events, 0.1 us)
Async XLA Ops:
  2.7 7.3 %collective-permute-start = (bf16[4,2,64,128]{3,2,1,0:T(8,128)(2,1)S(1)}, bf16[4,2,64,128]{3,2,1,0:T(8,128)(2,1)S(1)}, u32[]{:S(2)}, u32[]{:S(2)}) collective-permute-start(bf16[4,2,64,128]{3,2,1,0:T(8,128)(2,1)S(1)} %get-tuple-element.28.given_ref), channel_id=1, source_target_pairs={{0,1},{1,0},{2,3},{3,2},{4,5},{5,4},{6,7},{7,6},{8,9},{9,8},{10,11... | collective-permute-start | bytes 393224 | tf_op jit(solution)/shard_map/ppermute | solution.py:614
  10.0 21.5 %copy-start.1 = (bf16[128,32,128]{2,1,0:T(8,128)(2,1)S(1)}, bf16[128,32,128]{2,1,0:T(8,128)(2,1)}, u32[]{:S(2)}) copy-start(bf16[128,32,128]{2,1,0:T(8,128)(2,1)} %param.9) | copy-start | bytes 3145732
  10.1 21.3 %copy-start = (bf16[128,32,128]{2,1,0:T(8,128)(2,1)S(1)}, bf16[128,32,128]{2,1,0:T(8,128)(2,1)}, u32[]{:S(2)}) copy-start(bf16[128,32,128]{2,1,0:T(8,128)(2,1)} %param.6) | copy-start | bytes 3145732
  30.5 4.5 %collective-permute-start.1 = (bf16[2,2,64,128]{3,2,1,0:T(8,128)(2,1)S(1)}, bf16[2,2,64,128]{3,2,1,0:T(8,128)(2,1)S(1)}, u32[]{:S(2)}, u32[]{:S(2)}) collective-permute-start(bf16[2,2,64,128]{3,2,1,0:T(8,128)(2,1)S(1)} %get-tuple-element.34), channel_id=1, source_target_pairs={{0,1},{1,0},{2,3},{3,2},{4,5},{5,4},{6,7},{7,6},{8,9},{9,8},{10,11... | collective-permute-start | bytes 196616 | tf_op jit(solution)/shard_map/ppermute | solution.py:651
  32.3 4.4 %collective-permute-start.3 = (bf16[2,2,64,128]{3,2,1,0:T(8,128)(2,1)S(1)}, bf16[2,2,64,128]{3,2,1,0:T(8,128)(2,1)S(1)}, u32[]{:S(2)}, u32[]{:S(2)}) collective-permute-start(bf16[2,2,64,128]{3,2,1,0:T(8,128)(2,1)S(1)} %get-tuple-element.38), channel_id=1, source_target_pairs={{0,1},{1,0},{2,3},{3,2},{4,5},{5,4},{6,7},{7,6},{8,9},{9,8},{10,11... | collective-permute-start | bytes 196616 | tf_op jit(solution)/shard_map/ppermute | solution.py:651
  35.9 4.4 %collective-permute-start.2 = (bf16[2,2,64,128]{3,2,1,0:T(8,128)(2,1)S(1)}, bf16[2,2,64,128]{3,2,1,0:T(8,128)(2,1)S(1)}, u32[]{:S(2)}, u32[]{:S(2)}) collective-permute-start(bf16[2,2,64,128]{3,2,1,0:T(8,128)(2,1)S(1)} %get-tuple-element.35), channel_id=1, source_target_pairs={{0,1},{1,0},{2,3},{3,2},{4,5},{5,4},{6,7},{7,6},{8,9},{9,8},{10,11... | collective-permute-start | bytes 196616 | tf_op jit(solution)/shard_map/ppermute | solution.py:661
  37.6 4.3 %collective-permute-start.4 = (bf16[2,2,64,128]{3,2,1,0:T(8,128)(2,1)S(1)}, bf16[2,2,64,128]{3,2,1,0:T(8,128)(2,1)S(1)}, u32[]{:S(2)}, u32[]{:S(2)}) collective-permute-start(bf16[2,2,64,128]{3,2,1,0:T(8,128)(2,1)S(1)} %get-tuple-element.41), channel_id=1, source_target_pairs={{0,1},{1,0},{2,3},{3,2},{4,5},{5,4},{6,7},{7,6},{8,9},{9,8},{10,11... | collective-permute-start | bytes 196616 | tf_op jit(solution)/shard_map/ppermute | solution.py:661
  42.7 18.6 %all-to-all-start.1 = ((bf16[16,2,64,128]{3,2,1,0:T(8,128)(2,1)}), bf16[16,2,64,128]{3,2,1,0:T(8,128)(2,1)S(1)}, u32[]{:S(2)}, u32[]{:S(2)}) async-start(bf16[16,2,64,128]{3,2,1,0:T(8,128)(2,1)} %return.1), calls=%async_computation.1 | async-start | bytes 1048576 | tf_op jit(solution)/shard_map/all_to_all | solution.py:679
  46.9 0.9 %copy-start.4 = (bf16[128,4,128]{2,1,0:T(4,128)(2,1)S(1)}, bf16[128,4,128]{2,1,0:T(4,128)(2,1)}, u32[]{:S(2)}) copy-start(bf16[128,4,128]{2,1,0:T(4,128)(2,1)} %param.7) | copy-start | bytes 393220
  46.9 1.0 %copy-start.5 = (bf16[128,4,128]{2,1,0:T(4,128)(2,1)S(1)}, bf16[128,4,128]{2,1,0:T(4,128)(2,1)}, u32[]{:S(2)}) copy-start(bf16[128,4,128]{2,1,0:T(4,128)(2,1)} %param.8) | copy-start | bytes 393220
  54.7 0.7 %copy-start.2 = (f32[512,128]{1,0:T(8,128)}, f32[512,128]{1,0:T(8,128)S(1)}, u32[]{:S(2)}) copy-start(f32[512,128]{1,0:T(8,128)S(1)} %get-tuple-element.48.dv_near_ref) | copy-start | bytes 786436
  61.3 1.6 %copy-start.3 = (f32[512,128]{1,0:T(8,128)S(1)}, f32[512,128]{1,0:T(8,128)}, u32[]{:S(2)}) copy-start(f32[512,128]{1,0:T(8,128)} %copy-done.2) | copy-start | bytes 786436
  61.5 5.5 %collective-permute-start.5 = (bf16[4,2,64,128]{3,2,1,0:T(8,128)(2,1)S(1)}, bf16[4,2,64,128]{3,2,1,0:T(8,128)(2,1)S(1)}, u32[]{:S(2)}, u32[]{:S(2)}) collective-permute-start(bf16[4,2,64,128]{3,2,1,0:T(8,128)(2,1)S(1)} %land_sibling.1), channel_id=1, source_target_pairs={{0,1},{1,0},{2,3},{3,2},{4,5},{5,4},{6,7},{7,6},{8,9},{9,8},{10,11... | collective-permute-start | bytes 393224 | tf_op jit(solution)/shard_map/ppermute | solution.py:707

commit v17 on v14

--- a/solution.py
+++ b/solution.py
@@ -215,6 +215,13 @@
     col = lax.broadcasted_iota(jnp.int32, (half, cols), 1)
     token = which * place + row % place
     return jnp.where(col == token * kv_heads + row // place, 1.0, 0.0).astype(BF16)
+
+
+def token_major(half, kv_heads):
+    place = half // kv_heads
+    row = lax.broadcasted_iota(jnp.int32, (half, half), 0)
+    col = lax.broadcasted_iota(jnp.int32, (half, half), 1)
+    return jnp.where(col == row % kv_heads * place + row // kv_heads, 1.0, 0.0).astype(BF16)
 
 
 def reorder(one_hot, array):
@@ -326,13 +333,12 @@
     rows = q_ref.shape[0] // blocks
     half = given_ref.shape[2]
     place = half // kv_heads
-    copies = []
-    for block in range(blocks):
-        span = pl.ds(block * rows, rows)
-        for which, (source, target) in enumerate(((q_hbm, q_ref), (g_hbm, g_ref))):
-            sem = sems.at[which, block]
-            copies.append(pltpu.make_async_copy(source.at[span], target.at[span], sem))
-            copies[-1].start()
+    copies = [
+        pltpu.make_async_copy(q_hbm, q_ref, sems.at[0]),
+        pltpu.make_async_copy(g_hbm, g_ref, sems.at[1]),
+    ]
+    for copy in copies:
+        copy.start()
     fill_plan(lists_ref, counts_ref, plan_ref, grp_count, blocks)
     mine = lax.axis_index("uly")
     order = half_order(2 * half, kv_heads, mine)
@@ -348,7 +354,8 @@
         span = slice(block * rows, (block + 1) * rows)
         pieces = []
         for which, ref in enumerate((q_ref, g_ref)):
-            copies[2 * block + which].wait()
+            if block == 0:
+                copies[which].wait()
             both = jnp.concatenate([kept_ref[block, which], given_ref[block, which]], axis=0)
             full = dot_last(both, ref[span])
             pieces.append(
@@ -511,20 +518,40 @@
     out_ref[...] = sum_ref[...].astype(out_ref.dtype)
 
 
+def own_half_kernel(
+    plan_ref, landed_ref, dk_near_ref, dv_near_ref, out_ref, sum_ref, *, kv_heads
+):
+    sum_ref[...] = jnp.zeros_like(sum_ref)
+    for group in range(landed_ref.shape[0]):
+        place = plan_ref[group]
+
+        @pl.when(place >= 0)
+        def _():
+            sum_ref[place] = sum_ref[place] + landed_ref[group].astype(F32)
+
+    blocks, _, half, _ = out_ref.shape
+    order = token_major(half, kv_heads)
+    mine = lax.axis_index("uly")
+    for block in range(blocks):
+        span = pl.ds(pl.multiple_of((2 * block + mine) * half, half), half)
+        for which, near_ref in enumerate((dk_near_ref, dv_near_ref)):
+            summed = (near_ref[span] + sum_ref[block, which]).astype(BF16)
+            out_ref[block, which] = reorder(order, summed)
+
+
 def finish_kernel(
     dk_near_ref, dv_near_ref, own_ref, back_ref, dk_ref, dv_ref, *, kv_heads
 ):
     blocks, _, half, _ = back_ref.shape
-    mine = lax.axis_index("uly") == 0
-    order = head_major(2 * half, kv_heads)
-    for block in range(blocks):
-        span = slice(block * 2 * half, (block + 1) * 2 * half)
-        for near_ref, out_ref, which in ((dk_near_ref, dk_ref, 0), (dv_near_ref, dv_ref, 1)):
-            own = own_ref[block, which]
-            back = back_ref[block, which].astype(F32)
-            far = jnp.concatenate([jnp.where(mine, own, back), jnp.where(mine, back, own)], axis=0)
-            summed = (near_ref[span] + far).astype(BF16)
-            out_ref[span] = dot_first(order, summed).astype(BF16)
+    order = token_major(half, kv_heads)
+    mine = lax.axis_index("uly")
+    for which, (near_ref, out_ref) in enumerate(((dk_near_ref, dk_ref), (dv_near_ref, dv_ref))):
+        for block in range(blocks):
+            here = pl.ds(pl.multiple_of((2 * block + mine) * half, half), half)
+            there = pl.ds(pl.multiple_of((2 * block + 1 - mine) * half, half), half)
+            summed = (near_ref[there] + back_ref[block, which].astype(F32)).astype(BF16)
+            out_ref[here] = own_ref[block, which]
+            out_ref[there] = reorder(order, summed)
 
 
 def take_rows(array, index):
@@ -606,7 +633,7 @@
             pltpu.SMEM((seen_at + mine_blocks,), jnp.int32), stat_shape, part_shape,
             pltpu.VMEM(q2.shape, BF16), pltpu.VMEM(q2.shape, BF16),
         ],
-        scratch_shapes=[pltpu.SemaphoreType.DMA((2, mine_blocks))],
+        scratch_shapes=[pltpu.SemaphoreType.DMA((2,))],
         compiler_params=limit,
         name="near",
     )(
@@ -696,8 +723,8 @@
     )
     back = lax.ppermute(give, "uly", swap)
     own = call(
-        partial(landing_kernel, first=0), "land_own", (plan,), (landed,),
-        jax.ShapeDtypeStruct(part_shape.shape, F32), sum_scratch,
+        partial(own_half_kernel, kv_heads=kv_heads), "land_own", (plan,),
+        (landed, dk_near, dv_near), part_shape, sum_scratch,
     )
     dk, dv = call(
         partial(finish_kernel, kv_heads=kv_heads), "finish", (),

time: 67.4 us -> 67.6 us (level)
  waiting for transfers between devices: 12.9 us -> 14.3 us
  starting transfers between devices: 12.7 us -> 11.6 us
  Pallas kernels: 18.9 us -> 18 us
    ppermute x2, waiting for transfers between devices: 1.46 us -> 2.51 us  [whole_blocks(): from_sib = [lax.ppermute(part, 'uly', swap) for part in grads]]
    ppermute x1, starting transfers between devices: 1.12 us -> 0.22 us  [whole_blocks(): back = lax.ppermute(give, 'uly', swap)]
    pallas_call x1, Pallas kernels: 4.01 us -> 3.31 us  [whole_blocks(): pl.pallas_call(partial(near_kernel, grp_count=grp_count, **sizes), in_spe...]
  transfers between devices with their start and end apart: 7 -> 7, of which waited for: 5 -> 6; matrix products, arithmetic and copies ran while one was open for 0% -> 0% of each run, Pallas kernels for 23% -> 22%
where the time goes in v17:
time: 67.6 us; the launch traced here: 67.2 us
  blocking collectives  20.3 us (30%)
  Pallas kernels  18 us (27%)
  waiting for transfers between devices  14.3 us (21%)
  starting transfers between devices  11.6 us (17%)
  local copies, waits for them, and re-layouts  2.18 us (3%)
  between operations  0.76 us (1%)
    all_to_all x1, blocking collectives, whole_blocks(): lax.all_to_all(outgoing, 'grp', split_axis=0, concat_axis=0, tiled=True)  20.3 us
    pallas_call x1, Pallas kernels, whole_blocks(): pl.pallas_call(partial(local_kernel, seen_at=seen_at, **sizes), grid_spec...  6.86 us
    pallas_call x12, Pallas kernels, call(): pl.pallas_call(kernel, in_specs=[smem] * len(scalars) + [vmem] * (len(ope...  6.61 us
    all_to_all x1, waiting for transfers between devices, whole_blocks(): lax.all_to_all(returning, 'grp', split_axis=0, concat_axis=0, tiled=True)  5.93 us
    ppermute x1, waiting for transfers between devices, whole_blocks(): back = lax.ppermute(give, 'uly', swap)  4.38 us
    all_to_all x1, starting transfers between devices, whole_blocks(): lax.all_to_all(returning, 'grp', split_axis=0, concat_axis=0, tiled=True)  4 us
    pallas_call x1, Pallas kernels, whole_blocks(): pl.pallas_call(partial(near_kernel, grp_count=grp_count, **sizes), in_spe...  3.31 us
    ppermute x1, starting transfers between devices, whole_blocks(): gotten = lax.ppermute(given, 'uly', swap)  3.03 us
  transfers between devices with their start and end apart: 7, of which 6 were waited for; matrix products, arithmetic and copies ran while one was open for 0% of the time, Pallas kernels for 22%

profile of v17, /device:TPU:0, one launch (start us, length us, event | category | flops | bytes accessed | tf_op | source)
XLA Modules:
  0.0 67.2 jit_solution(831653817666478735)
XLA Ops:
  0.6 1.3 %pack.1 = (bf16[512,128]{1,0:T(8,128)(2,1)S(1)}, bf16[512,128]{1,0:T(8,128)(2,1)S(1)}, bf16[4,2,64,128]{3,2,1,0:T(8,128)(2,1)S(1)}) custom-call(bf16[512,128]{1,0:T(8,128)(2,1)} %bitcast.9, bf16[512,128]{1,0:T(8,128)(2,1)} %bitcast.11), custom_call_target="tpu_custom_call" | custom-call | tf_op jit(solution)/shard_map/pack/pallas_call | solution.py:616
  1.9 3.0 %collective-permute-start = (bf16[4,2,64,128]{3,2,1,0:T(8,128)(2,1)S(1)}, bf16[4,2,64,128]{3,2,1,0:T(8,128)(2,1)S(1)}, u32[]{:S(2)}, u32[]{:S(2)}) collective-permute-start(bf16[4,2,64,128]{3,2,1,0:T(8,128)(2,1)S(1)} %get-tuple-element.36.given_ref), channel_id=1, source_target_pairs={{0,1},{1,0},{2,3},{3,2},{4,5},{5,4},{6,7},{7,6},{8,9},{9,8},{10,11... | collective-permute-start | bytes 393224 | tf_op jit(solution)/shard_map/ppermute | solution.py:625
  4.9 3.3 %near.1 = (s32[44]{0:T(128)S(4)}, f32[4,8,1024]{2,1,0:T(8,128)S(1)}, bf16[4,2,64,128]{3,2,1,0:T(8,128)(2,1)S(1)}, bf16[4096,128]{1,0:T(8,128)(2,1)S(1)}, bf16[4096,128]{1,0:T(8,128)(2,1)S(1)}) custom-call(s32[128]{0:T(128)} %bitcast.15, s32[128]{0:T(128)} %counts_ref.1, bf16[4096,128]{1,0:T(8,128)(2,1)} %bitcast.13, bf16[4096,128]{1,0:T(8,128)(2,1)} %bitcast.14, ...), custom_call_target="tpu_custom_call" | custom-call | tf_op jit(solution)/shard_map/near/pallas_call | solution.py:628
  8.3 0.1 collective-permute-done.blocks_ref
  8.5 20.3 %all_to_all.10.arrived_ref.mine_ref = bf16[16,2,64,128]{3,2,1,0:T(8,128)(2,1)S(1)} all-to-all(bf16[16,2,64,128]{3,2,1,0:T(8,128)(2,1)S(1)} %send_sibling.1), channel_id=1, replica_groups=mesh['grp'=16,'uly'=2] {'grp'}, dimensions={0} | all-to-all | bytes 1048576 | tf_op jit(solution)/shard_map/all_to_all | solution.py:652
  28.8 1.6 %collective-permute-start.1 = (bf16[2,2,64,128]{3,2,1,0:T(8,128)(2,1)S(1)}, bf16[2,2,64,128]{3,2,1,0:T(8,128)(2,1)S(1)}, u32[]{:S(2)}, u32[]{:S(2)}) collective-permute-start(bf16[2,2,64,128]{3,2,1,0:T(8,128)(2,1)S(1)} %get-tuple-element.46), channel_id=1, source_target_pairs={{0,1},{1,0},{2,3},{3,2},{4,5},{5,4},{6,7},{7,6},{8,9},{9,8},{10,11... | collective-permute-start | bytes 196616 | tf_op jit(solution)/shard_map/ppermute | solution.py:668
  30.4 0.8 %mid.1.stat_ref = f32[4,8,1024]{2,1,0:T(8,128)S(1)} custom-call(s32[44]{0:T(128)S(4)} %get-tuple-element.37.plan_ref, bf16[4096,128]{1,0:T(8,128)(2,1)S(1)} %get-tuple-element.38.q_ref, bf16[4096,128]{1,0:T(8,128)(2,1)S(1)} %get-tuple-element.39.g_ref, f32[4,8,1024]{2,1,0:T(8,128)S(1)} %get-tuple-element.44.stat_ref, ...), custom_call_target="tpu_custom_call" | custom-call | tf_op jit(solution)/shard_map/mid/pallas_call | solution.py:596
  31.3 0.6 collective-permute-start.3
  31.8 1.3 %collective-permute-done.1.other_ref = bf16[2,2,64,128]{3,2,1,0:T(8,128)(2,1)S(1)} collective-permute-done((bf16[2,2,64,128]{3,2,1,0:T(8,128)(2,1)S(1)}, bf16[2,2,64,128]{3,2,1,0:T(8,128)(2,1)S(1)}, u32[]{:S(2)}, u32[]{:S(2)}) %collective-permute-start.1) | collective-permute-done | bytes 65568 | tf_op jit(solution)/shard_map/ppermute | solution.py:668
  33.2 0.9 %far.2 = (bf16[2,2,64,128]{3,2,1,0:T(8,128)(2,1)S(1)}, f32[2,8,1024]{2,1,0:T(8,128)S(1)}) custom-call(s32[44]{0:T(128)S(4)} %get-tuple-element.37.plan_ref, bf16[4096,128]{1,0:T(8,128)(2,1)S(1)} %get-tuple-element.38.q_ref, bf16[4096,128]{1,0:T(8,128)(2,1)S(1)} %get-tuple-element.39.g_ref, f32[4,8,1024]{2,1,0:T(8,128)S(1)} %mid.1.stat_ref, ...), custom_call_target="tpu_custom_call" | custom-call | tf_op jit(solution)/shard_map/far/pallas_call | solution.py:596
  34.1 2.1 %collective-permute-start.2 = (bf16[2,2,64,128]{3,2,1,0:T(8,128)(2,1)S(1)}, bf16[2,2,64,128]{3,2,1,0:T(8,128)(2,1)S(1)}, u32[]{:S(2)}, u32[]{:S(2)}) collective-permute-start(bf16[2,2,64,128]{3,2,1,0:T(8,128)(2,1)S(1)} %get-tuple-element.47), channel_id=1, source_target_pairs={{0,1},{1,0},{2,3},{3,2},{4,5},{5,4},{6,7},{7,6},{8,9},{9,8},{10,11... | collective-permute-start | bytes 196616 | tf_op jit(solution)/shard_map/ppermute | solution.py:678
  36.2 0.9 %far.3 = (bf16[2,2,64,128]{3,2,1,0:T(8,128)(2,1)S(1)}, f32[2,8,1024]{2,1,0:T(8,128)S(1)}) custom-call(s32[44]{0:T(128)S(4)} %get-tuple-element.37.plan_ref, bf16[4096,128]{1,0:T(8,128)(2,1)S(1)} %get-tuple-element.38.q_ref, bf16[4096,128]{1,0:T(8,128)(2,1)S(1)} %get-tuple-element.39.g_ref, f32[4,8,1024]{2,1,0:T(8,128)S(1)} %mid.1.stat_ref, ...), custom_call_target="tpu_custom_call" | custom-call | tf_op jit(solution)/shard_map/far/pallas_call | solution.py:596
  37.1 0.1 collective-permute-start.4
  37.2 0.9 %mine.3.refs_1_ = bf16[2,2,64,128]{3,2,1,0:T(8,128)(2,1)S(1)} custom-call(s32[44]{0:T(128)S(4)} %get-tuple-element.37.plan_ref, bf16[4096,128]{1,0:T(8,128)(2,1)S(1)} %get-tuple-element.38.q_ref, bf16[4096,128]{1,0:T(8,128)(2,1)S(1)} %get-tuple-element.39.g_ref, bf16[16,2,64,128]{3,2,1,0:T(8,128)(2,1)S(1)} %all_to_all.10.arrived_ref.mine_ref, ...), custom_call_target="tpu_custom_call" | custom-call | tf_op jit(solution)/shard_map/mine/pallas_call | solution.py:596
  38.1 0.9 %collective-permute-done.2.refs_2_ = bf16[2,2,64,128]{3,2,1,0:T(8,128)(2,1)S(1)} collective-permute-done((bf16[2,2,64,128]{3,2,1,0:T(8,128)(2,1)S(1)}, bf16[2,2,64,128]{3,2,1,0:T(8,128)(2,1)S(1)}, u32[]{:S(2)}, u32[]{:S(2)}) %collective-permute-start.2) | collective-permute-done | bytes 65568 | tf_op jit(solution)/shard_map/ppermute | solution.py:678
  39.0 0.9 %mine.2.refs_0_ = bf16[2,2,64,128]{3,2,1,0:T(8,128)(2,1)S(1)} custom-call(s32[44]{0:T(128)S(4)} %get-tuple-element.37.plan_ref, bf16[4096,128]{1,0:T(8,128)(2,1)S(1)} %get-tuple-element.38.q_ref, bf16[4096,128]{1,0:T(8,128)(2,1)S(1)} %get-tuple-element.39.g_ref, bf16[16,2,64,128]{3,2,1,0:T(8,128)(2,1)S(1)} %all_to_all.10.arrived_ref.mine_ref, ...), custom_call_target="tpu_custom_call" | custom-call | tf_op jit(solution)/shard_map/mine/pallas_call | solution.py:596
  39.9 1.6 %collective-permute-done.4.refs_3_ = bf16[2,2,64,128]{3,2,1,0:T(8,128)(2,1)S(1)} collective-permute-done((bf16[2,2,64,128]{3,2,1,0:T(8,128)(2,1)S(1)}, bf16[2,2,64,128]{3,2,1,0:T(8,128)(2,1)S(1)}, u32[]{:S(2)}, u32[]{:S(2)}) %collective-permute-start.4) | collective-permute-done | bytes 65568 | tf_op jit(solution)/shard_map/ppermute | solution.py:678
  41.4 0.8 %return.1 = bf16[16,2,64,128]{3,2,1,0:T(8,128)(2,1)} custom-call(s32[44]{0:T(128)S(4)} %get-tuple-element.37.plan_ref, bf16[2,2,64,128]{3,2,1,0:T(8,128)(2,1)S(1)} %mine.2.refs_0_, bf16[2,2,64,128]{3,2,1,0:T(8,128)(2,1)S(1)} %mine.3.refs_1_, bf16[2,2,64,128]{3,2,1,0:T(8,128)(2,1)S(1)} %collective-permute-done.2.refs_2_, ...), custom_call_target="tpu_custom_call" | custom-call | tf_op jit(solution)/shard_map/return/pallas_call | solution.py:596
  42.2 4.0 %all-to-all-start.1 = ((bf16[16,2,64,128]{3,2,1,0:T(8,128)(2,1)}), bf16[16,2,64,128]{3,2,1,0:T(8,128)(2,1)S(1)}, u32[]{:S(2)}, u32[]{:S(2)}) async-start(bf16[16,2,64,128]{3,2,1,0:T(8,128)(2,1)} %return.1), calls=%async_computation.1 | async-start | bytes 1048576 | tf_op jit(solution)/shard_map/all_to_all | solution.py:696
  46.2 0.0 copy-start.2
  46.2 0.0 copy-start.3
  46.3 0.9 %copy-done.2 = bf16[128,4,128]{2,1,0:T(4,128)(2,1)S(1)} copy-done((bf16[128,4,128]{2,1,0:T(4,128)(2,1)S(1)}, bf16[128,4,128]{2,1,0:T(4,128)(2,1)}, u32[]{:S(2)}) %copy-start.2) | copy-done | bytes 131096
  47.1 0.1 copy-done.3
  47.2 6.9 %local.1 = (bf16[4096,128]{1,0:T(8,128)(2,1)}, bf16[4096,128]{1,0:T(8,128)(2,1)}, f32[512,128]{1,0:T(8,128)S(1)}, f32[512,128]{1,0:T(8,128)S(1)}) custom-call(s32[44]{0:T(128)S(4)} %get-tuple-element.37.plan_ref, bf16[4096,128]{1,0:T(8,128)(2,1)S(1)} %get-tuple-element.38.q_ref, bf16[4096,128]{1,0:T(8,128)(2,1)S(1)} %get-tuple-element.39.g_ref, ...), custom_call_target="tpu_custom_call" | custom-call | tf_op jit(solution)/shard_map/local/pallas_call | solution.py:702
  54.1 0.7 %copy-done = f32[512,128]{1,0:T(8,128)} copy-done((f32[512,128]{1,0:T(8,128)}, f32[512,128]{1,0:T(8,128)S(1)}, u32[]{:S(2)}) %copy-start) | copy-done | bytes 262168
  54.8 5.9 %all-to-all-done.1.landed_ref = bf16[16,2,64,128]{3,2,1,0:T(8,128)(2,1)S(1)} async-done(((bf16[16,2,64,128]{3,2,1,0:T(8,128)(2,1)}), bf16[16,2,64,128]{3,2,1,0:T(8,128)(2,1)S(1)}, u32[]{:S(2)}, u32[]{:S(2)}) %all-to-all-start.1) | async-done | bytes 524320 | tf_op jit(solution)/shard_map/all_to_all | solution.py:696
  60.7 0.2 land_sibling.1
  60.9 0.2 collective-permute-start.5
  61.1 0.5 copy-done.1
  61.7 0.3 land_own.1.own_ref
  62.0 4.4 %collective-permute-done.5.back_ref = bf16[4,2,64,128]{3,2,1,0:T(8,128)(2,1)S(1)} collective-permute-done((bf16[4,2,64,128]{3,2,1,0:T(8,128)(2,1)S(1)}, bf16[4,2,64,128]{3,2,1,0:T(8,128)(2,1)S(1)}, u32[]{:S(2)}, u32[]{:S(2)}) %collective-permute-start.5) | collective-permute-done | bytes 131104 | tf_op jit(solution)/shard_map/ppermute | solution.py:724
  66.4 0.9 %finish.1 = (bf16[512,128]{1,0:T(8,128)(2,1)}, bf16[512,128]{1,0:T(8,128)(2,1)}) custom-call(f32[512,128]{1,0:T(8,128)S(1)} %get-tuple-element.59.dk_near_ref, f32[512,128]{1,0:T(8,128)S(1)} %copy-done.1, bf16[4,2,64,128]{3,2,1,0:T(8,128)(2,1)S(1)} %land_own.1.own_ref, bf16[4,2,64,128]{3,2,1,0:T(8,128)(2,1)S(1)} %collective-permute-done.5.back_ref), custom_call_target="tpu_custom_call" | custom-call | tf_op jit(solution)/shard_map/finish/pallas_call | solution.py:596
  (7 shorter events, 0.1 us)
Async XLA Ops:
  1.9 6.5 %collective-permute-start = (bf16[4,2,64,128]{3,2,1,0:T(8,128)(2,1)S(1)}, bf16[4,2,64,128]{3,2,1,0:T(8,128)(2,1)S(1)}, u32[]{:S(2)}, u32[]{:S(2)}) collective-permute-start(bf16[4,2,64,128]{3,2,1,0:T(8,128)(2,1)S(1)} %get-tuple-element.36.given_ref), channel_id=1, source_target_pairs={{0,1},{1,0},{2,3},{3,2},{4,5},{5,4},{6,7},{7,6},{8,9},{9,8},{10,11... | collective-permute-start | bytes 393224 | tf_op jit(solution)/shard_map/ppermute | solution.py:625
  28.8 4.3 %collective-permute-start.1 = (bf16[2,2,64,128]{3,2,1,0:T(8,128)(2,1)S(1)}, bf16[2,2,64,128]{3,2,1,0:T(8,128)(2,1)S(1)}, u32[]{:S(2)}, u32[]{:S(2)}) collective-permute-start(bf16[2,2,64,128]{3,2,1,0:T(8,128)(2,1)S(1)} %get-tuple-element.46), channel_id=1, source_target_pairs={{0,1},{1,0},{2,3},{3,2},{4,5},{5,4},{6,7},{7,6},{8,9},{9,8},{10,11... | collective-permute-start | bytes 196616 | tf_op jit(solution)/shard_map/ppermute | solution.py:668
  31.3 4.9 %collective-permute-start.3 = (bf16[2,2,64,128]{3,2,1,0:T(8,128)(2,1)S(1)}, bf16[2,2,64,128]{3,2,1,0:T(8,128)(2,1)S(1)}, u32[]{:S(2)}, u32[]{:S(2)}) collective-permute-start(bf16[2,2,64,128]{3,2,1,0:T(8,128)(2,1)S(1)} %get-tuple-element.50), channel_id=1, source_target_pairs={{0,1},{1,0},{2,3},{3,2},{4,5},{5,4},{6,7},{7,6},{8,9},{9,8},{10,11... | collective-permute-start | bytes 196616 | tf_op jit(solution)/shard_map/ppermute | solution.py:668
  34.1 4.9 %collective-permute-start.2 = (bf16[2,2,64,128]{3,2,1,0:T(8,128)(2,1)S(1)}, bf16[2,2,64,128]{3,2,1,0:T(8,128)(2,1)S(1)}, u32[]{:S(2)}, u32[]{:S(2)}) collective-permute-start(bf16[2,2,64,128]{3,2,1,0:T(8,128)(2,1)S(1)} %get-tuple-element.47), channel_id=1, source_target_pairs={{0,1},{1,0},{2,3},{3,2},{4,5},{5,4},{6,7},{7,6},{8,9},{9,8},{10,11... | collective-permute-start | bytes 196616 | tf_op jit(solution)/shard_map/ppermute | solution.py:678
  37.1 4.3 %collective-permute-start.4 = (bf16[2,2,64,128]{3,2,1,0:T(8,128)(2,1)S(1)}, bf16[2,2,64,128]{3,2,1,0:T(8,128)(2,1)S(1)}, u32[]{:S(2)}, u32[]{:S(2)}) collective-permute-start(bf16[2,2,64,128]{3,2,1,0:T(8,128)(2,1)S(1)} %get-tuple-element.53), channel_id=1, source_target_pairs={{0,1},{1,0},{2,3},{3,2},{4,5},{5,4},{6,7},{7,6},{8,9},{9,8},{10,11... | collective-permute-start | bytes 196616 | tf_op jit(solution)/shard_map/ppermute | solution.py:678
  42.2 18.5 %all-to-all-start.1 = ((bf16[16,2,64,128]{3,2,1,0:T(8,128)(2,1)}), bf16[16,2,64,128]{3,2,1,0:T(8,128)(2,1)S(1)}, u32[]{:S(2)}, u32[]{:S(2)}) async-start(bf16[16,2,64,128]{3,2,1,0:T(8,128)(2,1)} %return.1), calls=%async_computation.1 | async-start | bytes 1048576 | tf_op jit(solution)/shard_map/all_to_all | solution.py:696
  46.2 0.9 %copy-start.2 = (bf16[128,4,128]{2,1,0:T(4,128)(2,1)S(1)}, bf16[128,4,128]{2,1,0:T(4,128)(2,1)}, u32[]{:S(2)}) copy-start(bf16[128,4,128]{2,1,0:T(4,128)(2,1)} %param.7) | copy-start | bytes 393220
  46.2 1.0 %copy-start.3 = (bf16[128,4,128]{2,1,0:T(4,128)(2,1)S(1)}, bf16[128,4,128]{2,1,0:T(4,128)(2,1)}, u32[]{:S(2)}) copy-start(bf16[128,4,128]{2,1,0:T(4,128)(2,1)} %param.8) | copy-start | bytes 393220
  54.1 0.7 %copy-start = (f32[512,128]{1,0:T(8,128)}, f32[512,128]{1,0:T(8,128)S(1)}, u32[]{:S(2)}) copy-start(f32[512,128]{1,0:T(8,128)S(1)} %get-tuple-element.60.dv_near_ref) | copy-start | bytes 786436
  60.7 1.0 %copy-start.1 = (f32[512,128]{1,0:T(8,128)S(1)}, f32[512,128]{1,0:T(8,128)}, u32[]{:S(2)}) copy-start(f32[512,128]{1,0:T(8,128)} %copy-done) | copy-start | bytes 786436
  60.9 5.5 %collective-permute-start.5 = (bf16[4,2,64,128]{3,2,1,0:T(8,128)(2,1)S(1)}, bf16[4,2,64,128]{3,2,1,0:T(8,128)(2,1)S(1)}, u32[]{:S(2)}, u32[]{:S(2)}) collective-permute-start(bf16[4,2,64,128]{3,2,1,0:T(8,128)(2,1)S(1)} %land_sibling.1), channel_id=1, source_target_pairs={{0,1},{1,0},{2,3},{3,2},{4,5},{5,4},{6,7},{7,6},{8,9},{9,8},{10,11... | collective-permute-start | bytes 393224 | tf_op jit(solution)/shard_map/ppermute | solution.py:724

commit v18 on v16

--- a/solution.py
+++ b/solution.py
@@ -268,19 +268,17 @@
 
 def pack_kernel(k_hbm, v_hbm, kept_ref, given_ref, k_ref, v_ref, sems, *, kv_heads):
     blocks, _, half, _ = kept_ref.shape
-    arrays = ((k_hbm, k_ref), (v_hbm, v_ref))
-    copies = []
-    for block in range(blocks):
-        span = pl.ds(block * 2 * half, 2 * half)
-        for which, (source, target) in enumerate(arrays):
-            sem = sems.at[which, block]
-            copies.append(pltpu.make_async_copy(source.at[span], target.at[span], sem))
-            copies[-1].start()
+    copies = [
+        pltpu.make_async_copy(k_hbm, k_ref, sems.at[0]),
+        pltpu.make_async_copy(v_hbm, v_ref, sems.at[1]),
+    ]
+    for copy in copies:
+        copy.start()
     first = lax.axis_index("uly") == 0
     order = head_major(2 * half, kv_heads)
-    for block in range(blocks):
-        for which, (_, ref) in enumerate(arrays):
-            copies[2 * block + which].wait()
+    for which, ref in enumerate((k_ref, v_ref)):
+        copies[which].wait()
+        for block in range(blocks):
             ordered = reorder(order, ref[block * 2 * half:(block + 1) * 2 * half])
             kept_ref[block, which] = jnp.where(first, ordered[:half], ordered[half:])
             given_ref[block, which] = jnp.where(first, ordered[half:], ordered[:half])
@@ -598,7 +596,7 @@
         out_shape=[part_shape, part_shape],
         scratch_shapes=[
             pltpu.VMEM(k2.shape, BF16), pltpu.VMEM(k2.shape, BF16),
-            pltpu.SemaphoreType.DMA((2, mine_blocks)),
+            pltpu.SemaphoreType.DMA((2,)),
         ],
         compiler_params=limit,
         name="pack",

time: 68.3 us -> 67.5 us (0.988)
  Pallas kernels: 19.8 us -> 19.1 us
    pallas_call x1, Pallas kernels: 2.03 us -> 1.29 us  [whole_blocks(): pl.pallas_call(partial(pack_kernel, kv_heads=kv_heads), in_specs=[anywher...]
  transfers between devices with their start and end apart: 7 -> 7, of which waited for: 5 -> 5; matrix products, arithmetic and copies ran while one was open for 0% -> 0% of each run, Pallas kernels for 23% -> 24%
where the time goes in v18:
time: 67.5 us; the launch traced here: 67 us
  blocking collectives  20.3 us (30%)
  Pallas kernels  19.1 us (28%)
  starting transfers between devices  12.9 us (19%)
  waiting for transfers between devices  12.3 us (18%)
  local copies, waits for them, and re-layouts  1.64 us (2%)
  between operations  0.79 us (1%)
    all_to_all x1, blocking collectives, whole_blocks(): lax.all_to_all(outgoing, 'grp', split_axis=0, concat_axis=0, tiled=True)  20.3 us
    pallas_call x1, Pallas kernels, whole_blocks(): pl.pallas_call(partial(local_kernel, seen_at=seen_at, **sizes), grid_spec...  6.87 us
    pallas_call x12, Pallas kernels, call(): pl.pallas_call(kernel, in_specs=[smem] * len(scalars) + [vmem] * (len(ope...  6.75 us
    all_to_all x1, waiting for transfers between devices, whole_blocks(): lax.all_to_all(returning, 'grp', split_axis=0, concat_axis=0, tiled=True)  5.93 us
    all_to_all x1, starting transfers between devices, whole_blocks(): lax.all_to_all(returning, 'grp', split_axis=0, concat_axis=0, tiled=True)  4.13 us
    ppermute x1, waiting for transfers between devices, whole_blocks(): back = lax.ppermute(give, 'uly', swap)  3.74 us
    pallas_call x1, Pallas kernels, whole_blocks(): pl.pallas_call(partial(near_kernel, **sizes), grid=(mine_blocks,), in_spe...  3.08 us
    ppermute x1, starting transfers between devices, whole_blocks(): gotten = lax.ppermute(given, 'uly', swap)  3.03 us
  transfers between devices with their start and end apart: 7, of which 5 were waited for; matrix products, arithmetic and copies ran while one was open for 0% of the time, Pallas kernels for 24%

profile of v18, /device:TPU:0, one launch (start us, length us, event | category | flops | bytes accessed | tf_op | source)
XLA Modules:
  0.0 67.0 jit_solution(3715941238601563829)
XLA Ops:
  0.6 1.3 %pack.1 = (bf16[4,2,64,128]{3,2,1,0:T(8,128)(2,1)S(1)}, bf16[4,2,64,128]{3,2,1,0:T(8,128)(2,1)S(1)}) custom-call(bf16[512,128]{1,0:T(8,128)(2,1)} %bitcast.23, bf16[512,128]{1,0:T(8,128)(2,1)} %bitcast.25), custom_call_target="tpu_custom_call" | custom-call | tf_op jit(solution)/shard_map/pack/pallas_call | solution.py:592
  1.9 3.0 %collective-permute-start = (bf16[4,2,64,128]{3,2,1,0:T(8,128)(2,1)S(1)}, bf16[4,2,64,128]{3,2,1,0:T(8,128)(2,1)S(1)}, u32[]{:S(2)}, u32[]{:S(2)}) collective-permute-start(bf16[4,2,64,128]{3,2,1,0:T(8,128)(2,1)S(1)} %get-tuple-element.28.given_ref), channel_id=1, source_target_pairs={{0,1},{1,0},{2,3},{3,2},{4,5},{5,4},{6,7},{7,6},{8,9},{9,8},{10,11... | collective-permute-start | bytes 393224 | tf_op jit(solution)/shard_map/ppermute | solution.py:612
  5.0 1.1 %plan.1.plan_ref = s32[44]{0:T(128)S(4)} custom-call(s32[128]{0:T(128)} %bitcast.31, s32[128]{0:T(128)} %counts_ref.1), custom_call_target="tpu_custom_call" | custom-call | tf_op jit(solution)/shard_map/plan/pallas_call | solution.py:604
  6.1 3.1 %near.1.stat_ref = f32[4,8,1024]{2,1,0:T(8,128)S(1)} custom-call(bf16[4096,128]{1,0:T(8,128)(2,1)} %bitcast.9, bf16[4096,128]{1,0:T(8,128)(2,1)} %bitcast.16, bf16[4,2,64,128]{3,2,1,0:T(8,128)(2,1)S(1)} %get-tuple-element.29.kept_ref.blocks_ref, bf16[4,2,64,128]{3,2,1,0:T(8,128)(2,1)S(1)} %get-tuple-element.28.given_ref), custom_call_target="tpu_custom_call" | custom-call | tf_op jit(solution)/shard_map/near/pallas_call | solution.py:615
  9.2 0.0 copy-start.1
  9.2 0.1 send_sibling.1
  9.4 0.0 copy-start
  9.4 20.3 %all_to_all.10.arrived_ref.mine_ref = bf16[16,2,64,128]{3,2,1,0:T(8,128)(2,1)S(1)} all-to-all(bf16[16,2,64,128]{3,2,1,0:T(8,128)(2,1)S(1)} %send_sibling.1), channel_id=1, replica_groups=mesh['grp'=16,'uly'=2] {'grp'}, dimensions={0} | all-to-all | bytes 1048576 | tf_op jit(solution)/shard_map/all_to_all | solution.py:633
  29.7 0.9 %collective-permute-start.1 = (bf16[2,2,64,128]{3,2,1,0:T(8,128)(2,1)S(1)}, bf16[2,2,64,128]{3,2,1,0:T(8,128)(2,1)S(1)}, u32[]{:S(2)}, u32[]{:S(2)}) collective-permute-start(bf16[2,2,64,128]{3,2,1,0:T(8,128)(2,1)S(1)} %get-tuple-element.34), channel_id=1, source_target_pairs={{0,1},{1,0},{2,3},{3,2},{4,5},{5,4},{6,7},{7,6},{8,9},{9,8},{10,11... | collective-permute-start | bytes 196616 | tf_op jit(solution)/shard_map/ppermute | solution.py:649
  30.6 0.9 %mid.1.stat_ref = f32[4,8,1024]{2,1,0:T(8,128)S(1)} custom-call(s32[44]{0:T(128)S(4)} %plan.1.plan_ref, bf16[4096,128]{1,0:T(8,128)(2,1)S(1)} %bitcast.10, bf16[4096,128]{1,0:T(8,128)(2,1)S(1)} %bitcast.17, f32[4,8,1024]{2,1,0:T(8,128)S(1)} %near.1.stat_ref, bf16[16,2,64,128]{3,2,1,0:T(8,128)(2,1)S(1)} %all_to_all.10.arrived_ref.mine_ref), custom_call_target="tpu_custom_call" | custom-call | tf_op jit(solution)/shard_map/mid/pallas_call | solution.py:572
  31.5 1.3 %collective-permute-start.3 = (bf16[2,2,64,128]{3,2,1,0:T(8,128)(2,1)S(1)}, bf16[2,2,64,128]{3,2,1,0:T(8,128)(2,1)S(1)}, u32[]{:S(2)}, u32[]{:S(2)}) collective-permute-start(bf16[2,2,64,128]{3,2,1,0:T(8,128)(2,1)S(1)} %get-tuple-element.38), channel_id=1, source_target_pairs={{0,1},{1,0},{2,3},{3,2},{4,5},{5,4},{6,7},{7,6},{8,9},{9,8},{10,11... | collective-permute-start | bytes 196616 | tf_op jit(solution)/shard_map/ppermute | solution.py:649
  32.7 1.6 %collective-permute-done.1.other_ref = bf16[2,2,64,128]{3,2,1,0:T(8,128)(2,1)S(1)} collective-permute-done((bf16[2,2,64,128]{3,2,1,0:T(8,128)(2,1)S(1)}, bf16[2,2,64,128]{3,2,1,0:T(8,128)(2,1)S(1)}, u32[]{:S(2)}, u32[]{:S(2)}) %collective-permute-start.1) | collective-permute-done | bytes 65568 | tf_op jit(solution)/shard_map/ppermute | solution.py:649
  34.3 0.9 %far.2 = (bf16[2,2,64,128]{3,2,1,0:T(8,128)(2,1)S(1)}, f32[2,8,1024]{2,1,0:T(8,128)S(1)}) custom-call(s32[44]{0:T(128)S(4)} %plan.1.plan_ref, bf16[4096,128]{1,0:T(8,128)(2,1)S(1)} %bitcast.11, bf16[4096,128]{1,0:T(8,128)(2,1)S(1)} %bitcast.18, f32[4,8,1024]{2,1,0:T(8,128)S(1)} %mid.1.stat_ref, bf16[2,2,64,128]{3,2,1,0:T(8,128)(2,1)S(1)} %collective-permute-done.1.other_ref), custom_call_target="tpu_custom_call" | custom-call | tf_op jit(solution)/shard_map/far/pallas_call | solution.py:572
  35.2 0.6 collective-permute-start.2
  35.9 0.9 %far.3 = (bf16[2,2,64,128]{3,2,1,0:T(8,128)(2,1)S(1)}, f32[2,8,1024]{2,1,0:T(8,128)S(1)}) custom-call(s32[44]{0:T(128)S(4)} %plan.1.plan_ref, bf16[4096,128]{1,0:T(8,128)(2,1)S(1)} %bitcast.12, bf16[4096,128]{1,0:T(8,128)(2,1)S(1)} %bitcast.19, f32[4,8,1024]{2,1,0:T(8,128)S(1)} %mid.1.stat_ref, bf16[2,2,64,128]{3,2,1,0:T(8,128)(2,1)S(1)} %collective-permute-done.3.other_ref), custom_call_target="tpu_custom_call" | custom-call | tf_op jit(solution)/shard_map/far/pallas_call | solution.py:572
  36.8 1.5 %collective-permute-start.4 = (bf16[2,2,64,128]{3,2,1,0:T(8,128)(2,1)S(1)}, bf16[2,2,64,128]{3,2,1,0:T(8,128)(2,1)S(1)}, u32[]{:S(2)}, u32[]{:S(2)}) collective-permute-start(bf16[2,2,64,128]{3,2,1,0:T(8,128)(2,1)S(1)} %get-tuple-element.41), channel_id=1, source_target_pairs={{0,1},{1,0},{2,3},{3,2},{4,5},{5,4},{6,7},{7,6},{8,9},{9,8},{10,11... | collective-permute-start | bytes 196616 | tf_op jit(solution)/shard_map/ppermute | solution.py:659
  38.3 0.9 %mine.3.refs_1_ = bf16[2,2,64,128]{3,2,1,0:T(8,128)(2,1)S(1)} custom-call(s32[44]{0:T(128)S(4)} %plan.1.plan_ref, bf16[4096,128]{1,0:T(8,128)(2,1)S(1)} %bitcast.13, bf16[4096,128]{1,0:T(8,128)(2,1)S(1)} %bitcast.20, bf16[16,2,64,128]{3,2,1,0:T(8,128)(2,1)S(1)} %all_to_all.10.arrived_ref.mine_ref, f32[2,8,1024]{2,1,0:T(8,128)S(1)} %get-tuple-element.39.stat_ref), custom_call_target="tpu_custom_call" | custom-call | tf_op jit(solution)/shard_map/mine/pallas_call | solution.py:572
  39.2 0.4 collective-permute-done.2.refs_2_
  39.6 0.9 %mine.2.refs_0_ = bf16[2,2,64,128]{3,2,1,0:T(8,128)(2,1)S(1)} custom-call(s32[44]{0:T(128)S(4)} %plan.1.plan_ref, bf16[4096,128]{1,0:T(8,128)(2,1)S(1)} %bitcast.14, bf16[4096,128]{1,0:T(8,128)(2,1)S(1)} %bitcast.21, bf16[16,2,64,128]{3,2,1,0:T(8,128)(2,1)S(1)} %all_to_all.10.arrived_ref.mine_ref, f32[2,8,1024]{2,1,0:T(8,128)S(1)} %get-tuple-element.37.stat_ref), custom_call_target="tpu_custom_call" | custom-call | tf_op jit(solution)/shard_map/mine/pallas_call | solution.py:572
  40.4 0.7 %collective-permute-done.4.refs_3_ = bf16[2,2,64,128]{3,2,1,0:T(8,128)(2,1)S(1)} collective-permute-done((bf16[2,2,64,128]{3,2,1,0:T(8,128)(2,1)S(1)}, bf16[2,2,64,128]{3,2,1,0:T(8,128)(2,1)S(1)}, u32[]{:S(2)}, u32[]{:S(2)}) %collective-permute-start.4) | collective-permute-done | bytes 65568 | tf_op jit(solution)/shard_map/ppermute | solution.py:659
  41.1 0.8 %return.1 = bf16[16,2,64,128]{3,2,1,0:T(8,128)(2,1)} custom-call(s32[44]{0:T(128)S(4)} %plan.1.plan_ref, bf16[2,2,64,128]{3,2,1,0:T(8,128)(2,1)S(1)} %mine.2.refs_0_, bf16[2,2,64,128]{3,2,1,0:T(8,128)(2,1)S(1)} %mine.3.refs_1_, bf16[2,2,64,128]{3,2,1,0:T(8,128)(2,1)S(1)} %collective-permute-done.2.refs_2_, ...), custom_call_target="tpu_custom_call" | custom-call | tf_op jit(solution)/shard_map/return/pallas_call | solution.py:572
  41.9 4.1 %all-to-all-start.1 = ((bf16[16,2,64,128]{3,2,1,0:T(8,128)(2,1)}), bf16[16,2,64,128]{3,2,1,0:T(8,128)(2,1)S(1)}, u32[]{:S(2)}, u32[]{:S(2)}) async-start(bf16[16,2,64,128]{3,2,1,0:T(8,128)(2,1)} %return.1), calls=%async_computation.1 | async-start | bytes 1048576 | tf_op jit(solution)/shard_map/all_to_all | solution.py:677
  46.1 0.9 %copy-done.4 = bf16[128,4,128]{2,1,0:T(4,128)(2,1)S(1)} copy-done((bf16[128,4,128]{2,1,0:T(4,128)(2,1)S(1)}, bf16[128,4,128]{2,1,0:T(4,128)(2,1)}, u32[]{:S(2)}) %copy-start.4) | copy-done | bytes 131096
  46.9 0.1 copy-done.5
  47.0 6.9 %local.1 = (bf16[4096,128]{1,0:T(8,128)(2,1)}, bf16[4096,128]{1,0:T(8,128)(2,1)}, f32[512,128]{1,0:T(8,128)S(1)}, f32[512,128]{1,0:T(8,128)S(1)}) custom-call(s32[44]{0:T(128)S(4)} %plan.1.plan_ref, bf16[4096,128]{1,0:T(8,128)(2,1)S(1)} %bitcast.15, bf16[4096,128]{1,0:T(8,128)(2,1)S(1)} %bitcast.22, bf16[512,128]{1,0:T(8,128)(2,1)S(1)} %bitcast.24, ...), custom_call_target="tpu_custom_call" | custom-call | tf_op jit(solution)/shard_map/local/pallas_call | solution.py:683
  53.9 0.7 %copy-done.2 = f32[512,128]{1,0:T(8,128)} copy-done((f32[512,128]{1,0:T(8,128)}, f32[512,128]{1,0:T(8,128)S(1)}, u32[]{:S(2)}) %copy-start.2) | copy-done | bytes 262168
  54.6 5.9 %all-to-all-done.1.landed_ref = bf16[16,2,64,128]{3,2,1,0:T(8,128)(2,1)S(1)} async-done(((bf16[16,2,64,128]{3,2,1,0:T(8,128)(2,1)}), bf16[16,2,64,128]{3,2,1,0:T(8,128)(2,1)S(1)}, u32[]{:S(2)}, u32[]{:S(2)}) %all-to-all-start.1) | async-done | bytes 524320 | tf_op jit(solution)/shard_map/all_to_all | solution.py:677
  60.5 0.2 land_sibling.1
  60.7 1.4 %collective-permute-start.5 = (bf16[4,2,64,128]{3,2,1,0:T(8,128)(2,1)S(1)}, bf16[4,2,64,128]{3,2,1,0:T(8,128)(2,1)S(1)}, u32[]{:S(2)}, u32[]{:S(2)}) collective-permute-start(bf16[4,2,64,128]{3,2,1,0:T(8,128)(2,1)S(1)} %land_sibling.1), channel_id=1, source_target_pairs={{0,1},{1,0},{2,3},{3,2},{4,5},{5,4},{6,7},{7,6},{8,9},{9,8},{10,11... | collective-permute-start | bytes 393224 | tf_op jit(solution)/shard_map/ppermute | solution.py:705
  62.1 0.3 land_own.1.own_ref
  62.4 3.7 %collective-permute-done.5.back_ref = bf16[4,2,64,128]{3,2,1,0:T(8,128)(2,1)S(1)} collective-permute-done((bf16[4,2,64,128]{3,2,1,0:T(8,128)(2,1)S(1)}, bf16[4,2,64,128]{3,2,1,0:T(8,128)(2,1)S(1)}, u32[]{:S(2)}, u32[]{:S(2)}) %collective-permute-start.5) | collective-permute-done | bytes 131104 | tf_op jit(solution)/shard_map/ppermute | solution.py:705
  66.2 0.9 %finish.1 = (bf16[512,128]{1,0:T(8,128)(2,1)}, bf16[512,128]{1,0:T(8,128)(2,1)}) custom-call(f32[512,128]{1,0:T(8,128)S(1)} %get-tuple-element.47.dk_near_ref, f32[512,128]{1,0:T(8,128)S(1)} %copy-done.3, bf16[4,2,64,128]{3,2,1,0:T(8,128)(2,1)S(1)} %land_own.1.own_ref, bf16[4,2,64,128]{3,2,1,0:T(8,128)(2,1)S(1)} %collective-permute-done.5.back_ref), custom_call_target="tpu_custom_call" | custom-call | tf_op jit(solution)/shard_map/finish/pallas_call | solution.py:572
  (12 shorter events, 0.1 us)
Async XLA Ops:
  1.9 7.3 %collective-permute-start = (bf16[4,2,64,128]{3,2,1,0:T(8,128)(2,1)S(1)}, bf16[4,2,64,128]{3,2,1,0:T(8,128)(2,1)S(1)}, u32[]{:S(2)}, u32[]{:S(2)}) collective-permute-start(bf16[4,2,64,128]{3,2,1,0:T(8,128)(2,1)S(1)} %get-tuple-element.28.given_ref), channel_id=1, source_target_pairs={{0,1},{1,0},{2,3},{3,2},{4,5},{5,4},{6,7},{7,6},{8,9},{9,8},{10,11... | collective-permute-start | bytes 393224 | tf_op jit(solution)/shard_map/ppermute | solution.py:612
  9.2 21.4 %copy-start.1 = (bf16[128,32,128]{2,1,0:T(8,128)(2,1)S(1)}, bf16[128,32,128]{2,1,0:T(8,128)(2,1)}, u32[]{:S(2)}) copy-start(bf16[128,32,128]{2,1,0:T(8,128)(2,1)} %param.9) | copy-start | bytes 3145732
  9.4 21.2 %copy-start = (bf16[128,32,128]{2,1,0:T(8,128)(2,1)S(1)}, bf16[128,32,128]{2,1,0:T(8,128)(2,1)}, u32[]{:S(2)}) copy-start(bf16[128,32,128]{2,1,0:T(8,128)(2,1)} %param.6) | copy-start | bytes 3145732
  29.7 4.6 %collective-permute-start.1 = (bf16[2,2,64,128]{3,2,1,0:T(8,128)(2,1)S(1)}, bf16[2,2,64,128]{3,2,1,0:T(8,128)(2,1)S(1)}, u32[]{:S(2)}, u32[]{:S(2)}) collective-permute-start(bf16[2,2,64,128]{3,2,1,0:T(8,128)(2,1)S(1)} %get-tuple-element.34), channel_id=1, source_target_pairs={{0,1},{1,0},{2,3},{3,2},{4,5},{5,4},{6,7},{7,6},{8,9},{9,8},{10,11... | collective-permute-start | bytes 196616 | tf_op jit(solution)/shard_map/ppermute | solution.py:649
  31.5 4.4 %collective-permute-start.3 = (bf16[2,2,64,128]{3,2,1,0:T(8,128)(2,1)S(1)}, bf16[2,2,64,128]{3,2,1,0:T(8,128)(2,1)S(1)}, u32[]{:S(2)}, u32[]{:S(2)}) collective-permute-start(bf16[2,2,64,128]{3,2,1,0:T(8,128)(2,1)S(1)} %get-tuple-element.38), channel_id=1, source_target_pairs={{0,1},{1,0},{2,3},{3,2},{4,5},{5,4},{6,7},{7,6},{8,9},{9,8},{10,11... | collective-permute-start | bytes 196616 | tf_op jit(solution)/shard_map/ppermute | solution.py:649
  35.2 4.3 %collective-permute-start.2 = (bf16[2,2,64,128]{3,2,1,0:T(8,128)(2,1)S(1)}, bf16[2,2,64,128]{3,2,1,0:T(8,128)(2,1)S(1)}, u32[]{:S(2)}, u32[]{:S(2)}) collective-permute-start(bf16[2,2,64,128]{3,2,1,0:T(8,128)(2,1)S(1)} %get-tuple-element.35), channel_id=1, source_target_pairs={{0,1},{1,0},{2,3},{3,2},{4,5},{5,4},{6,7},{7,6},{8,9},{9,8},{10,11... | collective-permute-start | bytes 196616 | tf_op jit(solution)/shard_map/ppermute | solution.py:659
  36.8 4.3 %collective-permute-start.4 = (bf16[2,2,64,128]{3,2,1,0:T(8,128)(2,1)S(1)}, bf16[2,2,64,128]{3,2,1,0:T(8,128)(2,1)S(1)}, u32[]{:S(2)}, u32[]{:S(2)}) collective-permute-start(bf16[2,2,64,128]{3,2,1,0:T(8,128)(2,1)S(1)} %get-tuple-element.41), channel_id=1, source_target_pairs={{0,1},{1,0},{2,3},{3,2},{4,5},{5,4},{6,7},{7,6},{8,9},{9,8},{10,11... | collective-permute-start | bytes 196616 | tf_op jit(solution)/shard_map/ppermute | solution.py:659
  41.9 18.6 %all-to-all-start.1 = ((bf16[16,2,64,128]{3,2,1,0:T(8,128)(2,1)}), bf16[16,2,64,128]{3,2,1,0:T(8,128)(2,1)S(1)}, u32[]{:S(2)}, u32[]{:S(2)}) async-start(bf16[16,2,64,128]{3,2,1,0:T(8,128)(2,1)} %return.1), calls=%async_computation.1 | async-start | bytes 1048576 | tf_op jit(solution)/shard_map/all_to_all | solution.py:677
  46.0 0.9 %copy-start.4 = (bf16[128,4,128]{2,1,0:T(4,128)(2,1)S(1)}, bf16[128,4,128]{2,1,0:T(4,128)(2,1)}, u32[]{:S(2)}) copy-start(bf16[128,4,128]{2,1,0:T(4,128)(2,1)} %param.7) | copy-start | bytes 393220
  46.1 1.0 %copy-start.5 = (bf16[128,4,128]{2,1,0:T(4,128)(2,1)S(1)}, bf16[128,4,128]{2,1,0:T(4,128)(2,1)}, u32[]{:S(2)}) copy-start(bf16[128,4,128]{2,1,0:T(4,128)(2,1)} %param.8) | copy-start | bytes 393220
  53.9 0.7 %copy-start.2 = (f32[512,128]{1,0:T(8,128)}, f32[512,128]{1,0:T(8,128)S(1)}, u32[]{:S(2)}) copy-start(f32[512,128]{1,0:T(8,128)S(1)} %get-tuple-element.48.dv_near_ref) | copy-start | bytes 786436
  60.5 1.6 %copy-start.3 = (f32[512,128]{1,0:T(8,128)S(1)}, f32[512,128]{1,0:T(8,128)}, u32[]{:S(2)}) copy-start(f32[512,128]{1,0:T(8,128)} %copy-done.2) | copy-start | bytes 786436
  60.7 5.5 %collective-permute-start.5 = (bf16[4,2,64,128]{3,2,1,0:T(8,128)(2,1)S(1)}, bf16[4,2,64,128]{3,2,1,0:T(8,128)(2,1)S(1)}, u32[]{:S(2)}, u32[]{:S(2)}) collective-permute-start(bf16[4,2,64,128]{3,2,1,0:T(8,128)(2,1)S(1)} %land_sibling.1), channel_id=1, source_target_pairs={{0,1},{1,0},{2,3},{3,2},{4,5},{5,4},{6,7},{7,6},{8,9},{9,8},{10,11... | collective-permute-start | bytes 393224 | tf_op jit(solution)/shard_map/ppermute | solution.py:705

commit v19 on v18

--- a/solution.py
+++ b/solution.py
@@ -644,8 +644,6 @@
     )
     others = []
     for part in giving:
-        if others:
-            part, stats = lax.optimization_barrier((part, stats))
         others.append(lax.ppermute(part, "uly", swap))
     grads, final = [], []
     for at, other in enumerate(others):

time: 67.5 us -> 68.1 us (level)
  waiting for transfers between devices: 12.3 us -> 13.3 us
  transfers between devices with their start and end apart: 7 -> 7, of which waited for: 5 -> 5; matrix products, arithmetic and copies ran while one was open for 0% -> 0% of each run, Pallas kernels for 24% -> 23%
where the time goes in v19:
time: 68.1 us; the launch traced here: 67.8 us
  blocking collectives  20.3 us (30%)
  Pallas kernels  19.1 us (28%)
  waiting for transfers between devices  13.3 us (20%)
  starting transfers between devices  12.6 us (19%)
  local copies, waits for them, and re-layouts  1.64 us (2%)
  between operations  0.79 us (1%)
    all_to_all x1, blocking collectives, whole_blocks(): lax.all_to_all(outgoing, 'grp', split_axis=0, concat_axis=0, tiled=True)  20.3 us
    pallas_call x1, Pallas kernels, whole_blocks(): pl.pallas_call(partial(local_kernel, seen_at=seen_at, **sizes), grid_spec...  6.87 us
    pallas_call x12, Pallas kernels, call(): pl.pallas_call(kernel, in_specs=[smem] * len(scalars) + [vmem] * (len(ope...  6.75 us
    all_to_all x1, waiting for transfers between devices, whole_blocks(): lax.all_to_all(returning, 'grp', split_axis=0, concat_axis=0, tiled=True)  5.93 us
    all_to_all x1, starting transfers between devices, whole_blocks(): lax.all_to_all(returning, 'grp', split_axis=0, concat_axis=0, tiled=True)  4.2 us
    ppermute x1, waiting for transfers between devices, whole_blocks(): back = lax.ppermute(give, 'uly', swap)  4 us
    pallas_call x1, Pallas kernels, whole_blocks(): pl.pallas_call(partial(near_kernel, **sizes), grid=(mine_blocks,), in_spe...  3.08 us
    ppermute x1, starting transfers between devices, whole_blocks(): gotten = lax.ppermute(given, 'uly', swap)  3.03 us
  transfers between devices with their start and end apart: 7, of which 5 were waited for; matrix products, arithmetic and copies ran while one was open for 0% of the time, Pallas kernels for 23%

profile of v19, /device:TPU:0, one launch (start us, length us, event | category | flops | bytes accessed | tf_op | source)
XLA Modules:
  0.0 67.8 jit_solution(11599634589128140485)
XLA Ops:
  0.6 1.3 %pack.1 = (bf16[4,2,64,128]{3,2,1,0:T(8,128)(2,1)S(1)}, bf16[4,2,64,128]{3,2,1,0:T(8,128)(2,1)S(1)}) custom-call(bf16[512,128]{1,0:T(8,128)(2,1)} %bitcast.23, bf16[512,128]{1,0:T(8,128)(2,1)} %bitcast.25), custom_call_target="tpu_custom_call" | custom-call | tf_op jit(solution)/shard_map/pack/pallas_call | solution.py:592
  1.9 3.0 %collective-permute-start = (bf16[4,2,64,128]{3,2,1,0:T(8,128)(2,1)S(1)}, bf16[4,2,64,128]{3,2,1,0:T(8,128)(2,1)S(1)}, u32[]{:S(2)}, u32[]{:S(2)}) collective-permute-start(bf16[4,2,64,128]{3,2,1,0:T(8,128)(2,1)S(1)} %get-tuple-element.26.given_ref), channel_id=1, source_target_pairs={{0,1},{1,0},{2,3},{3,2},{4,5},{5,4},{6,7},{7,6},{8,9},{9,8},{10,11... | collective-permute-start | bytes 393224 | tf_op jit(solution)/shard_map/ppermute | solution.py:612
  5.0 1.1 %plan.1.plan_ref = s32[44]{0:T(128)S(4)} custom-call(s32[128]{0:T(128)} %bitcast.31, s32[128]{0:T(128)} %counts_ref.1), custom_call_target="tpu_custom_call" | custom-call | tf_op jit(solution)/shard_map/plan/pallas_call | solution.py:604
  6.1 3.1 %near.1.stat_ref = f32[4,8,1024]{2,1,0:T(8,128)S(1)} custom-call(bf16[4096,128]{1,0:T(8,128)(2,1)} %bitcast.9, bf16[4096,128]{1,0:T(8,128)(2,1)} %bitcast.16, bf16[4,2,64,128]{3,2,1,0:T(8,128)(2,1)S(1)} %get-tuple-element.27.kept_ref.blocks_ref, bf16[4,2,64,128]{3,2,1,0:T(8,128)(2,1)S(1)} %get-tuple-element.26.given_ref), custom_call_target="tpu_custom_call" | custom-call | tf_op jit(solution)/shard_map/near/pallas_call | solution.py:615
  9.2 0.0 copy-start.1
  9.2 0.1 send_sibling.1
  9.4 0.0 copy-start
  9.4 20.3 %all_to_all.10.arrived_ref.mine_ref = bf16[16,2,64,128]{3,2,1,0:T(8,128)(2,1)S(1)} all-to-all(bf16[16,2,64,128]{3,2,1,0:T(8,128)(2,1)S(1)} %send_sibling.1), channel_id=1, replica_groups=mesh['grp'=16,'uly'=2] {'grp'}, dimensions={0} | all-to-all | bytes 1048576 | tf_op jit(solution)/shard_map/all_to_all | solution.py:633
  29.7 1.0 %collective-permute-start.1 = (bf16[2,2,64,128]{3,2,1,0:T(8,128)(2,1)S(1)}, bf16[2,2,64,128]{3,2,1,0:T(8,128)(2,1)S(1)}, u32[]{:S(2)}, u32[]{:S(2)}) collective-permute-start(bf16[2,2,64,128]{3,2,1,0:T(8,128)(2,1)S(1)} %get-tuple-element.30), channel_id=1, source_target_pairs={{0,1},{1,0},{2,3},{3,2},{4,5},{5,4},{6,7},{7,6},{8,9},{9,8},{10,11... | collective-permute-start | bytes 196616 | tf_op jit(solution)/shard_map/ppermute | solution.py:647
  30.7 1.1 %collective-permute-start.3 = (bf16[2,2,64,128]{3,2,1,0:T(8,128)(2,1)S(1)}, bf16[2,2,64,128]{3,2,1,0:T(8,128)(2,1)S(1)}, u32[]{:S(2)}, u32[]{:S(2)}) collective-permute-start(bf16[2,2,64,128]{3,2,1,0:T(8,128)(2,1)S(1)} %get-tuple-element.34), channel_id=1, source_target_pairs={{0,1},{1,0},{2,3},{3,2},{4,5},{5,4},{6,7},{7,6},{8,9},{9,8},{10,11... | collective-permute-start | bytes 196616 | tf_op jit(solution)/shard_map/ppermute | solution.py:647
  31.8 0.8 %mid.1.stat_ref = f32[4,8,1024]{2,1,0:T(8,128)S(1)} custom-call(s32[44]{0:T(128)S(4)} %plan.1.plan_ref, bf16[4096,128]{1,0:T(8,128)(2,1)S(1)} %bitcast.10, bf16[4096,128]{1,0:T(8,128)(2,1)S(1)} %bitcast.17, f32[4,8,1024]{2,1,0:T(8,128)S(1)} %near.1.stat_ref, bf16[16,2,64,128]{3,2,1,0:T(8,128)(2,1)S(1)} %all_to_all.10.arrived_ref.mine_ref), custom_call_target="tpu_custom_call" | custom-call | tf_op jit(solution)/shard_map/mid/pallas_call | solution.py:572
  32.7 1.8 %collective-permute-done.1.other_ref = bf16[2,2,64,128]{3,2,1,0:T(8,128)(2,1)S(1)} collective-permute-done((bf16[2,2,64,128]{3,2,1,0:T(8,128)(2,1)S(1)}, bf16[2,2,64,128]{3,2,1,0:T(8,128)(2,1)S(1)}, u32[]{:S(2)}, u32[]{:S(2)}) %collective-permute-start.1) | collective-permute-done | bytes 65568 | tf_op jit(solution)/shard_map/ppermute | solution.py:647
  34.5 0.9 %far.2 = (bf16[2,2,64,128]{3,2,1,0:T(8,128)(2,1)S(1)}, f32[2,8,1024]{2,1,0:T(8,128)S(1)}) custom-call(s32[44]{0:T(128)S(4)} %plan.1.plan_ref, bf16[4096,128]{1,0:T(8,128)(2,1)S(1)} %bitcast.11, bf16[4096,128]{1,0:T(8,128)(2,1)S(1)} %bitcast.18, f32[4,8,1024]{2,1,0:T(8,128)S(1)} %mid.1.stat_ref, bf16[2,2,64,128]{3,2,1,0:T(8,128)(2,1)S(1)} %collective-permute-done.1.other_ref), custom_call_target="tpu_custom_call" | custom-call | tf_op jit(solution)/shard_map/far/pallas_call | solution.py:572
  35.4 1.1 %collective-permute-start.2 = (bf16[2,2,64,128]{3,2,1,0:T(8,128)(2,1)S(1)}, bf16[2,2,64,128]{3,2,1,0:T(8,128)(2,1)S(1)}, u32[]{:S(2)}, u32[]{:S(2)}) collective-permute-start(bf16[2,2,64,128]{3,2,1,0:T(8,128)(2,1)S(1)} %get-tuple-element.31), channel_id=1, source_target_pairs={{0,1},{1,0},{2,3},{3,2},{4,5},{5,4},{6,7},{7,6},{8,9},{9,8},{10,11... | collective-permute-start | bytes 196616 | tf_op jit(solution)/shard_map/ppermute | solution.py:657
  36.5 0.9 %far.3 = (bf16[2,2,64,128]{3,2,1,0:T(8,128)(2,1)S(1)}, f32[2,8,1024]{2,1,0:T(8,128)S(1)}) custom-call(s32[44]{0:T(128)S(4)} %plan.1.plan_ref, bf16[4096,128]{1,0:T(8,128)(2,1)S(1)} %bitcast.12, bf16[4096,128]{1,0:T(8,128)(2,1)S(1)} %bitcast.19, f32[4,8,1024]{2,1,0:T(8,128)S(1)} %mid.1.stat_ref, bf16[2,2,64,128]{3,2,1,0:T(8,128)(2,1)S(1)} %collective-permute-done.3.other_ref), custom_call_target="tpu_custom_call" | custom-call | tf_op jit(solution)/shard_map/far/pallas_call | solution.py:572
  37.5 1.0 %collective-permute-start.4 = (bf16[2,2,64,128]{3,2,1,0:T(8,128)(2,1)S(1)}, bf16[2,2,64,128]{3,2,1,0:T(8,128)(2,1)S(1)}, u32[]{:S(2)}, u32[]{:S(2)}) collective-permute-start(bf16[2,2,64,128]{3,2,1,0:T(8,128)(2,1)S(1)} %get-tuple-element.37), channel_id=1, source_target_pairs={{0,1},{1,0},{2,3},{3,2},{4,5},{5,4},{6,7},{7,6},{8,9},{9,8},{10,11... | collective-permute-start | bytes 196616 | tf_op jit(solution)/shard_map/ppermute | solution.py:657
  38.5 0.9 %mine.3.refs_1_ = bf16[2,2,64,128]{3,2,1,0:T(8,128)(2,1)S(1)} custom-call(s32[44]{0:T(128)S(4)} %plan.1.plan_ref, bf16[4096,128]{1,0:T(8,128)(2,1)S(1)} %bitcast.13, bf16[4096,128]{1,0:T(8,128)(2,1)S(1)} %bitcast.20, bf16[16,2,64,128]{3,2,1,0:T(8,128)(2,1)S(1)} %all_to_all.10.arrived_ref.mine_ref, f32[2,8,1024]{2,1,0:T(8,128)S(1)} %get-tuple-element.35.stat_ref), custom_call_target="tpu_custom_call" | custom-call | tf_op jit(solution)/shard_map/mine/pallas_call | solution.py:572
  39.4 0.4 collective-permute-done.2.refs_2_
  39.8 0.9 %mine.2.refs_0_ = bf16[2,2,64,128]{3,2,1,0:T(8,128)(2,1)S(1)} custom-call(s32[44]{0:T(128)S(4)} %plan.1.plan_ref, bf16[4096,128]{1,0:T(8,128)(2,1)S(1)} %bitcast.14, bf16[4096,128]{1,0:T(8,128)(2,1)S(1)} %bitcast.21, bf16[16,2,64,128]{3,2,1,0:T(8,128)(2,1)S(1)} %all_to_all.10.arrived_ref.mine_ref, f32[2,8,1024]{2,1,0:T(8,128)S(1)} %get-tuple-element.33.stat_ref), custom_call_target="tpu_custom_call" | custom-call | tf_op jit(solution)/shard_map/mine/pallas_call | solution.py:572
  40.6 1.2 %collective-permute-done.4.refs_3_ = bf16[2,2,64,128]{3,2,1,0:T(8,128)(2,1)S(1)} collective-permute-done((bf16[2,2,64,128]{3,2,1,0:T(8,128)(2,1)S(1)}, bf16[2,2,64,128]{3,2,1,0:T(8,128)(2,1)S(1)}, u32[]{:S(2)}, u32[]{:S(2)}) %collective-permute-start.4) | collective-permute-done | bytes 65568 | tf_op jit(solution)/shard_map/ppermute | solution.py:657
  41.8 0.8 %return.1 = bf16[16,2,64,128]{3,2,1,0:T(8,128)(2,1)} custom-call(s32[44]{0:T(128)S(4)} %plan.1.plan_ref, bf16[2,2,64,128]{3,2,1,0:T(8,128)(2,1)S(1)} %mine.2.refs_0_, bf16[2,2,64,128]{3,2,1,0:T(8,128)(2,1)S(1)} %mine.3.refs_1_, bf16[2,2,64,128]{3,2,1,0:T(8,128)(2,1)S(1)} %collective-permute-done.2.refs_2_, ...), custom_call_target="tpu_custom_call" | custom-call | tf_op jit(solution)/shard_map/return/pallas_call | solution.py:572
  42.6 4.2 %all-to-all-start.1 = ((bf16[16,2,64,128]{3,2,1,0:T(8,128)(2,1)}), bf16[16,2,64,128]{3,2,1,0:T(8,128)(2,1)S(1)}, u32[]{:S(2)}, u32[]{:S(2)}) async-start(bf16[16,2,64,128]{3,2,1,0:T(8,128)(2,1)} %return.1), calls=%async_computation.1 | async-start | bytes 1048576 | tf_op jit(solution)/shard_map/all_to_all | solution.py:675
  46.8 0.9 %copy-done.4 = bf16[128,4,128]{2,1,0:T(4,128)(2,1)S(1)} copy-done((bf16[128,4,128]{2,1,0:T(4,128)(2,1)S(1)}, bf16[128,4,128]{2,1,0:T(4,128)(2,1)}, u32[]{:S(2)}) %copy-start.4) | copy-done | bytes 131096
  47.7 0.1 copy-done.5
  47.8 6.9 %local.1 = (bf16[4096,128]{1,0:T(8,128)(2,1)}, bf16[4096,128]{1,0:T(8,128)(2,1)}, f32[512,128]{1,0:T(8,128)S(1)}, f32[512,128]{1,0:T(8,128)S(1)}) custom-call(s32[44]{0:T(128)S(4)} %plan.1.plan_ref, bf16[4096,128]{1,0:T(8,128)(2,1)S(1)} %bitcast.15, bf16[4096,128]{1,0:T(8,128)(2,1)S(1)} %bitcast.22, bf16[512,128]{1,0:T(8,128)(2,1)S(1)} %bitcast.24, ...), custom_call_target="tpu_custom_call" | custom-call | tf_op jit(solution)/shard_map/local/pallas_call | solution.py:681
  54.6 0.7 %copy-done.2 = f32[512,128]{1,0:T(8,128)} copy-done((f32[512,128]{1,0:T(8,128)}, f32[512,128]{1,0:T(8,128)S(1)}, u32[]{:S(2)}) %copy-start.2) | copy-done | bytes 262168
  55.3 5.9 %all-to-all-done.1.landed_ref = bf16[16,2,64,128]{3,2,1,0:T(8,128)(2,1)S(1)} async-done(((bf16[16,2,64,128]{3,2,1,0:T(8,128)(2,1)}), bf16[16,2,64,128]{3,2,1,0:T(8,128)(2,1)S(1)}, u32[]{:S(2)}, u32[]{:S(2)}) %all-to-all-start.1) | async-done | bytes 524320 | tf_op jit(solution)/shard_map/all_to_all | solution.py:675
  61.3 0.2 land_sibling.1
  61.4 1.1 %collective-permute-start.5 = (bf16[4,2,64,128]{3,2,1,0:T(8,128)(2,1)S(1)}, bf16[4,2,64,128]{3,2,1,0:T(8,128)(2,1)S(1)}, u32[]{:S(2)}, u32[]{:S(2)}) collective-permute-start(bf16[4,2,64,128]{3,2,1,0:T(8,128)(2,1)S(1)} %land_sibling.1), channel_id=1, source_target_pairs={{0,1},{1,0},{2,3},{3,2},{4,5},{5,4},{6,7},{7,6},{8,9},{9,8},{10,11... | collective-permute-start | bytes 393224 | tf_op jit(solution)/shard_map/ppermute | solution.py:703
  62.6 0.3 land_own.1.own_ref
  62.9 4.0 %collective-permute-done.5.back_ref = bf16[4,2,64,128]{3,2,1,0:T(8,128)(2,1)S(1)} collective-permute-done((bf16[4,2,64,128]{3,2,1,0:T(8,128)(2,1)S(1)}, bf16[4,2,64,128]{3,2,1,0:T(8,128)(2,1)S(1)}, u32[]{:S(2)}, u32[]{:S(2)}) %collective-permute-start.5) | collective-permute-done | bytes 131104 | tf_op jit(solution)/shard_map/ppermute | solution.py:703
  66.9 0.9 %finish.1 = (bf16[512,128]{1,0:T(8,128)(2,1)}, bf16[512,128]{1,0:T(8,128)(2,1)}) custom-call(f32[512,128]{1,0:T(8,128)S(1)} %get-tuple-element.43.dk_near_ref, f32[512,128]{1,0:T(8,128)S(1)} %copy-done.3, bf16[4,2,64,128]{3,2,1,0:T(8,128)(2,1)S(1)} %land_own.1.own_ref, bf16[4,2,64,128]{3,2,1,0:T(8,128)(2,1)S(1)} %collective-permute-done.5.back_ref), custom_call_target="tpu_custom_call" | custom-call | tf_op jit(solution)/shard_map/finish/pallas_call | solution.py:572
  (12 shorter events, 0.1 us)
Async XLA Ops:
  1.9 7.3 %collective-permute-start = (bf16[4,2,64,128]{3,2,1,0:T(8,128)(2,1)S(1)}, bf16[4,2,64,128]{3,2,1,0:T(8,128)(2,1)S(1)}, u32[]{:S(2)}, u32[]{:S(2)}) collective-permute-start(bf16[4,2,64,128]{3,2,1,0:T(8,128)(2,1)S(1)} %get-tuple-element.26.given_ref), channel_id=1, source_target_pairs={{0,1},{1,0},{2,3},{3,2},{4,5},{5,4},{6,7},{7,6},{8,9},{9,8},{10,11... | collective-permute-start | bytes 393224 | tf_op jit(solution)/shard_map/ppermute | solution.py:612
  9.2 22.6 %copy-start.1 = (bf16[128,32,128]{2,1,0:T(8,128)(2,1)S(1)}, bf16[128,32,128]{2,1,0:T(8,128)(2,1)}, u32[]{:S(2)}) copy-start(bf16[128,32,128]{2,1,0:T(8,128)(2,1)} %param.9) | copy-start | bytes 3145732
  9.4 22.4 %copy-start = (bf16[128,32,128]{2,1,0:T(8,128)(2,1)S(1)}, bf16[128,32,128]{2,1,0:T(8,128)(2,1)}, u32[]{:S(2)}) copy-start(bf16[128,32,128]{2,1,0:T(8,128)(2,1)} %param.6) | copy-start | bytes 3145732
  29.7 4.8 %collective-permute-start.1 = (bf16[2,2,64,128]{3,2,1,0:T(8,128)(2,1)S(1)}, bf16[2,2,64,128]{3,2,1,0:T(8,128)(2,1)S(1)}, u32[]{:S(2)}, u32[]{:S(2)}) collective-permute-start(bf16[2,2,64,128]{3,2,1,0:T(8,128)(2,1)S(1)} %get-tuple-element.30), channel_id=1, source_target_pairs={{0,1},{1,0},{2,3},{3,2},{4,5},{5,4},{6,7},{7,6},{8,9},{9,8},{10,11... | collective-permute-start | bytes 196616 | tf_op jit(solution)/shard_map/ppermute | solution.py:647
  30.7 5.8 %collective-permute-start.3 = (bf16[2,2,64,128]{3,2,1,0:T(8,128)(2,1)S(1)}, bf16[2,2,64,128]{3,2,1,0:T(8,128)(2,1)S(1)}, u32[]{:S(2)}, u32[]{:S(2)}) collective-permute-start(bf16[2,2,64,128]{3,2,1,0:T(8,128)(2,1)S(1)} %get-tuple-element.34), channel_id=1, source_target_pairs={{0,1},{1,0},{2,3},{3,2},{4,5},{5,4},{6,7},{7,6},{8,9},{9,8},{10,11... | collective-permute-start | bytes 196616 | tf_op jit(solution)/shard_map/ppermute | solution.py:647
  35.4 4.3 %collective-permute-start.2 = (bf16[2,2,64,128]{3,2,1,0:T(8,128)(2,1)S(1)}, bf16[2,2,64,128]{3,2,1,0:T(8,128)(2,1)S(1)}, u32[]{:S(2)}, u32[]{:S(2)}) collective-permute-start(bf16[2,2,64,128]{3,2,1,0:T(8,128)(2,1)S(1)} %get-tuple-element.31), channel_id=1, source_target_pairs={{0,1},{1,0},{2,3},{3,2},{4,5},{5,4},{6,7},{7,6},{8,9},{9,8},{10,11... | collective-permute-start | bytes 196616 | tf_op jit(solution)/shard_map/ppermute | solution.py:657
  37.5 4.3 %collective-permute-start.4 = (bf16[2,2,64,128]{3,2,1,0:T(8,128)(2,1)S(1)}, bf16[2,2,64,128]{3,2,1,0:T(8,128)(2,1)S(1)}, u32[]{:S(2)}, u32[]{:S(2)}) collective-permute-start(bf16[2,2,64,128]{3,2,1,0:T(8,128)(2,1)S(1)} %get-tuple-element.37), channel_id=1, source_target_pairs={{0,1},{1,0},{2,3},{3,2},{4,5},{5,4},{6,7},{7,6},{8,9},{9,8},{10,11... | collective-permute-start | bytes 196616 | tf_op jit(solution)/shard_map/ppermute | solution.py:657
  42.6 18.7 %all-to-all-start.1 = ((bf16[16,2,64,128]{3,2,1,0:T(8,128)(2,1)}), bf16[16,2,64,128]{3,2,1,0:T(8,128)(2,1)S(1)}, u32[]{:S(2)}, u32[]{:S(2)}) async-start(bf16[16,2,64,128]{3,2,1,0:T(8,128)(2,1)} %return.1), calls=%async_computation.1 | async-start | bytes 1048576 | tf_op jit(solution)/shard_map/all_to_all | solution.py:675
  46.8 0.9 %copy-start.4 = (bf16[128,4,128]{2,1,0:T(4,128)(2,1)S(1)}, bf16[128,4,128]{2,1,0:T(4,128)(2,1)}, u32[]{:S(2)}) copy-start(bf16[128,4,128]{2,1,0:T(4,128)(2,1)} %param.7) | copy-start | bytes 393220
  46.8 1.0 %copy-start.5 = (bf16[128,4,128]{2,1,0:T(4,128)(2,1)S(1)}, bf16[128,4,128]{2,1,0:T(4,128)(2,1)}, u32[]{:S(2)}) copy-start(bf16[128,4,128]{2,1,0:T(4,128)(2,1)} %param.8) | copy-start | bytes 393220
  54.6 0.7 %copy-start.2 = (f32[512,128]{1,0:T(8,128)}, f32[512,128]{1,0:T(8,128)S(1)}, u32[]{:S(2)}) copy-start(f32[512,128]{1,0:T(8,128)S(1)} %get-tuple-element.44.dv_near_ref) | copy-start | bytes 786436
  61.3 1.3 %copy-start.3 = (f32[512,128]{1,0:T(8,128)S(1)}, f32[512,128]{1,0:T(8,128)}, u32[]{:S(2)}) copy-start(f32[512,128]{1,0:T(8,128)} %copy-done.2) | copy-start | bytes 786436
  61.4 5.5 %collective-permute-start.5 = (bf16[4,2,64,128]{3,2,1,0:T(8,128)(2,1)S(1)}, bf16[4,2,64,128]{3,2,1,0:T(8,128)(2,1)S(1)}, u32[]{:S(2)}, u32[]{:S(2)}) collective-permute-start(bf16[4,2,64,128]{3,2,1,0:T(8,128)(2,1)S(1)} %land_sibling.1), channel_id=1, source_target_pairs={{0,1},{1,0},{2,3},{3,2},{4,5},{5,4},{6,7},{7,6},{8,9},{9,8},{10,11... | collective-permute-start | bytes 393224 | tf_op jit(solution)/shard_map/ppermute | solution.py:703
